TPU v7x, 32 devices: a whole 2x2x4 slice. The times are simulated.
32 devices in a mesh: groups: 2 (over y), ctx: 4 (over z), fsdp: 2 (over x), head: 2 (over core).
Axes of the slice: x: 2, y: 2, z: 4, core: 2. Of those that a mesh axis runs over, the one named last changes fastest.
Arguments:
- tokens: bfloat16 [4096, 3072], P(('groups', 'ctx')), parts along dimension 0, may hold values from -6 to 6
- query_weight: bfloat16 [3072, 4096], P('ctx', ('fsdp', 'head')), may hold values from -0.109375 to 0.109375
- key_weight: bfloat16 [3072, 4096], P('ctx', ('fsdp', 'head')), may hold values from -0.109375 to 0.109375
- value_weight: bfloat16 [3072, 4096], P('ctx', ('fsdp', 'head')), may hold values from -0.109375 to 0.109375
- log_decay: float32 [32, 4096], P(('fsdp', 'head'), ('groups', 'ctx')), parts along dimension 1, may hold values from -1 to 0
Outputs:
- attended: bfloat16 [4096, 4096], P(('groups', 'ctx'), ('fsdp', 'head')), parts along dimension 0
There are 2 independent parts, one for each index of `groups`. A program takes and returns all parts, laid end to end along the dimension named above; an argument that names none is the same for every part. Nothing has to cross between parts.
All inputs are finite; a program needn't handle non-finite values.
Results may differ from a plain program's by a relative error of at most 0.008.
Values may be sent and summed in bfloat16 or wider, within the bound.
No kernel may reach another device: no remote copies, remote signals or barrier semaphores. Data moves between devices by JAX's collectives and lax.ppermute only.
A program may use at most 128 MiB of HBM per device.

v0:
```python
import jax
import jax.numpy as jnp
from jax import lax
from jax.sharding import PartitionSpec as P

EPSILON = 1e-06


def prefix(shard, axis, join, neutral):
    place = lax.axis_index(axis)
    gathered = jax.tree.map(
        lambda a, kind: lax.all_gather(a.astype(kind), axis), shard, (jnp.bfloat16, jnp.bfloat16)
    )
    state = jax.tree.map(lambda a, e: jnp.zeros_like(a) + jnp.asarray(e, a.dtype), shard, neutral)

    def one(turn, state):
        return join(
            state,
            jax.tree.map(
                lambda a, own: lax.dynamic_index_in_dim(a, turn, 0, False).astype(own.dtype),
                gathered,
                shard,
            ),
        )

    return lax.fori_loop(0, place, one, state)


def row_folder(tokens):

    def accumulate(running, portions, offset):
        return tuple(
            (jnp.dot(tokens, portion, preferred_element_type=jnp.float32) for portion in portions)
        )

    return accumulate


def combine_states(earlier, later):
    return (earlier[0] + later[0], jnp.exp(later[0])[:, None, None] * earlier[1] + later[1])


def local_summary(key_rows, value_rows, cumulative):
    heads_here, row_count = cumulative.shape
    head_size = key_rows.shape[1] // heads_here
    to_end = jnp.exp(cumulative[:, -1:] - cumulative)
    scaled = (
        key_rows.reshape(row_count, heads_here, head_size).astype(jnp.float32)
        * to_end.T[:, :, None]
    ).astype(jnp.bfloat16)
    valueset = value_rows.reshape(row_count, heads_here, head_size)
    return jnp.einsum("khd,khe->hde", scaled, valueset, preferred_element_type=jnp.float32)


def carried(total_decay, own_state):
    identity = (jnp.zeros_like(total_decay), jnp.zeros_like(own_state))
    return prefix((total_decay, own_state), "ctx", combine_states, identity)


def attend(query_rows, key_rows, value_rows, cumulative, incoming):
    heads_here, row_count = cumulative.shape
    head_size = query_rows.shape[1] // heads_here
    block_rows = min(row_count, 512)
    queries = query_rows.reshape(row_count, heads_here, head_size)
    keyset = key_rows.reshape(row_count, heads_here, head_size)
    valueset = value_rows.reshape(row_count, heads_here, head_size)
    incoming_bf = incoming.astype(jnp.bfloat16)
    key_index = jnp.arange(row_count)

    def one_block(block_index):
        first_row = block_index * block_rows
        query_index = first_row + jnp.arange(block_rows)
        scores = jnp.einsum("qhd,khd->hqk", queries, keyset, preferred_element_type=jnp.float32)
        causal = key_index[None, :] <= query_index[:, None]
        decay_gaps = jnp.where(
            causal[None], cumulative[:, :, None] - cumulative[:, None, :], -jnp.inf
        )
        weights = (scores * jnp.exp(decay_gaps)).astype(jnp.bfloat16)
        within_part = jnp.einsum(
            "hqk,khe->qhe", weights, valueset, preferred_element_type=jnp.float32
        )
        carried_part = (
            jnp.einsum("qhd,hde->qhe", queries, incoming_bf, preferred_element_type=jnp.float32)
            * jnp.exp(cumulative).T[:, :, None]
        )
        raw_out = within_part + carried_part
        inverse_rms = lax.rsqrt(jnp.mean(raw_out * raw_out, axis=-1, keepdims=True) + EPSILON)
        return (raw_out * inverse_rms).astype(jnp.bfloat16)

    blocks = lax.map(one_block, jnp.arange(row_count // block_rows))
    return blocks.reshape(row_count, heads_here * head_size)


def body(tokens, query_weight, key_weight, value_weight, log_decay):
    row_count = tokens.shape[0]
    zero_rows = jnp.zeros((row_count, query_weight.shape[1]), jnp.float32)
    accumulate = row_folder(tokens)
    cumulative = jnp.cumsum(log_decay, axis=1)
    total_decay = cumulative[:, -1]
    query_sum, key_sum, value_sum = accumulate(
        (zero_rows, zero_rows, zero_rows),
        (
            lax.all_gather(query_weight, "ctx", axis=0, tiled=True),
            lax.all_gather(key_weight, "ctx", axis=0, tiled=True),
            lax.all_gather(value_weight, "ctx", axis=0, tiled=True),
        ),
        jnp.int32(0),
    )
    query_rows = jax.nn.silu(query_sum).astype(jnp.bfloat16)
    key_rows = jax.nn.silu(key_sum).astype(jnp.bfloat16)
    value_rows = value_sum.astype(jnp.bfloat16)
    incoming = carried(total_decay, local_summary(key_rows, value_rows, cumulative))[1]
    return attend(query_rows, key_rows, value_rows, cumulative, incoming)


def solution(mesh):
    return jax.shard_map(
        body,
        mesh=mesh,
        in_specs=(
            P(("groups", "ctx"), None),
            P("ctx", ("fsdp", "head")),
            P("ctx", ("fsdp", "head")),
            P("ctx", ("fsdp", "head")),
            P(("fsdp", "head"), ("groups", "ctx")),
        ),
        out_specs=P(("groups", "ctx"), ("fsdp", "head")),
        check_vma=False,
    )
```

profile of v0, /device:TPU:0, one launch (start us, length us, event | category | flops | bytes accessed | tf_op | source)
XLA Modules:
  0.0 408.4 jit_solution(6005550997467748737)
XLA Ops:
  6.5 0.0 copy-start
  6.5 0.0 copy-start.2
  6.5 0.0 all-gather.11.cloned.1.call-start
  6.5 0.7 all-gather.11.cloned.1.call-update
  7.3 0.0 all-gather.7.cloned.1.call-start
  7.3 0.7 all-gather.7.cloned.1.call-update
  8.0 0.0 all-gather.9.cloned.1.call-start
  8.1 0.7 all-gather.9.cloned.1.call-update
  8.7 0.0 all-gather.13.cloned.1.call-start
  8.8 0.0 copy-done.2
  8.8 1.1 reduce-window.6
  10.0 0.2 slice_reduce_fusion
  10.1 0.1 exponential_bitcast_fusion.1
  10.2 0.2 slice_reduce_fusion.1
  10.4 0.1 exponential_bitcast_fusion.2
  10.5 116.5 %all-gather.11.cloned.1.call-done = bf16[3072,1024]{1,0:T(8,128)(2,1)} async-done(((bf16[768,1024]{1,0:T(8,128)(2,1)}), bf16[3072,1024]{1,0:T(8,128)(2,1)}) %all-gather.11.cloned.1.call-update) | async-done | bytes 6291472 | tf_op jit(solution)/shard_map/all_gather | solution.py:104
  127.0 0.0 copy-done
  127.0 7.4 %multiply_convert_fusion.4 = bf16[512,1024]{1,0:T(8,128)(2,1)} fusion(bf16[512,3072]{1,0:T(8,128)(2,1)S(1)} %copy-done, bf16[3072,1024]{1,0:T(8,128)(2,1)} %all-gather.11.cloned.1.call-done), kind=kOutput, calls=%fused_computation.14 | convolution fusion | flops 3223846912 | bytes 10485760 | tf_op jit(solution)/shard_map/dot_general | solution.py:33
  134.4 2.4 copy.39
  136.8 105.4 %all-gather.7.cloned.1.call-done = bf16[3072,1024]{1,0:T(8,128)(2,1)} async-done(((bf16[768,1024]{1,0:T(8,128)(2,1)}), bf16[3072,1024]{1,0:T(8,128)(2,1)}) %all-gather.7.cloned.1.call-update) | async-done | bytes 6291472 | tf_op jit(solution)/shard_map/all_gather | solution.py:105
  242.2 0.0 copy-start.1
  242.2 6.3 %fusion.8 = bf16[64,8,8,128]{3,2,1,0:T(8,128)(2,1)S(1)} fusion(bf16[512,3072]{1,0:T(8,128)(2,1)S(1)} %copy-done, bf16[3072,1024]{1,0:T(8,128)(2,1)} %all-gather.7.cloned.1.call-done), kind=kOutput, calls=%fused_computation.17 | convolution fusion | flops 3221749760 | bytes 10485760 | tf_op jit(solution)/shard_map/dot_general | solution.py:33
  248.5 0.0 copy-start.4
  248.5 0.0 copy-start.3
  248.5 1.0 copy-done.4
  249.5 0.0 copy-done.1
  249.5 1.2 convolution_convert_fusion.1
  250.7 0.0 all-gather.13.cloned.1.call-update
  250.7 0.0 copy-done.3
  250.7 0.6 dynamic-slice
  252.0 0.2 fusion.23
  252.1 0.2 dynamic-update-slice
  252.4 8.9 %all-reduce = bf16[32]{0:T(256)(128)(2,1)S(1)} all-reduce(bf16[32]{0:T(256)(128)(2,1)S(1)} %dynamic-update-slice), channel_id=2, replica_groups=mesh['groups'=2,'ctx'=4,'fsdp'=2,'head'=2] {'ctx'}, use_global_device_ids=true, to_apply=%add | all-reduce | flops 32 | bytes 128
  261.3 0.1 reshape.104
  261.4 0.1 iota_compare_fusion
  261.5 96.1 %all-gather.9.cloned.1.call-done = bf16[3072,1024]{1,0:T(8,128)(2,1)} async-done(((bf16[768,1024]{1,0:T(8,128)(2,1)}), bf16[3072,1024]{1,0:T(8,128)(2,1)}) %all-gather.9.cloned.1.call-update) | async-done | bytes 6291472 | tf_op jit(solution)/shard_map/all_gather | solution.py:103
  357.6 7.4 %fusion.16 = bf16[64,8,8,128]{3,2,1,0:T(8,128)(2,1)} fusion(bf16[512,3072]{1,0:T(8,128)(2,1)S(1)} %copy-done, bf16[3072,1024]{1,0:T(8,128)(2,1)} %all-gather.9.cloned.1.call-done), kind=kOutput, calls=%fused_computation.26 | convolution fusion | flops 3223846912 | bytes 10485760 | tf_op jit(solution)/shard_map/dot_general | solution.py:33
  365.0 20.3 %all-gather.13.cloned.1.call-done = bf16[32,128,128]{2,1,0:T(8,128)(2,1)} async-done(((bf16[8,128,128]{2,1,0:T(8,128)(2,1)}), bf16[32,128,128]{2,1,0:T(8,128)(2,1)}) %all-gather.13.cloned.1.call-update) | async-done | bytes 1048592 | tf_op jit(solution)/shard_map/all_gather | solution.py:12
  385.3 0.8 broadcast_in_dim.42
  386.1 3.2 fusion.9
  389.3 7.4 %multiply_reduce_fusion = (f32[512,8]{0,1:T(8,128)S(1)}, f32[512,8,128]{0,2,1:T(8,128)}) fusion(f32[512,8]{0,1:T(8,128)S(1)} %get-tuple-element.84, f32[8,128,512]{2,1,0:T(8,128)} %fusion.9, f32[8,512]{1,0:T(8,128)S(1)} %get-tuple-element.85, pred[512,512]{1,0:T(8,128)(4,1)S(1)} %iota_compare_fusion, bf16[512,8,128]{0,2,1:T(8,128)(2,1)} %bitcast.55, ...), kind=kOutput, calls=%fused_computation.12 | convolution fusion | flops 1084223488 | bytes 7651328 | tf_op jit(solution)/shard_map/while/body/eval_jaxpr/hqk,khe->qhe/dot_general | solution.py:79
  396.8 2.9 multiply_convert_fusion.2
  399.6 2.3 copy.37
  (5 shorter events, 0.1 us)
Async XLA Ops:
  6.5 120.5 %copy-start = (bf16[512,3072]{1,0:T(8,128)(2,1)S(1)}, bf16[512,3072]{1,0:T(8,128)(2,1)}, u32[]{:S(2)}) copy-start(bf16[512,3072]{1,0:T(8,128)(2,1)} %param.7) | copy-start | bytes 9437188
  6.5 2.3 copy-start.2
  6.5 120.5 %all-gather.11.cloned.1.call-start = ((), (), s32[]{:S(2)}) async-start(), calls=%async_computation.2 | async-start | bytes 7864320 | tf_op jit(solution)/shard_map/all_gather | solution.py:104
  7.3 234.9 %all-gather.7.cloned.1.call-start = ((), (), s32[]{:S(2)}) async-start(), calls=%async_computation | async-start | bytes 7864320 | tf_op jit(solution)/shard_map/all_gather | solution.py:105
  8.0 349.6 %all-gather.9.cloned.1.call-start = ((), (), s32[]{:S(2)}) async-start(), calls=%async_computation.1 | async-start | bytes 7864320 | tf_op jit(solution)/shard_map/all_gather | solution.py:103
  8.7 376.5 %all-gather.13.cloned.1.call-start = ((), (), s32[]{:S(2)}) async-start(), calls=%async_computation.3 | async-start | bytes 1310720 | tf_op jit(solution)/shard_map/all_gather | solution.py:12
  242.2 7.3 %copy-start.1 = (bf16[512,1024]{0,1:T(8,128)(2,1)S(1)}, bf16[512,1024]{0,1:T(8,128)(2,1)}, u32[]{:S(2)}) copy-start(bf16[512,1024]{0,1:T(8,128)(2,1)} %copy.39) | copy-start | bytes 3145732
  248.5 1.0 copy-start.4
  248.5 2.2 copy-start.3
Sparse Core Ops, SparseCore 0:
  8.9 118.0 all-gather.10
  128.6 113.5 all-gather.6
  243.8 113.7 all-gather.8
  359.0 26.2 all-gather.12
where the time goes:
time: 412 us; the launch traced here: 408 us
  waiting for transfers between devices  340 us (83%)
  matrix products  32.9 us (8%)
  between operations  13.8 us (3%)
  blocking collectives  8.94 us (2%)
  local copies, waits for them, and re-layouts  7.96 us (2%)
  other arithmetic  4.31 us (1%)
    all_gather x1, waiting for transfers between devices, body(): lax.all_gather(key_weight, 'ctx', axis=0, tiled=True)  117 us
    all_gather x1, waiting for transfers between devices, body(): lax.all_gather(value_weight, 'ctx', axis=0, tiled=True)  105 us
    all_gather x1, waiting for transfers between devices, body(): lax.all_gather(query_weight, 'ctx', axis=0, tiled=True)  96.1 us
    dot_general x3, matrix products, accumulate(): jnp.dot(tokens, portion, preferred_element_type=jnp.float32)  21.1 us
    all_gather x1, waiting for transfers between devices, prefix(): lax.all_gather(a.astype(kind), axis)  20.3 us
    unnamed x1, blocking collectives  8.94 us
  transfers between devices with their start and end apart: 4, of which 4 were waited for; matrix products, arithmetic and copies ran while one was open for 7% of the time, Pallas kernels for 0%

commit v1 on v0

--- a/solution.py
+++ b/solution.py
@@ -1,6 +1,9 @@
+import functools
 import jax
 import jax.numpy as jnp
 from jax import lax
+from jax.experimental import pallas as pl
+from jax.experimental.pallas import tpu as pltpu
 from jax.sharding import PartitionSpec as P
 
 EPSILON = 1e-06
@@ -113,9 +116,338 @@
     return attend(query_rows, key_rows, value_rows, cumulative, incoming)
 
 
+SIDES = ("own", "ctx", "groups", "both")
+
+
+def xor_permute(array, mesh, axis, flip):
+    return lax.ppermute(array, axis, [(at, at ^ flip) for at in range(mesh.shape[axis])])
+
+
+def after(array, *earlier):
+    return lax.optimization_barrier((array, *earlier))[0]
+
+
+def silu(rows):
+    return rows / (1.0 + jnp.exp(-rows))
+
+
+def project(places, token_refs, weight_refs, accumulators, step):
+    for flip in range(len(weight_refs)):
+
+        @pl.when(step == flip)
+        def _(flip=flip):
+            weight = jnp.concatenate(
+                [
+                    jnp.concatenate([half[...] for half in halves], axis=0)
+                    for halves in weight_refs[flip]
+                ],
+                axis=1,
+            )
+            for token_ref, accumulator in zip(token_refs, accumulators):
+                product = jnp.dot(token_ref[...], weight, preferred_element_type=jnp.float32)
+                if flip == 0:
+                    accumulator[...] = product
+                else:
+                    accumulator[...] += product
+
+
+def column_of(row, width):
+    return jnp.transpose(jnp.broadcast_to(row, (width, row.shape[1])))
+
+
+def key_value_kernel(heads, size, parts, places, *refs):
+    sides = len(SIDES)
+    token_refs, refs = refs[:sides], refs[sides:]
+    decay_refs, refs = refs[:sides], refs[sides:]
+    flips = parts[0]
+    count = flips * 2 * heads * 2
+    flat, refs = refs[:count], refs[count:]
+    weight_refs = [
+        [[flat[(flip * 2 * heads + block) * 2 + half] for half in range(2)] for block in range(2 * heads)]
+        for flip in range(flips)
+    ]
+    key_refs, refs = refs[:sides], refs[sides:]
+    value_refs, refs = refs[:sides], refs[sides:]
+    state_ref, refs = refs[0], refs[1:]
+    accumulators = refs
+    step = pl.program_id(0)
+    project(places, token_refs, weight_refs, accumulators, step)
+
+    @pl.when(step == flips - 1)
+    def _():
+        for side in range(sides):
+            for head in range(heads):
+                at = 2 * head * size
+                key = silu(accumulators[side][:, at : at + size]).astype(jnp.bfloat16)
+                value = accumulators[side][:, at + size : at + 2 * size].astype(jnp.bfloat16)
+                row = decay_refs[side][head : head + 1, :]
+                column = column_of(row, size)
+                to_end = jnp.exp(column[-1:, :] - column)
+                scaled = (key.astype(jnp.float32) * to_end).astype(jnp.bfloat16)
+                state_ref[head, side] = lax.dot_general(
+                    scaled, value, (((0,), (0,)), ((), ())), preferred_element_type=jnp.float32
+                )
+                key_refs[side][:, head * size : (head + 1) * size] = key
+                value_refs[side][:, head * size : (head + 1) * size] = value
+
+
+def query_kernel(heads, size, parts, places, *refs):
+    sides = len(SIDES)
+    token_refs, refs = refs[:sides], refs[sides:]
+    decay_refs, refs = refs[:sides], refs[sides:]
+    flips, head = parts
+    count = flips * 2
+    flat, refs = refs[:count], refs[count:]
+    weight_refs = [[[flat[flip * 2 + half] for half in range(2)]] for flip in range(flips)]
+    key_refs, refs = refs[:sides], refs[sides:]
+    value_refs, refs = refs[:sides], refs[sides:]
+    incoming_ref, refs = refs[0], refs[1:]
+    out_refs, accumulators = refs[:sides], refs[sides:]
+    step = pl.program_id(0)
+    project(places, token_refs, weight_refs, accumulators, step)
+
+    @pl.when(step == flips - 1)
+    def _():
+        rows = token_refs[0].shape[0]
+        causal = lax.broadcasted_iota(jnp.int32, (rows, rows), 1) <= lax.broadcasted_iota(
+            jnp.int32, (rows, rows), 0
+        )
+        for side in range(sides):
+            query = silu(accumulators[side][...]).astype(jnp.bfloat16)
+            key, value = key_refs[side][...], value_refs[side][...]
+            row = decay_refs[side][head : head + 1, :]
+            column = column_of(row, size)
+            wide = jnp.concatenate([column] * (rows // size), axis=1)
+            scores = lax.dot_general(
+                query, key, (((1,), (1,)), ((), ())), preferred_element_type=jnp.float32
+            )
+            weights = (scores * jnp.exp(jnp.where(causal, wide - row, -jnp.inf))).astype(jnp.bfloat16)
+            raw = jnp.dot(weights, value, preferred_element_type=jnp.float32)
+            raw += jnp.exp(column) * jnp.dot(
+                query, incoming_ref[side], preferred_element_type=jnp.float32
+            )
+            scale = lax.rsqrt(jnp.mean(raw * raw, axis=1, keepdims=True) + EPSILON)
+            out_refs[side][...] = (raw * scale).astype(jnp.bfloat16)
+
+
+def merge_kernel(heads, size, place, *refs):
+    pieces, out_ref = refs[:-1], refs[-1]
+    for side in range(len(SIDES)):
+        for head in range(heads):
+            at = pl.multiple_of(((place[0] ^ side) * heads + head) * size, size)
+            out_ref[:, pl.ds(at, size)] = pieces[side * heads + head][...]
+
+
+def whole(shape):
+    return pl.BlockSpec(shape, lambda step, places: (0,) * len(shape))
+
+
+def spread_body(mesh, tokens, query_weight, key_weight, value_weight, log_decay):
+    rows, width = tokens.shape
+    depth = query_weight.shape[0]
+    heads_here = log_decay.shape[0]
+    size = query_weight.shape[1] // heads_here
+    flips = mesh.shape["ctx"]
+    shares = mesh.shape["fsdp"] * mesh.shape["head"]
+    heads = heads_here // 4
+    group, turn = lax.axis_index("groups"), lax.axis_index("ctx")
+    share = lax.axis_index("fsdp") * 2 + lax.axis_index("head")
+    mine = group * 2 + turn % 2
+    half_rows = depth // 2
+
+    blocks = [(weight, head) for head in range(heads) for weight in (key_weight, value_weight)]
+    blocks += [(query_weight, head) for head in range(heads)]
+
+    def stacked(owner, first, last):
+        cut = []
+        for half in range(first, last):
+            weight, head = blocks[half // 2]
+            cut.append(
+                lax.dynamic_slice(
+                    weight,
+                    ((half % 2) * half_rows, (owner * heads + head) * size),
+                    (half_rows, size),
+                )
+            )
+        return jnp.concatenate(cut, axis=0)
+
+    bounds = [0] + list(range(1, 2 * len(blocks), 2)) + [2 * len(blocks)]
+    chunks = []
+    for number, (first, last) in enumerate(zip(bounds[:-1], bounds[1:])):
+        kept, sent = stacked(mine, first, last), stacked(mine ^ 1, first, last)
+        if number >= 2:
+            kept, sent = lax.optimization_barrier((kept, sent, *chunks[number - 2][1:]))[:2]
+        chunks.append(
+            [kept] + [xor_permute(sent if flip % 2 else kept, mesh, "ctx", flip) for flip in range(1, flips)]
+        )
+
+    quarter_width = width // shares
+
+    def quarter(at):
+        return lax.dynamic_slice(tokens, (0, at * quarter_width), (rows, quarter_width))
+
+    def over_cores(first, second):
+        return jnp.concatenate(
+            [first, xor_permute(first, mesh, "head", 1), second, xor_permute(second, mesh, "head", 1)],
+            axis=1,
+        )
+
+    from_ctx = xor_permute(quarter(share), mesh, "ctx", 1)
+    from_groups = [xor_permute(quarter(share ^ flip), mesh, "groups", 1) for flip in (0, 2)]
+    from_both = xor_permute(from_ctx, mesh, "groups", 1)
+    token_sets = [
+        tokens,
+        over_cores(from_ctx, xor_permute(from_ctx, mesh, "fsdp", 1)),
+        over_cores(*from_groups),
+        over_cores(from_both, xor_permute(from_both, mesh, "fsdp", 1)),
+    ]
+    places = jnp.stack([turn, turn ^ share]).astype(jnp.int32)
+
+    cumulative = jnp.cumsum(log_decay, axis=1)
+    ctx_decay = xor_permute(cumulative, mesh, "ctx", 1)
+    decays = [
+        lax.dynamic_slice(array, (mine * heads, 0), (heads, rows))
+        for array in (
+            cumulative,
+            ctx_decay,
+            xor_permute(cumulative, mesh, "groups", 1),
+            xor_permute(ctx_decay, mesh, "groups", 1),
+        )
+    ]
+
+    def token_spec(side):
+        kind = 0 if side == 0 else 1
+        return pl.BlockSpec((rows, depth), lambda step, places: (0, places[kind] ^ step))
+
+    def weight_operands(wanted):
+        arrays, specs = [], []
+        for flip in range(flips):
+            for block in wanted:
+                for half in (2 * block, 2 * block + 1):
+                    number = (half + 1) // 2
+                    offset = half - bounds[number]
+                    arrays.append(chunks[number][flip])
+                    specs.append(
+                        pl.BlockSpec((half_rows, size), lambda step, places, offset=offset: (offset, 0))
+                    )
+        return arrays, specs
+
+    sides = len(SIDES)
+    token_specs = [token_spec(side) for side in range(sides)]
+    decay_specs = [whole((heads, rows))] * sides
+    params = pltpu.CompilerParams(vmem_limit_bytes=56 * 1024 * 1024)
+    arrays, specs = weight_operands(range(2 * heads))
+    results = pl.pallas_call(
+        functools.partial(key_value_kernel, heads, size, (flips,)),
+        grid_spec=pltpu.PrefetchScalarGridSpec(
+            num_scalar_prefetch=1,
+            grid=(flips,),
+            in_specs=token_specs + decay_specs + specs,
+            out_specs=[whole((rows, heads * size))] * (2 * sides) + [whole((heads, sides, size, size))],
+            scratch_shapes=[pltpu.VMEM((rows, 2 * heads * size), jnp.float32)] * sides,
+        ),
+        out_shape=[jax.ShapeDtypeStruct((rows, heads * size), jnp.bfloat16)] * (2 * sides)
+        + [jax.ShapeDtypeStruct((heads, sides, size, size), jnp.float32)],
+        compiler_params=params,
+        cost_estimate=pl.CostEstimate(
+            flops=2 * sides * rows * width * 2 * heads * size,
+            bytes_accessed=2 * (sides * rows * width + width * 2 * heads * size),
+            transcendentals=sides * rows * 2 * heads * size,
+        ),
+        name="key_value",
+    )(places, *token_sets, *decays, *arrays)
+    keys, values, states = results[:sides], results[sides : 2 * sides], results[2 * sides]
+
+    totals = jnp.stack([decay[:, -1] for decay in decays], axis=1)
+    fresh = states.reshape(heads, 2, 2, size, size)
+    total = totals.reshape(heads, 2, 2)
+    fade = jnp.exp(total)[..., None, None]
+    odd = turn % 2 == 1
+    first_fresh = jnp.where(odd, fresh[:, :, 1], fresh[:, :, 0])
+    last_fresh = jnp.where(odd, fresh[:, :, 0], fresh[:, :, 1])
+    first_fade = jnp.where(odd, fade[:, :, 1], fade[:, :, 0])
+    last_fade = jnp.where(odd, fade[:, :, 0], fade[:, :, 1])
+    pair_state = (last_fade * first_fresh + last_fresh).astype(jnp.bfloat16)
+    before = lax.ppermute(pair_state, "ctx", [(0, 2), (1, 3)]).astype(jnp.float32)
+    between = first_fade * before + first_fresh
+    incoming = jnp.stack(
+        [jnp.where(odd, between, before), jnp.where(odd, before, between)], axis=2
+    ).reshape(heads, sides, size, size).astype(jnp.bfloat16)
+
+    pieces = [[] for _ in SIDES]
+    both = [
+        (at, (at // flips ^ 1) * flips + (at % flips ^ 1)) for at in range(mesh.shape["groups"] * flips)
+    ]
+    for head in range(heads):
+        arrays, specs = weight_operands([2 * heads + head])
+        head_spec = pl.BlockSpec((rows, size), lambda step, places, head=head: (0, head))
+        attended = pl.pallas_call(
+            functools.partial(query_kernel, heads, size, (flips, head)),
+            grid_spec=pltpu.PrefetchScalarGridSpec(
+                num_scalar_prefetch=1,
+                grid=(flips,),
+                in_specs=token_specs
+                + decay_specs
+                + specs
+                + [head_spec] * (2 * sides)
+                + [whole((sides, size, size))],
+                out_specs=[whole((rows, size))] * sides,
+                scratch_shapes=[pltpu.VMEM((rows, size), jnp.float32)] * sides,
+            ),
+            out_shape=[jax.ShapeDtypeStruct((rows, size), jnp.bfloat16)] * sides,
+            compiler_params=params,
+            cost_estimate=pl.CostEstimate(
+                flops=2 * sides * rows * size * (width + 2 * rows + size),
+                bytes_accessed=2 * (sides * rows * width + width * size),
+                transcendentals=sides * rows * (rows + 2 * size),
+            ),
+            name="query",
+        )(places, *token_sets, *decays, *arrays, *keys, *values, incoming[head])
+        pieces[0].append(attended[0])
+        pieces[1].append(xor_permute(attended[1], mesh, "ctx", 1))
+        pieces[2].append(xor_permute(attended[2], mesh, "groups", 1))
+        pieces[3].append(lax.ppermute(attended[3], ("groups", "ctx"), both))
+
+    flat = [piece for side in pieces for piece in side]
+    return pl.pallas_call(
+        functools.partial(merge_kernel, heads, size),
+        grid_spec=pltpu.PrefetchScalarGridSpec(
+            num_scalar_prefetch=1,
+            grid=(1,),
+            in_specs=[whole((rows, size))] * len(flat),
+            out_specs=whole((rows, heads_here * size)),
+        ),
+        out_shape=jax.ShapeDtypeStruct((rows, heads_here * size), jnp.bfloat16),
+        name="merge",
+    )(mine[None].astype(jnp.int32), *flat)
+
+
+def spreads(mesh, tokens, query_weight, key_weight, value_weight, log_decay):
+    sizes = tuple(mesh.shape[axis] for axis in ("groups", "ctx", "fsdp", "head"))
+    if sizes != (2, 4, 2, 2):
+        return False
+    heads_here = log_decay.shape[0]
+    depth = query_weight.shape[0]
+    size = query_weight.shape[1] // heads_here
+    return (
+        heads_here % 4 == 0
+        and size == 128
+        and depth % 256 == 0
+        and depth * 4 == tokens.shape[1]
+        and tokens.shape[0] % 128 == 0
+        and tokens.shape[0] <= 512
+    )
+
+
+def local_body(mesh, *arrays):
+    if spreads(mesh, *arrays):
+        return spread_body(mesh, *arrays)
+    return body(*arrays)
+
+
 def solution(mesh):
     return jax.shard_map(
-        body,
+        functools.partial(local_body, mesh),
         mesh=mesh,
         in_specs=(
             P(("groups", "ctx"), None),

time: 412 us -> 234 us (0.57)
  waiting for transfers between devices: 340 us -> 108 us
  starting transfers between devices: 0.12 us -> 48.6 us
  Pallas kernels: 0 us -> 37.4 us
  matrix products: 32.9 us -> 0 us
  local copies, waits for them, and re-layouts: 7.96 us -> 25.9 us
  between operations: 13.8 us -> 0.59 us
  blocking collectives: 8.94 us -> 0 us
  other arithmetic: 4.31 us -> 12.2 us
    all_gather x4 -> x0, waiting for transfers between devices: 338 us -> none  [the longest x1 117 us: body(): lax.all_gather(key_weight, 'ctx', axis=0, tiled=True)]
    ppermute x0 -> x43, waiting for transfers between devices: none -> 108 us  [the longest x40 108 us: xor_permute(): lax.ppermute(array, axis, [(at, at ^ flip) for at in range(mesh.shape[axi...]
    ppermute x0 -> x43, starting transfers between devices: none -> 48.6 us  [the longest x40 44.1 us: xor_permute(): lax.ppermute(array, axis, [(at, at ^ flip) for at in range(mesh.shape[axi...]
    pallas_call x0 -> x4, Pallas kernels: none -> 37.4 us  [the longest x2 21.6 us: spread_body(): pl.pallas_call(functools.partial(query_kernel, heads, size, (flips, head)...]
    dot_general x6 -> x0, matrix products: 32.9 us -> none  [the longest x3 21.1 us: accumulate(): jnp.dot(tokens, portion, preferred_element_type=jnp.float32)]
    unnamed x13 -> x93, local copies, waits for them, and re-layouts: 1.84 us -> 12.6 us
    dynamic_slice x0 -> x7, local copies, waits for them, and re-layouts: none -> 10.5 us  [the longest x4 4.55 us: spread_body(): lax.dynamic_slice(array, (mine * heads, 0), (heads, rows))]
    unnamed x1 -> x0, blocking collectives: 8.94 us -> none
  transfers between devices with their start and end apart: 4 -> 43, of which waited for: 4 -> 15; matrix products, arithmetic and copies ran while one was open for 7% -> 13% of each run, Pallas kernels for 0% -> 9%
where the time goes in v1:
time: 234 us; the launch traced here: 233 us
  waiting for transfers between devices  108 us (46%)
  starting transfers between devices  48.6 us (21%)
  Pallas kernels  37.4 us (16%)
  local copies, waits for them, and re-layouts  25.9 us (11%)
  other arithmetic  12.2 us (5%)
    ppermute x40, waiting for transfers between devices, xor_permute(): lax.ppermute(array, axis, [(at, at ^ flip) for at in range(mesh.shape[axi...  108 us
    ppermute x40, starting transfers between devices, xor_permute(): lax.ppermute(array, axis, [(at, at ^ flip) for at in range(mesh.shape[axi...  44.1 us
    pallas_call x2, Pallas kernels, spread_body(): pl.pallas_call(functools.partial(query_kernel, heads, size, (flips, head)...  21.6 us
    pallas_call x1, Pallas kernels, spread_body(): pl.pallas_call(functools.partial(key_value_kernel, heads, size, (flips,))...  13.3 us
    unnamed x93, local copies, waits for them, and re-layouts  12.6 us
    concatenate x10, other arithmetic, stacked(): return jnp.concatenate(cut, axis=0)  7.08 us
  transfers between devices with their start and end apart: 43, of which 15 were waited for; matrix products, arithmetic and copies ran while one was open for 13% of the time, Pallas kernels for 9%

profile of v1, /device:TPU:0, one launch (start us, length us, event | category | flops | bytes accessed | tf_op | source)
XLA Modules:
  0.0 232.8 jit_solution(8202286018735042039)
XLA Ops:
  0.0 2.2 reduce-window.6
  2.5 3.0 %collective-permute-start.12 = (f32[8,512]{1,0:T(8,128)S(1)}, f32[8,512]{1,0:T(8,128)S(1)}, u32[]{:S(2)}, u32[]{:S(2)}) collective-permute-start(f32[8,512]{1,0:T(8,128)S(1)} %add_bitcast_fusion), channel_id=1, source_target_pairs={{0,4},{4,0},{8,12},{12,8},{1,5},{5,1},{9,13},{13,9},{2,6},{6,2},{1... | collective-permute-start | bytes 49160 | tf_op jit(solution)/shard_map/ppermute | solution.py:123
  5.5 1.5 collective-permute-start.13
  7.0 1.5 constant_dynamic-slice_fusion.16
  9.0 2.0 constant_dynamic-slice_fusion.20
  11.1 1.6 collective-permute-start.15
  12.6 2.5 %collective-permute-start.17 = (bf16[384,128]{1,0:T(8,128)(2,1)}, bf16[384,128]{1,0:T(8,128)(2,1)}, u32[]{:S(2)}, u32[]{:S(2)}) collective-permute-start(bf16[384,128]{1,0:T(8,128)(2,1)} %get-tuple-element.77), channel_id=1, source_target_pairs={{0,12},{4,8},{8,4},{12,0},{1,13},{5,9},{9,5},{13,1},{2,14},{6,10},... | collective-permute-start | bytes 294920 | tf_op jit(solution)/shard_map/ppermute | solution.py:123
  15.1 2.4 %constant_dynamic-slice_fusion = (bf16[384,128]{1,0:T(8,128)(2,1)}, bf16[384,128]{1,0:T(8,128)(2,1)}, bf16[384,128]{1,0:T(8,128)(2,1)}, bf16[384,128]{1,0:T(8,12...) fusion(bf16[768,1024]{1,0:T(8,128)(2,1)} %param.8, ...), kind=kLoop, calls=%fused_computation.42 | loop fusion | bytes 3145744 | tf_op jit(solution)/shard_map/dynamic_slice | solution.py:266
  17.5 0.7 pad_maximum_fusion.1
  18.3 0.7 pad_maximum_fusion.2.refs_11_.refs_12_
  19.0 0.7 pad_maximum_fusion.3
  21.0 2.4 %collective-permute-done.14 = f32[8,512]{1,0:T(8,128)S(1)} collective-permute-done((f32[8,512]{1,0:T(8,128)S(1)}, f32[8,512]{1,0:T(8,128)S(1)}, u32[]{:S(2)}, u32[]{:S(2)}) %collective-permute-start.14) | collective-permute-done | bytes 16416 | tf_op jit(solution)/shard_map/ppermute | solution.py:123
  24.1 8.1 %collective-permute-done = bf16[512,768]{1,0:T(8,128)(2,1)S(1)} collective-permute-done((bf16[512,768]{1,0:T(8,128)(2,1)S(1)}, bf16[512,768]{1,0:T(8,128)(2,1)S(1)}, u32[]{:S(2)}, u32[]{:S(2)}) %collective-permute-start) | collective-permute-done | bytes 786464 | tf_op jit(solution)/shard_map/ppermute | solution.py:123
  32.7 1.0 pad_maximum_fusion.9.refs_9_.refs_10_
  33.7 1.8 collective-permute-done.15.refs_16_
  36.0 2.8 %collective-permute-start.23 = (bf16[768,128]{1,0:T(8,128)(2,1)}, bf16[768,128]{1,0:T(8,128)(2,1)}, u32[]{:S(2)}, u32[]{:S(2)}) collective-permute-start(bf16[768,128]{1,0:T(8,128)(2,1)} %pad_maximum_fusion.8), channel_id=1, source_target_pairs={{0,12},{4,8},{8,4},{12,0},{1,13},{5,9},{9,5},{13,1},{2,14},{6,10},... | collective-permute-start | bytes 589832 | tf_op jit(solution)/shard_map/ppermute | solution.py:123
  39.4 1.6 pad_maximum_fusion.6.refs_13_.refs_14_
  41.1 1.0 collective-permute-start.18
  42.0 1.6 pad_maximum_fusion.7
  43.7 10.2 %collective-permute-done.22.refs_25_.refs_26_ = bf16[768,128]{1,0:T(8,128)(2,1)S(1)} collective-permute-done((bf16[768,128]{1,0:T(8,128)(2,1)S(1)}, bf16[768,128]{1,0:T(8,128)(2,1)S(1)}, u32[]{:S(2)}, u32[]{:S(2)}) %collective-permute-start.22) | collective-permute-done | bytes 196640 | tf_op jit(solution)/shard_map/ppermute | solution.py:123
  55.7 0.7 collective-permute-start.20
  57.1 10.7 %collective-permute-done.19.refs_27_.refs_28_ = bf16[768,128]{1,0:T(8,128)(2,1)S(1)} collective-permute-done((bf16[768,128]{1,0:T(8,128)(2,1)}, bf16[768,128]{1,0:T(8,128)(2,1)S(1)}, u32[]{:S(2)}, u32[]{:S(2)}) %collective-permute-start.19) | collective-permute-done | bytes 196640 | tf_op jit(solution)/shard_map/ppermute | solution.py:123
  67.8 1.3 constant_dynamic-slice_fusion.14.refs_5_
  69.2 1.5 collective-permute-start.2
  70.7 1.3 constant_dynamic-slice_fusion.13.refs_6_
  72.0 0.8 dynamic-slice.2
  72.7 0.8 dynamic-slice.1
  74.0 1.3 constant_dynamic-slice_fusion.12.refs_7_
  75.3 0.8 dynamic-slice.3
  76.4 4.6 %collective-permute-done.6 = bf16[512,768]{1,0:T(8,128)(2,1)} collective-permute-done((bf16[512,768]{1,0:T(8,128)(2,1)S(1)}, bf16[512,768]{1,0:T(8,128)(2,1)}, u32[]{:S(2)}, u32[]{:S(2)}) %collective-permute-start.6) | collective-permute-done | bytes 786464 | tf_op jit(solution)/shard_map/ppermute | solution.py:123
  81.1 1.3 constant_dynamic-update-slice_fusion.7
  83.1 6.5 %collective-permute-done.2 = bf16[512,768]{1,0:T(8,128)(2,1)} collective-permute-done((bf16[512,768]{1,0:T(8,128)(2,1)S(1)}, bf16[512,768]{1,0:T(8,128)(2,1)}, u32[]{:S(2)}, u32[]{:S(2)}) %collective-permute-start.2) | collective-permute-done | bytes 786464 | tf_op jit(solution)/shard_map/ppermute | solution.py:123
  89.6 1.2 constant_dynamic-update-slice_fusion.2
  90.8 15.2 %collective-permute-done.10 = bf16[512,768]{1,0:T(8,128)(2,1)} collective-permute-done((bf16[512,768]{1,0:T(8,128)(2,1)S(1)}, bf16[512,768]{1,0:T(8,128)(2,1)}, u32[]{:S(2)}, u32[]{:S(2)}) %collective-permute-start.10) | collective-permute-done | bytes 786464 | tf_op jit(solution)/shard_map/ppermute | solution.py:123
  106.1 1.2 constant_dynamic-update-slice_fusion.1
  107.3 1.1 collective-permute-start.24
  108.4 1.2 constant_dynamic-update-slice_fusion.6
  109.6 1.3 constant_dynamic-update-slice_fusion.5
  110.9 3.4 %collective-permute-start.26 = (bf16[768,128]{1,0:T(8,128)(2,1)S(1)}, bf16[768,128]{1,0:T(8,128)(2,1)S(1)}, u32[]{:S(2)}, u32[]{:S(2)}) collective-permute-start(bf16[768,128]{1,0:T(8,128)(2,1)S(1)} %copy-done.18), channel_id=1, source_target_pairs={{0,12},{4,8},{8,4},{12,0},{1,13},{5,9},{9,5},{13,1},{2,14},{6,10},... | collective-permute-start | bytes 589832 | tf_op jit(solution)/shard_map/ppermute | solution.py:123
  114.6 1.8 constant_dynamic-update-slice_fusion.9
  117.0 3.4 %collective-permute-start.31 = (bf16[768,128]{1,0:T(8,128)(2,1)S(1)}, bf16[768,128]{1,0:T(8,128)(2,1)S(1)}, u32[]{:S(2)}, u32[]{:S(2)}) collective-permute-start(bf16[768,128]{1,0:T(8,128)(2,1)S(1)} %copy-done.15), channel_id=1, source_target_pairs={{0,12},{4,8},{8,4},{12,0},{1,13},{5,9},{9,5},{13,1},{2,14},{6,10},... | collective-permute-start | bytes 589832 | tf_op jit(solution)/shard_map/ppermute | solution.py:123
  120.6 19.6 %collective-permute-done.25.refs_29_.refs_30_ = bf16[768,128]{1,0:T(8,128)(2,1)S(1)} collective-permute-done((bf16[768,128]{1,0:T(8,128)(2,1)S(1)}, bf16[768,128]{1,0:T(8,128)(2,1)S(1)}, u32[]{:S(2)}, u32[]{:S(2)}) %collective-permute-start.25) | collective-permute-done | bytes 196640 | tf_op jit(solution)/shard_map/ppermute | solution.py:123
  140.3 7.7 %collective-permute-done.29.refs_31_.refs_12_ = bf16[768,128]{1,0:T(8,128)(2,1)S(1)} collective-permute-done((bf16[768,128]{1,0:T(8,128)(2,1)S(1)}, bf16[768,128]{1,0:T(8,128)(2,1)S(1)}, u32[]{:S(2)}, u32[]{:S(2)}) %collective-permute-start.29) | collective-permute-done | bytes 196640 | tf_op jit(solution)/shard_map/ppermute | solution.py:123
  149.3 13.3 %key_value.1 = (bf16[512,256]{1,0:T(8,128)(2,1)}, bf16[512,256]{1,0:T(8,128)(2,1)}, bf16[512,256]{1,0:T(8,128)(2,1)}, bf16[512,256]{1,0:T(8,128)(2,1)}, bf16[512...) custom-call(s32[2]{0:T(128)} %pad_add_fusion.places, ...), custom_call_target="tpu_custom_call" | custom-call | flops 6442450944 | bytes 15728640 | tf_op jit(solution)/shard_map/key_value/pallas_call | solution.py:340
  162.7 1.1 fusion.3
  163.8 1.6 collective-permute-start.33
  165.5 3.7 %collective-permute-start.28 = (bf16[768,128]{1,0:T(8,128)(2,1)S(1)}, bf16[768,128]{1,0:T(8,128)(2,1)S(1)}, u32[]{:S(2)}, u32[]{:S(2)}) collective-permute-start(bf16[768,128]{1,0:T(8,128)(2,1)S(1)} %pad_maximum_fusion.5), channel_id=1, source_target_pairs={{0,4},{4,0},{8,12},{12,8},{1,5},{5,1},{9,13},{13,9},{2,6},{6,2},{1... | collective-permute-start | bytes 589832 | tf_op jit(solution)/shard_map/ppermute | solution.py:123
  169.3 1.5 collective-permute-start.30
  170.8 2.8 %collective-permute-start.34 = (bf16[384,128]{1,0:T(8,128)(2,1)S(1)}, bf16[384,128]{1,0:T(8,128)(2,1)S(1)}, u32[]{:S(2)}, u32[]{:S(2)}) collective-permute-start(bf16[384,128]{1,0:T(8,128)(2,1)S(1)} %copy-done.28), channel_id=1, source_target_pairs={{0,4},{4,0},{8,12},{12,8},{1,5},{5,1},{9,13},{13,9},{2,6},{6,2},{1... | collective-permute-start | bytes 294920 | tf_op jit(solution)/shard_map/ppermute | solution.py:123
  173.7 2.0 collective-permute-start.36
  175.8 0.7 pad_maximum_fusion.10
  176.6 1.9 collective-permute-done.28.refs_11_.refs_10_
  178.4 1.6 collective-permute-start.35
  180.1 13.4 %collective-permute-done.30.refs_13_.refs_12_ = bf16[768,128]{1,0:T(8,128)(2,1)S(1)} collective-permute-done((bf16[768,128]{1,0:T(8,128)(2,1)S(1)}, bf16[768,128]{1,0:T(8,128)(2,1)S(1)}, u32[]{:S(2)}, u32[]{:S(2)}) %collective-permute-start.30) | collective-permute-done | bytes 196640 | tf_op jit(solution)/shard_map/ppermute | solution.py:123
  194.2 10.7 %query.2 = (bf16[512,128]{1,0:T(8,128)(2,1)}, bf16[512,128]{1,0:T(8,128)(2,1)}, bf16[512,128]{1,0:T(8,128)(2,1)}, bf16[512,128]{1,0:T(8,128)(2,1)}) custom-call(s32[2]{0:T(128)} %pad_add_fusion.places, bf16[512,3072]{1,0:T(8,128)(2,1)} %refs_0_.5, bf16[512,3072]{1,0:T(8,128)(2,1)} %copy-done.2, bf16[512,3072]{1,0:T(8,128)(2,1)} %copy-done.1, ...), custom_call_target="tpu_custom_call" | custom-call | flops 2214592512 | bytes 13369344 | tf_op jit(solution)/shard_map/query/pallas_call | solution.py:384
  206.2 10.9 %query.3 = (bf16[512,128]{1,0:T(8,128)(2,1)}, bf16[512,128]{1,0:T(8,128)(2,1)}, bf16[512,128]{1,0:T(8,128)(2,1)}, bf16[512,128]{1,0:T(8,128)(2,1)}) custom-call(s32[2]{0:T(128)} %pad_add_fusion.places, bf16[512,3072]{1,0:T(8,128)(2,1)} %refs_0_.5, bf16[512,3072]{1,0:T(8,128)(2,1)} %copy-done.2, bf16[512,3072]{1,0:T(8,128)(2,1)} %copy-done.1, ...), custom_call_target="tpu_custom_call" | custom-call | flops 2214592512 | bytes 13369344 | tf_op jit(solution)/shard_map/query/pallas_call | solution.py:384
  217.1 1.6 collective-permute-start.38
  218.7 1.2 collective-permute-start.39
  219.9 0.8 collective-permute-start.40
  220.7 1.2 collective-permute-start.41
  221.9 1.8 collective-permute-start.42
  223.7 4.4 %collective-permute-done.39.refs_4_ = bf16[512,128]{1,0:T(8,128)(2,1)S(1)} collective-permute-done((bf16[512,128]{1,0:T(8,128)(2,1)S(1)}, bf16[512,128]{1,0:T(8,128)(2,1)S(1)}, u32[]{:S(2)}, u32[]{:S(2)}) %collective-permute-start.39) | collective-permute-done | bytes 131104 | tf_op jit(solution)/shard_map/ppermute | solution.py:123
  228.1 1.4 collective-permute-done.40.refs_5_
  230.3 2.6 %merge.1 = bf16[512,1024]{1,0:T(8,128)(2,1)} custom-call(s32[1]{0:T(128)} %bitcast.place, bf16[512,128]{1,0:T(8,128)(2,1)} %get-tuple-element.49.refs_0_, bf16[512,128]{1,0:T(8,128)(2,1)} %get-tuple-element.52.refs_1_, bf16[512,128]{1,0:T(8,128)(2,1)} %copy-done.19, bf16[512,128]{1,0:T(8,128)(2,1)} %copy-done.20, bf16[512,128]{1,0:T(8,128)(2,1)} %copy-done.21, ...), custom_call_target="tpu_custom_call" | custom-call | tf_op jit(solution)/shard_map/merge/pallas_call | solution.py:412
  (155 shorter events, 13.9 us)
Async XLA Ops:
  2.5 17.2 %collective-permute-start.12 = (f32[8,512]{1,0:T(8,128)S(1)}, f32[8,512]{1,0:T(8,128)S(1)}, u32[]{:S(2)}, u32[]{:S(2)}) collective-permute-start(f32[8,512]{1,0:T(8,128)S(1)} %add_bitcast_fusion), channel_id=1, source_target_pairs={{0,4},{4,0},{8,12},{12,8},{1,5},{5,1},{9,13},{13,9},{2,6},{6,2},{1... | collective-permute-start | bytes 49160 | tf_op jit(solution)/shard_map/ppermute | solution.py:123
  5.5 15.4 %collective-permute-start.13 = (f32[8,512]{1,0:T(8,128)S(1)}, f32[8,512]{1,0:T(8,128)S(1)}, u32[]{:S(2)}, u32[]{:S(2)}) collective-permute-start(f32[8,512]{1,0:T(8,128)S(1)} %add_bitcast_fusion), channel_id=1, source_target_pairs={{0,16},{16,0},{1,17},{17,1},{2,18},{18,2},{3,19},{19,3},{4,20},{20... | collective-permute-start | bytes 49160 | tf_op jit(solution)/shard_map/ppermute | solution.py:123
  8.5 23.7 %collective-permute-start = (bf16[512,768]{1,0:T(8,128)(2,1)S(1)}, bf16[512,768]{1,0:T(8,128)(2,1)S(1)}, u32[]{:S(2)}, u32[]{:S(2)}) collective-permute-start(bf16[512,768]{1,0:T(8,128)(2,1)S(1)} %get-tuple-element.64), channel_id=1, source_target_pairs={{0,4},{4,0},{8,12},{12,8},{1,5},{5,1},{9,13},{13,9},{2,6},{6,2},{1... | collective-permute-start | bytes 2359304 | tf_op jit(solution)/shard_map/ppermute | solution.py:123
  11.1 24.4 %collective-permute-start.15 = (bf16[384,128]{1,0:T(8,128)(2,1)}, bf16[384,128]{1,0:T(8,128)(2,1)}, u32[]{:S(2)}, u32[]{:S(2)}) collective-permute-start(bf16[384,128]{1,0:T(8,128)(2,1)} %get-tuple-element.77), channel_id=1, source_target_pairs={{0,4},{4,0},{8,12},{12,8},{1,5},{5,1},{9,13},{13,9},{2,6},{6,2},{1... | collective-permute-start | bytes 294920 | tf_op jit(solution)/shard_map/ppermute | solution.py:123
  12.6 26.2 %collective-permute-start.17 = (bf16[384,128]{1,0:T(8,128)(2,1)}, bf16[384,128]{1,0:T(8,128)(2,1)}, u32[]{:S(2)}, u32[]{:S(2)}) collective-permute-start(bf16[384,128]{1,0:T(8,128)(2,1)} %get-tuple-element.77), channel_id=1, source_target_pairs={{0,12},{4,8},{8,4},{12,0},{1,13},{5,9},{9,5},{13,1},{2,14},{6,10},... | collective-permute-start | bytes 294920 | tf_op jit(solution)/shard_map/ppermute | solution.py:123
  17.5 160.9 %copy-start.8 = (bf16[384,128]{1,0:T(8,128)(2,1)}, bf16[384,128]{1,0:T(8,128)(2,1)S(1)}, u32[]{:S(2)}) copy-start(bf16[384,128]{1,0:T(8,128)(2,1)S(1)} %get-tuple-element.50.refs_9_) | copy-start | bytes 294916
  17.5 102.8 %copy-start.7 = (bf16[768,128]{1,0:T(8,128)(2,1)}, bf16[768,128]{1,0:T(8,128)(2,1)S(1)}, u32[]{:S(2)}) copy-start(bf16[768,128]{1,0:T(8,128)(2,1)S(1)} %pad_maximum_fusion.refs_15_.refs_8_) | copy-start | bytes 589828
  19.7 3.7 %collective-permute-start.14 = (f32[8,512]{1,0:T(8,128)S(1)}, f32[8,512]{1,0:T(8,128)S(1)}, u32[]{:S(2)}, u32[]{:S(2)}) collective-permute-start(f32[8,512]{1,0:T(8,128)S(1)} %collective-permute-done.12), channel_id=1, source_target_pairs={{0,16},{16,0},{1,17},{17,1},{2,18},{18,2},{3,19},{19,3},{4,20},{20... | collective-permute-start | bytes 49160 | tf_op jit(solution)/shard_map/ppermute | solution.py:123
  20.9 15.1 %collective-permute-start.16 = (bf16[384,128]{1,0:T(8,128)(2,1)}, bf16[384,128]{1,0:T(8,128)(2,1)S(1)}, u32[]{:S(2)}, u32[]{:S(2)}) collective-permute-start(bf16[384,128]{1,0:T(8,128)(2,1)} %get-tuple-element.76.refs_8_), channel_id=1, source_target_pairs={{0,8},{4,12},{8,0},{12,4},{1,9},{5,13},{9,1},{13,5},{2,10},{6,14},... | collective-permute-start | bytes 294920 | tf_op jit(solution)/shard_map/ppermute | solution.py:123
  23.4 17.7 %collective-permute-start.21 = (bf16[768,128]{1,0:T(8,128)(2,1)}, bf16[768,128]{1,0:T(8,128)(2,1)S(1)}, u32[]{:S(2)}, u32[]{:S(2)}) collective-permute-start(bf16[768,128]{1,0:T(8,128)(2,1)} %pad_maximum_fusion.8), channel_id=1, source_target_pairs={{0,4},{4,0},{8,12},{12,8},{1,5},{5,1},{9,13},{13,9},{2,6},{6,2},{1... | collective-permute-start | bytes 589832 | tf_op jit(solution)/shard_map/ppermute | solution.py:123
  32.2 41.3 %collective-permute-start.8 = (bf16[512,768]{1,0:T(8,128)(2,1)S(1)}, bf16[512,768]{1,0:T(8,128)(2,1)S(1)}, u32[]{:S(2)}, u32[]{:S(2)}) collective-permute-start(bf16[512,768]{1,0:T(8,128)(2,1)S(1)} %collective-permute-done), channel_id=1, source_target_pairs={{0,16},{16,0},{1,17},{17,1},{2,18},{18,2},{3,19},{19,3},{4,20},{20... | collective-permute-start | bytes 2359304 | tf_op jit(solution)/shard_map/ppermute | solution.py:123
  33.7 20.2 %copy-start.16 = (bf16[768,128]{1,0:T(8,128)(2,1)}, bf16[768,128]{1,0:T(8,128)(2,1)S(1)}, u32[]{:S(2)}) copy-start(bf16[768,128]{1,0:T(8,128)(2,1)S(1)} %pad_maximum_fusion.9.refs_9_.refs_10_) | copy-start | bytes 589828
  35.5 40.6 %collective-permute-start.4 = (bf16[512,768]{1,0:T(8,128)(2,1)S(1)}, bf16[512,768]{1,0:T(8,128)(2,1)}, u32[]{:S(2)}, u32[]{:S(2)}) collective-permute-start(bf16[512,768]{1,0:T(8,128)(2,1)S(1)} %get-tuple-element.64), channel_id=1, source_target_pairs={{0,16},{16,0},{1,17},{17,1},{2,18},{18,2},{3,19},{19,3},{4,20},{20... | collective-permute-start | bytes 2359304 | tf_op jit(solution)/shard_map/ppermute | solution.py:123
  36.0 19.1 %collective-permute-start.23 = (bf16[768,128]{1,0:T(8,128)(2,1)}, bf16[768,128]{1,0:T(8,128)(2,1)}, u32[]{:S(2)}, u32[]{:S(2)}) collective-permute-start(bf16[768,128]{1,0:T(8,128)(2,1)} %pad_maximum_fusion.8), channel_id=1, source_target_pairs={{0,12},{4,8},{8,4},{12,0},{1,13},{5,9},{9,5},{13,1},{2,14},{6,10},... | collective-permute-start | bytes 589832 | tf_op jit(solution)/shard_map/ppermute | solution.py:123
  38.8 15.0 %collective-permute-start.22 = (bf16[768,128]{1,0:T(8,128)(2,1)S(1)}, bf16[768,128]{1,0:T(8,128)(2,1)S(1)}, u32[]{:S(2)}, u32[]{:S(2)}) collective-permute-start(bf16[768,128]{1,0:T(8,128)(2,1)S(1)} %pad_maximum_fusion.9.refs_9_.refs_10_), channel_id=1, source_target_pairs={{0,8},{4,12},{8,0},{12,4},{1,9},{5,13},{9,1},{13,5},{2,10},{6,14},... | collective-permute-start | bytes 589832 | tf_op jit(solution)/shard_map/ppermute | solution.py:123
  41.1 12.8 %copy-start.32 = (bf16[768,128]{1,0:T(8,128)(2,1)}, bf16[768,128]{1,0:T(8,128)(2,1)S(1)}, u32[]{:S(2)}) copy-start(bf16[768,128]{1,0:T(8,128)(2,1)S(1)} %collective-permute-done.21.refs_17_.refs_18_) | copy-start | bytes 589828
  41.1 14.7 %collective-permute-start.18 = (bf16[768,128]{1,0:T(8,128)(2,1)}, bf16[768,128]{1,0:T(8,128)(2,1)}, u32[]{:S(2)}, u32[]{:S(2)}) collective-permute-start(bf16[768,128]{1,0:T(8,128)(2,1)} %pad_maximum_fusion.3), channel_id=1, source_target_pairs={{0,4},{4,0},{8,12},{12,8},{1,5},{5,1},{9,13},{13,9},{2,6},{6,2},{1... | collective-permute-start | bytes 589832 | tf_op jit(solution)/shard_map/ppermute | solution.py:123
  54.5 26.5 %collective-permute-start.6 = (bf16[512,768]{1,0:T(8,128)(2,1)S(1)}, bf16[512,768]{1,0:T(8,128)(2,1)}, u32[]{:S(2)}, u32[]{:S(2)}) collective-permute-start(bf16[512,768]{1,0:T(8,128)(2,1)S(1)} %get-tuple-element.63), channel_id=1, source_target_pairs={{0,16},{16,0},{1,17},{17,1},{2,18},{18,2},{3,19},{19,3},{4,20},{20... | collective-permute-start | bytes 2359304 | tf_op jit(solution)/shard_map/ppermute | solution.py:123
  55.1 12.7 %collective-permute-start.19 = (bf16[768,128]{1,0:T(8,128)(2,1)}, bf16[768,128]{1,0:T(8,128)(2,1)S(1)}, u32[]{:S(2)}, u32[]{:S(2)}) collective-permute-start(bf16[768,128]{1,0:T(8,128)(2,1)} %pad_maximum_fusion.2.refs_11_.refs_12_), channel_id=1, source_target_pairs={{0,8},{4,12},{8,0},{12,4},{1,9},{5,13},{9,1},{13,5},{2,10},{6,14},... | collective-permute-start | bytes 589832 | tf_op jit(solution)/shard_map/ppermute | solution.py:123
  55.7 13.4 %collective-permute-start.20 = (bf16[768,128]{1,0:T(8,128)(2,1)}, bf16[768,128]{1,0:T(8,128)(2,1)S(1)}, u32[]{:S(2)}, u32[]{:S(2)}) collective-permute-start(bf16[768,128]{1,0:T(8,128)(2,1)} %pad_maximum_fusion.3), channel_id=1, source_target_pairs={{0,12},{4,8},{8,4},{12,0},{1,13},{5,9},{9,5},{13,1},{2,14},{6,10},... | collective-permute-start | bytes 589832 | tf_op jit(solution)/shard_map/ppermute | solution.py:123
  67.8 14.6 %collective-permute-start.1 = (bf16[512,768]{1,0:T(8,128)(2,1)S(1)}, bf16[512,768]{1,0:T(8,128)(2,1)}, u32[]{:S(2)}, u32[]{:S(2)}) collective-permute-start(bf16[512,768]{1,0:T(8,128)(2,1)S(1)} %collective-permute-done), channel_id=1, source_target_pairs={{0,1},{1,0},{2,3},{3,2},{4,5},{5,4},{6,7},{7,6},{8,9},{9,8},{10,11... | collective-permute-start | bytes 2359304 | tf_op jit(solution)/shard_map/ppermute | solution.py:123
  69.2 20.4 %collective-permute-start.2 = (bf16[512,768]{1,0:T(8,128)(2,1)S(1)}, bf16[512,768]{1,0:T(8,128)(2,1)}, u32[]{:S(2)}, u32[]{:S(2)}) collective-permute-start(bf16[512,768]{1,0:T(8,128)(2,1)S(1)} %collective-permute-done), channel_id=1, source_target_pairs={{0,2},{2,0},{1,3},{3,1},{4,6},{6,4},{5,7},{7,5},{8,10},{10,8},{9,1... | collective-permute-start | bytes 2359304 | tf_op jit(solution)/shard_map/ppermute | solution.py:123
  73.5 32.6 %collective-permute-start.10 = (bf16[512,768]{1,0:T(8,128)(2,1)S(1)}, bf16[512,768]{1,0:T(8,128)(2,1)}, u32[]{:S(2)}, u32[]{:S(2)}) collective-permute-start(bf16[512,768]{1,0:T(8,128)(2,1)S(1)} %collective-permute-done.8), channel_id=1, source_target_pairs={{0,2},{2,0},{1,3},{3,1},{4,6},{6,4},{5,7},{7,5},{8,10},{10,8},{9,1... | collective-permute-start | bytes 2359304 | tf_op jit(solution)/shard_map/ppermute | solution.py:123
  76.1 31.2 %collective-permute-start.5 = (bf16[512,768]{1,0:T(8,128)(2,1)}, bf16[512,768]{1,0:T(8,128)(2,1)}, u32[]{:S(2)}, u32[]{:S(2)}) collective-permute-start(bf16[512,768]{1,0:T(8,128)(2,1)} %collective-permute-done.4), channel_id=1, source_target_pairs={{0,1},{1,0},{2,3},{3,2},{4,5},{5,4},{6,7},{7,6},{8,9},{9,8},{10,11... | collective-permute-start | bytes 2359304 | tf_op jit(solution)/shard_map/ppermute | solution.py:123
  81.0 29.9 %collective-permute-start.7 = (bf16[512,768]{1,0:T(8,128)(2,1)}, bf16[512,768]{1,0:T(8,128)(2,1)S(1)}, u32[]{:S(2)}, u32[]{:S(2)}) collective-permute-start(bf16[512,768]{1,0:T(8,128)(2,1)} %collective-permute-done.6), channel_id=1, source_target_pairs={{0,1},{1,0},{2,3},{3,2},{4,5},{5,4},{6,7},{7,6},{8,9},{9,8},{10,11... | collective-permute-start | bytes 2359304 | tf_op jit(solution)/shard_map/ppermute | solution.py:123
  81.1 26.2 %copy-start.18 = (bf16[768,128]{1,0:T(8,128)(2,1)S(1)}, bf16[768,128]{1,0:T(8,128)(2,1)}, u32[]{:S(2)}) copy-start(bf16[768,128]{1,0:T(8,128)(2,1)} %pad_maximum_fusion.7) | copy-start | bytes 589828
  82.4 32.0 %collective-permute-start.9 = (bf16[512,768]{1,0:T(8,128)(2,1)S(1)}, bf16[512,768]{1,0:T(8,128)(2,1)S(1)}, u32[]{:S(2)}, u32[]{:S(2)}) collective-permute-start(bf16[512,768]{1,0:T(8,128)(2,1)S(1)} %collective-permute-done.8), channel_id=1, source_target_pairs={{0,1},{1,0},{2,3},{3,2},{4,5},{5,4},{6,7},{7,6},{8,9},{9,8},{10,11... | collective-permute-start | bytes 2359304 | tf_op jit(solution)/shard_map/ppermute | solution.py:123
  89.6 27.4 %collective-permute-start.3 = (bf16[512,768]{1,0:T(8,128)(2,1)}, bf16[512,768]{1,0:T(8,128)(2,1)S(1)}, u32[]{:S(2)}, u32[]{:S(2)}) collective-permute-start(bf16[512,768]{1,0:T(8,128)(2,1)} %collective-permute-done.2), channel_id=1, source_target_pairs={{0,1},{1,0},{2,3},{3,2},{4,5},{5,4},{6,7},{7,6},{8,9},{9,8},{10,11... | collective-permute-start | bytes 2359304 | tf_op jit(solution)/shard_map/ppermute | solution.py:123
  90.8 23.6 %copy-start.17 = (bf16[768,128]{1,0:T(8,128)(2,1)S(1)}, bf16[768,128]{1,0:T(8,128)(2,1)}, u32[]{:S(2)}) copy-start(bf16[768,128]{1,0:T(8,128)(2,1)} %pad_maximum_fusion.6.refs_13_.refs_14_) | copy-start | bytes 589828
  106.1 14.3 %collective-permute-start.11 = (bf16[512,768]{1,0:T(8,128)(2,1)}, bf16[512,768]{1,0:T(8,128)(2,1)S(1)}, u32[]{:S(2)}, u32[]{:S(2)}) collective-permute-start(bf16[512,768]{1,0:T(8,128)(2,1)} %collective-permute-done.10), channel_id=1, source_target_pairs={{0,1},{1,0},{2,3},{3,2},{4,5},{5,4},{6,7},{7,6},{8,9},{9,8},{10,11... | collective-permute-start | bytes 2359304 | tf_op jit(solution)/shard_map/ppermute | solution.py:123
  107.3 9.1 %collective-permute-start.24 = (bf16[768,128]{1,0:T(8,128)(2,1)S(1)}, bf16[768,128]{1,0:T(8,128)(2,1)S(1)}, u32[]{:S(2)}, u32[]{:S(2)}) collective-permute-start(bf16[768,128]{1,0:T(8,128)(2,1)S(1)} %copy-done.18), channel_id=1, source_target_pairs={{0,4},{4,0},{8,12},{12,8},{1,5},{5,1},{9,13},{13,9},{2,6},{6,2},{1... | collective-permute-start | bytes 589832 | tf_op jit(solution)/shard_map/ppermute | solution.py:123
  110.9 29.4 %collective-permute-start.26 = (bf16[768,128]{1,0:T(8,128)(2,1)S(1)}, bf16[768,128]{1,0:T(8,128)(2,1)S(1)}, u32[]{:S(2)}, u32[]{:S(2)}) collective-permute-start(bf16[768,128]{1,0:T(8,128)(2,1)S(1)} %copy-done.18), channel_id=1, source_target_pairs={{0,12},{4,8},{8,4},{12,0},{1,13},{5,9},{9,5},{13,1},{2,14},{6,10},... | collective-permute-start | bytes 589832 | tf_op jit(solution)/shard_map/ppermute | solution.py:123
  114.5 25.8 %collective-permute-start.25 = (bf16[768,128]{1,0:T(8,128)(2,1)S(1)}, bf16[768,128]{1,0:T(8,128)(2,1)S(1)}, u32[]{:S(2)}, u32[]{:S(2)}) collective-permute-start(bf16[768,128]{1,0:T(8,128)(2,1)S(1)} %copy-done.17), channel_id=1, source_target_pairs={{0,8},{4,12},{8,0},{12,4},{1,9},{5,13},{9,1},{13,5},{2,10},{6,14},... | collective-permute-start | bytes 589832 | tf_op jit(solution)/shard_map/ppermute | solution.py:123
  116.5 31.5 %copy-start.36 = (bf16[768,128]{1,0:T(8,128)(2,1)}, bf16[768,128]{1,0:T(8,128)(2,1)S(1)}, u32[]{:S(2)}) copy-start(bf16[768,128]{1,0:T(8,128)(2,1)S(1)} %collective-permute-done.24.refs_21_.refs_22_) | copy-start | bytes 589828
  116.5 23.8 %collective-permute-start.27 = (bf16[768,128]{1,0:T(8,128)(2,1)S(1)}, bf16[768,128]{1,0:T(8,128)(2,1)S(1)}, u32[]{:S(2)}, u32[]{:S(2)}) collective-permute-start(bf16[768,128]{1,0:T(8,128)(2,1)S(1)} %copy-done.15), channel_id=1, source_target_pairs={{0,4},{4,0},{8,12},{12,8},{1,5},{5,1},{9,13},{13,9},{2,6},{6,2},{1... | collective-permute-start | bytes 589832 | tf_op jit(solution)/shard_map/ppermute | solution.py:123
  117.0 31.0 %collective-permute-start.31 = (bf16[768,128]{1,0:T(8,128)(2,1)S(1)}, bf16[768,128]{1,0:T(8,128)(2,1)S(1)}, u32[]{:S(2)}, u32[]{:S(2)}) collective-permute-start(bf16[768,128]{1,0:T(8,128)(2,1)S(1)} %copy-done.15), channel_id=1, source_target_pairs={{0,12},{4,8},{8,4},{12,0},{1,13},{5,9},{9,5},{13,1},{2,14},{6,10},... | collective-permute-start | bytes 589832 | tf_op jit(solution)/shard_map/ppermute | solution.py:123
  120.4 27.6 %collective-permute-start.29 = (bf16[768,128]{1,0:T(8,128)(2,1)S(1)}, bf16[768,128]{1,0:T(8,128)(2,1)S(1)}, u32[]{:S(2)}, u32[]{:S(2)}) collective-permute-start(bf16[768,128]{1,0:T(8,128)(2,1)S(1)} %pad_maximum_fusion.refs_15_.refs_8_), channel_id=1, source_target_pairs={{0,8},{4,12},{8,0},{12,4},{1,9},{5,13},{9,1},{13,5},{2,10},{6,14},... | collective-permute-start | bytes 589832 | tf_op jit(solution)/shard_map/ppermute | solution.py:123
  120.5 19.8 %copy-start.2 = (bf16[512,3072]{1,0:T(8,128)(2,1)}, bf16[512,3072]{1,0:T(8,128)(2,1)S(1)}, u32[]{:S(2)}) copy-start(bf16[512,3072]{1,0:T(8,128)(2,1)S(1)} %constant_dynamic-update-slice_fusion.refs_1_) | copy-start | bytes 9437188
  120.6 27.4 %copy-start = (bf16[512,3072]{1,0:T(8,128)(2,1)}, bf16[512,3072]{1,0:T(8,128)(2,1)S(1)}, u32[]{:S(2)}) copy-start(bf16[512,3072]{1,0:T(8,128)(2,1)S(1)} %constant_dynamic-update-slice_fusion.8.refs_3_) | copy-start | bytes 9437188
  120.6 44.9 %copy-start.10 = (bf16[384,128]{1,0:T(8,128)(2,1)S(1)}, bf16[384,128]{1,0:T(8,128)(2,1)}, u32[]{:S(2)}) copy-start(bf16[384,128]{1,0:T(8,128)(2,1)} %get-tuple-element.96) | copy-start | bytes 294916
  120.6 44.9 %copy-start.11 = (bf16[384,128]{1,0:T(8,128)(2,1)S(1)}, bf16[384,128]{1,0:T(8,128)(2,1)}, u32[]{:S(2)}) copy-start(bf16[384,128]{1,0:T(8,128)(2,1)} %get-tuple-element.97) | copy-start | bytes 294916
  120.6 44.9 %copy-start.9 = (bf16[384,128]{1,0:T(8,128)(2,1)S(1)}, bf16[384,128]{1,0:T(8,128)(2,1)}, u32[]{:S(2)}) copy-start(bf16[384,128]{1,0:T(8,128)(2,1)} %get-tuple-element.99) | copy-start | bytes 294916
  120.6 50.2 %copy-start.28 = (bf16[384,128]{1,0:T(8,128)(2,1)S(1)}, bf16[384,128]{1,0:T(8,128)(2,1)}, u32[]{:S(2)}) copy-start(bf16[384,128]{1,0:T(8,128)(2,1)} %get-tuple-element.51) | copy-start | bytes 294916
  140.2 7.8 %copy-start.38 = (bf16[768,128]{1,0:T(8,128)(2,1)}, bf16[768,128]{1,0:T(8,128)(2,1)S(1)}, u32[]{:S(2)}) copy-start(bf16[768,128]{1,0:T(8,128)(2,1)S(1)} %collective-permute-done.25.refs_29_.refs_30_) | copy-start | bytes 589828
  140.2 7.7 %copy-start.37 = (bf16[768,128]{1,0:T(8,128)(2,1)}, bf16[768,128]{1,0:T(8,128)(2,1)S(1)}, u32[]{:S(2)}) copy-start(bf16[768,128]{1,0:T(8,128)(2,1)S(1)} %collective-permute-done.26.refs_37_.refs_38_) | copy-start | bytes 589828
  140.3 7.7 %copy-start.12 = (bf16[768,128]{1,0:T(8,128)(2,1)}, bf16[768,128]{1,0:T(8,128)(2,1)S(1)}, u32[]{:S(2)}) copy-start(bf16[768,128]{1,0:T(8,128)(2,1)S(1)} %collective-permute-done.27.refs_23_.refs_10_) | copy-start | bytes 589828
  163.8 9.9 %collective-permute-start.33 = (bf16[2,2,128,128]{3,2,1,0:T(8,128)(2,1)S(1)}, bf16[2,2,128,128]{3,2,1,0:T(8,128)(2,1)S(1)}, u32[]{:S(2)}, u32[]{:S(2)}) collective-permute-start(bf16[2,2,128,128]{3,2,1,0:T(8,128)(2,1)S(1)} %get-tuple-element.61), channel_id=1, source_target_pairs={{0,8},{4,12},{1,9},{5,13},{2,10},{6,14},{3,11},{7,15},{16,24},{20,... | collective-permute-start | bytes 393224 | tf_op jit(solution)/shard_map/ppermute | solution.py:371
  165.5 28.0 %copy-start.3 = (bf16[768,128]{1,0:T(8,128)(2,1)}, bf16[768,128]{1,0:T(8,128)(2,1)S(1)}, u32[]{:S(2)}) copy-start(bf16[768,128]{1,0:T(8,128)(2,1)S(1)} %pad_maximum_fusion.4.refs_9_.refs_8_) | copy-start | bytes 589828
  165.5 12.9 %collective-permute-start.28 = (bf16[768,128]{1,0:T(8,128)(2,1)S(1)}, bf16[768,128]{1,0:T(8,128)(2,1)S(1)}, u32[]{:S(2)}, u32[]{:S(2)}) collective-permute-start(bf16[768,128]{1,0:T(8,128)(2,1)S(1)} %pad_maximum_fusion.5), channel_id=1, source_target_pairs={{0,4},{4,0},{8,12},{12,8},{1,5},{5,1},{9,13},{13,9},{2,6},{6,2},{1... | collective-permute-start | bytes 589832 | tf_op jit(solution)/shard_map/ppermute | solution.py:123
  169.3 24.2 %collective-permute-start.32 = (bf16[768,128]{1,0:T(8,128)(2,1)S(1)}, bf16[768,128]{1,0:T(8,128)(2,1)S(1)}, u32[]{:S(2)}, u32[]{:S(2)}) collective-permute-start(bf16[768,128]{1,0:T(8,128)(2,1)S(1)} %pad_maximum_fusion.5), channel_id=1, source_target_pairs={{0,12},{4,8},{8,4},{12,0},{1,13},{5,9},{9,5},{13,1},{2,14},{6,10},... | collective-permute-start | bytes 589832 | tf_op jit(solution)/shard_map/ppermute | solution.py:123
  169.3 24.2 %collective-permute-start.30 = (bf16[768,128]{1,0:T(8,128)(2,1)S(1)}, bf16[768,128]{1,0:T(8,128)(2,1)S(1)}, u32[]{:S(2)}, u32[]{:S(2)}) collective-permute-start(bf16[768,128]{1,0:T(8,128)(2,1)S(1)} %pad_maximum_fusion.4.refs_9_.refs_8_), channel_id=1, source_target_pairs={{0,8},{4,12},{8,0},{12,4},{1,9},{5,13},{9,1},{13,5},{2,10},{6,14},... | collective-permute-start | bytes 589832 | tf_op jit(solution)/shard_map/ppermute | solution.py:123
  170.8 34.7 %collective-permute-start.34 = (bf16[384,128]{1,0:T(8,128)(2,1)S(1)}, bf16[384,128]{1,0:T(8,128)(2,1)S(1)}, u32[]{:S(2)}, u32[]{:S(2)}) collective-permute-start(bf16[384,128]{1,0:T(8,128)(2,1)S(1)} %copy-done.28), channel_id=1, source_target_pairs={{0,4},{4,0},{8,12},{12,8},{1,5},{5,1},{9,13},{13,9},{2,6},{6,2},{1... | collective-permute-start | bytes 294920 | tf_op jit(solution)/shard_map/ppermute | solution.py:123
  173.7 31.8 %collective-permute-start.36 = (bf16[384,128]{1,0:T(8,128)(2,1)S(1)}, bf16[384,128]{1,0:T(8,128)(2,1)S(1)}, u32[]{:S(2)}, u32[]{:S(2)}) collective-permute-start(bf16[384,128]{1,0:T(8,128)(2,1)S(1)} %copy-done.28), channel_id=1, source_target_pairs={{0,12},{4,8},{8,4},{12,0},{1,13},{5,9},{9,5},{13,1},{2,14},{6,10},... | collective-permute-start | bytes 294920 | tf_op jit(solution)/shard_map/ppermute | solution.py:123
  178.4 15.1 %copy-start.4 = (bf16[768,128]{1,0:T(8,128)(2,1)}, bf16[768,128]{1,0:T(8,128)(2,1)S(1)}, u32[]{:S(2)}) copy-start(bf16[768,128]{1,0:T(8,128)(2,1)S(1)} %collective-permute-done.28.refs_11_.refs_10_) | copy-start | bytes 589828
  178.4 27.0 %collective-permute-start.35 = (bf16[384,128]{1,0:T(8,128)(2,1)S(1)}, bf16[384,128]{1,0:T(8,128)(2,1)S(1)}, u32[]{:S(2)}, u32[]{:S(2)}) collective-permute-start(bf16[384,128]{1,0:T(8,128)(2,1)S(1)} %get-tuple-element.50.refs_9_), channel_id=1, source_target_pairs={{0,8},{4,12},{8,0},{12,4},{1,9},{5,13},{9,1},{13,5},{2,10},{6,14},... | collective-permute-start | bytes 294920 | tf_op jit(solution)/shard_map/ppermute | solution.py:123
  204.9 16.9 %collective-permute-start.37 = (bf16[512,128]{1,0:T(8,128)(2,1)}, bf16[512,128]{1,0:T(8,128)(2,1)S(1)}, u32[]{:S(2)}, u32[]{:S(2)}) collective-permute-start(bf16[512,128]{1,0:T(8,128)(2,1)} %get-tuple-element.53), channel_id=1, source_target_pairs={{0,4},{4,0},{8,12},{12,8},{1,5},{5,1},{9,13},{13,9},{2,6},{6,2},{1... | collective-permute-start | bytes 393224 | tf_op jit(solution)/shard_map/ppermute | solution.py:123
  206.2 12.5 %copy-start.40 = (bf16[512,128]{1,0:T(8,128)(2,1)S(1)}, bf16[512,128]{1,0:T(8,128)(2,1)}, u32[]{:S(2)}) copy-start(bf16[512,128]{1,0:T(8,128)(2,1)} %get-tuple-element.55) | copy-start | bytes 393220
  206.2 14.5 %copy-start.39 = (bf16[512,128]{1,0:T(8,128)(2,1)S(1)}, bf16[512,128]{1,0:T(8,128)(2,1)}, u32[]{:S(2)}) copy-start(bf16[512,128]{1,0:T(8,128)(2,1)} %get-tuple-element.57) | copy-start | bytes 393220
  217.1 6.6 %collective-permute-start.38 = (bf16[512,128]{1,0:T(8,128)(2,1)}, bf16[512,128]{1,0:T(8,128)(2,1)S(1)}, u32[]{:S(2)}, u32[]{:S(2)}) collective-permute-start(bf16[512,128]{1,0:T(8,128)(2,1)} %get-tuple-element.54), channel_id=1, source_target_pairs={{0,4},{4,0},{8,12},{12,8},{1,5},{5,1},{9,13},{13,9},{2,6},{6,2},{1... | collective-permute-start | bytes 393224 | tf_op jit(solution)/shard_map/ppermute | solution.py:123
  218.7 9.4 %collective-permute-start.39 = (bf16[512,128]{1,0:T(8,128)(2,1)S(1)}, bf16[512,128]{1,0:T(8,128)(2,1)S(1)}, u32[]{:S(2)}, u32[]{:S(2)}) collective-permute-start(bf16[512,128]{1,0:T(8,128)(2,1)S(1)} %copy-done.40), channel_id=1, source_target_pairs={{0,16},{16,0},{1,17},{17,1},{2,18},{18,2},{3,19},{19,3},{4,20},{20... | collective-permute-start | bytes 393224 | tf_op jit(solution)/shard_map/ppermute | solution.py:123
  219.9 9.6 %collective-permute-start.40 = (bf16[512,128]{1,0:T(8,128)(2,1)}, bf16[512,128]{1,0:T(8,128)(2,1)S(1)}, u32[]{:S(2)}, u32[]{:S(2)}) collective-permute-start(bf16[512,128]{1,0:T(8,128)(2,1)} %get-tuple-element.56), channel_id=1, source_target_pairs={{0,16},{16,0},{1,17},{17,1},{2,18},{18,2},{3,19},{19,3},{4,20},{20... | collective-permute-start | bytes 393224 | tf_op jit(solution)/shard_map/ppermute | solution.py:123
  220.7 8.8 %collective-permute-start.41 = (bf16[512,128]{1,0:T(8,128)(2,1)S(1)}, bf16[512,128]{1,0:T(8,128)(2,1)S(1)}, u32[]{:S(2)}, u32[]{:S(2)}) collective-permute-start(bf16[512,128]{1,0:T(8,128)(2,1)S(1)} %copy-done.39), channel_id=1, source_target_pairs={{0,20},{4,16},{8,28},{12,24},{16,4},{20,0},{24,12},{28,8},{1,21},{... | collective-permute-start | bytes 393224 | tf_op jit(solution)/shard_map/ppermute | solution.py:409
  221.9 7.7 %copy-start.19 = (bf16[512,128]{1,0:T(8,128)(2,1)}, bf16[512,128]{1,0:T(8,128)(2,1)S(1)}, u32[]{:S(2)}) copy-start(bf16[512,128]{1,0:T(8,128)(2,1)S(1)} %collective-permute-done.37.refs_2_) | copy-start | bytes 393220
  221.9 7.7 %collective-permute-start.42 = (bf16[512,128]{1,0:T(8,128)(2,1)}, bf16[512,128]{1,0:T(8,128)(2,1)S(1)}, u32[]{:S(2)}, u32[]{:S(2)}) collective-permute-start(bf16[512,128]{1,0:T(8,128)(2,1)} %get-tuple-element.58), channel_id=1, source_target_pairs={{0,20},{4,16},{8,28},{12,24},{16,4},{20,0},{24,12},{28,8},{1,21},{... | collective-permute-start | bytes 393224 | tf_op jit(solution)/shard_map/ppermute | solution.py:409
  (21 other events, 48.9 us)

commit v2 on v0

--- a/solution.py
+++ b/solution.py
@@ -1,6 +1,9 @@
+import functools
 import jax
 import jax.numpy as jnp
 from jax import lax
+from jax.experimental import pallas as pl
+from jax.experimental.pallas import tpu as pltpu
 from jax.sharding import PartitionSpec as P
 
 EPSILON = 1e-06
@@ -113,9 +116,399 @@
     return attend(query_rows, key_rows, value_rows, cumulative, incoming)
 
 
+SIDES = ("own", "ctx", "groups", "both")
+PIECE = 128
+ANY = pl.BlockSpec(memory_space=pl.ANY)
+VMEM = pl.BlockSpec(memory_space=pltpu.VMEM)
+SCALARS = pl.BlockSpec(memory_space=pltpu.SMEM)
+
+
+def xor_permute(array, mesh, axis, flip):
+    return lax.ppermute(array, axis, [(at, at ^ flip) for at in range(mesh.shape[axis])])
+
+
+def after(arrays, *earlier):
+    return lax.optimization_barrier((*arrays, *earlier))[: len(arrays)]
+
+
+def in_three(array):
+    parts = []
+    for _ in range(3):
+        part = lax.reduce_precision(array, 8, 7)
+        parts.append(part.astype(jnp.bfloat16))
+        array = array - part
+    return jnp.concatenate(parts, axis=0)
+
+
+def silu(rows):
+    return rows / (1.0 + jnp.exp(-rows))
+
+
+def running_sum(rows):
+    lane = lax.broadcasted_iota(jnp.int32, rows.shape, 1)
+    shift = 1
+    while shift < rows.shape[1]:
+        rows += jnp.where(lane >= shift, pltpu.roll(rows, shift, 1), 0.0)
+        shift *= 2
+    return rows
+
+
+def column_of(row):
+    return jnp.transpose(jnp.broadcast_to(row, (PIECE, row.shape[1])))
+
+
+def token_copies(places, token_refs, held, semaphores):
+    turn, share = places[0], places[1] * 2 + places[2]
+    own_ref, quarter_refs = token_refs[0], token_refs[1:]
+    width = held.shape[3]
+
+    def copy(source, side, flip):
+        return pltpu.make_async_copy(source, held.at[side, flip], semaphores.at[side, flip])
+
+    def start():
+        for side in range(len(SIDES)):
+            for flip in range(held.shape[1]):
+                block = turn ^ flip
+                if side == 0:
+                    at = pl.multiple_of(block * width, width)
+                    copy(own_ref.at[:, pl.ds(at, width)], side, flip).start()
+                    continue
+                for place, ref in enumerate(quarter_refs[4 * (side - 1) : 4 * side]):
+
+                    @pl.when(block ^ share == place)
+                    def _(ref=ref):
+                        copy(ref.at[0 : held.shape[2], :], side, flip).start()
+
+    def wait(side):
+        for flip in range(held.shape[1]):
+            copy(quarter_refs[0].at[0 : held.shape[2], :], side, flip).wait()
+
+    return start, wait
+
+
+def project(token_refs, weights):
+    total = None
+    for token_ref, weight in zip(token_refs, weights):
+        product = jnp.dot(token_ref[...], weight, preferred_element_type=jnp.float32)
+        total = product if total is None else total + product
+    return total
+
+
+def piece_rows(rows):
+    return [slice(at, at + PIECE) for at in range(0, rows, PIECE)]
+
+
+def key_value_kernel(heads, size, flips, places, *refs):
+    sides = len(SIDES)
+    token_refs, refs = refs[:13], refs[13:]
+    decay_refs, refs = refs[:sides], refs[sides:]
+    source_ref, held, key_ref, value_ref, state_ref, sum_ref, fade_ref, mask_ref, pair_ref = refs[:9]
+    weight_ref, decay_ref, semaphores, weight_semaphores = refs[9:]
+    loads = [
+        pltpu.make_async_copy(
+            source_ref.at[places[0] ^ flip], weight_ref.at[flip], weight_semaphores.at[flip]
+        )
+        for flip in range(flips)
+    ]
+    for load in loads:
+        load.start()
+    start, wait = token_copies(places, token_refs, held, semaphores)
+    start()
+    odd = places[0] % 2 == 1
+    causal = lax.broadcasted_iota(jnp.int32, (PIECE, PIECE), 1) <= lax.broadcasted_iota(
+        jnp.int32, (PIECE, PIECE), 0
+    )
+    cuts = piece_rows(key_ref.shape[1])
+    for side in range(sides):
+        part = decay_refs[side][...].astype(jnp.float32)
+        count = part.shape[0] // 3
+        log_decay = part[:count] + (part[count : 2 * count] + part[2 * count :])
+        decay_ref[...] = running_sum(log_decay[:, : sum_ref.shape[2]])
+        for head in range(heads):
+            sum_ref[side, head : head + 1, :] = decay_ref[pl.ds(places[3] * heads + head, 1), :]
+    for load in loads:
+        load.wait()
+    for side in range(sides):
+        wait(side)
+        for head in range(heads):
+            at = slice(2 * head * size, 2 * (head + 1) * size)
+            both = project(
+                [held.at[side, flip] for flip in range(flips)],
+                [weight_ref[flip, :, at] for flip in range(flips)],
+            )
+            key = silu(both[:, :size])
+            key_bf = key.astype(jnp.bfloat16)
+            key = key_bf.astype(jnp.float32)
+            value = both[:, size:].astype(jnp.bfloat16)
+            key_ref[side, :, head * size : (head + 1) * size] = key_bf
+            value_ref[side, :, head * size : (head + 1) * size] = value
+            row = sum_ref[side, head : head + 1, :]
+            column = column_of(row)
+            ends = [column[cut.stop - 1 : cut.stop, :] for cut in cuts]
+            fresh = []
+            for cut, end in zip(cuts, ends):
+                scaled = (key[cut] * jnp.exp(end - column[cut])).astype(jnp.bfloat16)
+                fresh.append(
+                    lax.dot_general(
+                        scaled, value[cut], (((0,), (0,)), ((), ())), preferred_element_type=jnp.float32
+                    )
+                )
+            state = fresh[0]
+            for piece, cut in enumerate(cuts):
+                begin = ends[piece - 1] if piece else jnp.zeros_like(ends[0])
+                if piece:
+                    state = jnp.exp(ends[piece] - begin) * state + fresh[piece]
+                state_ref[head, side, piece] = state
+                fade_ref[head, side, cut, :] = jnp.exp(column[cut] - begin)
+                gaps = jnp.where(causal, column[cut] - row[:, cut], -jnp.inf)
+                mask_ref[head, side, cut, :] = jnp.exp(gaps)
+    last = len(cuts) - 1
+    end = sum_ref.shape[2] - 1
+    for head in range(heads):
+        for pair in range(2):
+            own, other = state_ref[head, 2 * pair, last], state_ref[head, 2 * pair + 1, last]
+            own_total = sum_ref[2 * pair, head : head + 1, end:]
+            other_total = sum_ref[2 * pair + 1, head : head + 1, end:]
+            total = jnp.where(odd, own_total, other_total)
+            first, second = jnp.where(odd, other, own), jnp.where(odd, own, other)
+            pair_ref[head, pair] = (jnp.exp(total) * first + second).astype(jnp.bfloat16)
+
+
+def query_kernel(head, columns, flips, places, *refs):
+    sides = len(SIDES)
+    held, refs = refs[0], refs[1:]
+    weight_refs, refs = refs[:flips], refs[flips:]
+    key_ref, value_ref, state_ref, sum_ref, fade_ref, mask_ref, before_ref = refs[:7]
+    out_refs = refs[7:]
+    odd = places[0] % 2 == 1
+    cuts = piece_rows(key_ref.shape[1])
+    last = len(cuts) - 1
+    end = sum_ref.shape[2] - 1
+    for side in range(sides):
+        partner = side ^ 1
+        before = before_ref[head, side // 2].astype(jnp.float32)
+        total = sum_ref[partner, head : head + 1, end:]
+        later = jnp.exp(total) * before + state_ref[head, partner, last]
+        second = odd if side % 2 == 0 else jnp.logical_not(odd)
+        incoming = jnp.where(second, later, before)
+        states = [incoming.astype(jnp.bfloat16)]
+        for piece in range(1, len(cuts)):
+            stop = cuts[piece].start - 1
+            sofar = jnp.exp(sum_ref[side, head : head + 1, stop : stop + 1])
+            states.append((state_ref[head, side, piece - 1] + sofar * incoming).astype(jnp.bfloat16))
+        query = project(
+            [held.at[side, flip] for flip in range(flips)],
+            [ref[:, columns] if flip == 1 else ref[...] for flip, ref in enumerate(weight_refs)],
+        )
+        query = silu(query).astype(jnp.bfloat16)
+        at = slice(head * PIECE, (head + 1) * PIECE)
+        weights = [
+            (
+                lax.dot_general(
+                    query[cut],
+                    key_ref[side, cut, at],
+                    (((1,), (1,)), ((), ())),
+                    preferred_element_type=jnp.float32,
+                )
+                * mask_ref[head, side, cut, :]
+            ).astype(jnp.bfloat16)
+            for cut in cuts
+        ]
+        raws = [
+            jnp.dot(query[cut], state, preferred_element_type=jnp.float32) * fade_ref[head, side, cut, :]
+            for cut, state in zip(cuts, states)
+        ]
+        raws = [
+            raw + jnp.dot(weight, value_ref[side, cut, at], preferred_element_type=jnp.float32)
+            for raw, weight, cut in zip(raws, weights, cuts)
+        ]
+        for raw, cut in zip(raws, cuts):
+            scale = lax.rsqrt(jnp.mean(raw * raw, axis=1, keepdims=True) + EPSILON)
+            out_refs[side][cut, :] = (raw * scale).astype(jnp.bfloat16)
+
+
+def merge_kernel(heads, size, places, *refs):
+    pieces, out_ref = refs[:-1], refs[-1]
+    for side in range(len(SIDES)):
+        for head in range(heads):
+            at = pl.multiple_of(((places[3] ^ side) * heads + head) * size, size)
+            out_ref[:, pl.ds(at, size)] = pieces[side * heads + head][...]
+
+
+def pack_kernel(heads, size, places, key_ref, value_ref, out_ref):
+    for head in range(heads):
+        at, to = head * size, 2 * head * size
+        out_ref[0, :, to : to + size] = key_ref[:, at : at + size]
+        out_ref[0, :, to + size : to + 2 * size] = value_ref[:, at : at + size]
+
+
+def spread_body(mesh, tokens, query_weight, key_weight, value_weight, log_decay):
+    rows, width = tokens.shape
+    depth = query_weight.shape[0]
+    heads_here = log_decay.shape[0]
+    size = query_weight.shape[1] // heads_here
+    flips = mesh.shape["ctx"]
+    heads = heads_here // 4
+    sides = len(SIDES)
+    group, turn = lax.axis_index("groups"), lax.axis_index("ctx")
+    plane, core = lax.axis_index("fsdp"), lax.axis_index("head")
+    mine = group * 2 + turn % 2
+    places = jnp.stack([turn, core, plane, mine]).astype(jnp.int32)
+    both = [
+        (at, (at // flips ^ 1) * flips + (at % flips ^ 1)) for at in range(mesh.shape["groups"] * flips)
+    ]
+
+    share = core * 2 + plane
+    quarter = lax.dynamic_slice(tokens, (0, share * depth), (rows, depth))
+    tail = jnp.pad(in_three(log_decay), ((0, 0), (0, depth - rows)))
+    quarter = jnp.concatenate([quarter, tail], axis=0)
+    beside = lax.dynamic_slice(tokens, (0, (share ^ 1) * depth), (rows, depth))
+
+    block = (depth, heads * size)
+    packed_shape = (flips, depth, 2 * heads * size)
+    owner = pl.BlockSpec(block, lambda step, places: (0, places[3] ^ ((places[0] ^ step) % 2)))
+    packed = pl.pallas_call(
+        functools.partial(pack_kernel, heads, size),
+        grid_spec=pltpu.PrefetchScalarGridSpec(
+            num_scalar_prefetch=1,
+            grid=(flips,),
+            in_specs=[owner, owner],
+            out_specs=pl.BlockSpec((1,) + packed_shape[1:], lambda step, places: (step, 0, 0)),
+        ),
+        out_shape=jax.ShapeDtypeStruct(packed_shape, jnp.bfloat16),
+        cost_estimate=pl.CostEstimate(flops=0, bytes_accessed=32 * depth * heads * size, transcendentals=0),
+        name="pack",
+    )(places, key_weight, value_weight)
+
+    key_value = lax.all_to_all(packed, "ctx", 0, 0)
+
+    from_ctx = xor_permute(quarter, mesh, "ctx", 1)
+    ctx_core = xor_permute(from_ctx, mesh, "head", 1)
+    (from_ctx,) = after((from_ctx,), ctx_core)
+    from_groups = xor_permute(quarter, mesh, "groups", 1)
+    ctx_plane = xor_permute(from_ctx, mesh, "fsdp", 1)
+    from_both = xor_permute(from_ctx, mesh, "groups", 1)
+    groups_plane = xor_permute(after((beside,), from_ctx)[0], mesh, "groups", 1)
+    both_core = xor_permute(from_both, mesh, "head", 1)
+    (from_both,) = after((from_both,), both_core)
+    both_plane = xor_permute(from_both, mesh, "fsdp", 1)
+    token_sets = [tokens]
+    token_sets += [from_ctx, ctx_plane, ctx_core, xor_permute(ctx_plane, mesh, "head", 1)]
+    for array in (from_groups, groups_plane):
+        token_sets.append(array)
+    token_sets += [xor_permute(array, mesh, "head", 1) for array in (from_groups, groups_plane)]
+    token_sets += [from_both, both_plane, both_core, xor_permute(both_plane, mesh, "head", 1)]
+    decays = [tail, *(array[rows:] for array in (from_ctx, from_groups, from_both))]
+
+    def query_block(owner, head, count):
+        return lax.dynamic_slice(query_weight, (0, (owner * heads + head) * size), (depth, count * size))
+
+    query_own = [query_block(mine, head, 1) for head in range(heads)]
+    query_sent = [query_block(mine ^ 1, head, 1) for head in range(heads)]
+    near_block, own, other = after(
+        (query_block(mine ^ 1, 0, heads), query_own[0], query_sent[0]), both_plane
+    )
+    query_near = xor_permute(near_block, mesh, "ctx", 1)
+    parts = [
+        [xor_permute(other if flip % 2 else own, mesh, "ctx", flip) for flip in range(2, flips)]
+    ]
+
+    large, small = (pltpu.CompilerParams(vmem_limit_bytes=size << 20) for size in (38, 12))
+    pieces = rows // PIECE
+    column_shape = (sides, rows, heads * size)
+    shapes = [
+        ((sides, flips, rows, depth), jnp.bfloat16),
+        (column_shape, jnp.bfloat16),
+        (column_shape, jnp.bfloat16),
+        ((heads, sides, pieces, size, size), jnp.float32),
+        ((sides, heads, rows), jnp.float32),
+        ((heads, sides, rows, size), jnp.float32),
+        ((heads, sides, rows, size), jnp.float32),
+        ((heads, 2, size, size), jnp.bfloat16),
+    ]
+    held, *memory, pair_state = pl.pallas_call(
+        functools.partial(key_value_kernel, heads, size, flips),
+        in_specs=[SCALARS] + [ANY] * len(token_sets) + [VMEM] * sides + [ANY],
+        out_specs=[VMEM] * len(shapes),
+        scratch_shapes=[
+            pltpu.VMEM(packed_shape, jnp.bfloat16),
+            pltpu.VMEM(log_decay.shape, jnp.float32),
+            pltpu.SemaphoreType.DMA((sides, flips)),
+            pltpu.SemaphoreType.DMA((flips,)),
+        ],
+        out_shape=[jax.ShapeDtypeStruct(*shape) for shape in shapes],
+        compiler_params=large,
+        cost_estimate=pl.CostEstimate(
+            flops=2 * sides * rows * width * 2 * heads * size,
+            bytes_accessed=2 * (sides * rows * width + width * 2 * heads * size),
+            transcendentals=sides * rows * 2 * heads * size,
+        ),
+        name="key_value",
+    )(places, *token_sets, *decays, key_value)
+
+    before = lax.ppermute(pair_state, "ctx", [(at, at + 2) for at in range(flips - 2)])
+    for head in range(1, heads):
+        own, other, _ = lax.optimization_barrier((query_own[head], query_sent[head], pair_state))
+        parts.append(
+            [xor_permute(other if flip % 2 else own, mesh, "ctx", flip) for flip in range(2, flips)]
+        )
+
+    returned = [[] for _ in SIDES]
+    for head in range(heads):
+        attended = pl.pallas_call(
+            functools.partial(query_kernel, head, slice(head * size, (head + 1) * size), flips),
+            in_specs=[SCALARS] + [VMEM] * (1 + flips + len(memory) + 1),
+            out_specs=[VMEM] * sides,
+            out_shape=[jax.ShapeDtypeStruct((rows, size), jnp.bfloat16)] * sides,
+            compiler_params=small,
+            cost_estimate=pl.CostEstimate(
+                flops=2 * sides * rows * size * (width + 4 * size),
+                bytes_accessed=2 * (sides * rows * width + width * size),
+                transcendentals=sides * rows * 4 * size,
+            ),
+            name="query",
+        )(places, held, query_own[head], query_near, *parts[head], *memory, before)
+        returned[0].append(attended[0])
+        returned[1].append(xor_permute(attended[1], mesh, "ctx", 1))
+        returned[2].append(xor_permute(attended[2], mesh, "groups", 1))
+        returned[3].append(lax.ppermute(attended[3], ("groups", "ctx"), both))
+
+    flat = [piece for side in returned for piece in side]
+    return pl.pallas_call(
+        functools.partial(merge_kernel, heads, size),
+        in_specs=[SCALARS] + [VMEM] * len(flat),
+        out_specs=VMEM,
+        out_shape=jax.ShapeDtypeStruct((rows, heads_here * size), jnp.bfloat16),
+        name="merge",
+    )(places, *flat)
+
+
+def spreads(mesh, tokens, query_weight, key_weight, value_weight, log_decay):
+    sizes = tuple(mesh.shape[axis] for axis in ("groups", "ctx", "fsdp", "head"))
+    if sizes != (2, 4, 2, 2):
+        return False
+    heads_here = log_decay.shape[0]
+    depth = query_weight.shape[0]
+    size = query_weight.shape[1] // heads_here
+    return (
+        heads_here % 4 == 0
+        and size == PIECE
+        and depth % 128 == 0
+        and depth * 4 == tokens.shape[1]
+        and tokens.shape[0] % PIECE == 0
+        and tokens.shape[0] <= 512
+    )
+
+
+def local_body(mesh, *arrays):
+    if spreads(mesh, *arrays):
+        return spread_body(mesh, *arrays)
+    return body(*arrays)
+
+
 def solution(mesh):
     return jax.shard_map(
-        body,
+        functools.partial(local_body, mesh),
         mesh=mesh,
         in_specs=(
             P(("groups", "ctx"), None),

time: 412 us -> 177 us (0.43)
  waiting for transfers between devices: 340 us -> 68.9 us
  Pallas kernels: 0 us -> 44.6 us
  starting transfers between devices: 0.12 us -> 43.8 us
  matrix products: 32.9 us -> 0 us
  between operations: 13.8 us -> 0.22 us
  local copies, waits for them, and re-layouts: 7.96 us -> 17 us
  blocking collectives: 8.94 us -> 0 us
    all_gather x4 -> x0, waiting for transfers between devices: 338 us -> none  [the longest x1 117 us: body(): lax.all_gather(key_weight, 'ctx', axis=0, tiled=True)]
    ppermute x0 -> x24, waiting for transfers between devices: none -> 68.9 us  [the longest x21 68.9 us: xor_permute(): lax.ppermute(array, axis, [(at, at ^ flip) for at in range(mesh.shape[axi...]
    pallas_call x0 -> x5, Pallas kernels: none -> 44.6 us  [the longest x1 20.2 us: spread_body(): pl.pallas_call(functools.partial(key_value_kernel, heads, size, flips), i...]
    ppermute x0 -> x24, starting transfers between devices: none -> 39.1 us  [the longest x21 33.5 us: xor_permute(): lax.ppermute(array, axis, [(at, at ^ flip) for at in range(mesh.shape[axi...]
    dot_general x6 -> x0, matrix products: 32.9 us -> none  [the longest x3 21.1 us: accumulate(): jnp.dot(tokens, portion, preferred_element_type=jnp.float32)]
    unnamed x13 -> x32, local copies, waits for them, and re-layouts: 1.84 us -> 11.6 us
    unnamed x1 -> x0, blocking collectives: 8.94 us -> none
    reshape x2 -> x0, local copies, waits for them, and re-layouts: 4.67 us -> none  [the longest x1 2.4 us: attend(): keyset = key_rows.reshape(row_count, heads_here, head_size)]
  transfers between devices with their start and end apart: 4 -> 25, of which waited for: 4 -> 8; matrix products, arithmetic and copies ran while one was open for 7% -> 3% of each run, Pallas kernels for 0% -> 24%
where the time goes in v2:
time: 177 us; the launch traced here: 176 us
  waiting for transfers between devices  68.9 us (39%)
  Pallas kernels  44.6 us (25%)
  starting transfers between devices  43.8 us (25%)
  local copies, waits for them, and re-layouts  17 us (10%)
    ppermute x21, waiting for transfers between devices, xor_permute(): lax.ppermute(array, axis, [(at, at ^ flip) for at in range(mesh.shape[axi...  68.9 us
    ppermute x21, starting transfers between devices, xor_permute(): lax.ppermute(array, axis, [(at, at ^ flip) for at in range(mesh.shape[axi...  33.5 us
    pallas_call x1, Pallas kernels, spread_body(): pl.pallas_call(functools.partial(key_value_kernel, heads, size, flips), i...  20.2 us
    pallas_call x2, Pallas kernels, spread_body(): pl.pallas_call(functools.partial(query_kernel, head, slice(head * size, (...  16.8 us
    unnamed x32, local copies, waits for them, and re-layouts  11.6 us
    pallas_call x1, Pallas kernels, spread_body(): pl.pallas_call(functools.partial(pack_kernel, heads, size), grid_spec=plt...  5.04 us
    all_to_all x1, starting transfers between devices, spread_body(): key_value = lax.all_to_all(packed, 'ctx', 0, 0)  4.64 us
  transfers between devices with their start and end apart: 25, of which 8 were waited for; matrix products, arithmetic and copies ran while one was open for 3% of the time, Pallas kernels for 24%

profile of v2, /device:TPU:0, one launch (start us, length us, event | category | flops | bytes accessed | tf_op | source)
XLA Modules:
  0.0 175.9 jit_solution(14780469405651761870)
XLA Ops:
  0.0 0.7 reduce-precision_convert_fusion.1
  0.7 1.5 constant_dynamic-slice_fusion.5
  2.2 0.1 pad_maximum_fusion
  2.3 3.1 %collective-permute-start = (bf16[536,768]{1,0:T(8,128)(2,1)S(1)}, bf16[536,768]{1,0:T(8,128)(2,1)S(1)}, u32[]{:S(2)}, u32[]{:S(2)}) collective-permute-start(bf16[536,768]{1,0:T(8,128)(2,1)S(1)} %pad_maximum_fusion), channel_id=1, source_target_pairs={{0,4},{4,0},{8,12},{12,8},{1,5},{5,1},{9,13},{13,9},{2,6},{6,2},{1... | collective-permute-start | bytes 2469896 | tf_op jit(solution)/shard_map/ppermute | solution.py:127
  5.4 0.7 pad_add_fusion.places
  6.0 5.0 %pack.1 = bf16[4,768,512]{2,1,0:T(8,128)(2,1)} custom-call(s32[4]{0:T(128)} %pad_add_fusion.places, bf16[768,1024]{1,0:T(8,128)(2,1)} %key_ref.1, bf16[768,1024]{1,0:T(8,128)(2,1)} %value_ref.1), custom_call_target="tpu_custom_call" | custom-call | bytes 6291456 | tf_op jit(solution)/shard_map/pack/pallas_call | solution.py:370
  11.1 4.6 %all-to-all-start = ((bf16[4,768,512]{2,1,0:T(8,128)(2,1)}), bf16[4,768,512]{2,1,0:T(8,128)(2,1)}, u32[]{:S(2)}, u32[]{:S(2)}) async-start(bf16[4,768,512]{2,1,0:T(8,128)(2,1)} %pack.1), calls=%async_computation | async-start | bytes 6291456 | tf_op jit(solution)/shard_map/all_to_all | solution.py:383
  15.7 8.8 %collective-permute-done.refs_1_ = bf16[536,768]{1,0:T(8,128)(2,1)S(1)} collective-permute-done((bf16[536,768]{1,0:T(8,128)(2,1)S(1)}, bf16[536,768]{1,0:T(8,128)(2,1)S(1)}, u32[]{:S(2)}, u32[]{:S(2)}) %collective-permute-start) | collective-permute-done | bytes 823328 | tf_op jit(solution)/shard_map/ppermute | solution.py:127
  24.5 0.0 collective-permute-start.1
  24.5 2.3 %collective-permute-done.1.refs_3_ = bf16[536,768]{1,0:T(8,128)(2,1)S(1)} collective-permute-done((bf16[536,768]{1,0:T(8,128)(2,1)S(1)}, bf16[536,768]{1,0:T(8,128)(2,1)S(1)}, u32[]{:S(2)}, u32[]{:S(2)}) %collective-permute-start.1) | collective-permute-done | bytes 823328 | tf_op jit(solution)/shard_map/ppermute | solution.py:127
  26.9 0.9 copy-done.5
  27.8 2.3 %collective-permute-start.8 = (bf16[536,768]{1,0:T(8,128)(2,1)S(1)}, bf16[536,768]{1,0:T(8,128)(2,1)S(1)}, u32[]{:S(2)}, u32[]{:S(2)}) collective-permute-start(bf16[536,768]{1,0:T(8,128)(2,1)S(1)} %collective-permute-done.refs_1_), channel_id=1, source_target_pairs={{0,16},{16,0},{1,17},{17,1},{2,18},{18,2},{3,19},{19,3},{4,20},{20... | collective-permute-start | bytes 2469896 | tf_op jit(solution)/shard_map/ppermute | solution.py:127
  30.0 18.6 %collective-permute-done.8.refs_9_ = bf16[536,768]{1,0:T(8,128)(2,1)S(1)} collective-permute-done((bf16[536,768]{1,0:T(8,128)(2,1)S(1)}, bf16[536,768]{1,0:T(8,128)(2,1)S(1)}, u32[]{:S(2)}, u32[]{:S(2)}) %collective-permute-start.8) | collective-permute-done | bytes 823328 | tf_op jit(solution)/shard_map/ppermute | solution.py:127
  48.6 0.0 collective-permute-start.9
  48.7 1.7 collective-permute-start.4
  50.4 1.5 collective-permute-start.2
  51.9 0.9 copy-done.7
  52.8 0.8 collective-permute-start.10
  53.6 1.5 collective-permute-start.5
  55.1 14.8 %collective-permute-done.4.refs_5_ = bf16[536,768]{1,0:T(8,128)(2,1)} collective-permute-done((bf16[536,768]{1,0:T(8,128)(2,1)S(1)}, bf16[536,768]{1,0:T(8,128)(2,1)}, u32[]{:S(2)}, u32[]{:S(2)}) %collective-permute-start.4) | collective-permute-done | bytes 823328 | tf_op jit(solution)/shard_map/ppermute | solution.py:127
  69.9 1.8 %collective-permute-done.2.refs_2_ = bf16[536,768]{1,0:T(8,128)(2,1)} collective-permute-done((bf16[536,768]{1,0:T(8,128)(2,1)S(1)}, bf16[536,768]{1,0:T(8,128)(2,1)}, u32[]{:S(2)}, u32[]{:S(2)}) %collective-permute-start.2) | collective-permute-done | bytes 823328 | tf_op jit(solution)/shard_map/ppermute | solution.py:127
  71.7 16.9 %collective-permute-done.10.refs_10_ = bf16[536,768]{1,0:T(8,128)(2,1)} collective-permute-done((bf16[536,768]{1,0:T(8,128)(2,1)S(1)}, bf16[536,768]{1,0:T(8,128)(2,1)}, u32[]{:S(2)}, u32[]{:S(2)}) %collective-permute-start.10) | collective-permute-done | bytes 823328 | tf_op jit(solution)/shard_map/ppermute | solution.py:127
  88.6 0.0 collective-permute-start.11
  88.6 0.0 collective-permute-done.5.refs_6_
  88.6 0.5 collective-permute-start.7
  89.1 1.0 constant_dynamic-slice_fusion.3
  90.1 2.1 %constant_dynamic-slice_fusion = (bf16[768,128]{1,0:T(8,128)(2,1)}, bf16[768,128]{1,0:T(8,128)(2,1)}, bf16[768,128]{1,0:T(8,128)(2,1)S(1)}, bf16[768,128]{1,0:T(8,128)(2,1)S(1)}) fusion(bf16[768,1024]{1,0:T(8,128)(2,1)} %param.6, s32[]{:T(128)S(6)} %select_n.32, s32[]{:T(128)S(6)} %select_n.30, s32[]{:T(128)S(6)} %select_n.29, s32[]{:T(128)S(6)} %select_n.31), kind=kLoop, calls=%fused_computation.13 | loop fusion | bytes 1572880 | tf_op jit(solution)/shard_map/dynamic_slice | solution.py:404
  92.2 0.8 slice.12.refs_15_
  93.0 1.4 collective-permute-start.12
  94.4 0.0 collective-permute-done.6.refs_7_
  94.4 2.6 %collective-permute-start.13 = (bf16[768,128]{1,0:T(8,128)(2,1)S(1)}, bf16[768,128]{1,0:T(8,128)(2,1)S(1)}, u32[]{:S(2)}, u32[]{:S(2)}) collective-permute-start(bf16[768,128]{1,0:T(8,128)(2,1)S(1)} %get-tuple-element.34.refs_1_), channel_id=1, source_target_pairs={{0,8},{4,12},{8,0},{12,4},{1,9},{5,13},{9,1},{13,5},{2,10},{6,14},... | collective-permute-start | bytes 589832 | tf_op jit(solution)/shard_map/ppermute | solution.py:127
  97.0 0.0 collective-permute-done.7.refs_8_
  97.0 0.5 collective-permute-start.14
  97.5 0.0 collective-permute-done.3.refs_4_
  97.5 0.0 all-to-all-done.refs_17_
  97.5 0.0 collective-permute-done.11.refs_12_
  97.5 0.0 copy-start.6
  97.5 1.1 copy-done.6
  98.7 1.1 copy-done.8
  99.8 20.2 %key_value.1 = (bf16[4,4,512,768]{3,2,1,0:T(8,128)(2,1)}, bf16[4,512,256]{2,1,0:T(8,128)(2,1)S(1)}, bf16[4,512,256]{2,1,0:T(8,128)(2,1)S(1)}, f32[2,4,4,128,128]...) custom-call(s32[4]{0:T(128)S(1)} %copy-done.4, ...), custom_call_target="tpu_custom_call" | custom-call | flops 6442450944 | bytes 15728640 | tf_op jit(solution)/shard_map/key_value/pallas_call | solution.py:429
  120.0 3.5 %collective-permute-start.15 = (bf16[2,2,128,128]{3,2,1,0:T(8,128)(2,1)S(1)}, bf16[2,2,128,128]{3,2,1,0:T(8,128)(2,1)S(1)}, u32[]{:S(2)}, u32[]{:S(2)}) collective-permute-start(bf16[2,2,128,128]{3,2,1,0:T(8,128)(2,1)S(1)} %get-tuple-element.42), channel_id=1, source_target_pairs={{0,8},{4,12},{1,9},{5,13},{2,10},{6,14},{3,11},{7,15},{16,24},{20,... | collective-permute-start | bytes 393224 | tf_op jit(solution)/shard_map/ppermute | solution.py:449
  123.5 0.1 collective-permute-start.16
  123.6 0.0 collective-permute-done.13.refs_3_
  123.6 4.8 %collective-permute-start.17 = (bf16[768,128]{1,0:T(8,128)(2,1)S(1)}, bf16[768,128]{1,0:T(8,128)(2,1)S(1)}, u32[]{:S(2)}, u32[]{:S(2)}) collective-permute-start(bf16[768,128]{1,0:T(8,128)(2,1)S(1)} %copy-done.9), channel_id=1, source_target_pairs={{0,12},{4,8},{8,4},{12,0},{1,13},{5,9},{9,5},{13,1},{2,14},{6,10},... | collective-permute-start | bytes 589832 | tf_op jit(solution)/shard_map/ppermute | solution.py:127
  128.5 0.0 collective-permute-done.12.refs_2_
  128.5 0.0 collective-permute-done.15.refs_11_
  128.5 4.6 %copy-done = bf16[4,4,512,768]{3,2,1,0:T(8,128)(2,1)S(1)} copy-done((bf16[4,4,512,768]{3,2,1,0:T(8,128)(2,1)S(1)}, bf16[4,4,512,768]{3,2,1,0:T(8,128)(2,1)}, u32[]{:S(2)}) %copy-start) | copy-done | bytes 12582936
  133.0 1.6 copy-done.1
  134.6 8.4 %query.2 = (bf16[512,128]{1,0:T(8,128)(2,1)S(1)}, bf16[512,128]{1,0:T(8,128)(2,1)S(1)}, bf16[512,128]{1,0:T(8,128)(2,1)S(1)}, bf16[512,128]{1,0:T(8,128)(2,1)S(1)}) custom-call(s32[4]{0:T(128)S(1)} %copy-done.4, bf16[4,4,512,768]{3,2,1,0:T(8,128)(2,1)S(1)} %copy-done, bf16[768,128]{1,0:T(8,128)(2,1)S(1)} %get-tuple-element.34.refs_1_, ...), custom_call_target="tpu_custom_call" | custom-call | flops 1879048192 | bytes 13369344 | tf_op jit(solution)/shard_map/query/pallas_call | solution.py:458
  143.1 9.8 %collective-permute-start.18 = (bf16[512,128]{1,0:T(8,128)(2,1)S(1)}, bf16[512,128]{1,0:T(8,128)(2,1)S(1)}, u32[]{:S(2)}, u32[]{:S(2)}) collective-permute-start(bf16[512,128]{1,0:T(8,128)(2,1)S(1)} %get-tuple-element.47), channel_id=1, source_target_pairs={{0,4},{4,0},{8,12},{12,8},{1,5},{5,1},{9,13},{13,9},{2,6},{6,2},{1... | collective-permute-start | bytes 393224 | tf_op jit(solution)/shard_map/ppermute | solution.py:127
  152.9 0.5 collective-permute-start.20
  153.4 1.0 collective-permute-start.22
  154.4 8.4 %query.3 = (bf16[512,128]{1,0:T(8,128)(2,1)S(1)}, bf16[512,128]{1,0:T(8,128)(2,1)S(1)}, bf16[512,128]{1,0:T(8,128)(2,1)S(1)}, bf16[512,128]{1,0:T(8,128)(2,1)S(1)}) custom-call(s32[4]{0:T(128)S(1)} %copy-done.4, bf16[4,4,512,768]{3,2,1,0:T(8,128)(2,1)S(1)} %copy-done, bf16[768,128]{1,0:T(8,128)(2,1)S(1)} %get-tuple-element.44.refs_1_, ...), custom_call_target="tpu_custom_call" | custom-call | flops 1879048192 | bytes 13369344 | tf_op jit(solution)/shard_map/query/pallas_call | solution.py:458
  162.9 0.7 copy-done.3
  163.5 1.9 %collective-permute-start.19 = (bf16[512,128]{1,0:T(8,128)(2,1)S(1)}, bf16[512,128]{1,0:T(8,128)(2,1)S(1)}, u32[]{:S(2)}, u32[]{:S(2)}) collective-permute-start(bf16[512,128]{1,0:T(8,128)(2,1)S(1)} %get-tuple-element.48), channel_id=1, source_target_pairs={{0,4},{4,0},{8,12},{12,8},{1,5},{5,1},{9,13},{13,9},{2,6},{6,2},{1... | collective-permute-start | bytes 393224 | tf_op jit(solution)/shard_map/ppermute | solution.py:127
  165.5 0.5 collective-permute-start.21
  166.0 1.0 collective-permute-start.23
  167.0 0.0 collective-permute-done.22.refs_6_
  167.0 1.9 %collective-permute-done.19.refs_3_ = bf16[512,128]{1,0:T(8,128)(2,1)S(1)} collective-permute-done((bf16[512,128]{1,0:T(8,128)(2,1)S(1)}, bf16[512,128]{1,0:T(8,128)(2,1)S(1)}, u32[]{:S(2)}, u32[]{:S(2)}) %collective-permute-start.19) | collective-permute-done | bytes 131104 | tf_op jit(solution)/shard_map/ppermute | solution.py:127
  168.9 3.7 %collective-permute-done.21.refs_5_ = bf16[512,128]{1,0:T(8,128)(2,1)S(1)} collective-permute-done((bf16[512,128]{1,0:T(8,128)(2,1)S(1)}, bf16[512,128]{1,0:T(8,128)(2,1)S(1)}, u32[]{:S(2)}, u32[]{:S(2)}) %collective-permute-start.21) | collective-permute-done | bytes 131104 | tf_op jit(solution)/shard_map/ppermute | solution.py:127
  172.7 0.0 collective-permute-done.23.refs_7_
  172.7 0.6 copy-done.14
  173.3 0.1 copy-done.15
  173.4 2.6 %merge.1 = bf16[512,1024]{1,0:T(8,128)(2,1)} custom-call(s32[4]{0:T(128)} %pad_add_fusion.places, bf16[512,128]{1,0:T(8,128)(2,1)} %copy-done.2, bf16[512,128]{1,0:T(8,128)(2,1)} %copy-done.3, bf16[512,128]{1,0:T(8,128)(2,1)} %copy-done.10, bf16[512,128]{1,0:T(8,128)(2,1)} %copy-done.13, bf16[512,128]{1,0:T(8,128)(2,1)} %copy-done.11, ...), custom_call_target="tpu_custom_call" | custom-call | tf_op jit(solution)/shard_map/merge/pallas_call | solution.py:477
  (33 shorter events, 0.1 us)
Async XLA Ops:
  2.3 22.2 %collective-permute-start = (bf16[536,768]{1,0:T(8,128)(2,1)S(1)}, bf16[536,768]{1,0:T(8,128)(2,1)S(1)}, u32[]{:S(2)}, u32[]{:S(2)}) collective-permute-start(bf16[536,768]{1,0:T(8,128)(2,1)S(1)} %pad_maximum_fusion), channel_id=1, source_target_pairs={{0,4},{4,0},{8,12},{12,8},{1,5},{5,1},{9,13},{13,9},{2,6},{6,2},{1... | collective-permute-start | bytes 2469896 | tf_op jit(solution)/shard_map/ppermute | solution.py:127
  11.1 86.4 %all-to-all-start = ((bf16[4,768,512]{2,1,0:T(8,128)(2,1)}), bf16[4,768,512]{2,1,0:T(8,128)(2,1)}, u32[]{:S(2)}, u32[]{:S(2)}) async-start(bf16[4,768,512]{2,1,0:T(8,128)(2,1)} %pack.1), calls=%async_computation | async-start | bytes 6291456 | tf_op jit(solution)/shard_map/all_to_all | solution.py:383
  15.7 81.8 %copy-start.4 = (s32[4]{0:T(128)S(1)}, s32[4]{0:T(128)}, u32[]{:S(2)}) copy-start(s32[4]{0:T(128)} %pad_add_fusion.places) | copy-start | bytes 52
  24.5 2.3 %collective-permute-start.1 = (bf16[536,768]{1,0:T(8,128)(2,1)S(1)}, bf16[536,768]{1,0:T(8,128)(2,1)S(1)}, u32[]{:S(2)}, u32[]{:S(2)}) collective-permute-start(bf16[536,768]{1,0:T(8,128)(2,1)S(1)} %collective-permute-done.refs_1_), channel_id=1, source_target_pairs={{0,1},{1,0},{2,3},{3,2},{4,5},{5,4},{6,7},{7,6},{8,9},{9,8},{10,11... | collective-permute-start | bytes 2469896 | tf_op jit(solution)/shard_map/ppermute | solution.py:127
  26.9 0.9 copy-start.5
  27.8 20.9 %collective-permute-start.8 = (bf16[536,768]{1,0:T(8,128)(2,1)S(1)}, bf16[536,768]{1,0:T(8,128)(2,1)S(1)}, u32[]{:S(2)}, u32[]{:S(2)}) collective-permute-start(bf16[536,768]{1,0:T(8,128)(2,1)S(1)} %collective-permute-done.refs_1_), channel_id=1, source_target_pairs={{0,16},{16,0},{1,17},{17,1},{2,18},{18,2},{3,19},{19,3},{4,20},{20... | collective-permute-start | bytes 2469896 | tf_op jit(solution)/shard_map/ppermute | solution.py:127
  48.6 3.2 %collective-permute-start.9 = (bf16[536,768]{1,0:T(8,128)(2,1)S(1)}, bf16[536,768]{1,0:T(8,128)(2,1)S(1)}, u32[]{:S(2)}, u32[]{:S(2)}) collective-permute-start(bf16[536,768]{1,0:T(8,128)(2,1)S(1)} %collective-permute-done.8.refs_9_), channel_id=1, source_target_pairs={{0,1},{1,0},{2,3},{3,2},{4,5},{5,4},{6,7},{7,6},{8,9},{9,8},{10,11... | collective-permute-start | bytes 2469896 | tf_op jit(solution)/shard_map/ppermute | solution.py:127
  48.7 21.2 %collective-permute-start.4 = (bf16[536,768]{1,0:T(8,128)(2,1)S(1)}, bf16[536,768]{1,0:T(8,128)(2,1)}, u32[]{:S(2)}, u32[]{:S(2)}) collective-permute-start(bf16[536,768]{1,0:T(8,128)(2,1)S(1)} %pad_maximum_fusion), channel_id=1, source_target_pairs={{0,16},{16,0},{1,17},{17,1},{2,18},{18,2},{3,19},{19,3},{4,20},{20... | collective-permute-start | bytes 2469896 | tf_op jit(solution)/shard_map/ppermute | solution.py:127
  50.4 21.3 %collective-permute-start.2 = (bf16[536,768]{1,0:T(8,128)(2,1)S(1)}, bf16[536,768]{1,0:T(8,128)(2,1)}, u32[]{:S(2)}, u32[]{:S(2)}) collective-permute-start(bf16[536,768]{1,0:T(8,128)(2,1)S(1)} %collective-permute-done.refs_1_), channel_id=1, source_target_pairs={{0,2},{2,0},{1,3},{3,1},{4,6},{6,4},{5,7},{7,5},{8,10},{10,8},{9,1... | collective-permute-start | bytes 2469896 | tf_op jit(solution)/shard_map/ppermute | solution.py:127
  51.9 0.9 copy-start.7
  52.8 35.8 %collective-permute-start.10 = (bf16[536,768]{1,0:T(8,128)(2,1)S(1)}, bf16[536,768]{1,0:T(8,128)(2,1)}, u32[]{:S(2)}, u32[]{:S(2)}) collective-permute-start(bf16[536,768]{1,0:T(8,128)(2,1)S(1)} %collective-permute-done.8.refs_9_), channel_id=1, source_target_pairs={{0,2},{2,0},{1,3},{3,1},{4,6},{6,4},{5,7},{7,5},{8,10},{10,8},{9,1... | collective-permute-start | bytes 2469896 | tf_op jit(solution)/shard_map/ppermute | solution.py:127
  53.6 35.0 %collective-permute-start.5 = (bf16[512,768]{1,0:T(8,128)(2,1)S(1)}, bf16[512,768]{1,0:T(8,128)(2,1)}, u32[]{:S(2)}, u32[]{:S(2)}) collective-permute-start(bf16[512,768]{1,0:T(8,128)(2,1)S(1)} %get-tuple-element.30), channel_id=1, source_target_pairs={{0,16},{16,0},{1,17},{17,1},{2,18},{18,2},{3,19},{19,3},{4,20},{20... | collective-permute-start | bytes 2359304 | tf_op jit(solution)/shard_map/ppermute | solution.py:127
  69.9 24.5 %collective-permute-start.6 = (bf16[536,768]{1,0:T(8,128)(2,1)}, bf16[536,768]{1,0:T(8,128)(2,1)}, u32[]{:S(2)}, u32[]{:S(2)}) collective-permute-start(bf16[536,768]{1,0:T(8,128)(2,1)} %collective-permute-done.4.refs_5_), channel_id=1, source_target_pairs={{0,1},{1,0},{2,3},{3,2},{4,5},{5,4},{6,7},{7,6},{8,9},{9,8},{10,11... | collective-permute-start | bytes 2469896 | tf_op jit(solution)/shard_map/ppermute | solution.py:127
  71.7 25.8 %collective-permute-start.3 = (bf16[536,768]{1,0:T(8,128)(2,1)}, bf16[536,768]{1,0:T(8,128)(2,1)}, u32[]{:S(2)}, u32[]{:S(2)}) collective-permute-start(bf16[536,768]{1,0:T(8,128)(2,1)} %collective-permute-done.2.refs_2_), channel_id=1, source_target_pairs={{0,1},{1,0},{2,3},{3,2},{4,5},{5,4},{6,7},{7,6},{8,9},{9,8},{10,11... | collective-permute-start | bytes 2469896 | tf_op jit(solution)/shard_map/ppermute | solution.py:127
  88.6 8.9 %collective-permute-start.11 = (bf16[536,768]{1,0:T(8,128)(2,1)}, bf16[536,768]{1,0:T(8,128)(2,1)}, u32[]{:S(2)}, u32[]{:S(2)}) collective-permute-start(bf16[536,768]{1,0:T(8,128)(2,1)} %collective-permute-done.10.refs_10_), channel_id=1, source_target_pairs={{0,1},{1,0},{2,3},{3,2},{4,5},{5,4},{6,7},{7,6},{8,9},{9,8},{10,11... | collective-permute-start | bytes 2469896 | tf_op jit(solution)/shard_map/ppermute | solution.py:127
  88.6 8.4 %collective-permute-start.7 = (bf16[512,768]{1,0:T(8,128)(2,1)}, bf16[512,768]{1,0:T(8,128)(2,1)}, u32[]{:S(2)}, u32[]{:S(2)}) collective-permute-start(bf16[512,768]{1,0:T(8,128)(2,1)} %collective-permute-done.5.refs_6_), channel_id=1, source_target_pairs={{0,1},{1,0},{2,3},{3,2},{4,5},{5,4},{6,7},{7,6},{8,9},{9,8},{10,11... | collective-permute-start | bytes 2359304 | tf_op jit(solution)/shard_map/ppermute | solution.py:127
  93.0 35.4 %collective-permute-start.12 = (bf16[768,256]{1,0:T(8,128)(2,1)S(1)}, bf16[768,256]{1,0:T(8,128)(2,1)S(1)}, u32[]{:S(2)}, u32[]{:S(2)}) collective-permute-start(bf16[768,256]{1,0:T(8,128)(2,1)S(1)} %constant_dynamic-slice_fusion.3), channel_id=1, source_target_pairs={{0,4},{4,0},{8,12},{12,8},{1,5},{5,1},{9,13},{13,9},{2,6},{6,2},{1... | collective-permute-start | bytes 1179656 | tf_op jit(solution)/shard_map/ppermute | solution.py:127
  94.4 29.2 %collective-permute-start.13 = (bf16[768,128]{1,0:T(8,128)(2,1)S(1)}, bf16[768,128]{1,0:T(8,128)(2,1)S(1)}, u32[]{:S(2)}, u32[]{:S(2)}) collective-permute-start(bf16[768,128]{1,0:T(8,128)(2,1)S(1)} %get-tuple-element.34.refs_1_), channel_id=1, source_target_pairs={{0,8},{4,12},{8,0},{12,4},{1,9},{5,13},{9,1},{13,5},{2,10},{6,14},... | collective-permute-start | bytes 589832 | tf_op jit(solution)/shard_map/ppermute | solution.py:127
  97.0 31.4 %collective-permute-start.14 = (bf16[768,128]{1,0:T(8,128)(2,1)}, bf16[768,128]{1,0:T(8,128)(2,1)S(1)}, u32[]{:S(2)}, u32[]{:S(2)}) collective-permute-start(bf16[768,128]{1,0:T(8,128)(2,1)} %get-tuple-element.35), channel_id=1, source_target_pairs={{0,12},{4,8},{8,4},{12,0},{1,13},{5,9},{9,5},{13,1},{2,14},{6,10},... | collective-permute-start | bytes 589832 | tf_op jit(solution)/shard_map/ppermute | solution.py:127
  97.5 1.1 copy-start.6
  98.7 1.1 copy-start.8
  99.8 23.8 %copy-start.9 = (bf16[768,128]{1,0:T(8,128)(2,1)S(1)}, bf16[768,128]{1,0:T(8,128)(2,1)}, u32[]{:S(2)}) copy-start(bf16[768,128]{1,0:T(8,128)(2,1)} %get-tuple-element.45) | copy-start | bytes 589828
  120.0 8.5 %collective-permute-start.15 = (bf16[2,2,128,128]{3,2,1,0:T(8,128)(2,1)S(1)}, bf16[2,2,128,128]{3,2,1,0:T(8,128)(2,1)S(1)}, u32[]{:S(2)}, u32[]{:S(2)}) collective-permute-start(bf16[2,2,128,128]{3,2,1,0:T(8,128)(2,1)S(1)} %get-tuple-element.42), channel_id=1, source_target_pairs={{0,8},{4,12},{1,9},{5,13},{2,10},{6,14},{3,11},{7,15},{16,24},{20,... | collective-permute-start | bytes 393224 | tf_op jit(solution)/shard_map/ppermute | solution.py:449
  123.5 30.9 %collective-permute-start.16 = (bf16[768,128]{1,0:T(8,128)(2,1)S(1)}, bf16[768,128]{1,0:T(8,128)(2,1)S(1)}, u32[]{:S(2)}, u32[]{:S(2)}) collective-permute-start(bf16[768,128]{1,0:T(8,128)(2,1)S(1)} %get-tuple-element.44.refs_1_), channel_id=1, source_target_pairs={{0,8},{4,12},{8,0},{12,4},{1,9},{5,13},{9,1},{13,5},{2,10},{6,14},... | collective-permute-start | bytes 589832 | tf_op jit(solution)/shard_map/ppermute | solution.py:127
  123.6 30.8 %collective-permute-start.17 = (bf16[768,128]{1,0:T(8,128)(2,1)S(1)}, bf16[768,128]{1,0:T(8,128)(2,1)S(1)}, u32[]{:S(2)}, u32[]{:S(2)}) collective-permute-start(bf16[768,128]{1,0:T(8,128)(2,1)S(1)} %copy-done.9), channel_id=1, source_target_pairs={{0,12},{4,8},{8,4},{12,0},{1,13},{5,9},{9,5},{13,1},{2,14},{6,10},... | collective-permute-start | bytes 589832 | tf_op jit(solution)/shard_map/ppermute | solution.py:127
  128.5 4.6 %copy-start = (bf16[4,4,512,768]{3,2,1,0:T(8,128)(2,1)S(1)}, bf16[4,4,512,768]{3,2,1,0:T(8,128)(2,1)}, u32[]{:S(2)}) copy-start(bf16[4,4,512,768]{3,2,1,0:T(8,128)(2,1)} %get-tuple-element.32.refs_0_) | copy-start | bytes 37748740
  133.0 1.6 copy-start.1
  143.1 19.8 %copy-start.2 = (bf16[512,128]{1,0:T(8,128)(2,1)}, bf16[512,128]{1,0:T(8,128)(2,1)S(1)}, u32[]{:S(2)}) copy-start(bf16[512,128]{1,0:T(8,128)(2,1)S(1)} %get-tuple-element.43.refs_0_) | copy-start | bytes 393220
  143.1 22.9 %collective-permute-start.18 = (bf16[512,128]{1,0:T(8,128)(2,1)S(1)}, bf16[512,128]{1,0:T(8,128)(2,1)S(1)}, u32[]{:S(2)}, u32[]{:S(2)}) collective-permute-start(bf16[512,128]{1,0:T(8,128)(2,1)S(1)} %get-tuple-element.47), channel_id=1, source_target_pairs={{0,4},{4,0},{8,12},{12,8},{1,5},{5,1},{9,13},{13,9},{2,6},{6,2},{1... | collective-permute-start | bytes 393224 | tf_op jit(solution)/shard_map/ppermute | solution.py:127
  152.9 14.1 %collective-permute-start.20 = (bf16[512,128]{1,0:T(8,128)(2,1)S(1)}, bf16[512,128]{1,0:T(8,128)(2,1)S(1)}, u32[]{:S(2)}, u32[]{:S(2)}) collective-permute-start(bf16[512,128]{1,0:T(8,128)(2,1)S(1)} %get-tuple-element.49), channel_id=1, source_target_pairs={{0,16},{16,0},{1,17},{17,1},{2,18},{18,2},{3,19},{19,3},{4,20},{20... | collective-permute-start | bytes 393224 | tf_op jit(solution)/shard_map/ppermute | solution.py:127
  153.4 13.6 %collective-permute-start.22 = (bf16[512,128]{1,0:T(8,128)(2,1)S(1)}, bf16[512,128]{1,0:T(8,128)(2,1)S(1)}, u32[]{:S(2)}, u32[]{:S(2)}) collective-permute-start(bf16[512,128]{1,0:T(8,128)(2,1)S(1)} %get-tuple-element.51), channel_id=1, source_target_pairs={{0,20},{4,16},{8,28},{12,24},{16,4},{20,0},{24,12},{28,8},{1,21},{... | collective-permute-start | bytes 393224 | tf_op jit(solution)/shard_map/ppermute | solution.py:474
  162.9 0.7 copy-start.3
  163.5 5.4 %collective-permute-start.19 = (bf16[512,128]{1,0:T(8,128)(2,1)S(1)}, bf16[512,128]{1,0:T(8,128)(2,1)S(1)}, u32[]{:S(2)}, u32[]{:S(2)}) collective-permute-start(bf16[512,128]{1,0:T(8,128)(2,1)S(1)} %get-tuple-element.48), channel_id=1, source_target_pairs={{0,4},{4,0},{8,12},{12,8},{1,5},{5,1},{9,13},{13,9},{2,6},{6,2},{1... | collective-permute-start | bytes 393224 | tf_op jit(solution)/shard_map/ppermute | solution.py:127
  165.5 7.2 %collective-permute-start.21 = (bf16[512,128]{1,0:T(8,128)(2,1)S(1)}, bf16[512,128]{1,0:T(8,128)(2,1)S(1)}, u32[]{:S(2)}, u32[]{:S(2)}) collective-permute-start(bf16[512,128]{1,0:T(8,128)(2,1)S(1)} %get-tuple-element.50), channel_id=1, source_target_pairs={{0,16},{16,0},{1,17},{17,1},{2,18},{18,2},{3,19},{19,3},{4,20},{20... | collective-permute-start | bytes 393224 | tf_op jit(solution)/shard_map/ppermute | solution.py:127
  166.0 6.7 %copy-start.10 = (bf16[512,128]{1,0:T(8,128)(2,1)}, bf16[512,128]{1,0:T(8,128)(2,1)S(1)}, u32[]{:S(2)}) copy-start(bf16[512,128]{1,0:T(8,128)(2,1)S(1)} %collective-permute-done.18.refs_2_) | copy-start | bytes 393220
  166.0 6.7 %collective-permute-start.23 = (bf16[512,128]{1,0:T(8,128)(2,1)S(1)}, bf16[512,128]{1,0:T(8,128)(2,1)S(1)}, u32[]{:S(2)}, u32[]{:S(2)}) collective-permute-start(bf16[512,128]{1,0:T(8,128)(2,1)S(1)} %get-tuple-element.52), channel_id=1, source_target_pairs={{0,20},{4,16},{8,28},{12,24},{16,4},{20,0},{24,12},{28,8},{1,21},{... | collective-permute-start | bytes 393224 | tf_op jit(solution)/shard_map/ppermute | solution.py:474
  167.0 5.6 %copy-start.11 = (bf16[512,128]{1,0:T(8,128)(2,1)}, bf16[512,128]{1,0:T(8,128)(2,1)S(1)}, u32[]{:S(2)}) copy-start(bf16[512,128]{1,0:T(8,128)(2,1)S(1)} %collective-permute-done.20.refs_4_) | copy-start | bytes 393220
  167.0 5.6 %copy-start.12 = (bf16[512,128]{1,0:T(8,128)(2,1)}, bf16[512,128]{1,0:T(8,128)(2,1)S(1)}, u32[]{:S(2)}) copy-start(bf16[512,128]{1,0:T(8,128)(2,1)S(1)} %collective-permute-done.22.refs_6_) | copy-start | bytes 393220
  168.9 3.8 %copy-start.13 = (bf16[512,128]{1,0:T(8,128)(2,1)}, bf16[512,128]{1,0:T(8,128)(2,1)S(1)}, u32[]{:S(2)}) copy-start(bf16[512,128]{1,0:T(8,128)(2,1)S(1)} %collective-permute-done.19.refs_3_) | copy-start | bytes 393220
  172.7 0.7 copy-start.14
  172.7 0.7 copy-start.15

commit v3 on v2

--- a/solution.py
+++ b/solution.py
@@ -383,15 +383,16 @@
     key_value = lax.all_to_all(packed, "ctx", 0, 0)
 
     from_ctx = xor_permute(quarter, mesh, "ctx", 1)
+    from_groups = xor_permute(quarter, mesh, "groups", 1)
     ctx_core = xor_permute(from_ctx, mesh, "head", 1)
-    (from_ctx,) = after((from_ctx,), ctx_core)
-    from_groups = xor_permute(quarter, mesh, "groups", 1)
+    (from_ctx,) = after((from_ctx,), ctx_core, from_groups)
     ctx_plane = xor_permute(from_ctx, mesh, "fsdp", 1)
     from_both = xor_permute(from_ctx, mesh, "groups", 1)
     groups_plane = xor_permute(after((beside,), from_ctx)[0], mesh, "groups", 1)
     both_core = xor_permute(from_both, mesh, "head", 1)
-    (from_both,) = after((from_both,), both_core)
+    (from_both,) = after((from_both,), both_core, ctx_plane)
     both_plane = xor_permute(from_both, mesh, "fsdp", 1)
+    (both_plane,) = after((both_plane,), groups_plane)
     token_sets = [tokens]
     token_sets += [from_ctx, ctx_plane, ctx_core, xor_permute(ctx_plane, mesh, "head", 1)]
     for array in (from_groups, groups_plane):

time: 177 us -> 169 us (0.955)
  waiting for transfers between devices: 68.9 us -> 60.2 us
    ppermute x21, waiting for transfers between devices: 68.9 us -> 60.2 us  [xor_permute(): lax.ppermute(array, axis, [(at, at ^ flip) for at in range(mesh.shape[axi...]
    ppermute x21, starting transfers between devices: 33.5 us -> 35.8 us  [xor_permute(): lax.ppermute(array, axis, [(at, at ^ flip) for at in range(mesh.shape[axi...]
    ppermute x2, starting transfers between devices: 2.07 us -> 0.04 us  [spread_body(): returned[3].append(lax.ppermute(attended[3], ('groups', 'ctx'), both))]
    unnamed x32 -> x36, local copies, waits for them, and re-layouts: 11.6 us -> 12.7 us
  transfers between devices with their start and end apart: 25 -> 25, of which waited for: 8 -> 8; matrix products, arithmetic and copies ran while one was open for 3% -> 3% of each run, Pallas kernels for 24% -> 25%
where the time goes in v3:
time: 169 us; the launch traced here: 168 us
  waiting for transfers between devices  60.2 us (36%)
  Pallas kernels  44.6 us (26%)
  starting transfers between devices  44 us (26%)
  local copies, waits for them, and re-layouts  18 us (11%)
    ppermute x21, waiting for transfers between devices, xor_permute(): lax.ppermute(array, axis, [(at, at ^ flip) for at in range(mesh.shape[axi...  60.2 us
    ppermute x21, starting transfers between devices, xor_permute(): lax.ppermute(array, axis, [(at, at ^ flip) for at in range(mesh.shape[axi...  35.8 us
    pallas_call x1, Pallas kernels, spread_body(): pl.pallas_call(functools.partial(key_value_kernel, heads, size, flips), i...  20.2 us
    pallas_call x2, Pallas kernels, spread_body(): pl.pallas_call(functools.partial(query_kernel, head, slice(head * size, (...  16.8 us
    unnamed x36, local copies, waits for them, and re-layouts  12.7 us
    pallas_call x1, Pallas kernels, spread_body(): pl.pallas_call(functools.partial(pack_kernel, heads, size), grid_spec=plt...  5.02 us
    all_to_all x1, starting transfers between devices, spread_body(): key_value = lax.all_to_all(packed, 'ctx', 0, 0)  4.65 us
    ppermute x1, starting transfers between devices, spread_body(): lax.ppermute(pair_state, 'ctx', [(at, at + 2) for at in range(flips - 2)])  3.56 us
  transfers between devices with their start and end apart: 25, of which 8 were waited for; matrix products, arithmetic and copies ran while one was open for 3% of the time, Pallas kernels for 25%

profile of v3, /device:TPU:0, one launch (start us, length us, event | category | flops | bytes accessed | tf_op | source)
XLA Modules:
  0.0 168.5 jit_solution(7324646040322205089)
XLA Ops:
  0.0 0.7 reduce-precision_convert_fusion.1
  0.7 1.5 constant_dynamic-slice_fusion.5
  2.2 0.1 pad_maximum_fusion
  2.3 3.1 %collective-permute-start = (bf16[536,768]{1,0:T(8,128)(2,1)S(1)}, bf16[536,768]{1,0:T(8,128)(2,1)S(1)}, u32[]{:S(2)}, u32[]{:S(2)}) collective-permute-start(bf16[536,768]{1,0:T(8,128)(2,1)S(1)} %pad_maximum_fusion), channel_id=1, source_target_pairs={{0,4},{4,0},{8,12},{12,8},{1,5},{5,1},{9,13},{13,9},{2,6},{6,2},{1... | collective-permute-start | bytes 2469896 | tf_op jit(solution)/shard_map/ppermute | solution.py:127
  5.4 0.6 pad_add_fusion.places
  5.9 5.0 %pack.1 = bf16[4,768,512]{2,1,0:T(8,128)(2,1)} custom-call(s32[4]{0:T(128)} %pad_add_fusion.places, bf16[768,1024]{1,0:T(8,128)(2,1)} %key_ref.1, bf16[768,1024]{1,0:T(8,128)(2,1)} %value_ref.1), custom_call_target="tpu_custom_call" | custom-call | bytes 6291456 | tf_op jit(solution)/shard_map/pack/pallas_call | solution.py:370
  10.9 4.6 %all-to-all-start = ((bf16[4,768,512]{2,1,0:T(8,128)(2,1)}), bf16[4,768,512]{2,1,0:T(8,128)(2,1)}, u32[]{:S(2)}, u32[]{:S(2)}) async-start(bf16[4,768,512]{2,1,0:T(8,128)(2,1)} %pack.1), calls=%async_computation | async-start | bytes 6291456 | tf_op jit(solution)/shard_map/all_to_all | solution.py:383
  15.6 1.6 collective-permute-start.2
  17.2 7.3 %collective-permute-done.refs_1_ = bf16[536,768]{1,0:T(8,128)(2,1)S(1)} collective-permute-done((bf16[536,768]{1,0:T(8,128)(2,1)S(1)}, bf16[536,768]{1,0:T(8,128)(2,1)S(1)}, u32[]{:S(2)}, u32[]{:S(2)}) %collective-permute-start) | collective-permute-done | bytes 823328 | tf_op jit(solution)/shard_map/ppermute | solution.py:127
  24.5 10.9 %collective-permute-done.2.refs_5_ = bf16[536,768]{1,0:T(8,128)(2,1)S(1)} collective-permute-done((bf16[536,768]{1,0:T(8,128)(2,1)S(1)}, bf16[536,768]{1,0:T(8,128)(2,1)S(1)}, u32[]{:S(2)}, u32[]{:S(2)}) %collective-permute-start.2) | collective-permute-done | bytes 823328 | tf_op jit(solution)/shard_map/ppermute | solution.py:127
  35.5 0.9 copy-done.7
  36.4 1.5 collective-permute-start.8
  37.9 1.5 collective-permute-start.3
  39.4 16.0 %collective-permute-done.8.refs_9_ = bf16[536,768]{1,0:T(8,128)(2,1)S(1)} collective-permute-done((bf16[536,768]{1,0:T(8,128)(2,1)S(1)}, bf16[536,768]{1,0:T(8,128)(2,1)S(1)}, u32[]{:S(2)}, u32[]{:S(2)}) %collective-permute-start.8) | collective-permute-done | bytes 823328 | tf_op jit(solution)/shard_map/ppermute | solution.py:127
  55.4 0.0 collective-permute-start.9
  55.4 1.3 collective-permute-done.3.refs_2_
  56.7 1.0 collective-permute-done.9.refs_11_
  57.7 0.9 copy-done.9
  58.6 1.5 collective-permute-start.10
  60.1 1.5 collective-permute-start.5
  61.6 0.0 collective-permute-start.6
  61.6 0.5 collective-permute-start.4
  62.1 17.4 %collective-permute-done.5.refs_6_ = bf16[512,768]{1,0:T(8,128)(2,1)} collective-permute-done((bf16[512,768]{1,0:T(8,128)(2,1)S(1)}, bf16[512,768]{1,0:T(8,128)(2,1)}, u32[]{:S(2)}, u32[]{:S(2)}) %collective-permute-start.5) | collective-permute-done | bytes 786464 | tf_op jit(solution)/shard_map/ppermute | solution.py:127
  79.5 0.0 collective-permute-done.10.refs_10_
  79.5 0.0 collective-permute-start.11
  79.5 0.5 collective-permute-start.7
  80.0 1.0 constant_dynamic-slice_fusion.3
  81.0 2.0 %constant_dynamic-slice_fusion = (bf16[768,128]{1,0:T(8,128)(2,1)}, bf16[768,128]{1,0:T(8,128)(2,1)}, bf16[768,128]{1,0:T(8,128)(2,1)S(1)}, bf16[768,128]{1,0:T(8,128)(2,1)S(1)}) fusion(bf16[768,1024]{1,0:T(8,128)(2,1)} %param.6, s32[]{:T(128)S(6)} %select_n.32, s32[]{:T(128)S(6)} %select_n.30, s32[]{:T(128)S(6)} %select_n.29, s32[]{:T(128)S(6)} %select_n.31), kind=kLoop, calls=%fused_computation.13 | loop fusion | bytes 1572880 | tf_op jit(solution)/shard_map/dynamic_slice | solution.py:405
  83.1 0.8 slice.11.refs_16_
  83.9 1.3 collective-permute-start.12
  85.2 2.4 %collective-permute-start.13 = (bf16[768,128]{1,0:T(8,128)(2,1)S(1)}, bf16[768,128]{1,0:T(8,128)(2,1)S(1)}, u32[]{:S(2)}, u32[]{:S(2)}) collective-permute-start(bf16[768,128]{1,0:T(8,128)(2,1)S(1)} %get-tuple-element.36.refs_1_), channel_id=1, source_target_pairs={{0,8},{4,12},{8,0},{12,4},{1,9},{5,13},{9,1},{13,5},{2,10},{6,14},... | collective-permute-start | bytes 589832 | tf_op jit(solution)/shard_map/ppermute | solution.py:127
  87.6 0.0 collective-permute-done.7.refs_8_
  87.6 0.7 collective-permute-start.14
  88.3 0.0 all-to-all-done.refs_17_
  88.3 0.0 collective-permute-done.11.refs_12_
  88.3 1.1 copy-done.6
  89.4 1.1 copy-done.8
  90.6 1.1 copy-done.10
  91.7 20.2 %key_value.1 = (bf16[4,4,512,768]{3,2,1,0:T(8,128)(2,1)}, bf16[4,512,256]{2,1,0:T(8,128)(2,1)S(1)}, bf16[4,512,256]{2,1,0:T(8,128)(2,1)S(1)}, f32[2,4,4,128,128]...) custom-call(s32[4]{0:T(128)S(1)} %copy-done.4, ...), custom_call_target="tpu_custom_call" | custom-call | flops 6442450944 | bytes 15728640 | tf_op jit(solution)/shard_map/key_value/pallas_call | solution.py:430
  112.0 3.6 %collective-permute-start.15 = (bf16[2,2,128,128]{3,2,1,0:T(8,128)(2,1)S(1)}, bf16[2,2,128,128]{3,2,1,0:T(8,128)(2,1)S(1)}, u32[]{:S(2)}, u32[]{:S(2)}) collective-permute-start(bf16[2,2,128,128]{3,2,1,0:T(8,128)(2,1)S(1)} %get-tuple-element.44), channel_id=1, source_target_pairs={{0,8},{4,12},{1,9},{5,13},{2,10},{6,14},{3,11},{7,15},{16,24},{20,... | collective-permute-start | bytes 393224 | tf_op jit(solution)/shard_map/ppermute | solution.py:450
  115.5 0.1 collective-permute-start.16
  115.6 0.0 collective-permute-done.13.refs_3_
  115.6 4.6 %collective-permute-start.17 = (bf16[768,128]{1,0:T(8,128)(2,1)S(1)}, bf16[768,128]{1,0:T(8,128)(2,1)S(1)}, u32[]{:S(2)}, u32[]{:S(2)}) collective-permute-start(bf16[768,128]{1,0:T(8,128)(2,1)S(1)} %copy-done.11), channel_id=1, source_target_pairs={{0,12},{4,8},{8,4},{12,0},{1,13},{5,9},{9,5},{13,1},{2,14},{6,10},... | collective-permute-start | bytes 589832 | tf_op jit(solution)/shard_map/ppermute | solution.py:127
  120.2 0.0 collective-permute-done.14.refs_4_
  120.2 0.0 collective-permute-done.12.refs_2_
  120.2 4.6 %copy-done = bf16[4,4,512,768]{3,2,1,0:T(8,128)(2,1)S(1)} copy-done((bf16[4,4,512,768]{3,2,1,0:T(8,128)(2,1)S(1)}, bf16[4,4,512,768]{3,2,1,0:T(8,128)(2,1)}, u32[]{:S(2)}) %copy-start) | copy-done | bytes 12582936
  124.8 1.6 copy-done.1
  126.4 8.4 %query.2 = (bf16[512,128]{1,0:T(8,128)(2,1)S(1)}, bf16[512,128]{1,0:T(8,128)(2,1)S(1)}, bf16[512,128]{1,0:T(8,128)(2,1)S(1)}, bf16[512,128]{1,0:T(8,128)(2,1)S(1)}) custom-call(s32[4]{0:T(128)S(1)} %copy-done.4, bf16[4,4,512,768]{3,2,1,0:T(8,128)(2,1)S(1)} %copy-done, bf16[768,128]{1,0:T(8,128)(2,1)S(1)} %get-tuple-element.36.refs_1_, ...), custom_call_target="tpu_custom_call" | custom-call | flops 1879048192 | bytes 13369344 | tf_op jit(solution)/shard_map/query/pallas_call | solution.py:459
  134.8 10.1 %collective-permute-start.18 = (bf16[512,128]{1,0:T(8,128)(2,1)S(1)}, bf16[512,128]{1,0:T(8,128)(2,1)S(1)}, u32[]{:S(2)}, u32[]{:S(2)}) collective-permute-start(bf16[512,128]{1,0:T(8,128)(2,1)S(1)} %get-tuple-element.49), channel_id=1, source_target_pairs={{0,4},{4,0},{8,12},{12,8},{1,5},{5,1},{9,13},{13,9},{2,6},{6,2},{1... | collective-permute-start | bytes 393224 | tf_op jit(solution)/shard_map/ppermute | solution.py:127
  144.9 1.5 collective-permute-start.20
  146.4 0.0 collective-permute-start.22
  146.4 0.0 collective-permute-done.16.refs_3_
  146.4 0.0 collective-permute-done.17.refs_4_
  146.4 8.4 %query.3 = (bf16[512,128]{1,0:T(8,128)(2,1)S(1)}, bf16[512,128]{1,0:T(8,128)(2,1)S(1)}, bf16[512,128]{1,0:T(8,128)(2,1)S(1)}, bf16[512,128]{1,0:T(8,128)(2,1)S(1)}) custom-call(s32[4]{0:T(128)S(1)} %copy-done.4, bf16[4,4,512,768]{3,2,1,0:T(8,128)(2,1)S(1)} %copy-done, bf16[768,128]{1,0:T(8,128)(2,1)S(1)} %get-tuple-element.46.refs_1_, ...), custom_call_target="tpu_custom_call" | custom-call | flops 1879048192 | bytes 13369344 | tf_op jit(solution)/shard_map/query/pallas_call | solution.py:459
  154.8 0.6 copy-done.3
  155.5 1.9 %collective-permute-start.19 = (bf16[512,128]{1,0:T(8,128)(2,1)S(1)}, bf16[512,128]{1,0:T(8,128)(2,1)S(1)}, u32[]{:S(2)}, u32[]{:S(2)}) collective-permute-start(bf16[512,128]{1,0:T(8,128)(2,1)S(1)} %get-tuple-element.50), channel_id=1, source_target_pairs={{0,4},{4,0},{8,12},{12,8},{1,5},{5,1},{9,13},{13,9},{2,6},{6,2},{1... | collective-permute-start | bytes 393224 | tf_op jit(solution)/shard_map/ppermute | solution.py:127
  157.4 1.5 collective-permute-start.21
  159.0 0.0 collective-permute-done.18.refs_2_
  159.0 0.0 collective-permute-start.23
  159.0 1.9 %collective-permute-done.19.refs_3_ = bf16[512,128]{1,0:T(8,128)(2,1)S(1)} collective-permute-done((bf16[512,128]{1,0:T(8,128)(2,1)S(1)}, bf16[512,128]{1,0:T(8,128)(2,1)S(1)}, u32[]{:S(2)}, u32[]{:S(2)}) %collective-permute-start.19) | collective-permute-done | bytes 131104 | tf_op jit(solution)/shard_map/ppermute | solution.py:127
  160.9 4.3 %collective-permute-done.21.refs_5_ = bf16[512,128]{1,0:T(8,128)(2,1)S(1)} collective-permute-done((bf16[512,128]{1,0:T(8,128)(2,1)S(1)}, bf16[512,128]{1,0:T(8,128)(2,1)S(1)}, u32[]{:S(2)}, u32[]{:S(2)}) %collective-permute-start.21) | collective-permute-done | bytes 131104 | tf_op jit(solution)/shard_map/ppermute | solution.py:127
  165.2 0.6 copy-done.16
  165.9 0.1 copy-done.17
  165.9 2.6 %merge.1 = bf16[512,1024]{1,0:T(8,128)(2,1)} custom-call(s32[4]{0:T(128)} %pad_add_fusion.places, bf16[512,128]{1,0:T(8,128)(2,1)} %copy-done.2, bf16[512,128]{1,0:T(8,128)(2,1)} %copy-done.3, bf16[512,128]{1,0:T(8,128)(2,1)} %copy-done.12, bf16[512,128]{1,0:T(8,128)(2,1)} %copy-done.15, bf16[512,128]{1,0:T(8,128)(2,1)} %copy-done.13, ...), custom_call_target="tpu_custom_call" | custom-call | tf_op jit(solution)/shard_map/merge/pallas_call | solution.py:478
  (37 shorter events, 0.1 us)
Async XLA Ops:
  2.3 22.2 %collective-permute-start = (bf16[536,768]{1,0:T(8,128)(2,1)S(1)}, bf16[536,768]{1,0:T(8,128)(2,1)S(1)}, u32[]{:S(2)}, u32[]{:S(2)}) collective-permute-start(bf16[536,768]{1,0:T(8,128)(2,1)S(1)} %pad_maximum_fusion), channel_id=1, source_target_pairs={{0,4},{4,0},{8,12},{12,8},{1,5},{5,1},{9,13},{13,9},{2,6},{6,2},{1... | collective-permute-start | bytes 2469896 | tf_op jit(solution)/shard_map/ppermute | solution.py:127
  10.9 77.3 %all-to-all-start = ((bf16[4,768,512]{2,1,0:T(8,128)(2,1)}), bf16[4,768,512]{2,1,0:T(8,128)(2,1)}, u32[]{:S(2)}, u32[]{:S(2)}) async-start(bf16[4,768,512]{2,1,0:T(8,128)(2,1)} %pack.1), calls=%async_computation | async-start | bytes 6291456 | tf_op jit(solution)/shard_map/all_to_all | solution.py:383
  15.6 72.7 %copy-start.4 = (s32[4]{0:T(128)S(1)}, s32[4]{0:T(128)}, u32[]{:S(2)}) copy-start(s32[4]{0:T(128)} %pad_add_fusion.places) | copy-start | bytes 52
  15.6 19.9 %collective-permute-start.2 = (bf16[536,768]{1,0:T(8,128)(2,1)S(1)}, bf16[536,768]{1,0:T(8,128)(2,1)S(1)}, u32[]{:S(2)}, u32[]{:S(2)}) collective-permute-start(bf16[536,768]{1,0:T(8,128)(2,1)S(1)} %pad_maximum_fusion), channel_id=1, source_target_pairs={{0,16},{16,0},{1,17},{17,1},{2,18},{18,2},{3,19},{19,3},{4,20},{20... | collective-permute-start | bytes 2469896 | tf_op jit(solution)/shard_map/ppermute | solution.py:127
  24.5 10.9 %collective-permute-start.1 = (bf16[536,768]{1,0:T(8,128)(2,1)S(1)}, bf16[536,768]{1,0:T(8,128)(2,1)S(1)}, u32[]{:S(2)}, u32[]{:S(2)}) collective-permute-start(bf16[536,768]{1,0:T(8,128)(2,1)S(1)} %collective-permute-done.refs_1_), channel_id=1, source_target_pairs={{0,1},{1,0},{2,3},{3,2},{4,5},{5,4},{6,7},{7,6},{8,9},{9,8},{10,11... | collective-permute-start | bytes 2469896 | tf_op jit(solution)/shard_map/ppermute | solution.py:127
  35.5 0.9 copy-start.7
  36.4 19.0 %collective-permute-start.8 = (bf16[536,768]{1,0:T(8,128)(2,1)S(1)}, bf16[536,768]{1,0:T(8,128)(2,1)S(1)}, u32[]{:S(2)}, u32[]{:S(2)}) collective-permute-start(bf16[536,768]{1,0:T(8,128)(2,1)S(1)} %collective-permute-done.refs_1_), channel_id=1, source_target_pairs={{0,16},{16,0},{1,17},{17,1},{2,18},{18,2},{3,19},{19,3},{4,20},{20... | collective-permute-start | bytes 2469896 | tf_op jit(solution)/shard_map/ppermute | solution.py:127
  37.9 18.8 %collective-permute-start.3 = (bf16[536,768]{1,0:T(8,128)(2,1)S(1)}, bf16[536,768]{1,0:T(8,128)(2,1)}, u32[]{:S(2)}, u32[]{:S(2)}) collective-permute-start(bf16[536,768]{1,0:T(8,128)(2,1)S(1)} %collective-permute-done.refs_1_), channel_id=1, source_target_pairs={{0,2},{2,0},{1,3},{3,1},{4,6},{6,4},{5,7},{7,5},{8,10},{10,8},{9,1... | collective-permute-start | bytes 2469896 | tf_op jit(solution)/shard_map/ppermute | solution.py:127
  55.4 4.7 %copy-start.5 = (bf16[536,768]{1,0:T(8,128)(2,1)}, bf16[536,768]{1,0:T(8,128)(2,1)S(1)}, u32[]{:S(2)}) copy-start(bf16[536,768]{1,0:T(8,128)(2,1)S(1)} %collective-permute-done.8.refs_9_) | copy-start | bytes 2469892
  55.4 2.3 %collective-permute-start.9 = (bf16[536,768]{1,0:T(8,128)(2,1)S(1)}, bf16[536,768]{1,0:T(8,128)(2,1)S(1)}, u32[]{:S(2)}, u32[]{:S(2)}) collective-permute-start(bf16[536,768]{1,0:T(8,128)(2,1)S(1)} %collective-permute-done.8.refs_9_), channel_id=1, source_target_pairs={{0,1},{1,0},{2,3},{3,2},{4,5},{5,4},{6,7},{7,6},{8,9},{9,8},{10,11... | collective-permute-start | bytes 2469896 | tf_op jit(solution)/shard_map/ppermute | solution.py:127
  57.7 0.9 copy-start.9
  58.6 20.9 %collective-permute-start.10 = (bf16[536,768]{1,0:T(8,128)(2,1)S(1)}, bf16[536,768]{1,0:T(8,128)(2,1)}, u32[]{:S(2)}, u32[]{:S(2)}) collective-permute-start(bf16[536,768]{1,0:T(8,128)(2,1)S(1)} %collective-permute-done.8.refs_9_), channel_id=1, source_target_pairs={{0,2},{2,0},{1,3},{3,1},{4,6},{6,4},{5,7},{7,5},{8,10},{10,8},{9,1... | collective-permute-start | bytes 2469896 | tf_op jit(solution)/shard_map/ppermute | solution.py:127
  60.1 19.4 %collective-permute-start.5 = (bf16[512,768]{1,0:T(8,128)(2,1)S(1)}, bf16[512,768]{1,0:T(8,128)(2,1)}, u32[]{:S(2)}, u32[]{:S(2)}) collective-permute-start(bf16[512,768]{1,0:T(8,128)(2,1)S(1)} %get-tuple-element.31), channel_id=1, source_target_pairs={{0,16},{16,0},{1,17},{17,1},{2,18},{18,2},{3,19},{19,3},{4,20},{20... | collective-permute-start | bytes 2359304 | tf_op jit(solution)/shard_map/ppermute | solution.py:127
  61.6 23.6 %collective-permute-start.6 = (bf16[536,768]{1,0:T(8,128)(2,1)S(1)}, bf16[536,768]{1,0:T(8,128)(2,1)}, u32[]{:S(2)}, u32[]{:S(2)}) collective-permute-start(bf16[536,768]{1,0:T(8,128)(2,1)S(1)} %collective-permute-done.2.refs_5_), channel_id=1, source_target_pairs={{0,1},{1,0},{2,3},{3,2},{4,5},{5,4},{6,7},{7,6},{8,9},{9,8},{10,11... | collective-permute-start | bytes 2469896 | tf_op jit(solution)/shard_map/ppermute | solution.py:127
  61.6 26.7 %collective-permute-start.4 = (bf16[536,768]{1,0:T(8,128)(2,1)}, bf16[536,768]{1,0:T(8,128)(2,1)}, u32[]{:S(2)}, u32[]{:S(2)}) collective-permute-start(bf16[536,768]{1,0:T(8,128)(2,1)} %collective-permute-done.3.refs_2_), channel_id=1, source_target_pairs={{0,1},{1,0},{2,3},{3,2},{4,5},{5,4},{6,7},{7,6},{8,9},{9,8},{10,11... | collective-permute-start | bytes 2469896 | tf_op jit(solution)/shard_map/ppermute | solution.py:127
  79.5 8.8 %collective-permute-start.11 = (bf16[536,768]{1,0:T(8,128)(2,1)}, bf16[536,768]{1,0:T(8,128)(2,1)}, u32[]{:S(2)}, u32[]{:S(2)}) collective-permute-start(bf16[536,768]{1,0:T(8,128)(2,1)} %collective-permute-done.10.refs_10_), channel_id=1, source_target_pairs={{0,1},{1,0},{2,3},{3,2},{4,5},{5,4},{6,7},{7,6},{8,9},{9,8},{10,11... | collective-permute-start | bytes 2469896 | tf_op jit(solution)/shard_map/ppermute | solution.py:127
  79.5 8.1 %collective-permute-start.7 = (bf16[512,768]{1,0:T(8,128)(2,1)}, bf16[512,768]{1,0:T(8,128)(2,1)}, u32[]{:S(2)}, u32[]{:S(2)}) collective-permute-start(bf16[512,768]{1,0:T(8,128)(2,1)} %collective-permute-done.5.refs_6_), channel_id=1, source_target_pairs={{0,1},{1,0},{2,3},{3,2},{4,5},{5,4},{6,7},{7,6},{8,9},{9,8},{10,11... | collective-permute-start | bytes 2359304 | tf_op jit(solution)/shard_map/ppermute | solution.py:127
  83.9 36.3 %collective-permute-start.12 = (bf16[768,256]{1,0:T(8,128)(2,1)S(1)}, bf16[768,256]{1,0:T(8,128)(2,1)S(1)}, u32[]{:S(2)}, u32[]{:S(2)}) collective-permute-start(bf16[768,256]{1,0:T(8,128)(2,1)S(1)} %constant_dynamic-slice_fusion.3), channel_id=1, source_target_pairs={{0,4},{4,0},{8,12},{12,8},{1,5},{5,1},{9,13},{13,9},{2,6},{6,2},{1... | collective-permute-start | bytes 1179656 | tf_op jit(solution)/shard_map/ppermute | solution.py:127
  85.2 30.4 %collective-permute-start.13 = (bf16[768,128]{1,0:T(8,128)(2,1)S(1)}, bf16[768,128]{1,0:T(8,128)(2,1)S(1)}, u32[]{:S(2)}, u32[]{:S(2)}) collective-permute-start(bf16[768,128]{1,0:T(8,128)(2,1)S(1)} %get-tuple-element.36.refs_1_), channel_id=1, source_target_pairs={{0,8},{4,12},{8,0},{12,4},{1,9},{5,13},{9,1},{13,5},{2,10},{6,14},... | collective-permute-start | bytes 589832 | tf_op jit(solution)/shard_map/ppermute | solution.py:127
  87.6 32.6 %collective-permute-start.14 = (bf16[768,128]{1,0:T(8,128)(2,1)}, bf16[768,128]{1,0:T(8,128)(2,1)S(1)}, u32[]{:S(2)}, u32[]{:S(2)}) collective-permute-start(bf16[768,128]{1,0:T(8,128)(2,1)} %get-tuple-element.37), channel_id=1, source_target_pairs={{0,12},{4,8},{8,4},{12,0},{1,13},{5,9},{9,5},{13,1},{2,14},{6,10},... | collective-permute-start | bytes 589832 | tf_op jit(solution)/shard_map/ppermute | solution.py:127
  88.3 1.1 copy-start.6
  89.4 1.1 copy-start.8
  90.6 1.1 copy-start.10
  91.7 23.9 %copy-start.11 = (bf16[768,128]{1,0:T(8,128)(2,1)S(1)}, bf16[768,128]{1,0:T(8,128)(2,1)}, u32[]{:S(2)}) copy-start(bf16[768,128]{1,0:T(8,128)(2,1)} %get-tuple-element.47) | copy-start | bytes 589828
  112.0 8.2 %collective-permute-start.15 = (bf16[2,2,128,128]{3,2,1,0:T(8,128)(2,1)S(1)}, bf16[2,2,128,128]{3,2,1,0:T(8,128)(2,1)S(1)}, u32[]{:S(2)}, u32[]{:S(2)}) collective-permute-start(bf16[2,2,128,128]{3,2,1,0:T(8,128)(2,1)S(1)} %get-tuple-element.44), channel_id=1, source_target_pairs={{0,8},{4,12},{1,9},{5,13},{2,10},{6,14},{3,11},{7,15},{16,24},{20,... | collective-permute-start | bytes 393224 | tf_op jit(solution)/shard_map/ppermute | solution.py:450
  115.5 30.9 %collective-permute-start.16 = (bf16[768,128]{1,0:T(8,128)(2,1)S(1)}, bf16[768,128]{1,0:T(8,128)(2,1)S(1)}, u32[]{:S(2)}, u32[]{:S(2)}) collective-permute-start(bf16[768,128]{1,0:T(8,128)(2,1)S(1)} %get-tuple-element.46.refs_1_), channel_id=1, source_target_pairs={{0,8},{4,12},{8,0},{12,4},{1,9},{5,13},{9,1},{13,5},{2,10},{6,14},... | collective-permute-start | bytes 589832 | tf_op jit(solution)/shard_map/ppermute | solution.py:127
  115.6 30.8 %collective-permute-start.17 = (bf16[768,128]{1,0:T(8,128)(2,1)S(1)}, bf16[768,128]{1,0:T(8,128)(2,1)S(1)}, u32[]{:S(2)}, u32[]{:S(2)}) collective-permute-start(bf16[768,128]{1,0:T(8,128)(2,1)S(1)} %copy-done.11), channel_id=1, source_target_pairs={{0,12},{4,8},{8,4},{12,0},{1,13},{5,9},{9,5},{13,1},{2,14},{6,10},... | collective-permute-start | bytes 589832 | tf_op jit(solution)/shard_map/ppermute | solution.py:127
  120.2 4.6 %copy-start = (bf16[4,4,512,768]{3,2,1,0:T(8,128)(2,1)S(1)}, bf16[4,4,512,768]{3,2,1,0:T(8,128)(2,1)}, u32[]{:S(2)}) copy-start(bf16[4,4,512,768]{3,2,1,0:T(8,128)(2,1)} %get-tuple-element.34.refs_0_) | copy-start | bytes 37748740
  124.8 1.6 copy-start.1
  134.8 20.0 %copy-start.2 = (bf16[512,128]{1,0:T(8,128)(2,1)}, bf16[512,128]{1,0:T(8,128)(2,1)S(1)}, u32[]{:S(2)}) copy-start(bf16[512,128]{1,0:T(8,128)(2,1)S(1)} %get-tuple-element.45.refs_0_) | copy-start | bytes 393220
  134.8 24.2 %collective-permute-start.18 = (bf16[512,128]{1,0:T(8,128)(2,1)S(1)}, bf16[512,128]{1,0:T(8,128)(2,1)S(1)}, u32[]{:S(2)}, u32[]{:S(2)}) collective-permute-start(bf16[512,128]{1,0:T(8,128)(2,1)S(1)} %get-tuple-element.49), channel_id=1, source_target_pairs={{0,4},{4,0},{8,12},{12,8},{1,5},{5,1},{9,13},{13,9},{2,6},{6,2},{1... | collective-permute-start | bytes 393224 | tf_op jit(solution)/shard_map/ppermute | solution.py:127
  144.9 14.1 %collective-permute-start.20 = (bf16[512,128]{1,0:T(8,128)(2,1)S(1)}, bf16[512,128]{1,0:T(8,128)(2,1)S(1)}, u32[]{:S(2)}, u32[]{:S(2)}) collective-permute-start(bf16[512,128]{1,0:T(8,128)(2,1)S(1)} %get-tuple-element.51), channel_id=1, source_target_pairs={{0,16},{16,0},{1,17},{17,1},{2,18},{18,2},{3,19},{19,3},{4,20},{20... | collective-permute-start | bytes 393224 | tf_op jit(solution)/shard_map/ppermute | solution.py:127
  146.4 12.6 %collective-permute-start.22 = (bf16[512,128]{1,0:T(8,128)(2,1)S(1)}, bf16[512,128]{1,0:T(8,128)(2,1)S(1)}, u32[]{:S(2)}, u32[]{:S(2)}) collective-permute-start(bf16[512,128]{1,0:T(8,128)(2,1)S(1)} %get-tuple-element.53), channel_id=1, source_target_pairs={{0,20},{4,16},{8,28},{12,24},{16,4},{20,0},{24,12},{28,8},{1,21},{... | collective-permute-start | bytes 393224 | tf_op jit(solution)/shard_map/ppermute | solution.py:475
  154.8 0.7 copy-start.3
  155.5 5.4 %collective-permute-start.19 = (bf16[512,128]{1,0:T(8,128)(2,1)S(1)}, bf16[512,128]{1,0:T(8,128)(2,1)S(1)}, u32[]{:S(2)}, u32[]{:S(2)}) collective-permute-start(bf16[512,128]{1,0:T(8,128)(2,1)S(1)} %get-tuple-element.50), channel_id=1, source_target_pairs={{0,4},{4,0},{8,12},{12,8},{1,5},{5,1},{9,13},{13,9},{2,6},{6,2},{1... | collective-permute-start | bytes 393224 | tf_op jit(solution)/shard_map/ppermute | solution.py:127
  157.4 7.8 %collective-permute-start.21 = (bf16[512,128]{1,0:T(8,128)(2,1)S(1)}, bf16[512,128]{1,0:T(8,128)(2,1)S(1)}, u32[]{:S(2)}, u32[]{:S(2)}) collective-permute-start(bf16[512,128]{1,0:T(8,128)(2,1)S(1)} %get-tuple-element.52), channel_id=1, source_target_pairs={{0,16},{16,0},{1,17},{17,1},{2,18},{18,2},{3,19},{19,3},{4,20},{20... | collective-permute-start | bytes 393224 | tf_op jit(solution)/shard_map/ppermute | solution.py:127
  159.0 6.3 %copy-start.12 = (bf16[512,128]{1,0:T(8,128)(2,1)}, bf16[512,128]{1,0:T(8,128)(2,1)S(1)}, u32[]{:S(2)}) copy-start(bf16[512,128]{1,0:T(8,128)(2,1)S(1)} %collective-permute-done.18.refs_2_) | copy-start | bytes 393220
  159.0 6.2 %collective-permute-start.23 = (bf16[512,128]{1,0:T(8,128)(2,1)S(1)}, bf16[512,128]{1,0:T(8,128)(2,1)S(1)}, u32[]{:S(2)}, u32[]{:S(2)}) collective-permute-start(bf16[512,128]{1,0:T(8,128)(2,1)S(1)} %get-tuple-element.54), channel_id=1, source_target_pairs={{0,20},{4,16},{8,28},{12,24},{16,4},{20,0},{24,12},{28,8},{1,21},{... | collective-permute-start | bytes 393224 | tf_op jit(solution)/shard_map/ppermute | solution.py:475
  159.0 6.2 %copy-start.13 = (bf16[512,128]{1,0:T(8,128)(2,1)}, bf16[512,128]{1,0:T(8,128)(2,1)S(1)}, u32[]{:S(2)}) copy-start(bf16[512,128]{1,0:T(8,128)(2,1)S(1)} %collective-permute-done.20.refs_4_) | copy-start | bytes 393220
  159.0 6.2 %copy-start.14 = (bf16[512,128]{1,0:T(8,128)(2,1)}, bf16[512,128]{1,0:T(8,128)(2,1)S(1)}, u32[]{:S(2)}) copy-start(bf16[512,128]{1,0:T(8,128)(2,1)S(1)} %collective-permute-done.22.refs_6_) | copy-start | bytes 393220
  160.9 4.3 %copy-start.15 = (bf16[512,128]{1,0:T(8,128)(2,1)}, bf16[512,128]{1,0:T(8,128)(2,1)S(1)}, u32[]{:S(2)}) copy-start(bf16[512,128]{1,0:T(8,128)(2,1)S(1)} %collective-permute-done.19.refs_3_) | copy-start | bytes 393220
  165.2 0.6 copy-start.16
  165.2 0.7 copy-start.17

commit v4 on v3

--- a/solution.py
+++ b/solution.py
@@ -186,16 +186,25 @@
     return start, wait
 
 
-def project(token_refs, weights):
+def project(held, side, cut, weights):
     total = None
-    for token_ref, weight in zip(token_refs, weights):
-        product = jnp.dot(token_ref[...], weight, preferred_element_type=jnp.float32)
+    for flip, weight in enumerate(weights):
+        product = jnp.dot(held[side, flip, cut, :], weight, preferred_element_type=jnp.float32)
         total = product if total is None else total + product
     return total
 
 
 def piece_rows(rows):
     return [slice(at, at + PIECE) for at in range(0, rows, PIECE)]
+
+
+def staggered(items, *stages):
+    carried = {}
+    for turn in range(len(items) + len(stages) - 1):
+        for depth in reversed(range(len(stages))):
+            at = turn - depth
+            if 0 <= at < len(items):
+                carried[at] = stages[depth](items[at], carried.get(at))
 
 
 def key_value_kernel(heads, size, flips, places, *refs):
@@ -203,7 +212,7 @@
     token_refs, refs = refs[:13], refs[13:]
     decay_refs, refs = refs[:sides], refs[sides:]
     source_ref, held, key_ref, value_ref, state_ref, sum_ref, fade_ref, mask_ref, pair_ref = refs[:9]
-    weight_ref, decay_ref, semaphores, weight_semaphores = refs[9:]
+    weight_ref, decay_ref, end_ref, semaphores, weight_semaphores = refs[9:]
     loads = [
         pltpu.make_async_copy(
             source_ref.at[places[0] ^ flip], weight_ref.at[flip], weight_semaphores.at[flip]
@@ -225,43 +234,54 @@
         log_decay = part[:count] + (part[count : 2 * count] + part[2 * count :])
         decay_ref[...] = running_sum(log_decay[:, : sum_ref.shape[2]])
         for head in range(heads):
-            sum_ref[side, head : head + 1, :] = decay_ref[pl.ds(places[3] * heads + head, 1), :]
-    for load in loads:
-        load.wait()
-    for side in range(sides):
-        wait(side)
-        for head in range(heads):
-            at = slice(2 * head * size, 2 * (head + 1) * size)
-            both = project(
-                [held.at[side, flip] for flip in range(flips)],
-                [weight_ref[flip, :, at] for flip in range(flips)],
-            )
-            key = silu(both[:, :size])
-            key_bf = key.astype(jnp.bfloat16)
-            key = key_bf.astype(jnp.float32)
-            value = both[:, size:].astype(jnp.bfloat16)
-            key_ref[side, :, head * size : (head + 1) * size] = key_bf
-            value_ref[side, :, head * size : (head + 1) * size] = value
-            row = sum_ref[side, head : head + 1, :]
+            row = decay_ref[pl.ds(places[3] * heads + head, 1), :]
+            sum_ref[side, head : head + 1, :] = row
             column = column_of(row)
-            ends = [column[cut.stop - 1 : cut.stop, :] for cut in cuts]
-            fresh = []
-            for cut, end in zip(cuts, ends):
-                scaled = (key[cut] * jnp.exp(end - column[cut])).astype(jnp.bfloat16)
-                fresh.append(
-                    lax.dot_general(
-                        scaled, value[cut], (((0,), (0,)), ((), ())), preferred_element_type=jnp.float32
-                    )
-                )
-            state = fresh[0]
-            for piece, cut in enumerate(cuts):
-                begin = ends[piece - 1] if piece else jnp.zeros_like(ends[0])
-                if piece:
-                    state = jnp.exp(ends[piece] - begin) * state + fresh[piece]
-                state_ref[head, side, piece] = state
+            begin = jnp.zeros_like(column[:1])
+            for cut in cuts:
+                end = column[cut.stop - 1 : cut.stop, :]
+                end_ref[head, side, cut, :] = jnp.exp(end - column[cut])
                 fade_ref[head, side, cut, :] = jnp.exp(column[cut] - begin)
                 gaps = jnp.where(causal, column[cut] - row[:, cut], -jnp.inf)
                 mask_ref[head, side, cut, :] = jnp.exp(gaps)
+                begin = end
+    for load in loads:
+        load.wait()
+
+    def first(item, _):
+        side, head, piece = item
+        if head == 0 and piece == 0:
+            wait(side)
+        at = slice(2 * head * size, 2 * (head + 1) * size)
+        return project(held, side, cuts[piece], [weight_ref[flip, :, at] for flip in range(flips)])
+
+    def second(item, both):
+        side, head, piece = item
+        cut, to = cuts[piece], slice(head * size, (head + 1) * size)
+        key = silu(both[:, :size]).astype(jnp.bfloat16)
+        value = both[:, size:].astype(jnp.bfloat16)
+        key_ref[side, cut, to] = key
+        value_ref[side, cut, to] = value
+        scaled = (key.astype(jnp.float32) * end_ref[head, side, cut, :]).astype(jnp.bfloat16)
+        return scaled, value
+
+    def third(item, pair):
+        side, head, piece = item
+        state = lax.dot_general(
+            pair[0], pair[1], (((0,), (0,)), ((), ())), preferred_element_type=jnp.float32
+        )
+        if piece:
+            sums, cut = sum_ref[side, head : head + 1, :], cuts[piece]
+            fade = sums[:, cut.stop - 1 : cut.stop] - sums[:, cut.start - 1 : cut.start]
+            state += jnp.exp(fade) * state_ref[head, side, piece - 1]
+        state_ref[head, side, piece] = state
+
+    staggered(
+        [(side, head, piece) for side in range(sides) for head in range(heads) for piece in range(len(cuts))],
+        first,
+        second,
+        third,
+    )
     last = len(cuts) - 1
     end = sum_ref.shape[2] - 1
     for head in range(heads):
@@ -279,11 +299,13 @@
     held, refs = refs[0], refs[1:]
     weight_refs, refs = refs[:flips], refs[flips:]
     key_ref, value_ref, state_ref, sum_ref, fade_ref, mask_ref, before_ref = refs[:7]
-    out_refs = refs[7:]
+    out_refs, incoming_ref = refs[7:-1], refs[-1]
     odd = places[0] % 2 == 1
     cuts = piece_rows(key_ref.shape[1])
     last = len(cuts) - 1
     end = sum_ref.shape[2] - 1
+    at = slice(head * PIECE, (head + 1) * PIECE)
+    weights = [ref[:, columns] if flip == 1 else ref[...] for flip, ref in enumerate(weight_refs)]
     for side in range(sides):
         partner = side ^ 1
         before = before_ref[head, side // 2].astype(jnp.float32)
@@ -291,40 +313,37 @@
         later = jnp.exp(total) * before + state_ref[head, partner, last]
         second = odd if side % 2 == 0 else jnp.logical_not(odd)
         incoming = jnp.where(second, later, before)
-        states = [incoming.astype(jnp.bfloat16)]
-        for piece in range(1, len(cuts)):
-            stop = cuts[piece].start - 1
-            sofar = jnp.exp(sum_ref[side, head : head + 1, stop : stop + 1])
-            states.append((state_ref[head, side, piece - 1] + sofar * incoming).astype(jnp.bfloat16))
-        query = project(
-            [held.at[side, flip] for flip in range(flips)],
-            [ref[:, columns] if flip == 1 else ref[...] for flip, ref in enumerate(weight_refs)],
-        )
-        query = silu(query).astype(jnp.bfloat16)
-        at = slice(head * PIECE, (head + 1) * PIECE)
-        weights = [
-            (
-                lax.dot_general(
-                    query[cut],
-                    key_ref[side, cut, at],
-                    (((1,), (1,)), ((), ())),
-                    preferred_element_type=jnp.float32,
-                )
-                * mask_ref[head, side, cut, :]
-            ).astype(jnp.bfloat16)
-            for cut in cuts
-        ]
-        raws = [
-            jnp.dot(query[cut], state, preferred_element_type=jnp.float32) * fade_ref[head, side, cut, :]
-            for cut, state in zip(cuts, states)
-        ]
-        raws = [
-            raw + jnp.dot(weight, value_ref[side, cut, at], preferred_element_type=jnp.float32)
-            for raw, weight, cut in zip(raws, weights, cuts)
-        ]
-        for raw, cut in zip(raws, cuts):
-            scale = lax.rsqrt(jnp.mean(raw * raw, axis=1, keepdims=True) + EPSILON)
-            out_refs[side][cut, :] = (raw * scale).astype(jnp.bfloat16)
+        for piece, cut in enumerate(cuts):
+            state = incoming
+            if piece:
+                sofar = jnp.exp(sum_ref[side, head : head + 1, cut.start - 1 : cut.start])
+                state = state_ref[head, side, piece - 1] + sofar * incoming
+            incoming_ref[side, piece] = state.astype(jnp.bfloat16)
+
+    def first(item, _):
+        side, piece = item
+        return silu(project(held, side, cuts[piece], weights)).astype(jnp.bfloat16)
+
+    def second(item, query):
+        side, cut = item[0], cuts[item[1]]
+        scores = lax.dot_general(
+            query, key_ref[side, cut, at], (((1,), (1,)), ((), ())), preferred_element_type=jnp.float32
+        )
+        raw = jnp.dot(query, incoming_ref[side, item[1]], preferred_element_type=jnp.float32)
+        return (scores * mask_ref[head, side, cut, :]).astype(jnp.bfloat16), raw * fade_ref[head, side, cut, :]
+
+    def third(item, pair):
+        side, cut = item[0], cuts[item[1]]
+        return pair[1] + jnp.dot(pair[0], value_ref[side, cut, at], preferred_element_type=jnp.float32)
+
+    def fourth(item, raw):
+        side, cut = item[0], cuts[item[1]]
+        scale = lax.rsqrt(jnp.mean(raw * raw, axis=1, keepdims=True) + EPSILON)
+        out_refs[side][cut, :] = (raw * scale).astype(jnp.bfloat16)
+
+    staggered(
+        [(side, piece) for side in range(sides) for piece in range(len(cuts))], first, second, third, fourth
+    )
 
 
 def merge_kernel(heads, size, places, *refs):
@@ -384,8 +403,9 @@
 
     from_ctx = xor_permute(quarter, mesh, "ctx", 1)
     from_groups = xor_permute(quarter, mesh, "groups", 1)
+    (from_ctx,) = after((from_ctx,), from_groups)
     ctx_core = xor_permute(from_ctx, mesh, "head", 1)
-    (from_ctx,) = after((from_ctx,), ctx_core, from_groups)
+    (from_ctx,) = after((from_ctx,), ctx_core)
     ctx_plane = xor_permute(from_ctx, mesh, "fsdp", 1)
     from_both = xor_permute(from_ctx, mesh, "groups", 1)
     groups_plane = xor_permute(after((beside,), from_ctx)[0], mesh, "groups", 1)
@@ -434,6 +454,7 @@
         scratch_shapes=[
             pltpu.VMEM(packed_shape, jnp.bfloat16),
             pltpu.VMEM(log_decay.shape, jnp.float32),
+            pltpu.VMEM((heads, sides, rows, size), jnp.float32),
             pltpu.SemaphoreType.DMA((sides, flips)),
             pltpu.SemaphoreType.DMA((flips,)),
         ],
@@ -461,6 +482,7 @@
             in_specs=[SCALARS] + [VMEM] * (1 + flips + len(memory) + 1),
             out_specs=[VMEM] * sides,
             out_shape=[jax.ShapeDtypeStruct((rows, size), jnp.bfloat16)] * sides,
+            scratch_shapes=[pltpu.VMEM((sides, pieces, size, size), jnp.bfloat16)],
             compiler_params=small,
             cost_estimate=pl.CostEstimate(
                 flops=2 * sides * rows * size * (width + 4 * size),

time: 169 us -> 159 us (0.941)
  Pallas kernels: 44.6 us -> 38.4 us
  starting transfers between devices: 44 us -> 38.3 us
  waiting for transfers between devices: 60.2 us -> 62.1 us
    ppermute x21, starting transfers between devices: 35.8 us -> 30 us  [xor_permute(): lax.ppermute(array, axis, [(at, at ^ flip) for at in range(mesh.shape[axi...]
    all_to_all x1, waiting for transfers between devices: 0.01 us -> 5.49 us  [spread_body(): key_value = lax.all_to_all(packed, 'ctx', 0, 0)]
    ppermute x21, waiting for transfers between devices: 60.2 us -> 55.2 us  [xor_permute(): lax.ppermute(array, axis, [(at, at ^ flip) for at in range(mesh.shape[axi...]
    pallas_call x1, Pallas kernels: 20.2 us -> 16.7 us  [spread_body(): pl.pallas_call(functools.partial(key_value_kernel, heads, size, flips), i...]
    pallas_call x2, Pallas kernels: 16.8 us -> 14.2 us  [spread_body(): pl.pallas_call(functools.partial(query_kernel, head, slice(head * size, (...]
    ppermute x2, starting transfers between devices: 0.04 us -> 2.05 us  [spread_body(): returned[3].append(lax.ppermute(attended[3], ('groups', 'ctx'), both))]
    ppermute x1, starting transfers between devices: 3.56 us -> 1.62 us  [spread_body(): lax.ppermute(pair_state, 'ctx', [(at, at + 2) for at in range(flips - 2)])]
  transfers between devices with their start and end apart: 25 -> 25, of which waited for: 8 -> 11; matrix products, arithmetic and copies ran while one was open for 3% -> 3% of each run, Pallas kernels for 25% -> 23%
where the time goes in v4:
time: 159 us; the launch traced here: 158 us
  waiting for transfers between devices  62.1 us (39%)
  Pallas kernels  38.4 us (24%)
  starting transfers between devices  38.3 us (24%)
  local copies, waits for them, and re-layouts  18 us (11%)
    ppermute x21, waiting for transfers between devices, xor_permute(): lax.ppermute(array, axis, [(at, at ^ flip) for at in range(mesh.shape[axi...  55.2 us
    ppermute x21, starting transfers between devices, xor_permute(): lax.ppermute(array, axis, [(at, at ^ flip) for at in range(mesh.shape[axi...  30 us
    pallas_call x1, Pallas kernels, spread_body(): pl.pallas_call(functools.partial(key_value_kernel, heads, size, flips), i...  16.7 us
    pallas_call x2, Pallas kernels, spread_body(): pl.pallas_call(functools.partial(query_kernel, head, slice(head * size, (...  14.2 us
    unnamed x36, local copies, waits for them, and re-layouts  12.7 us
    all_to_all x1, waiting for transfers between devices, spread_body(): key_value = lax.all_to_all(packed, 'ctx', 0, 0)  5.49 us
    pallas_call x1, Pallas kernels, spread_body(): pl.pallas_call(functools.partial(pack_kernel, heads, size), grid_spec=plt...  5.02 us
    all_to_all x1, starting transfers between devices, spread_body(): key_value = lax.all_to_all(packed, 'ctx', 0, 0)  4.65 us
  transfers between devices with their start and end apart: 25, of which 11 were waited for; matrix products, arithmetic and copies ran while one was open for 3% of the time, Pallas kernels for 23%

profile of v4, /device:TPU:0, one launch (start us, length us, event | category | flops | bytes accessed | tf_op | source)
XLA Modules:
  0.0 158.4 jit_solution(13874464690159585153)
XLA Ops:
  0.0 0.7 reduce-precision_convert_fusion.1
  0.7 1.5 constant_dynamic-slice_fusion.5
  2.2 0.1 pad_maximum_fusion
  2.3 3.0 %collective-permute-start.1 = (bf16[536,768]{1,0:T(8,128)(2,1)S(1)}, bf16[536,768]{1,0:T(8,128)(2,1)S(1)}, u32[]{:S(2)}, u32[]{:S(2)}) collective-permute-start(bf16[536,768]{1,0:T(8,128)(2,1)S(1)} %pad_maximum_fusion), channel_id=1, source_target_pairs={{0,16},{16,0},{1,17},{17,1},{2,18},{18,2},{3,19},{19,3},{4,20},{20... | collective-permute-start | bytes 2469896 | tf_op jit(solution)/shard_map/ppermute | solution.py:127
  5.3 1.6 collective-permute-start
  6.9 0.6 pad_add_fusion.places
  7.4 5.0 %pack.1 = bf16[4,768,512]{2,1,0:T(8,128)(2,1)} custom-call(s32[4]{0:T(128)} %pad_add_fusion.places, bf16[768,1024]{1,0:T(8,128)(2,1)} %key_ref.1, bf16[768,1024]{1,0:T(8,128)(2,1)} %value_ref.1), custom_call_target="tpu_custom_call" | custom-call | bytes 6291456 | tf_op jit(solution)/shard_map/pack/pallas_call | solution.py:389
  12.5 4.6 %all-to-all-start = ((bf16[4,768,512]{2,1,0:T(8,128)(2,1)}), bf16[4,768,512]{2,1,0:T(8,128)(2,1)}, u32[]{:S(2)}, u32[]{:S(2)}) async-start(bf16[4,768,512]{2,1,0:T(8,128)(2,1)} %pack.1), calls=%async_computation | async-start | bytes 6291456 | tf_op jit(solution)/shard_map/all_to_all | solution.py:402
  17.1 6.5 %collective-permute-done.1.refs_5_ = bf16[536,768]{1,0:T(8,128)(2,1)S(1)} collective-permute-done((bf16[536,768]{1,0:T(8,128)(2,1)S(1)}, bf16[536,768]{1,0:T(8,128)(2,1)S(1)}, u32[]{:S(2)}, u32[]{:S(2)}) %collective-permute-start.1) | collective-permute-done | bytes 823328 | tf_op jit(solution)/shard_map/ppermute | solution.py:127
  23.6 3.8 %collective-permute-done.refs_1_ = bf16[536,768]{1,0:T(8,128)(2,1)S(1)} collective-permute-done((bf16[536,768]{1,0:T(8,128)(2,1)S(1)}, bf16[536,768]{1,0:T(8,128)(2,1)S(1)}, u32[]{:S(2)}, u32[]{:S(2)}) %collective-permute-start) | collective-permute-done | bytes 823328 | tf_op jit(solution)/shard_map/ppermute | solution.py:127
  27.5 0.0 collective-permute-start.2
  27.5 2.3 %collective-permute-done.2.refs_3_ = bf16[536,768]{1,0:T(8,128)(2,1)S(1)} collective-permute-done((bf16[536,768]{1,0:T(8,128)(2,1)S(1)}, bf16[536,768]{1,0:T(8,128)(2,1)S(1)}, u32[]{:S(2)}, u32[]{:S(2)}) %collective-permute-start.2) | collective-permute-done | bytes 823328 | tf_op jit(solution)/shard_map/ppermute | solution.py:127
  29.8 0.9 copy-done.7
  30.7 0.0 collective-permute-start.8
  30.7 2.0 %collective-permute-start.3 = (bf16[536,768]{1,0:T(8,128)(2,1)S(1)}, bf16[536,768]{1,0:T(8,128)(2,1)}, u32[]{:S(2)}, u32[]{:S(2)}) collective-permute-start(bf16[536,768]{1,0:T(8,128)(2,1)S(1)} %collective-permute-done.refs_1_), channel_id=1, source_target_pairs={{0,2},{2,0},{1,3},{3,1},{4,6},{6,4},{5,7},{7,5},{8,10},{10,8},{9,1... | collective-permute-start | bytes 2469896 | tf_op jit(solution)/shard_map/ppermute | solution.py:127
  32.7 18.4 %collective-permute-done.8.refs_9_ = bf16[536,768]{1,0:T(8,128)(2,1)S(1)} collective-permute-done((bf16[536,768]{1,0:T(8,128)(2,1)S(1)}, bf16[536,768]{1,0:T(8,128)(2,1)S(1)}, u32[]{:S(2)}, u32[]{:S(2)}) %collective-permute-start.8) | collective-permute-done | bytes 823328 | tf_op jit(solution)/shard_map/ppermute | solution.py:127
  51.1 0.1 collective-permute-done.3.refs_2_
  51.2 2.2 %collective-permute-done.9.refs_11_ = bf16[536,768]{1,0:T(8,128)(2,1)S(1)} collective-permute-done((bf16[536,768]{1,0:T(8,128)(2,1)S(1)}, bf16[536,768]{1,0:T(8,128)(2,1)S(1)}, u32[]{:S(2)}, u32[]{:S(2)}) %collective-permute-start.9) | collective-permute-done | bytes 823328 | tf_op jit(solution)/shard_map/ppermute | solution.py:127
  53.4 0.9 copy-done.9
  54.3 1.5 collective-permute-start.10
  55.8 0.5 collective-permute-start.5
  56.3 0.0 collective-permute-start.6
  56.3 0.5 collective-permute-start.4
  56.8 18.4 %collective-permute-done.5.refs_6_ = bf16[512,768]{1,0:T(8,128)(2,1)} collective-permute-done((bf16[512,768]{1,0:T(8,128)(2,1)S(1)}, bf16[512,768]{1,0:T(8,128)(2,1)}, u32[]{:S(2)}, u32[]{:S(2)}) %collective-permute-start.5) | collective-permute-done | bytes 786464 | tf_op jit(solution)/shard_map/ppermute | solution.py:127
  75.2 0.0 collective-permute-done.10.refs_10_
  75.2 0.0 collective-permute-start.11
  75.2 0.5 collective-permute-start.7
  75.7 1.0 constant_dynamic-slice_fusion.3
  76.8 2.0 %constant_dynamic-slice_fusion = (bf16[768,128]{1,0:T(8,128)(2,1)}, bf16[768,128]{1,0:T(8,128)(2,1)}, bf16[768,128]{1,0:T(8,128)(2,1)S(1)}, bf16[768,128]{1,0:T(8,128)(2,1)S(1)}) fusion(bf16[768,1024]{1,0:T(8,128)(2,1)} %param.6, s32[]{:T(128)S(6)} %select_n.32, s32[]{:T(128)S(6)} %select_n.30, s32[]{:T(128)S(6)} %select_n.29, s32[]{:T(128)S(6)} %select_n.31), kind=kLoop, calls=%fused_computation.13 | loop fusion | bytes 1572880 | tf_op jit(solution)/shard_map/dynamic_slice | solution.py:425
  78.8 0.8 slice.11.refs_16_
  79.6 0.7 collective-permute-start.12
  80.3 2.6 %collective-permute-start.13 = (bf16[768,128]{1,0:T(8,128)(2,1)S(1)}, bf16[768,128]{1,0:T(8,128)(2,1)S(1)}, u32[]{:S(2)}, u32[]{:S(2)}) collective-permute-start(bf16[768,128]{1,0:T(8,128)(2,1)S(1)} %get-tuple-element.38.refs_1_), channel_id=1, source_target_pairs={{0,8},{4,12},{8,0},{12,4},{1,9},{5,13},{9,1},{13,5},{2,10},{6,14},... | collective-permute-start | bytes 589832 | tf_op jit(solution)/shard_map/ppermute | solution.py:127
  82.9 1.1 collective-permute-start.14
  84.0 0.0 collective-permute-done.4.refs_4_
  84.0 5.5 %all-to-all-done.refs_17_ = bf16[4,768,512]{2,1,0:T(8,128)(2,1)} async-done(((bf16[4,768,512]{2,1,0:T(8,128)(2,1)}), bf16[4,768,512]{2,1,0:T(8,128)(2,1)}, u32[]{:S(2)}, u32[]{:S(2)}) %all-to-all-start) | async-done | bytes 3145760 | tf_op jit(solution)/shard_map/all_to_all | solution.py:402
  89.5 1.1 copy-done.6
  90.6 1.1 copy-done.8
  91.8 1.1 copy-done.10
  92.9 16.7 %key_value.1 = (bf16[4,4,512,768]{3,2,1,0:T(8,128)(2,1)}, bf16[4,512,256]{2,1,0:T(8,128)(2,1)S(1)}, bf16[4,512,256]{2,1,0:T(8,128)(2,1)S(1)}, f32[2,4,4,128,128]...) custom-call(s32[4]{0:T(128)S(1)} %copy-done.4, ...), custom_call_target="tpu_custom_call" | custom-call | flops 6442450944 | bytes 15728640 | tf_op jit(solution)/shard_map/key_value/pallas_call | solution.py:450
  109.6 1.6 %collective-permute-start.15 = (bf16[2,2,128,128]{3,2,1,0:T(8,128)(2,1)S(1)}, bf16[2,2,128,128]{3,2,1,0:T(8,128)(2,1)S(1)}, u32[]{:S(2)}, u32[]{:S(2)}) collective-permute-start(bf16[2,2,128,128]{3,2,1,0:T(8,128)(2,1)S(1)} %get-tuple-element.46), channel_id=1, source_target_pairs={{0,8},{4,12},{1,9},{5,13},{2,10},{6,14},{3,11},{7,15},{16,24},{20,... | collective-permute-start | bytes 393224 | tf_op jit(solution)/shard_map/ppermute | solution.py:471
  111.2 0.1 collective-permute-start.16
  111.3 4.9 %collective-permute-start.17 = (bf16[768,128]{1,0:T(8,128)(2,1)S(1)}, bf16[768,128]{1,0:T(8,128)(2,1)S(1)}, u32[]{:S(2)}, u32[]{:S(2)}) collective-permute-start(bf16[768,128]{1,0:T(8,128)(2,1)S(1)} %copy-done.11), channel_id=1, source_target_pairs={{0,12},{4,8},{8,4},{12,0},{1,13},{5,9},{9,5},{13,1},{2,14},{6,10},... | collective-permute-start | bytes 589832 | tf_op jit(solution)/shard_map/ppermute | solution.py:127
  116.2 0.0 collective-permute-done.14.refs_4_
  116.2 0.0 collective-permute-done.12.refs_2_
  116.2 4.6 %copy-done = bf16[4,4,512,768]{3,2,1,0:T(8,128)(2,1)S(1)} copy-done((bf16[4,4,512,768]{3,2,1,0:T(8,128)(2,1)S(1)}, bf16[4,4,512,768]{3,2,1,0:T(8,128)(2,1)}, u32[]{:S(2)}) %copy-start) | copy-done | bytes 12582936
  120.8 1.6 %copy-done.1 = f32[2,4,512,128]{3,2,1,0:T(8,128)S(1)} copy-done((f32[2,4,512,128]{3,2,1,0:T(8,128)S(1)}, f32[2,4,512,128]{3,2,1,0:T(8,128)}, u32[]{:S(2)}) %copy-start.1) | copy-done | bytes 2097176
  122.4 7.1 %query.2 = (bf16[512,128]{1,0:T(8,128)(2,1)S(1)}, bf16[512,128]{1,0:T(8,128)(2,1)S(1)}, bf16[512,128]{1,0:T(8,128)(2,1)S(1)}, bf16[512,128]{1,0:T(8,128)(2,1)S(1)}) custom-call(s32[4]{0:T(128)S(1)} %copy-done.4, bf16[4,4,512,768]{3,2,1,0:T(8,128)(2,1)S(1)} %copy-done, bf16[768,128]{1,0:T(8,128)(2,1)S(1)} %get-tuple-element.38.refs_1_, ...), custom_call_target="tpu_custom_call" | custom-call | flops 1879048192 | bytes 13369344 | tf_op jit(solution)/shard_map/query/pallas_call | solution.py:480
  129.5 8.1 %collective-permute-start.18 = (bf16[512,128]{1,0:T(8,128)(2,1)S(1)}, bf16[512,128]{1,0:T(8,128)(2,1)S(1)}, u32[]{:S(2)}, u32[]{:S(2)}) collective-permute-start(bf16[512,128]{1,0:T(8,128)(2,1)S(1)} %get-tuple-element.51), channel_id=1, source_target_pairs={{0,4},{4,0},{8,12},{12,8},{1,5},{5,1},{9,13},{13,9},{2,6},{6,2},{1... | collective-permute-start | bytes 393224 | tf_op jit(solution)/shard_map/ppermute | solution.py:127
  137.6 0.5 collective-permute-start.20
  138.1 1.0 collective-permute-start.22
  139.1 0.0 collective-permute-done.16.refs_3_
  139.1 0.0 collective-permute-done.17.refs_4_
  139.1 7.1 %query.3 = (bf16[512,128]{1,0:T(8,128)(2,1)S(1)}, bf16[512,128]{1,0:T(8,128)(2,1)S(1)}, bf16[512,128]{1,0:T(8,128)(2,1)S(1)}, bf16[512,128]{1,0:T(8,128)(2,1)S(1)}) custom-call(s32[4]{0:T(128)S(1)} %copy-done.4, bf16[4,4,512,768]{3,2,1,0:T(8,128)(2,1)S(1)} %copy-done, bf16[768,128]{1,0:T(8,128)(2,1)S(1)} %get-tuple-element.48.refs_1_, ...), custom_call_target="tpu_custom_call" | custom-call | flops 1879048192 | bytes 13369344 | tf_op jit(solution)/shard_map/query/pallas_call | solution.py:480
  146.2 0.6 copy-done.3
  146.9 1.9 %collective-permute-start.19 = (bf16[512,128]{1,0:T(8,128)(2,1)S(1)}, bf16[512,128]{1,0:T(8,128)(2,1)S(1)}, u32[]{:S(2)}, u32[]{:S(2)}) collective-permute-start(bf16[512,128]{1,0:T(8,128)(2,1)S(1)} %get-tuple-element.52), channel_id=1, source_target_pairs={{0,4},{4,0},{8,12},{12,8},{1,5},{5,1},{9,13},{13,9},{2,6},{6,2},{1... | collective-permute-start | bytes 393224 | tf_op jit(solution)/shard_map/ppermute | solution.py:127
  148.8 0.5 collective-permute-start.21
  149.3 0.0 collective-permute-done.18.refs_2_
  149.3 1.0 collective-permute-start.23
  150.4 0.0 collective-permute-done.20.refs_4_
  150.4 2.2 %collective-permute-done.19.refs_3_ = bf16[512,128]{1,0:T(8,128)(2,1)S(1)} collective-permute-done((bf16[512,128]{1,0:T(8,128)(2,1)S(1)}, bf16[512,128]{1,0:T(8,128)(2,1)S(1)}, u32[]{:S(2)}, u32[]{:S(2)}) %collective-permute-start.19) | collective-permute-done | bytes 131104 | tf_op jit(solution)/shard_map/ppermute | solution.py:127
  152.6 1.2 collective-permute-done.21.refs_5_
  153.8 1.4 collective-permute-done.23.refs_7_
  155.2 0.6 copy-done.17
  155.9 2.6 %merge.1 = bf16[512,1024]{1,0:T(8,128)(2,1)} custom-call(s32[4]{0:T(128)} %pad_add_fusion.places, bf16[512,128]{1,0:T(8,128)(2,1)} %copy-done.2, bf16[512,128]{1,0:T(8,128)(2,1)} %copy-done.3, bf16[512,128]{1,0:T(8,128)(2,1)} %copy-done.12, bf16[512,128]{1,0:T(8,128)(2,1)} %copy-done.15, bf16[512,128]{1,0:T(8,128)(2,1)} %copy-done.13, ...), custom_call_target="tpu_custom_call" | custom-call | tf_op jit(solution)/shard_map/merge/pallas_call | solution.py:500
  (37 shorter events, 0.1 us)
Async XLA Ops:
  2.3 21.4 %collective-permute-start.1 = (bf16[536,768]{1,0:T(8,128)(2,1)S(1)}, bf16[536,768]{1,0:T(8,128)(2,1)S(1)}, u32[]{:S(2)}, u32[]{:S(2)}) collective-permute-start(bf16[536,768]{1,0:T(8,128)(2,1)S(1)} %pad_maximum_fusion), channel_id=1, source_target_pairs={{0,16},{16,0},{1,17},{17,1},{2,18},{18,2},{3,19},{19,3},{4,20},{20... | collective-permute-start | bytes 2469896 | tf_op jit(solution)/shard_map/ppermute | solution.py:127
  5.3 22.2 %collective-permute-start = (bf16[536,768]{1,0:T(8,128)(2,1)S(1)}, bf16[536,768]{1,0:T(8,128)(2,1)S(1)}, u32[]{:S(2)}, u32[]{:S(2)}) collective-permute-start(bf16[536,768]{1,0:T(8,128)(2,1)S(1)} %pad_maximum_fusion), channel_id=1, source_target_pairs={{0,4},{4,0},{8,12},{12,8},{1,5},{5,1},{9,13},{13,9},{2,6},{6,2},{1... | collective-permute-start | bytes 2469896 | tf_op jit(solution)/shard_map/ppermute | solution.py:127
  12.5 77.0 %all-to-all-start = ((bf16[4,768,512]{2,1,0:T(8,128)(2,1)}), bf16[4,768,512]{2,1,0:T(8,128)(2,1)}, u32[]{:S(2)}, u32[]{:S(2)}) async-start(bf16[4,768,512]{2,1,0:T(8,128)(2,1)} %pack.1), calls=%async_computation | async-start | bytes 6291456 | tf_op jit(solution)/shard_map/all_to_all | solution.py:402
  17.1 72.4 %copy-start.4 = (s32[4]{0:T(128)S(1)}, s32[4]{0:T(128)}, u32[]{:S(2)}) copy-start(s32[4]{0:T(128)} %pad_add_fusion.places) | copy-start | bytes 52
  27.5 2.3 %collective-permute-start.2 = (bf16[536,768]{1,0:T(8,128)(2,1)S(1)}, bf16[536,768]{1,0:T(8,128)(2,1)S(1)}, u32[]{:S(2)}, u32[]{:S(2)}) collective-permute-start(bf16[536,768]{1,0:T(8,128)(2,1)S(1)} %collective-permute-done.refs_1_), channel_id=1, source_target_pairs={{0,1},{1,0},{2,3},{3,2},{4,5},{5,4},{6,7},{7,6},{8,9},{9,8},{10,11... | collective-permute-start | bytes 2469896 | tf_op jit(solution)/shard_map/ppermute | solution.py:127
  29.8 0.9 copy-start.7
  30.7 20.4 %collective-permute-start.8 = (bf16[536,768]{1,0:T(8,128)(2,1)S(1)}, bf16[536,768]{1,0:T(8,128)(2,1)S(1)}, u32[]{:S(2)}, u32[]{:S(2)}) collective-permute-start(bf16[536,768]{1,0:T(8,128)(2,1)S(1)} %collective-permute-done.refs_1_), channel_id=1, source_target_pairs={{0,16},{16,0},{1,17},{17,1},{2,18},{18,2},{3,19},{19,3},{4,20},{20... | collective-permute-start | bytes 2469896 | tf_op jit(solution)/shard_map/ppermute | solution.py:127
  30.7 20.5 %collective-permute-start.3 = (bf16[536,768]{1,0:T(8,128)(2,1)S(1)}, bf16[536,768]{1,0:T(8,128)(2,1)}, u32[]{:S(2)}, u32[]{:S(2)}) collective-permute-start(bf16[536,768]{1,0:T(8,128)(2,1)S(1)} %collective-permute-done.refs_1_), channel_id=1, source_target_pairs={{0,2},{2,0},{1,3},{3,1},{4,6},{6,4},{5,7},{7,5},{8,10},{10,8},{9,1... | collective-permute-start | bytes 2469896 | tf_op jit(solution)/shard_map/ppermute | solution.py:127
  51.1 4.7 %copy-start.5 = (bf16[536,768]{1,0:T(8,128)(2,1)}, bf16[536,768]{1,0:T(8,128)(2,1)S(1)}, u32[]{:S(2)}) copy-start(bf16[536,768]{1,0:T(8,128)(2,1)S(1)} %collective-permute-done.8.refs_9_) | copy-start | bytes 2469892
  51.1 2.3 %collective-permute-start.9 = (bf16[536,768]{1,0:T(8,128)(2,1)S(1)}, bf16[536,768]{1,0:T(8,128)(2,1)S(1)}, u32[]{:S(2)}, u32[]{:S(2)}) collective-permute-start(bf16[536,768]{1,0:T(8,128)(2,1)S(1)} %collective-permute-done.8.refs_9_), channel_id=1, source_target_pairs={{0,1},{1,0},{2,3},{3,2},{4,5},{5,4},{6,7},{7,6},{8,9},{9,8},{10,11... | collective-permute-start | bytes 2469896 | tf_op jit(solution)/shard_map/ppermute | solution.py:127
  53.4 0.9 copy-start.9
  54.3 20.9 %collective-permute-start.10 = (bf16[536,768]{1,0:T(8,128)(2,1)S(1)}, bf16[536,768]{1,0:T(8,128)(2,1)}, u32[]{:S(2)}, u32[]{:S(2)}) collective-permute-start(bf16[536,768]{1,0:T(8,128)(2,1)S(1)} %collective-permute-done.8.refs_9_), channel_id=1, source_target_pairs={{0,2},{2,0},{1,3},{3,1},{4,6},{6,4},{5,7},{7,5},{8,10},{10,8},{9,1... | collective-permute-start | bytes 2469896 | tf_op jit(solution)/shard_map/ppermute | solution.py:127
  55.8 19.4 %collective-permute-start.5 = (bf16[512,768]{1,0:T(8,128)(2,1)S(1)}, bf16[512,768]{1,0:T(8,128)(2,1)}, u32[]{:S(2)}, u32[]{:S(2)}) collective-permute-start(bf16[512,768]{1,0:T(8,128)(2,1)S(1)} %get-tuple-element.33), channel_id=1, source_target_pairs={{0,16},{16,0},{1,17},{17,1},{2,18},{18,2},{3,19},{19,3},{4,20},{20... | collective-permute-start | bytes 2359304 | tf_op jit(solution)/shard_map/ppermute | solution.py:127
  56.3 24.0 %collective-permute-start.6 = (bf16[536,768]{1,0:T(8,128)(2,1)S(1)}, bf16[536,768]{1,0:T(8,128)(2,1)}, u32[]{:S(2)}, u32[]{:S(2)}) collective-permute-start(bf16[536,768]{1,0:T(8,128)(2,1)S(1)} %collective-permute-done.1.refs_5_), channel_id=1, source_target_pairs={{0,1},{1,0},{2,3},{3,2},{4,5},{5,4},{6,7},{7,6},{8,9},{9,8},{10,11... | collective-permute-start | bytes 2469896 | tf_op jit(solution)/shard_map/ppermute | solution.py:127
  56.3 27.7 %collective-permute-start.4 = (bf16[536,768]{1,0:T(8,128)(2,1)}, bf16[536,768]{1,0:T(8,128)(2,1)}, u32[]{:S(2)}, u32[]{:S(2)}) collective-permute-start(bf16[536,768]{1,0:T(8,128)(2,1)} %collective-permute-done.3.refs_2_), channel_id=1, source_target_pairs={{0,1},{1,0},{2,3},{3,2},{4,5},{5,4},{6,7},{7,6},{8,9},{9,8},{10,11... | collective-permute-start | bytes 2469896 | tf_op jit(solution)/shard_map/ppermute | solution.py:127
  75.2 14.3 %collective-permute-start.11 = (bf16[536,768]{1,0:T(8,128)(2,1)}, bf16[536,768]{1,0:T(8,128)(2,1)}, u32[]{:S(2)}, u32[]{:S(2)}) collective-permute-start(bf16[536,768]{1,0:T(8,128)(2,1)} %collective-permute-done.10.refs_10_), channel_id=1, source_target_pairs={{0,1},{1,0},{2,3},{3,2},{4,5},{5,4},{6,7},{7,6},{8,9},{9,8},{10,11... | collective-permute-start | bytes 2469896 | tf_op jit(solution)/shard_map/ppermute | solution.py:127
  75.2 7.6 %collective-permute-start.7 = (bf16[512,768]{1,0:T(8,128)(2,1)}, bf16[512,768]{1,0:T(8,128)(2,1)}, u32[]{:S(2)}, u32[]{:S(2)}) collective-permute-start(bf16[512,768]{1,0:T(8,128)(2,1)} %collective-permute-done.5.refs_6_), channel_id=1, source_target_pairs={{0,1},{1,0},{2,3},{3,2},{4,5},{5,4},{6,7},{7,6},{8,9},{9,8},{10,11... | collective-permute-start | bytes 2359304 | tf_op jit(solution)/shard_map/ppermute | solution.py:127
  79.6 36.6 %collective-permute-start.12 = (bf16[768,256]{1,0:T(8,128)(2,1)S(1)}, bf16[768,256]{1,0:T(8,128)(2,1)S(1)}, u32[]{:S(2)}, u32[]{:S(2)}) collective-permute-start(bf16[768,256]{1,0:T(8,128)(2,1)S(1)} %constant_dynamic-slice_fusion.3), channel_id=1, source_target_pairs={{0,4},{4,0},{8,12},{12,8},{1,5},{5,1},{9,13},{13,9},{2,6},{6,2},{1... | collective-permute-start | bytes 1179656 | tf_op jit(solution)/shard_map/ppermute | solution.py:127
  80.3 31.0 %collective-permute-start.13 = (bf16[768,128]{1,0:T(8,128)(2,1)S(1)}, bf16[768,128]{1,0:T(8,128)(2,1)S(1)}, u32[]{:S(2)}, u32[]{:S(2)}) collective-permute-start(bf16[768,128]{1,0:T(8,128)(2,1)S(1)} %get-tuple-element.38.refs_1_), channel_id=1, source_target_pairs={{0,8},{4,12},{8,0},{12,4},{1,9},{5,13},{9,1},{13,5},{2,10},{6,14},... | collective-permute-start | bytes 589832 | tf_op jit(solution)/shard_map/ppermute | solution.py:127
  82.9 33.3 %collective-permute-start.14 = (bf16[768,128]{1,0:T(8,128)(2,1)}, bf16[768,128]{1,0:T(8,128)(2,1)S(1)}, u32[]{:S(2)}, u32[]{:S(2)}) collective-permute-start(bf16[768,128]{1,0:T(8,128)(2,1)} %get-tuple-element.39), channel_id=1, source_target_pairs={{0,12},{4,8},{8,4},{12,0},{1,13},{5,9},{9,5},{13,1},{2,14},{6,10},... | collective-permute-start | bytes 589832 | tf_op jit(solution)/shard_map/ppermute | solution.py:127
  89.5 1.1 copy-start.6
  90.6 1.1 copy-start.8
  91.8 1.1 copy-start.10
  92.9 18.4 %copy-start.11 = (bf16[768,128]{1,0:T(8,128)(2,1)S(1)}, bf16[768,128]{1,0:T(8,128)(2,1)}, u32[]{:S(2)}) copy-start(bf16[768,128]{1,0:T(8,128)(2,1)} %get-tuple-element.49) | copy-start | bytes 589828
  109.6 6.6 %collective-permute-start.15 = (bf16[2,2,128,128]{3,2,1,0:T(8,128)(2,1)S(1)}, bf16[2,2,128,128]{3,2,1,0:T(8,128)(2,1)S(1)}, u32[]{:S(2)}, u32[]{:S(2)}) collective-permute-start(bf16[2,2,128,128]{3,2,1,0:T(8,128)(2,1)S(1)} %get-tuple-element.46), channel_id=1, source_target_pairs={{0,8},{4,12},{1,9},{5,13},{2,10},{6,14},{3,11},{7,15},{16,24},{20,... | collective-permute-start | bytes 393224 | tf_op jit(solution)/shard_map/ppermute | solution.py:471
  111.2 27.9 %collective-permute-start.16 = (bf16[768,128]{1,0:T(8,128)(2,1)S(1)}, bf16[768,128]{1,0:T(8,128)(2,1)S(1)}, u32[]{:S(2)}, u32[]{:S(2)}) collective-permute-start(bf16[768,128]{1,0:T(8,128)(2,1)S(1)} %get-tuple-element.48.refs_1_), channel_id=1, source_target_pairs={{0,8},{4,12},{8,0},{12,4},{1,9},{5,13},{9,1},{13,5},{2,10},{6,14},... | collective-permute-start | bytes 589832 | tf_op jit(solution)/shard_map/ppermute | solution.py:127
  111.3 27.8 %collective-permute-start.17 = (bf16[768,128]{1,0:T(8,128)(2,1)S(1)}, bf16[768,128]{1,0:T(8,128)(2,1)S(1)}, u32[]{:S(2)}, u32[]{:S(2)}) collective-permute-start(bf16[768,128]{1,0:T(8,128)(2,1)S(1)} %copy-done.11), channel_id=1, source_target_pairs={{0,12},{4,8},{8,4},{12,0},{1,13},{5,9},{9,5},{13,1},{2,14},{6,10},... | collective-permute-start | bytes 589832 | tf_op jit(solution)/shard_map/ppermute | solution.py:127
  116.2 4.6 %copy-start = (bf16[4,4,512,768]{3,2,1,0:T(8,128)(2,1)S(1)}, bf16[4,4,512,768]{3,2,1,0:T(8,128)(2,1)}, u32[]{:S(2)}) copy-start(bf16[4,4,512,768]{3,2,1,0:T(8,128)(2,1)} %get-tuple-element.36.refs_0_) | copy-start | bytes 37748740
  120.8 1.6 %copy-start.1 = (f32[2,4,512,128]{3,2,1,0:T(8,128)S(1)}, f32[2,4,512,128]{3,2,1,0:T(8,128)}, u32[]{:S(2)}) copy-start(f32[2,4,512,128]{3,2,1,0:T(8,128)} %get-tuple-element.45.refs_10_) | copy-start | bytes 6291460
  129.5 16.7 %copy-start.2 = (bf16[512,128]{1,0:T(8,128)(2,1)}, bf16[512,128]{1,0:T(8,128)(2,1)S(1)}, u32[]{:S(2)}) copy-start(bf16[512,128]{1,0:T(8,128)(2,1)S(1)} %get-tuple-element.47.refs_0_) | copy-start | bytes 393220
  129.5 19.9 %collective-permute-start.18 = (bf16[512,128]{1,0:T(8,128)(2,1)S(1)}, bf16[512,128]{1,0:T(8,128)(2,1)S(1)}, u32[]{:S(2)}, u32[]{:S(2)}) collective-permute-start(bf16[512,128]{1,0:T(8,128)(2,1)S(1)} %get-tuple-element.51), channel_id=1, source_target_pairs={{0,4},{4,0},{8,12},{12,8},{1,5},{5,1},{9,13},{13,9},{2,6},{6,2},{1... | collective-permute-start | bytes 393224 | tf_op jit(solution)/shard_map/ppermute | solution.py:127
  137.6 12.8 %collective-permute-start.20 = (bf16[512,128]{1,0:T(8,128)(2,1)S(1)}, bf16[512,128]{1,0:T(8,128)(2,1)S(1)}, u32[]{:S(2)}, u32[]{:S(2)}) collective-permute-start(bf16[512,128]{1,0:T(8,128)(2,1)S(1)} %get-tuple-element.53), channel_id=1, source_target_pairs={{0,16},{16,0},{1,17},{17,1},{2,18},{18,2},{3,19},{19,3},{4,20},{20... | collective-permute-start | bytes 393224 | tf_op jit(solution)/shard_map/ppermute | solution.py:127
  138.1 12.3 %collective-permute-start.22 = (bf16[512,128]{1,0:T(8,128)(2,1)S(1)}, bf16[512,128]{1,0:T(8,128)(2,1)S(1)}, u32[]{:S(2)}, u32[]{:S(2)}) collective-permute-start(bf16[512,128]{1,0:T(8,128)(2,1)S(1)} %get-tuple-element.55), channel_id=1, source_target_pairs={{0,20},{4,16},{8,28},{12,24},{16,4},{20,0},{24,12},{28,8},{1,21},{... | collective-permute-start | bytes 393224 | tf_op jit(solution)/shard_map/ppermute | solution.py:497
  146.2 0.7 copy-start.3
  146.9 5.7 %collective-permute-start.19 = (bf16[512,128]{1,0:T(8,128)(2,1)S(1)}, bf16[512,128]{1,0:T(8,128)(2,1)S(1)}, u32[]{:S(2)}, u32[]{:S(2)}) collective-permute-start(bf16[512,128]{1,0:T(8,128)(2,1)S(1)} %get-tuple-element.52), channel_id=1, source_target_pairs={{0,4},{4,0},{8,12},{12,8},{1,5},{5,1},{9,13},{13,9},{2,6},{6,2},{1... | collective-permute-start | bytes 393224 | tf_op jit(solution)/shard_map/ppermute | solution.py:127
  148.8 5.0 %collective-permute-start.21 = (bf16[512,128]{1,0:T(8,128)(2,1)S(1)}, bf16[512,128]{1,0:T(8,128)(2,1)S(1)}, u32[]{:S(2)}, u32[]{:S(2)}) collective-permute-start(bf16[512,128]{1,0:T(8,128)(2,1)S(1)} %get-tuple-element.54), channel_id=1, source_target_pairs={{0,16},{16,0},{1,17},{17,1},{2,18},{18,2},{3,19},{19,3},{4,20},{20... | collective-permute-start | bytes 393224 | tf_op jit(solution)/shard_map/ppermute | solution.py:127
  149.3 5.9 %copy-start.12 = (bf16[512,128]{1,0:T(8,128)(2,1)}, bf16[512,128]{1,0:T(8,128)(2,1)S(1)}, u32[]{:S(2)}) copy-start(bf16[512,128]{1,0:T(8,128)(2,1)S(1)} %collective-permute-done.18.refs_2_) | copy-start | bytes 393220
  149.3 5.9 %collective-permute-start.23 = (bf16[512,128]{1,0:T(8,128)(2,1)S(1)}, bf16[512,128]{1,0:T(8,128)(2,1)S(1)}, u32[]{:S(2)}, u32[]{:S(2)}) collective-permute-start(bf16[512,128]{1,0:T(8,128)(2,1)S(1)} %get-tuple-element.56), channel_id=1, source_target_pairs={{0,20},{4,16},{8,28},{12,24},{16,4},{20,0},{24,12},{28,8},{1,21},{... | collective-permute-start | bytes 393224 | tf_op jit(solution)/shard_map/ppermute | solution.py:497
  150.4 4.8 %copy-start.13 = (bf16[512,128]{1,0:T(8,128)(2,1)}, bf16[512,128]{1,0:T(8,128)(2,1)S(1)}, u32[]{:S(2)}) copy-start(bf16[512,128]{1,0:T(8,128)(2,1)S(1)} %collective-permute-done.20.refs_4_) | copy-start | bytes 393220
  150.4 4.8 %copy-start.14 = (bf16[512,128]{1,0:T(8,128)(2,1)}, bf16[512,128]{1,0:T(8,128)(2,1)S(1)}, u32[]{:S(2)}) copy-start(bf16[512,128]{1,0:T(8,128)(2,1)S(1)} %collective-permute-done.22.refs_6_) | copy-start | bytes 393220
  152.6 2.6 %copy-start.15 = (bf16[512,128]{1,0:T(8,128)(2,1)}, bf16[512,128]{1,0:T(8,128)(2,1)S(1)}, u32[]{:S(2)}) copy-start(bf16[512,128]{1,0:T(8,128)(2,1)S(1)} %collective-permute-done.19.refs_3_) | copy-start | bytes 393220
  153.8 1.5 copy-start.16
  155.2 0.7 copy-start.17

commit v5 on v4

--- a/solution.py
+++ b/solution.py
@@ -207,15 +207,24 @@
                 carried[at] = stages[depth](items[at], carried.get(at))
 
 
-def key_value_kernel(heads, size, flips, places, *refs):
+def key_value_kernel(head_here, heads_all, size, flips, places, *refs):
+    heads = 1
     sides = len(SIDES)
     token_refs, refs = refs[:13], refs[13:]
-    decay_refs, refs = refs[:sides], refs[sides:]
-    source_ref, held, key_ref, value_ref, state_ref, sum_ref, fade_ref, mask_ref, pair_ref = refs[:9]
-    weight_ref, decay_ref, end_ref, semaphores, weight_semaphores = refs[9:]
+    tail_ref, refs = refs[0], refs[1:]
+    source_ref, key_ref, value_ref, state_ref, sum_ref, fade_ref, mask_ref, pair_ref, held = refs[:9]
+    weight_ref, decay_ref, end_ref, tails, semaphores, weight_semaphores, tail_semaphores = refs[9:]
+    tail_rows = pl.ds(held.shape[2], tails.shape[1])
+    tail_loads = [
+        pltpu.make_async_copy(source, tails.at[side], tail_semaphores.at[side])
+        for side, source in enumerate([tail_ref, *(ref.at[tail_rows, :] for ref in token_refs[1::4])])
+    ]
+    for load in tail_loads:
+        load.start()
+    columns = pl.ds(2 * head_here * size, 2 * size)
     loads = [
         pltpu.make_async_copy(
-            source_ref.at[places[0] ^ flip], weight_ref.at[flip], weight_semaphores.at[flip]
+            source_ref.at[places[0] ^ flip, :, columns], weight_ref.at[flip], weight_semaphores.at[flip]
         )
         for flip in range(flips)
     ]
@@ -228,13 +237,17 @@
         jnp.int32, (PIECE, PIECE), 0
     )
     cuts = piece_rows(key_ref.shape[1])
-    for side in range(sides):
-        part = decay_refs[side][...].astype(jnp.float32)
+    for load in loads:
+        load.wait()
+
+    def decays(side):
+        tail_loads[side].wait()
+        part = tails[side].astype(jnp.float32)
         count = part.shape[0] // 3
         log_decay = part[:count] + (part[count : 2 * count] + part[2 * count :])
         decay_ref[...] = running_sum(log_decay[:, : sum_ref.shape[2]])
         for head in range(heads):
-            row = decay_ref[pl.ds(places[3] * heads + head, 1), :]
+            row = decay_ref[pl.ds(places[3] * heads_all + head_here, 1), :]
             sum_ref[side, head : head + 1, :] = row
             column = column_of(row)
             begin = jnp.zeros_like(column[:1])
@@ -245,13 +258,12 @@
                 gaps = jnp.where(causal, column[cut] - row[:, cut], -jnp.inf)
                 mask_ref[head, side, cut, :] = jnp.exp(gaps)
                 begin = end
-    for load in loads:
-        load.wait()
 
     def first(item, _):
         side, head, piece = item
-        if head == 0 and piece == 0:
+        if piece == 0:
             wait(side)
+            decays(side)
         at = slice(2 * head * size, 2 * (head + 1) * size)
         return project(held, side, cuts[piece], [weight_ref[flip, :, at] for flip in range(flips)])
 
@@ -296,10 +308,12 @@
 
 def query_kernel(head, columns, flips, places, *refs):
     sides = len(SIDES)
-    held, refs = refs[0], refs[1:]
+    token_refs, refs = refs[:13], refs[13:]
     weight_refs, refs = refs[:flips], refs[flips:]
     key_ref, value_ref, state_ref, sum_ref, fade_ref, mask_ref, before_ref = refs[:7]
-    out_refs, incoming_ref = refs[7:-1], refs[-1]
+    out_refs, (incoming_ref, held, semaphores) = refs[7:-3], refs[-3:]
+    start, wait = token_copies(places, token_refs, held, semaphores)
+    start()
     odd = places[0] % 2 == 1
     cuts = piece_rows(key_ref.shape[1])
     last = len(cuts) - 1
@@ -322,6 +336,8 @@
 
     def first(item, _):
         side, piece = item
+        if piece == 0:
+            wait(side)
         return silu(project(held, side, cuts[piece], weights)).astype(jnp.bfloat16)
 
     def second(item, query):
@@ -354,11 +370,14 @@
             out_ref[:, pl.ds(at, size)] = pieces[side * heads + head][...]
 
 
-def pack_kernel(heads, size, places, key_ref, value_ref, out_ref):
-    for head in range(heads):
-        at, to = head * size, 2 * head * size
-        out_ref[0, :, to : to + size] = key_ref[:, at : at + size]
-        out_ref[0, :, to + size : to + 2 * size] = value_ref[:, at : at + size]
+def pack_kernel(heads, size, places, *refs):
+    out_ref = refs[4]
+    for flip in range(out_ref.shape[0]):
+        key_ref, value_ref = refs[2 * (flip % 2) : 2 * (flip % 2) + 2]
+        for head in range(heads):
+            at, to = head * size, 2 * head * size
+            out_ref[places[0] ^ flip, :, to : to + size] = key_ref[:, at : at + size]
+            out_ref[places[0] ^ flip, :, to + size : to + 2 * size] = value_ref[:, at : at + size]
 
 
 def spread_body(mesh, tokens, query_weight, key_weight, value_weight, log_decay):
@@ -381,23 +400,24 @@
     quarter = lax.dynamic_slice(tokens, (0, share * depth), (rows, depth))
     tail = jnp.pad(in_three(log_decay), ((0, 0), (0, depth - rows)))
     quarter = jnp.concatenate([quarter, tail], axis=0)
-    beside = lax.dynamic_slice(tokens, (0, (share ^ 1) * depth), (rows, depth))
-
-    block = (depth, heads * size)
+
+    steps = 2
+    block = (depth // steps, heads * size)
+    owners = pl.BlockSpec(block, lambda step, places: (step, places[3]))
+    partners = pl.BlockSpec(block, lambda step, places: (step, places[3] ^ 1))
     packed_shape = (flips, depth, 2 * heads * size)
-    owner = pl.BlockSpec(block, lambda step, places: (0, places[3] ^ ((places[0] ^ step) % 2)))
     packed = pl.pallas_call(
         functools.partial(pack_kernel, heads, size),
         grid_spec=pltpu.PrefetchScalarGridSpec(
             num_scalar_prefetch=1,
-            grid=(flips,),
-            in_specs=[owner, owner],
-            out_specs=pl.BlockSpec((1,) + packed_shape[1:], lambda step, places: (step, 0, 0)),
+            grid=(steps,),
+            in_specs=[owners, owners, partners, partners],
+            out_specs=pl.BlockSpec((flips, depth // steps, 2 * heads * size), lambda step, places: (0, step, 0)),
         ),
         out_shape=jax.ShapeDtypeStruct(packed_shape, jnp.bfloat16),
         cost_estimate=pl.CostEstimate(flops=0, bytes_accessed=32 * depth * heads * size, transcendentals=0),
         name="pack",
-    )(places, key_weight, value_weight)
+    )(places, key_weight, value_weight, key_weight, value_weight)
 
     key_value = lax.all_to_all(packed, "ctx", 0, 0)
 
@@ -408,7 +428,9 @@
     (from_ctx,) = after((from_ctx,), ctx_core)
     ctx_plane = xor_permute(from_ctx, mesh, "fsdp", 1)
     from_both = xor_permute(from_ctx, mesh, "groups", 1)
-    groups_plane = xor_permute(after((beside,), from_ctx)[0], mesh, "groups", 1)
+    beside = after((tokens,), from_ctx)[0]
+    beside = lax.dynamic_slice(beside, (0, (share ^ 1) * depth), (rows, depth))
+    groups_plane = xor_permute(beside, mesh, "groups", 1)
     both_core = xor_permute(from_both, mesh, "head", 1)
     (from_both,) = after((from_both,), both_core, ctx_plane)
     both_plane = xor_permute(from_both, mesh, "fsdp", 1)
@@ -419,8 +441,6 @@
         token_sets.append(array)
     token_sets += [xor_permute(array, mesh, "head", 1) for array in (from_groups, groups_plane)]
     token_sets += [from_both, both_plane, both_core, xor_permute(both_plane, mesh, "head", 1)]
-    decays = [tail, *(array[rows:] for array in (from_ctx, from_groups, from_both))]
-
     def query_block(owner, head, count):
         return lax.dynamic_slice(query_weight, (0, (owner * heads + head) * size), (depth, count * size))
 
@@ -434,55 +454,65 @@
         [xor_permute(other if flip % 2 else own, mesh, "ctx", flip) for flip in range(2, flips)]
     ]
 
-    large, small = (pltpu.CompilerParams(vmem_limit_bytes=size << 20) for size in (38, 12))
+    large, small = (pltpu.CompilerParams(vmem_limit_bytes=size << 20) for size in (38, 24))
     pieces = rows // PIECE
-    column_shape = (sides, rows, heads * size)
+    column_shape = (sides, rows, size)
     shapes = [
-        ((sides, flips, rows, depth), jnp.bfloat16),
         (column_shape, jnp.bfloat16),
         (column_shape, jnp.bfloat16),
-        ((heads, sides, pieces, size, size), jnp.float32),
-        ((sides, heads, rows), jnp.float32),
-        ((heads, sides, rows, size), jnp.float32),
-        ((heads, sides, rows, size), jnp.float32),
-        ((heads, 2, size, size), jnp.bfloat16),
+        ((1, sides, pieces, size, size), jnp.float32),
+        ((sides, 1, rows), jnp.float32),
+        ((1, sides, rows, size), jnp.float32),
+        ((1, sides, rows, size), jnp.float32),
+        ((1, 2, size, size), jnp.bfloat16),
     ]
-    held, *memory, pair_state = pl.pallas_call(
-        functools.partial(key_value_kernel, heads, size, flips),
-        in_specs=[SCALARS] + [ANY] * len(token_sets) + [VMEM] * sides + [ANY],
-        out_specs=[VMEM] * len(shapes),
-        scratch_shapes=[
-            pltpu.VMEM(packed_shape, jnp.bfloat16),
-            pltpu.VMEM(log_decay.shape, jnp.float32),
-            pltpu.VMEM((heads, sides, rows, size), jnp.float32),
-            pltpu.SemaphoreType.DMA((sides, flips)),
-            pltpu.SemaphoreType.DMA((flips,)),
-        ],
-        out_shape=[jax.ShapeDtypeStruct(*shape) for shape in shapes],
-        compiler_params=large,
-        cost_estimate=pl.CostEstimate(
-            flops=2 * sides * rows * width * 2 * heads * size,
-            bytes_accessed=2 * (sides * rows * width + width * 2 * heads * size),
-            transcendentals=sides * rows * 2 * heads * size,
-        ),
-        name="key_value",
-    )(places, *token_sets, *decays, key_value)
-
-    before = lax.ppermute(pair_state, "ctx", [(at, at + 2) for at in range(flips - 2)])
-    for head in range(1, heads):
-        own, other, _ = lax.optimization_barrier((query_own[head], query_sent[head], pair_state))
-        parts.append(
-            [xor_permute(other if flip % 2 else own, mesh, "ctx", flip) for flip in range(2, flips)]
-        )
+    held_shape = ((sides, flips, rows, depth), jnp.bfloat16)
+    memory, before = [], []
+    for head in range(heads):
+        results = pl.pallas_call(
+            functools.partial(key_value_kernel, head, heads, size, flips),
+            in_specs=[SCALARS] + [ANY] * (len(token_sets) + 2),
+            out_specs=[VMEM] * len(shapes),
+            scratch_shapes=[
+                pltpu.VMEM(*held_shape),
+                pltpu.VMEM((flips, depth, 2 * size), jnp.bfloat16),
+                pltpu.VMEM(log_decay.shape, jnp.float32),
+                pltpu.VMEM((1, sides, rows, size), jnp.float32),
+                pltpu.VMEM((sides, *tail.shape), jnp.bfloat16),
+                pltpu.SemaphoreType.DMA((sides, flips)),
+                pltpu.SemaphoreType.DMA((flips,)),
+                pltpu.SemaphoreType.DMA((sides,)),
+            ],
+            out_shape=[jax.ShapeDtypeStruct(*shape) for shape in shapes],
+            compiler_params=large,
+            cost_estimate=pl.CostEstimate(
+                flops=2 * sides * rows * width * 2 * size,
+                bytes_accessed=2 * (sides * rows * width + width * 2 * size),
+                transcendentals=sides * rows * 2 * size,
+            ),
+            name="key_value",
+        )(places, *token_sets, tail, key_value)
+        memory.append(results[:6])
+        pair_state = results[6]
+        before.append(lax.ppermute(pair_state, "ctx", [(at, at + 2) for at in range(flips - 2)]))
+        if head + 1 < heads:
+            own, other = after((query_own[head + 1], query_sent[head + 1]), pair_state, query_near)
+            parts.append(
+                [xor_permute(other if flip % 2 else own, mesh, "ctx", flip) for flip in range(2, flips)]
+            )
 
     returned = [[] for _ in SIDES]
     for head in range(heads):
         attended = pl.pallas_call(
-            functools.partial(query_kernel, head, slice(head * size, (head + 1) * size), flips),
-            in_specs=[SCALARS] + [VMEM] * (1 + flips + len(memory) + 1),
+            functools.partial(query_kernel, 0, slice(head * size, (head + 1) * size), flips),
+            in_specs=[SCALARS] + [ANY] * len(token_sets) + [VMEM] * (flips + 7),
             out_specs=[VMEM] * sides,
             out_shape=[jax.ShapeDtypeStruct((rows, size), jnp.bfloat16)] * sides,
-            scratch_shapes=[pltpu.VMEM((sides, pieces, size, size), jnp.bfloat16)],
+            scratch_shapes=[
+                pltpu.VMEM((sides, pieces, size, size), jnp.bfloat16),
+                pltpu.VMEM(*held_shape),
+                pltpu.SemaphoreType.DMA((sides, flips)),
+            ],
             compiler_params=small,
             cost_estimate=pl.CostEstimate(
                 flops=2 * sides * rows * size * (width + 4 * size),
@@ -490,7 +520,7 @@
                 transcendentals=sides * rows * 4 * size,
             ),
             name="query",
-        )(places, held, query_own[head], query_near, *parts[head], *memory, before)
+        )(places, *token_sets, query_own[head], query_near, *parts[head], *memory[head], before[head])
         returned[0].append(attended[0])
         returned[1].append(xor_permute(attended[1], mesh, "ctx", 1))
         returned[2].append(xor_permute(attended[2], mesh, "groups", 1))

time: 159 us -> 152 us (0.956)
  local copies, waits for them, and re-layouts: 18 us -> 8.17 us
  Pallas kernels: 38.4 us -> 42.9 us
  starting transfers between devices: 38.3 us -> 35.1 us
  waiting for transfers between devices: 62.1 us -> 63.8 us
    unnamed x36 -> x22, local copies, waits for them, and re-layouts: 12.7 us -> 1.97 us
    ppermute x21, starting transfers between devices: 30 us -> 20.4 us  [xor_permute(): lax.ppermute(array, axis, [(at, at ^ flip) for at in range(mesh.shape[axi...]
    pallas_call x3 -> x4, Pallas kernels: 30.9 us -> 36.5 us  [the longest x2 18.4 us: spread_body(): pl.pallas_call(functools.partial(key_value_kernel, head, heads, size, fli...]
    ppermute x1 -> x2, starting transfers between devices: 1.62 us -> 5.17 us  [spread_body(): lax.ppermute(pair_state, 'ctx', [(at, at + 2) for at in range(flips - 2)])]
    ppermute x2, starting transfers between devices: 2.05 us -> 4.78 us  [spread_body(): returned[3].append(lax.ppermute(attended[3], ('groups', 'ctx'), both))]
  transfers between devices with their start and end apart: 25 -> 26, of which waited for: 11 -> 11; matrix products, arithmetic and copies ran while one was open for 3% -> 4% of each run, Pallas kernels for 23% -> 27%
where the time goes in v5:
time: 152 us; the launch traced here: 151 us
  waiting for transfers between devices  63.8 us (42%)
  Pallas kernels  42.9 us (28%)
  starting transfers between devices  35.1 us (23%)
  local copies, waits for them, and re-layouts  8.17 us (5%)
    ppermute x21, waiting for transfers between devices, xor_permute(): lax.ppermute(array, axis, [(at, at ^ flip) for at in range(mesh.shape[axi...  56.7 us
    ppermute x21, starting transfers between devices, xor_permute(): lax.ppermute(array, axis, [(at, at ^ flip) for at in range(mesh.shape[axi...  20.4 us
    pallas_call x2, Pallas kernels, spread_body(): pl.pallas_call(functools.partial(key_value_kernel, head, heads, size, fli...  18.4 us
    pallas_call x2, Pallas kernels, spread_body(): pl.pallas_call(functools.partial(query_kernel, 0, slice(head * size, (hea...  18 us
    all_to_all x1, waiting for transfers between devices, spread_body(): key_value = lax.all_to_all(packed, 'ctx', 0, 0)  7.02 us
    ppermute x2, starting transfers between devices, spread_body(): lax.ppermute(pair_state, 'ctx', [(at, at + 2) for at in range(flips - 2)])  5.17 us
    ppermute x2, starting transfers between devices, spread_body(): returned[3].append(lax.ppermute(attended[3], ('groups', 'ctx'), both))  4.78 us
    all_to_all x1, starting transfers between devices, spread_body(): key_value = lax.all_to_all(packed, 'ctx', 0, 0)  4.66 us
  transfers between devices with their start and end apart: 26, of which 11 were waited for; matrix products, arithmetic and copies ran while one was open for 4% of the time, Pallas kernels for 27%

profile of v5, /device:TPU:0, one launch (start us, length us, event | category | flops | bytes accessed | tf_op | source)
XLA Modules:
  0.0 151.5 jit_solution(5341015365615902297)
XLA Ops:
  0.0 0.7 reduce-precision_convert_fusion.1
  0.7 1.2 constant_dynamic-slice_fusion.6
  1.9 0.1 pad_maximum_fusion
  2.0 3.1 %collective-permute-start = (bf16[536,768]{1,0:T(8,128)(2,1)S(1)}, bf16[536,768]{1,0:T(8,128)(2,1)S(1)}, u32[]{:S(2)}, u32[]{:S(2)}) collective-permute-start(bf16[536,768]{1,0:T(8,128)(2,1)S(1)} %pad_maximum_fusion), channel_id=1, source_target_pairs={{0,4},{4,0},{8,12},{12,8},{1,5},{5,1},{9,13},{13,9},{2,6},{6,2},{1... | collective-permute-start | bytes 2469896 | tf_op jit(solution)/shard_map/ppermute | solution.py:127
  5.1 1.5 %collective-permute-start.1 = (bf16[536,768]{1,0:T(8,128)(2,1)S(1)}, bf16[536,768]{1,0:T(8,128)(2,1)S(1)}, u32[]{:S(2)}, u32[]{:S(2)}) collective-permute-start(bf16[536,768]{1,0:T(8,128)(2,1)S(1)} %pad_maximum_fusion), channel_id=1, source_target_pairs={{0,16},{16,0},{1,17},{17,1},{2,18},{18,2},{3,19},{19,3},{4,20},{20... | collective-permute-start | bytes 2469896 | tf_op jit(solution)/shard_map/ppermute | solution.py:127
  6.6 0.6 pad_add_fusion.places
  7.2 3.8 %pack.1 = bf16[4,768,512]{2,1,0:T(8,128)(2,1)} custom-call(s32[4]{0:T(128)} %pad_add_fusion.places, bf16[768,1024]{1,0:T(8,128)(2,1)} %refs_2_.1, bf16[768,1024]{1,0:T(8,128)(2,1)} %refs_3_.1, bf16[768,1024]{1,0:T(8,128)(2,1)} %refs_2_.1, bf16[768,1024]{1,0:T(8,128)(2,1)} %refs_3_.1), custom_call_target="tpu_custom_call" | custom-call | bytes 6291456 | tf_op jit(solution)/shard_map/pack/pallas_call | solution.py:409
  11.1 4.7 %all-to-all-start = ((bf16[4,768,512]{2,1,0:T(8,128)(2,1)}), bf16[4,768,512]{2,1,0:T(8,128)(2,1)}, u32[]{:S(2)}, u32[]{:S(2)}) async-start(bf16[4,768,512]{2,1,0:T(8,128)(2,1)} %pack.1), calls=%async_computation | async-start | bytes 6291456 | tf_op jit(solution)/shard_map/all_to_all | solution.py:422
  15.7 8.5 %collective-permute-done.refs_1_ = bf16[536,768]{1,0:T(8,128)(2,1)S(1)} collective-permute-done((bf16[536,768]{1,0:T(8,128)(2,1)S(1)}, bf16[536,768]{1,0:T(8,128)(2,1)S(1)}, u32[]{:S(2)}, u32[]{:S(2)}) %collective-permute-start) | collective-permute-done | bytes 823328 | tf_op jit(solution)/shard_map/ppermute | solution.py:127
  24.2 0.6 collective-permute-done.1.refs_5_
  24.9 0.0 collective-permute-start.2
  24.9 2.3 %collective-permute-done.2.refs_3_ = bf16[536,768]{1,0:T(8,128)(2,1)S(1)} collective-permute-done((bf16[536,768]{1,0:T(8,128)(2,1)S(1)}, bf16[536,768]{1,0:T(8,128)(2,1)S(1)}, u32[]{:S(2)}, u32[]{:S(2)}) %collective-permute-start.2) | collective-permute-done | bytes 823328 | tf_op jit(solution)/shard_map/ppermute | solution.py:127
  27.2 1.6 %collective-permute-start.8 = (bf16[536,768]{1,0:T(8,128)(2,1)S(1)}, bf16[536,768]{1,0:T(8,128)(2,1)S(1)}, u32[]{:S(2)}, u32[]{:S(2)}) collective-permute-start(bf16[536,768]{1,0:T(8,128)(2,1)S(1)} %collective-permute-done.refs_1_), channel_id=1, source_target_pairs={{0,16},{16,0},{1,17},{17,1},{2,18},{18,2},{3,19},{19,3},{4,20},{20... | collective-permute-start | bytes 2469896 | tf_op jit(solution)/shard_map/ppermute | solution.py:127
  28.8 1.5 collective-permute-start.3
  30.3 17.2 %collective-permute-done.8.refs_9_ = bf16[536,768]{1,0:T(8,128)(2,1)S(1)} collective-permute-done((bf16[536,768]{1,0:T(8,128)(2,1)S(1)}, bf16[536,768]{1,0:T(8,128)(2,1)S(1)}, u32[]{:S(2)}, u32[]{:S(2)}) %collective-permute-start.8) | collective-permute-done | bytes 823328 | tf_op jit(solution)/shard_map/ppermute | solution.py:127
  47.6 0.0 collective-permute-start.9
  47.6 1.5 collective-permute-done.3.refs_2_
  49.0 1.0 collective-permute-done.9.refs_11_
  50.1 1.6 %collective-permute-start.10 = (bf16[536,768]{1,0:T(8,128)(2,1)S(1)}, bf16[536,768]{1,0:T(8,128)(2,1)}, u32[]{:S(2)}, u32[]{:S(2)}) collective-permute-start(bf16[536,768]{1,0:T(8,128)(2,1)S(1)} %collective-permute-done.8.refs_9_), channel_id=1, source_target_pairs={{0,2},{2,0},{1,3},{3,1},{4,6},{6,4},{5,7},{7,5},{8,10},{10,8},{9,1... | collective-permute-start | bytes 2469896 | tf_op jit(solution)/shard_map/ppermute | solution.py:127
  51.7 1.2 constant_dynamic-slice_fusion.5
  52.8 1.6 %collective-permute-start.5 = (bf16[512,768]{1,0:T(8,128)(2,1)S(1)}, bf16[512,768]{1,0:T(8,128)(2,1)}, u32[]{:S(2)}, u32[]{:S(2)}) collective-permute-start(bf16[512,768]{1,0:T(8,128)(2,1)S(1)} %constant_dynamic-slice_fusion.5), channel_id=1, source_target_pairs={{0,16},{16,0},{1,17},{17,1},{2,18},{18,2},{3,19},{19,3},{4,20},{20... | collective-permute-start | bytes 2359304 | tf_op jit(solution)/shard_map/ppermute | solution.py:127
  54.4 0.0 collective-permute-start.6
  54.4 0.5 collective-permute-start.4
  54.9 17.4 %collective-permute-done.5.refs_6_ = bf16[512,768]{1,0:T(8,128)(2,1)} collective-permute-done((bf16[512,768]{1,0:T(8,128)(2,1)S(1)}, bf16[512,768]{1,0:T(8,128)(2,1)}, u32[]{:S(2)}, u32[]{:S(2)}) %collective-permute-start.5) | collective-permute-done | bytes 786464 | tf_op jit(solution)/shard_map/ppermute | solution.py:127
  72.3 0.0 collective-permute-done.10.refs_10_
  72.3 0.0 collective-permute-start.11
  72.3 0.5 collective-permute-start.7
  72.8 1.8 %constant_dynamic-slice_fusion.3 = bf16[768,256]{1,0:T(8,128)(2,1)} fusion(bf16[768,1024]{1,0:T(8,128)(2,1)} %param.6, s32[]{:T(128)S(6)} %select_n.30), kind=kLoop, calls=%fused_computation.16 | loop fusion | bytes 786436 | tf_op jit(solution)/shard_map/dynamic_slice | solution.py:445
  74.6 2.1 %constant_dynamic-slice_fusion = (bf16[768,128]{1,0:T(8,128)(2,1)}, bf16[768,128]{1,0:T(8,128)(2,1)}, bf16[768,128]{1,0:T(8,128)(2,1)}, bf16[768,128]{1,0:T(8,128)(2,1)S(1)}) fusion(bf16[768,1024]{1,0:T(8,128)(2,1)} %param.6, s32[]{:T(128)S(6)} %select_n.32, s32[]{:T(128)S(6)} %select_n.30, s32[]{:T(128)S(6)} %select_n.29, s32[]{:T(128)S(6)} %select_n.31), kind=kLoop, calls=%fused_computation.13 | loop fusion | bytes 1572880 | tf_op jit(solution)/shard_map/dynamic_slice | solution.py:445
  76.7 1.3 collective-permute-start.12
  78.0 0.0 collective-permute-done.6.refs_7_
  78.0 2.6 %collective-permute-start.13 = (bf16[768,128]{1,0:T(8,128)(2,1)}, bf16[768,128]{1,0:T(8,128)(2,1)}, u32[]{:S(2)}, u32[]{:S(2)}) collective-permute-start(bf16[768,128]{1,0:T(8,128)(2,1)} %get-tuple-element.43.refs_13_), channel_id=1, source_target_pairs={{0,8},{4,12},{8,0},{12,4},{1,9},{5,13},{9,1},{13,5},{2,10},{6,14},... | collective-permute-start | bytes 589832 | tf_op jit(solution)/shard_map/ppermute | solution.py:127
  80.6 0.0 collective-permute-done.7.refs_8_
  80.6 0.5 collective-permute-start.14
  81.1 0.0 collective-permute-done.4.refs_4_
  81.1 7.0 %all-to-all-done.refs_14_ = bf16[4,768,512]{2,1,0:T(8,128)(2,1)} async-done(((bf16[4,768,512]{2,1,0:T(8,128)(2,1)}), bf16[4,768,512]{2,1,0:T(8,128)(2,1)}, u32[]{:S(2)}, u32[]{:S(2)}) %all-to-all-start) | async-done | bytes 3145760 | tf_op jit(solution)/shard_map/all_to_all | solution.py:422
  88.1 0.0 collective-permute-done.11.refs_12_
  88.1 9.2 %key_value.2 = (bf16[4,512,128]{2,1,0:T(8,128)(2,1)S(1)}, bf16[4,512,128]{2,1,0:T(8,128)(2,1)S(1)}, f32[1,4,4,128,128]{4,3,2,1,0:T(8,128)S(1)}, f32[4,1,512]{2,1...) custom-call(s32[4]{0:T(128)S(1)} %copy-done.3, ...), custom_call_target="tpu_custom_call" | custom-call | flops 3221225472 | bytes 14155776 | tf_op jit(solution)/shard_map/key_value/pallas_call | solution.py:472
  97.3 1.4 collective-permute-start.15
  98.7 4.4 %collective-permute-done.12.refs_14_ = bf16[768,256]{1,0:T(8,128)(2,1)} collective-permute-done((bf16[768,256]{1,0:T(8,128)(2,1)}, bf16[768,256]{1,0:T(8,128)(2,1)}, u32[]{:S(2)}, u32[]{:S(2)}) %collective-permute-start.12) | collective-permute-done | bytes 393248 | tf_op jit(solution)/shard_map/ppermute | solution.py:127
  103.1 0.0 collective-permute-start.16
  103.1 1.9 %collective-permute-start.17 = (bf16[768,128]{1,0:T(8,128)(2,1)S(1)}, bf16[768,128]{1,0:T(8,128)(2,1)S(1)}, u32[]{:S(2)}, u32[]{:S(2)}) collective-permute-start(bf16[768,128]{1,0:T(8,128)(2,1)S(1)} %copy-done.4), channel_id=1, source_target_pairs={{0,12},{4,8},{8,4},{12,0},{1,13},{5,9},{9,5},{13,1},{2,14},{6,10},... | collective-permute-start | bytes 589832 | tf_op jit(solution)/shard_map/ppermute | solution.py:127
  105.0 9.3 %key_value.3 = (bf16[4,512,128]{2,1,0:T(8,128)(2,1)S(1)}, bf16[4,512,128]{2,1,0:T(8,128)(2,1)S(1)}, f32[1,4,4,128,128]{4,3,2,1,0:T(8,128)S(1)}, f32[4,1,512]{2,1...) custom-call(s32[4]{0:T(128)S(1)} %copy-done.3, ...), custom_call_target="tpu_custom_call" | custom-call | flops 3221225472 | bytes 14155776 | tf_op jit(solution)/shard_map/key_value/pallas_call | solution.py:472
  114.3 0.0 collective-permute-done.13.refs_15_
  114.3 3.8 %collective-permute-start.18 = (bf16[1,2,128,128]{3,2,1,0:T(8,128)(2,1)S(1)}, bf16[1,2,128,128]{3,2,1,0:T(8,128)(2,1)S(1)}, u32[]{:S(2)}, u32[]{:S(2)}) collective-permute-start(bf16[1,2,128,128]{3,2,1,0:T(8,128)(2,1)S(1)} %get-tuple-element.61), channel_id=1, source_target_pairs={{0,8},{4,12},{1,9},{5,13},{2,10},{6,14},{3,11},{7,15},{16,24},{20,... | collective-permute-start | bytes 196616 | tf_op jit(solution)/shard_map/ppermute | solution.py:497
  118.1 0.0 collective-permute-done.14.refs_16_
  118.1 0.0 collective-permute-done.15.refs_23_
  118.1 9.0 %query.2 = (bf16[512,128]{1,0:T(8,128)(2,1)S(1)}, bf16[512,128]{1,0:T(8,128)(2,1)S(1)}, bf16[512,128]{1,0:T(8,128)(2,1)S(1)}, bf16[512,128]{1,0:T(8,128)(2,1)S(1)}) custom-call(s32[4]{0:T(128)S(1)} %copy-done.3, bf16[512,3072]{1,0:T(8,128)(2,1)S(1)} %copy-done, bf16[536,768]{1,0:T(8,128)(2,1)S(1)} %collective-permute-done.refs_1_, ...), custom_call_target="tpu_custom_call" | custom-call | flops 1879048192 | bytes 13369344 | tf_op jit(solution)/shard_map/query/pallas_call | solution.py:506
  127.2 0.6 copy-done.1
  127.8 0.6 collective-permute-start.19
  128.4 0.5 collective-permute-start.21
  128.9 0.0 collective-permute-done.18.refs_23_
  128.9 2.4 %collective-permute-start.23 = (bf16[512,128]{1,0:T(8,128)(2,1)S(1)}, bf16[512,128]{1,0:T(8,128)(2,1)S(1)}, u32[]{:S(2)}, u32[]{:S(2)}) collective-permute-start(bf16[512,128]{1,0:T(8,128)(2,1)S(1)} %get-tuple-element.67), channel_id=1, source_target_pairs={{0,20},{4,16},{8,28},{12,24},{16,4},{20,0},{24,12},{28,8},{1,21},{... | collective-permute-start | bytes 393224 | tf_op jit(solution)/shard_map/ppermute | solution.py:527
  131.3 9.0 %query.3 = (bf16[512,128]{1,0:T(8,128)(2,1)S(1)}, bf16[512,128]{1,0:T(8,128)(2,1)S(1)}, bf16[512,128]{1,0:T(8,128)(2,1)S(1)}, bf16[512,128]{1,0:T(8,128)(2,1)S(1)}) custom-call(s32[4]{0:T(128)S(1)} %copy-done.3, bf16[512,3072]{1,0:T(8,128)(2,1)S(1)} %copy-done, bf16[536,768]{1,0:T(8,128)(2,1)S(1)} %collective-permute-done.refs_1_, ...), custom_call_target="tpu_custom_call" | custom-call | flops 1879048192 | bytes 13369344 | tf_op jit(solution)/shard_map/query/pallas_call | solution.py:506
  140.3 0.6 copy-done.2
  141.0 0.6 collective-permute-start.20
  141.6 0.5 collective-permute-start.22
  142.1 2.4 %collective-permute-start.24 = (bf16[512,128]{1,0:T(8,128)(2,1)S(1)}, bf16[512,128]{1,0:T(8,128)(2,1)S(1)}, u32[]{:S(2)}, u32[]{:S(2)}) collective-permute-start(bf16[512,128]{1,0:T(8,128)(2,1)S(1)} %get-tuple-element.68), channel_id=1, source_target_pairs={{0,20},{4,16},{8,28},{12,24},{16,4},{20,0},{24,12},{28,8},{1,21},{... | collective-permute-start | bytes 393224 | tf_op jit(solution)/shard_map/ppermute | solution.py:527
  144.5 0.0 collective-permute-done.21.refs_4_
  144.5 2.0 %collective-permute-done.20.refs_3_ = bf16[512,128]{1,0:T(8,128)(2,1)S(1)} collective-permute-done((bf16[512,128]{1,0:T(8,128)(2,1)S(1)}, bf16[512,128]{1,0:T(8,128)(2,1)S(1)}, u32[]{:S(2)}, u32[]{:S(2)}) %collective-permute-start.20) | collective-permute-done | bytes 131104 | tf_op jit(solution)/shard_map/ppermute | solution.py:127
  146.5 1.7 %collective-permute-done.22.refs_5_ = bf16[512,128]{1,0:T(8,128)(2,1)S(1)} collective-permute-done((bf16[512,128]{1,0:T(8,128)(2,1)S(1)}, bf16[512,128]{1,0:T(8,128)(2,1)S(1)}, u32[]{:S(2)}, u32[]{:S(2)}) %collective-permute-start.22) | collective-permute-done | bytes 131104 | tf_op jit(solution)/shard_map/ppermute | solution.py:127
  148.3 0.6 copy-done.9
  148.9 0.1 copy-done.10
  148.9 2.6 %merge.1 = bf16[512,1024]{1,0:T(8,128)(2,1)} custom-call(s32[4]{0:T(128)} %pad_add_fusion.places, bf16[512,128]{1,0:T(8,128)(2,1)} %copy-done.1, bf16[512,128]{1,0:T(8,128)(2,1)} %copy-done.2, bf16[512,128]{1,0:T(8,128)(2,1)} %copy-done.5, bf16[512,128]{1,0:T(8,128)(2,1)} %copy-done.8, bf16[512,128]{1,0:T(8,128)(2,1)} %copy-done.6, ...), custom_call_target="tpu_custom_call" | custom-call | tf_op jit(solution)/shard_map/merge/pallas_call | solution.py:530
  (24 shorter events, 0.1 us)
Async XLA Ops:
  2.0 22.2 %collective-permute-start = (bf16[536,768]{1,0:T(8,128)(2,1)S(1)}, bf16[536,768]{1,0:T(8,128)(2,1)S(1)}, u32[]{:S(2)}, u32[]{:S(2)}) collective-permute-start(bf16[536,768]{1,0:T(8,128)(2,1)S(1)} %pad_maximum_fusion), channel_id=1, source_target_pairs={{0,4},{4,0},{8,12},{12,8},{1,5},{5,1},{9,13},{13,9},{2,6},{6,2},{1... | collective-permute-start | bytes 2469896 | tf_op jit(solution)/shard_map/ppermute | solution.py:127
  5.1 19.8 %collective-permute-start.1 = (bf16[536,768]{1,0:T(8,128)(2,1)S(1)}, bf16[536,768]{1,0:T(8,128)(2,1)S(1)}, u32[]{:S(2)}, u32[]{:S(2)}) collective-permute-start(bf16[536,768]{1,0:T(8,128)(2,1)S(1)} %pad_maximum_fusion), channel_id=1, source_target_pairs={{0,16},{16,0},{1,17},{17,1},{2,18},{18,2},{3,19},{19,3},{4,20},{20... | collective-permute-start | bytes 2469896 | tf_op jit(solution)/shard_map/ppermute | solution.py:127
  11.1 77.0 %all-to-all-start = ((bf16[4,768,512]{2,1,0:T(8,128)(2,1)}), bf16[4,768,512]{2,1,0:T(8,128)(2,1)}, u32[]{:S(2)}, u32[]{:S(2)}) async-start(bf16[4,768,512]{2,1,0:T(8,128)(2,1)} %pack.1), calls=%async_computation | async-start | bytes 6291456 | tf_op jit(solution)/shard_map/all_to_all | solution.py:422
  24.9 2.3 %collective-permute-start.2 = (bf16[536,768]{1,0:T(8,128)(2,1)S(1)}, bf16[536,768]{1,0:T(8,128)(2,1)S(1)}, u32[]{:S(2)}, u32[]{:S(2)}) collective-permute-start(bf16[536,768]{1,0:T(8,128)(2,1)S(1)} %collective-permute-done.refs_1_), channel_id=1, source_target_pairs={{0,1},{1,0},{2,3},{3,2},{4,5},{5,4},{6,7},{7,6},{8,9},{9,8},{10,11... | collective-permute-start | bytes 2469896 | tf_op jit(solution)/shard_map/ppermute | solution.py:127
  27.2 20.4 %collective-permute-start.8 = (bf16[536,768]{1,0:T(8,128)(2,1)S(1)}, bf16[536,768]{1,0:T(8,128)(2,1)S(1)}, u32[]{:S(2)}, u32[]{:S(2)}) collective-permute-start(bf16[536,768]{1,0:T(8,128)(2,1)S(1)} %collective-permute-done.refs_1_), channel_id=1, source_target_pairs={{0,16},{16,0},{1,17},{17,1},{2,18},{18,2},{3,19},{19,3},{4,20},{20... | collective-permute-start | bytes 2469896 | tf_op jit(solution)/shard_map/ppermute | solution.py:127
  28.8 20.2 %collective-permute-start.3 = (bf16[536,768]{1,0:T(8,128)(2,1)S(1)}, bf16[536,768]{1,0:T(8,128)(2,1)}, u32[]{:S(2)}, u32[]{:S(2)}) collective-permute-start(bf16[536,768]{1,0:T(8,128)(2,1)S(1)} %collective-permute-done.refs_1_), channel_id=1, source_target_pairs={{0,2},{2,0},{1,3},{3,1},{4,6},{6,4},{5,7},{7,5},{8,10},{10,8},{9,1... | collective-permute-start | bytes 2469896 | tf_op jit(solution)/shard_map/ppermute | solution.py:127
  47.6 2.5 %collective-permute-start.9 = (bf16[536,768]{1,0:T(8,128)(2,1)S(1)}, bf16[536,768]{1,0:T(8,128)(2,1)}, u32[]{:S(2)}, u32[]{:S(2)}) collective-permute-start(bf16[536,768]{1,0:T(8,128)(2,1)S(1)} %collective-permute-done.8.refs_9_), channel_id=1, source_target_pairs={{0,1},{1,0},{2,3},{3,2},{4,5},{5,4},{6,7},{7,6},{8,9},{9,8},{10,11... | collective-permute-start | bytes 2469896 | tf_op jit(solution)/shard_map/ppermute | solution.py:127
  47.6 40.5 %copy-start.3 = (s32[4]{0:T(128)S(1)}, s32[4]{0:T(128)}, u32[]{:S(2)}) copy-start(s32[4]{0:T(128)} %pad_add_fusion.places) | copy-start | bytes 52
  50.1 22.3 %collective-permute-start.10 = (bf16[536,768]{1,0:T(8,128)(2,1)S(1)}, bf16[536,768]{1,0:T(8,128)(2,1)}, u32[]{:S(2)}, u32[]{:S(2)}) collective-permute-start(bf16[536,768]{1,0:T(8,128)(2,1)S(1)} %collective-permute-done.8.refs_9_), channel_id=1, source_target_pairs={{0,2},{2,0},{1,3},{3,1},{4,6},{6,4},{5,7},{7,5},{8,10},{10,8},{9,1... | collective-permute-start | bytes 2469896 | tf_op jit(solution)/shard_map/ppermute | solution.py:127
  52.8 19.5 %collective-permute-start.5 = (bf16[512,768]{1,0:T(8,128)(2,1)S(1)}, bf16[512,768]{1,0:T(8,128)(2,1)}, u32[]{:S(2)}, u32[]{:S(2)}) collective-permute-start(bf16[512,768]{1,0:T(8,128)(2,1)S(1)} %constant_dynamic-slice_fusion.5), channel_id=1, source_target_pairs={{0,16},{16,0},{1,17},{17,1},{2,18},{18,2},{3,19},{19,3},{4,20},{20... | collective-permute-start | bytes 2359304 | tf_op jit(solution)/shard_map/ppermute | solution.py:127
  54.4 23.6 %collective-permute-start.6 = (bf16[536,768]{1,0:T(8,128)(2,1)S(1)}, bf16[536,768]{1,0:T(8,128)(2,1)}, u32[]{:S(2)}, u32[]{:S(2)}) collective-permute-start(bf16[536,768]{1,0:T(8,128)(2,1)S(1)} %collective-permute-done.1.refs_5_), channel_id=1, source_target_pairs={{0,1},{1,0},{2,3},{3,2},{4,5},{5,4},{6,7},{7,6},{8,9},{9,8},{10,11... | collective-permute-start | bytes 2469896 | tf_op jit(solution)/shard_map/ppermute | solution.py:127
  54.4 26.6 %collective-permute-start.4 = (bf16[536,768]{1,0:T(8,128)(2,1)}, bf16[536,768]{1,0:T(8,128)(2,1)}, u32[]{:S(2)}, u32[]{:S(2)}) collective-permute-start(bf16[536,768]{1,0:T(8,128)(2,1)} %collective-permute-done.3.refs_2_), channel_id=1, source_target_pairs={{0,1},{1,0},{2,3},{3,2},{4,5},{5,4},{6,7},{7,6},{8,9},{9,8},{10,11... | collective-permute-start | bytes 2469896 | tf_op jit(solution)/shard_map/ppermute | solution.py:127
  72.3 15.8 %collective-permute-start.11 = (bf16[536,768]{1,0:T(8,128)(2,1)}, bf16[536,768]{1,0:T(8,128)(2,1)}, u32[]{:S(2)}, u32[]{:S(2)}) collective-permute-start(bf16[536,768]{1,0:T(8,128)(2,1)} %collective-permute-done.10.refs_10_), channel_id=1, source_target_pairs={{0,1},{1,0},{2,3},{3,2},{4,5},{5,4},{6,7},{7,6},{8,9},{9,8},{10,11... | collective-permute-start | bytes 2469896 | tf_op jit(solution)/shard_map/ppermute | solution.py:127
  72.3 8.3 %collective-permute-start.7 = (bf16[512,768]{1,0:T(8,128)(2,1)}, bf16[512,768]{1,0:T(8,128)(2,1)}, u32[]{:S(2)}, u32[]{:S(2)}) collective-permute-start(bf16[512,768]{1,0:T(8,128)(2,1)} %collective-permute-done.5.refs_6_), channel_id=1, source_target_pairs={{0,1},{1,0},{2,3},{3,2},{4,5},{5,4},{6,7},{7,6},{8,9},{9,8},{10,11... | collective-permute-start | bytes 2359304 | tf_op jit(solution)/shard_map/ppermute | solution.py:127
  76.7 26.4 %collective-permute-start.12 = (bf16[768,256]{1,0:T(8,128)(2,1)}, bf16[768,256]{1,0:T(8,128)(2,1)}, u32[]{:S(2)}, u32[]{:S(2)}) collective-permute-start(bf16[768,256]{1,0:T(8,128)(2,1)} %constant_dynamic-slice_fusion.3), channel_id=1, source_target_pairs={{0,4},{4,0},{8,12},{12,8},{1,5},{5,1},{9,13},{13,9},{2,6},{6,2},{1... | collective-permute-start | bytes 1179656 | tf_op jit(solution)/shard_map/ppermute | solution.py:127
  78.0 36.3 %collective-permute-start.13 = (bf16[768,128]{1,0:T(8,128)(2,1)}, bf16[768,128]{1,0:T(8,128)(2,1)}, u32[]{:S(2)}, u32[]{:S(2)}) collective-permute-start(bf16[768,128]{1,0:T(8,128)(2,1)} %get-tuple-element.43.refs_13_), channel_id=1, source_target_pairs={{0,8},{4,12},{8,0},{12,4},{1,9},{5,13},{9,1},{13,5},{2,10},{6,14},... | collective-permute-start | bytes 589832 | tf_op jit(solution)/shard_map/ppermute | solution.py:127
  80.6 37.5 %collective-permute-start.14 = (bf16[768,128]{1,0:T(8,128)(2,1)}, bf16[768,128]{1,0:T(8,128)(2,1)}, u32[]{:S(2)}, u32[]{:S(2)}) collective-permute-start(bf16[768,128]{1,0:T(8,128)(2,1)} %get-tuple-element.44), channel_id=1, source_target_pairs={{0,12},{4,8},{8,4},{12,0},{1,13},{5,9},{9,5},{13,1},{2,14},{6,10},... | collective-permute-start | bytes 589832 | tf_op jit(solution)/shard_map/ppermute | solution.py:127
  88.1 15.0 %copy-start.4 = (bf16[768,128]{1,0:T(8,128)(2,1)S(1)}, bf16[768,128]{1,0:T(8,128)(2,1)}, u32[]{:S(2)}) copy-start(bf16[768,128]{1,0:T(8,128)(2,1)} %get-tuple-element.54) | copy-start | bytes 589828
  97.3 20.8 %collective-permute-start.15 = (bf16[1,2,128,128]{3,2,1,0:T(8,128)(2,1)S(1)}, bf16[1,2,128,128]{3,2,1,0:T(8,128)(2,1)S(1)}, u32[]{:S(2)}, u32[]{:S(2)}) collective-permute-start(bf16[1,2,128,128]{3,2,1,0:T(8,128)(2,1)S(1)} %get-tuple-element.51), channel_id=1, source_target_pairs={{0,8},{4,12},{1,9},{5,13},{2,10},{6,14},{3,11},{7,15},{16,24},{20,... | collective-permute-start | bytes 196616 | tf_op jit(solution)/shard_map/ppermute | solution.py:497
  103.1 28.2 %collective-permute-start.16 = (bf16[768,128]{1,0:T(8,128)(2,1)S(1)}, bf16[768,128]{1,0:T(8,128)(2,1)S(1)}, u32[]{:S(2)}, u32[]{:S(2)}) collective-permute-start(bf16[768,128]{1,0:T(8,128)(2,1)S(1)} %get-tuple-element.53.refs_13_), channel_id=1, source_target_pairs={{0,8},{4,12},{8,0},{12,4},{1,9},{5,13},{9,1},{13,5},{2,10},{6,14},... | collective-permute-start | bytes 589832 | tf_op jit(solution)/shard_map/ppermute | solution.py:127
  103.1 28.2 %collective-permute-start.17 = (bf16[768,128]{1,0:T(8,128)(2,1)S(1)}, bf16[768,128]{1,0:T(8,128)(2,1)S(1)}, u32[]{:S(2)}, u32[]{:S(2)}) collective-permute-start(bf16[768,128]{1,0:T(8,128)(2,1)S(1)} %copy-done.4), channel_id=1, source_target_pairs={{0,12},{4,8},{8,4},{12,0},{1,13},{5,9},{9,5},{13,1},{2,14},{6,10},... | collective-permute-start | bytes 589832 | tf_op jit(solution)/shard_map/ppermute | solution.py:127
  105.0 13.1 %copy-start = (bf16[512,3072]{1,0:T(8,128)(2,1)S(1)}, bf16[512,3072]{1,0:T(8,128)(2,1)}, u32[]{:S(2)}) copy-start(bf16[512,3072]{1,0:T(8,128)(2,1)} %refs_0_.9) | copy-start | bytes 9437188
  114.3 14.6 %collective-permute-start.18 = (bf16[1,2,128,128]{3,2,1,0:T(8,128)(2,1)S(1)}, bf16[1,2,128,128]{3,2,1,0:T(8,128)(2,1)S(1)}, u32[]{:S(2)}, u32[]{:S(2)}) collective-permute-start(bf16[1,2,128,128]{3,2,1,0:T(8,128)(2,1)S(1)} %get-tuple-element.61), channel_id=1, source_target_pairs={{0,8},{4,12},{1,9},{5,13},{2,10},{6,14},{3,11},{7,15},{16,24},{20,... | collective-permute-start | bytes 196616 | tf_op jit(solution)/shard_map/ppermute | solution.py:497
  127.1 0.6 copy-start.1
  127.8 14.3 %collective-permute-start.19 = (bf16[512,128]{1,0:T(8,128)(2,1)S(1)}, bf16[512,128]{1,0:T(8,128)(2,1)S(1)}, u32[]{:S(2)}, u32[]{:S(2)}) collective-permute-start(bf16[512,128]{1,0:T(8,128)(2,1)S(1)} %get-tuple-element.63), channel_id=1, source_target_pairs={{0,4},{4,0},{8,12},{12,8},{1,5},{5,1},{9,13},{13,9},{2,6},{6,2},{1... | collective-permute-start | bytes 393224 | tf_op jit(solution)/shard_map/ppermute | solution.py:127
  128.4 16.1 %collective-permute-start.21 = (bf16[512,128]{1,0:T(8,128)(2,1)S(1)}, bf16[512,128]{1,0:T(8,128)(2,1)S(1)}, u32[]{:S(2)}, u32[]{:S(2)}) collective-permute-start(bf16[512,128]{1,0:T(8,128)(2,1)S(1)} %get-tuple-element.65), channel_id=1, source_target_pairs={{0,16},{16,0},{1,17},{17,1},{2,18},{18,2},{3,19},{19,3},{4,20},{20... | collective-permute-start | bytes 393224 | tf_op jit(solution)/shard_map/ppermute | solution.py:127
  128.9 15.6 %collective-permute-start.23 = (bf16[512,128]{1,0:T(8,128)(2,1)S(1)}, bf16[512,128]{1,0:T(8,128)(2,1)S(1)}, u32[]{:S(2)}, u32[]{:S(2)}) collective-permute-start(bf16[512,128]{1,0:T(8,128)(2,1)S(1)} %get-tuple-element.67), channel_id=1, source_target_pairs={{0,20},{4,16},{8,28},{12,24},{16,4},{20,0},{24,12},{28,8},{1,21},{... | collective-permute-start | bytes 393224 | tf_op jit(solution)/shard_map/ppermute | solution.py:527
  140.3 0.6 copy-start.2
  141.0 5.5 %collective-permute-start.20 = (bf16[512,128]{1,0:T(8,128)(2,1)S(1)}, bf16[512,128]{1,0:T(8,128)(2,1)S(1)}, u32[]{:S(2)}, u32[]{:S(2)}) collective-permute-start(bf16[512,128]{1,0:T(8,128)(2,1)S(1)} %get-tuple-element.64), channel_id=1, source_target_pairs={{0,4},{4,0},{8,12},{12,8},{1,5},{5,1},{9,13},{13,9},{2,6},{6,2},{1... | collective-permute-start | bytes 393224 | tf_op jit(solution)/shard_map/ppermute | solution.py:127
  141.6 6.6 %collective-permute-start.22 = (bf16[512,128]{1,0:T(8,128)(2,1)S(1)}, bf16[512,128]{1,0:T(8,128)(2,1)S(1)}, u32[]{:S(2)}, u32[]{:S(2)}) collective-permute-start(bf16[512,128]{1,0:T(8,128)(2,1)S(1)} %get-tuple-element.66), channel_id=1, source_target_pairs={{0,16},{16,0},{1,17},{17,1},{2,18},{18,2},{3,19},{19,3},{4,20},{20... | collective-permute-start | bytes 393224 | tf_op jit(solution)/shard_map/ppermute | solution.py:127
  142.1 6.1 %copy-start.5 = (bf16[512,128]{1,0:T(8,128)(2,1)}, bf16[512,128]{1,0:T(8,128)(2,1)S(1)}, u32[]{:S(2)}) copy-start(bf16[512,128]{1,0:T(8,128)(2,1)S(1)} %collective-permute-done.19.refs_2_) | copy-start | bytes 393220
  142.1 6.1 %collective-permute-start.24 = (bf16[512,128]{1,0:T(8,128)(2,1)S(1)}, bf16[512,128]{1,0:T(8,128)(2,1)S(1)}, u32[]{:S(2)}, u32[]{:S(2)}) collective-permute-start(bf16[512,128]{1,0:T(8,128)(2,1)S(1)} %get-tuple-element.68), channel_id=1, source_target_pairs={{0,20},{4,16},{8,28},{12,24},{16,4},{20,0},{24,12},{28,8},{1,21},{... | collective-permute-start | bytes 393224 | tf_op jit(solution)/shard_map/ppermute | solution.py:527
  144.5 3.8 %copy-start.6 = (bf16[512,128]{1,0:T(8,128)(2,1)}, bf16[512,128]{1,0:T(8,128)(2,1)S(1)}, u32[]{:S(2)}) copy-start(bf16[512,128]{1,0:T(8,128)(2,1)S(1)} %collective-permute-done.21.refs_4_) | copy-start | bytes 393220
  144.5 3.8 %copy-start.7 = (bf16[512,128]{1,0:T(8,128)(2,1)}, bf16[512,128]{1,0:T(8,128)(2,1)S(1)}, u32[]{:S(2)}) copy-start(bf16[512,128]{1,0:T(8,128)(2,1)S(1)} %collective-permute-done.23.refs_6_) | copy-start | bytes 393220
  146.5 1.8 %copy-start.8 = (bf16[512,128]{1,0:T(8,128)(2,1)}, bf16[512,128]{1,0:T(8,128)(2,1)S(1)}, u32[]{:S(2)}) copy-start(bf16[512,128]{1,0:T(8,128)(2,1)S(1)} %collective-permute-done.20.refs_3_) | copy-start | bytes 393220
  148.2 0.7 copy-start.9
  148.2 0.7 copy-start.10

commit v6 on v5

--- a/solution.py
+++ b/solution.py
@@ -157,7 +157,7 @@
     return jnp.transpose(jnp.broadcast_to(row, (PIECE, row.shape[1])))
 
 
-def token_copies(places, token_refs, held, semaphores):
+def token_copies(places, token_refs, held, semaphores, chosen=range(len(SIDES))):
     turn, share = places[0], places[1] * 2 + places[2]
     own_ref, quarter_refs = token_refs[0], token_refs[1:]
     width = held.shape[3]
@@ -166,7 +166,7 @@
         return pltpu.make_async_copy(source, held.at[side, flip], semaphores.at[side, flip])
 
     def start():
-        for side in range(len(SIDES)):
+        for side in chosen:
             for flip in range(held.shape[1]):
                 block = turn ^ flip
                 if side == 0:
@@ -306,13 +306,13 @@
             pair_ref[head, pair] = (jnp.exp(total) * first + second).astype(jnp.bfloat16)
 
 
-def query_kernel(head, columns, flips, places, *refs):
-    sides = len(SIDES)
+def query_kernel(chosen, head, columns, flips, places, *refs):
     token_refs, refs = refs[:13], refs[13:]
     weight_refs, refs = refs[:flips], refs[flips:]
     key_ref, value_ref, state_ref, sum_ref, fade_ref, mask_ref, before_ref = refs[:7]
     out_refs, (incoming_ref, held, semaphores) = refs[7:-3], refs[-3:]
-    start, wait = token_copies(places, token_refs, held, semaphores)
+    out_refs = dict(zip(chosen, out_refs))
+    start, wait = token_copies(places, token_refs, held, semaphores, chosen)
     start()
     odd = places[0] % 2 == 1
     cuts = piece_rows(key_ref.shape[1])
@@ -320,7 +320,7 @@
     end = sum_ref.shape[2] - 1
     at = slice(head * PIECE, (head + 1) * PIECE)
     weights = [ref[:, columns] if flip == 1 else ref[...] for flip, ref in enumerate(weight_refs)]
-    for side in range(sides):
+    for side in chosen:
         partner = side ^ 1
         before = before_ref[head, side // 2].astype(jnp.float32)
         total = sum_ref[partner, head : head + 1, end:]
@@ -358,7 +358,7 @@
         out_refs[side][cut, :] = (raw * scale).astype(jnp.bfloat16)
 
     staggered(
-        [(side, piece) for side in range(sides) for piece in range(len(cuts))], first, second, third, fourth
+        [(side, piece) for side in chosen for piece in range(len(cuts))], first, second, third, fourth
     )
 
 
@@ -416,6 +416,7 @@
         ),
         out_shape=jax.ShapeDtypeStruct(packed_shape, jnp.bfloat16),
         cost_estimate=pl.CostEstimate(flops=0, bytes_accessed=32 * depth * heads * size, transcendentals=0),
+        compiler_params=pltpu.CompilerParams(vmem_limit_bytes=16 << 20),
         name="pack",
     )(places, key_weight, value_weight, key_weight, value_weight)
 
@@ -423,9 +424,8 @@
 
     from_ctx = xor_permute(quarter, mesh, "ctx", 1)
     from_groups = xor_permute(quarter, mesh, "groups", 1)
-    (from_ctx,) = after((from_ctx,), from_groups)
     ctx_core = xor_permute(from_ctx, mesh, "head", 1)
-    (from_ctx,) = after((from_ctx,), ctx_core)
+    (from_ctx,) = after((from_ctx,), ctx_core, from_groups)
     ctx_plane = xor_permute(from_ctx, mesh, "fsdp", 1)
     from_both = xor_permute(from_ctx, mesh, "groups", 1)
     beside = after((tokens,), from_ctx)[0]
@@ -447,7 +447,7 @@
     query_own = [query_block(mine, head, 1) for head in range(heads)]
     query_sent = [query_block(mine ^ 1, head, 1) for head in range(heads)]
     near_block, own, other = after(
-        (query_block(mine ^ 1, 0, heads), query_own[0], query_sent[0]), both_plane
+        (query_block(mine ^ 1, 0, heads), query_own[0], query_sent[0]), from_both
     )
     query_near = xor_permute(near_block, mesh, "ctx", 1)
     parts = [
@@ -501,13 +501,14 @@
                 [xor_permute(other if flip % 2 else own, mesh, "ctx", flip) for flip in range(2, flips)]
             )
 
-    returned = [[] for _ in SIDES]
-    for head in range(heads):
-        attended = pl.pallas_call(
-            functools.partial(query_kernel, 0, slice(head * size, (head + 1) * size), flips),
+    def query(head, chosen, *gate):
+        own = after((query_own[head],), *gate)[0] if gate else query_own[head]
+        count = len(chosen)
+        return pl.pallas_call(
+            functools.partial(query_kernel, chosen, 0, slice(head * size, (head + 1) * size), flips),
             in_specs=[SCALARS] + [ANY] * len(token_sets) + [VMEM] * (flips + 7),
-            out_specs=[VMEM] * sides,
-            out_shape=[jax.ShapeDtypeStruct((rows, size), jnp.bfloat16)] * sides,
+            out_specs=[VMEM] * count,
+            out_shape=[jax.ShapeDtypeStruct((rows, size), jnp.bfloat16)] * count,
             scratch_shapes=[
                 pltpu.VMEM((sides, pieces, size, size), jnp.bfloat16),
                 pltpu.VMEM(*held_shape),
@@ -515,12 +516,20 @@
             ],
             compiler_params=small,
             cost_estimate=pl.CostEstimate(
-                flops=2 * sides * rows * size * (width + 4 * size),
-                bytes_accessed=2 * (sides * rows * width + width * size),
-                transcendentals=sides * rows * 4 * size,
+                flops=2 * count * rows * size * (width + 4 * size),
+                bytes_accessed=2 * (count * rows * width + width * size),
+                transcendentals=count * rows * 4 * size,
             ),
             name="query",
-        )(places, *token_sets, query_own[head], query_near, *parts[head], *memory[head], before[head])
+        )(places, *token_sets, own, query_near, *parts[head], *memory[head], before[head])
+
+    returned = [[] for _ in SIDES]
+    for head in range(heads):
+        if head < heads - 1:
+            attended = query(head, tuple(range(sides)))
+        else:
+            away = query(head, tuple(range(1, sides)))
+            attended = [*query(head, (0,), away[0]), *away]
         returned[0].append(attended[0])
         returned[1].append(xor_permute(attended[1], mesh, "ctx", 1))
         returned[2].append(xor_permute(attended[2], mesh, "groups", 1))
@@ -532,6 +541,7 @@
         in_specs=[SCALARS] + [VMEM] * len(flat),
         out_specs=VMEM,
         out_shape=jax.ShapeDtypeStruct((rows, heads_here * size), jnp.bfloat16),
+        compiler_params=pltpu.CompilerParams(vmem_limit_bytes=8 << 20),
         name="merge",
     )(places, *flat)
 

time: 152 us -> 147 us (0.967)
  waiting for transfers between devices: 63.8 us -> 56 us
  starting transfers between devices: 35.1 us -> 37.8 us
    all_to_all x1, waiting for transfers between devices: 7.02 us -> 0.01 us  [spread_body(): key_value = lax.all_to_all(packed, 'ctx', 0, 0)]
    ppermute x21, starting transfers between devices: 20.4 us -> 27.2 us  [xor_permute(): lax.ppermute(array, axis, [(at, at ^ flip) for at in range(mesh.shape[axi...]
    ppermute x2, starting transfers between devices: 4.78 us -> 0.74 us  [spread_body(): returned[3].append(lax.ppermute(attended[3], ('groups', 'ctx'), both))]
    ppermute x21, waiting for transfers between devices: 56.7 us -> 54.1 us  [xor_permute(): lax.ppermute(array, axis, [(at, at ^ flip) for at in range(mesh.shape[axi...]
    pallas_call x2 -> x3, Pallas kernels: 18 us -> 20.2 us  [query(): pl.pallas_call(functools.partial(query_kernel, chosen, 0, slice(head * si...]
    pallas_call x1, Pallas kernels: 3.84 us -> 1.64 us  [spread_body(): pl.pallas_call(functools.partial(pack_kernel, heads, size), grid_spec=plt...]
    ppermute x2, waiting for transfers between devices: 0.01 us -> 1.88 us  [spread_body(): returned[3].append(lax.ppermute(attended[3], ('groups', 'ctx'), both))]
    unnamed x22 -> x10, local copies, waits for them, and re-layouts: 1.97 us -> 3.11 us
  transfers between devices with their start and end apart: 26 -> 26, of which waited for: 11 -> 7; matrix products, arithmetic and copies ran while one was open for 4% -> 3% of each run, Pallas kernels for 27% -> 28%
where the time goes in v6:
time: 147 us; the launch traced here: 146 us
  waiting for transfers between devices  56 us (38%)
  Pallas kernels  42.1 us (29%)
  starting transfers between devices  37.8 us (26%)
  local copies, waits for them, and re-layouts  9.46 us (6%)
    ppermute x21, waiting for transfers between devices, xor_permute(): lax.ppermute(array, axis, [(at, at ^ flip) for at in range(mesh.shape[axi...  54.1 us
    ppermute x21, starting transfers between devices, xor_permute(): lax.ppermute(array, axis, [(at, at ^ flip) for at in range(mesh.shape[axi...  27.2 us
    pallas_call x3, Pallas kernels, query(): pl.pallas_call(functools.partial(query_kernel, chosen, 0, slice(head * si...  20.2 us
    pallas_call x2, Pallas kernels, spread_body(): pl.pallas_call(functools.partial(key_value_kernel, head, heads, size, fli...  18.4 us
    ppermute x2, starting transfers between devices, spread_body(): lax.ppermute(pair_state, 'ctx', [(at, at + 2) for at in range(flips - 2)])  5.21 us
    all_to_all x1, starting transfers between devices, spread_body(): key_value = lax.all_to_all(packed, 'ctx', 0, 0)  4.64 us
    dynamic_slice x2, local copies, waits for them, and re-layouts, query_block(): lax.dynamic_slice(query_weight, (0, (owner * heads + head) * size), (dept...  3.86 us
    unnamed x10, local copies, waits for them, and re-layouts  3.11 us
  transfers between devices with their start and end apart: 26, of which 7 were waited for; matrix products, arithmetic and copies ran while one was open for 3% of the time, Pallas kernels for 28%

profile of v6, /device:TPU:0, one launch (start us, length us, event | category | flops | bytes accessed | tf_op | source)
XLA Modules:
  0.0 146.5 jit_solution(2180296505440527905)
XLA Ops:
  0.0 0.7 reduce-precision_convert_fusion.1
  0.7 1.3 constant_dynamic-slice_fusion.6
  2.1 0.1 pad_maximum_fusion
  2.1 3.1 %collective-permute-start = (bf16[536,768]{1,0:T(8,128)(2,1)S(1)}, bf16[536,768]{1,0:T(8,128)(2,1)S(1)}, u32[]{:S(2)}, u32[]{:S(2)}) collective-permute-start(bf16[536,768]{1,0:T(8,128)(2,1)S(1)} %pad_maximum_fusion), channel_id=1, source_target_pairs={{0,4},{4,0},{8,12},{12,8},{1,5},{5,1},{9,13},{13,9},{2,6},{6,2},{1... | collective-permute-start | bytes 2469896 | tf_op jit(solution)/shard_map/ppermute | solution.py:127
  5.2 0.1 pad_add_fusion.places
  5.3 1.4 copy-done.3
  6.7 1.6 %pack.1 = bf16[4,768,512]{2,1,0:T(8,128)(2,1)S(1)} custom-call(s32[4]{0:T(128)S(1)} %pad_add_fusion.places, bf16[768,1024]{1,0:T(8,128)(2,1)S(1)} %copy-done.2, bf16[768,1024]{1,0:T(8,128)(2,1)S(1)} %copy-done.3, bf16[768,1024]{1,0:T(8,128)(2,1)S(1)} %copy-done.2, bf16[768,1024]{1,0:T(8,128)(2,1)S(1)} %copy-done.3), custom_call_target="tpu_custom_call" | custom-call | bytes 6291456 | tf_op jit(solution)/shard_map/pack/pallas_call | solution.py:409
  8.4 1.7 %copy-done.1 = bf16[4,768,512]{2,1,0:T(8,128)(2,1)} copy-done((bf16[4,768,512]{2,1,0:T(8,128)(2,1)}, bf16[4,768,512]{2,1,0:T(8,128)(2,1)S(1)}, u32[]{:S(2)}) %copy-start.1) | copy-done | bytes 3145752
  10.0 4.6 %all-to-all-start = ((bf16[4,768,512]{2,1,0:T(8,128)(2,1)}), bf16[4,768,512]{2,1,0:T(8,128)(2,1)}, u32[]{:S(2)}, u32[]{:S(2)}) async-start(bf16[4,768,512]{2,1,0:T(8,128)(2,1)} %copy-done.1), calls=%async_computation | async-start | bytes 6291456 | tf_op jit(solution)/shard_map/all_to_all | solution.py:423
  14.7 1.6 %collective-permute-start.2 = (bf16[536,768]{1,0:T(8,128)(2,1)S(1)}, bf16[536,768]{1,0:T(8,128)(2,1)S(1)}, u32[]{:S(2)}, u32[]{:S(2)}) collective-permute-start(bf16[536,768]{1,0:T(8,128)(2,1)S(1)} %pad_maximum_fusion), channel_id=1, source_target_pairs={{0,16},{16,0},{1,17},{17,1},{2,18},{18,2},{3,19},{19,3},{4,20},{20... | collective-permute-start | bytes 2469896 | tf_op jit(solution)/shard_map/ppermute | solution.py:127
  16.3 8.1 %collective-permute-done.refs_1_ = bf16[536,768]{1,0:T(8,128)(2,1)S(1)} collective-permute-done((bf16[536,768]{1,0:T(8,128)(2,1)S(1)}, bf16[536,768]{1,0:T(8,128)(2,1)S(1)}, u32[]{:S(2)}, u32[]{:S(2)}) %collective-permute-start) | collective-permute-done | bytes 823328 | tf_op jit(solution)/shard_map/ppermute | solution.py:127
  24.4 0.0 collective-permute-start.1
  24.4 10.2 %collective-permute-done.2.refs_5_ = bf16[536,768]{1,0:T(8,128)(2,1)S(1)} collective-permute-done((bf16[536,768]{1,0:T(8,128)(2,1)S(1)}, bf16[536,768]{1,0:T(8,128)(2,1)S(1)}, u32[]{:S(2)}, u32[]{:S(2)}) %collective-permute-start.2) | collective-permute-done | bytes 823328 | tf_op jit(solution)/shard_map/ppermute | solution.py:127
  34.5 0.0 collective-permute-done.1.refs_3_
  34.5 1.5 %collective-permute-start.8 = (bf16[536,768]{1,0:T(8,128)(2,1)S(1)}, bf16[536,768]{1,0:T(8,128)(2,1)S(1)}, u32[]{:S(2)}, u32[]{:S(2)}) collective-permute-start(bf16[536,768]{1,0:T(8,128)(2,1)S(1)} %collective-permute-done.refs_1_), channel_id=1, source_target_pairs={{0,16},{16,0},{1,17},{17,1},{2,18},{18,2},{3,19},{19,3},{4,20},{20... | collective-permute-start | bytes 2469896 | tf_op jit(solution)/shard_map/ppermute | solution.py:127
  36.1 1.5 %collective-permute-start.3 = (bf16[536,768]{1,0:T(8,128)(2,1)S(1)}, bf16[536,768]{1,0:T(8,128)(2,1)}, u32[]{:S(2)}, u32[]{:S(2)}) collective-permute-start(bf16[536,768]{1,0:T(8,128)(2,1)S(1)} %collective-permute-done.refs_1_), channel_id=1, source_target_pairs={{0,2},{2,0},{1,3},{3,1},{4,6},{6,4},{5,7},{7,5},{8,10},{10,8},{9,1... | collective-permute-start | bytes 2469896 | tf_op jit(solution)/shard_map/ppermute | solution.py:127
  37.6 16.0 %collective-permute-done.8.refs_9_ = bf16[536,768]{1,0:T(8,128)(2,1)S(1)} collective-permute-done((bf16[536,768]{1,0:T(8,128)(2,1)S(1)}, bf16[536,768]{1,0:T(8,128)(2,1)S(1)}, u32[]{:S(2)}, u32[]{:S(2)}) %collective-permute-start.8) | collective-permute-done | bytes 823328 | tf_op jit(solution)/shard_map/ppermute | solution.py:127
  53.5 0.0 collective-permute-start.9
  53.5 1.3 collective-permute-done.3.refs_2_
  54.9 1.1 collective-permute-done.9.refs_11_
  56.0 1.5 %collective-permute-start.10 = (bf16[536,768]{1,0:T(8,128)(2,1)S(1)}, bf16[536,768]{1,0:T(8,128)(2,1)}, u32[]{:S(2)}, u32[]{:S(2)}) collective-permute-start(bf16[536,768]{1,0:T(8,128)(2,1)S(1)} %collective-permute-done.8.refs_9_), channel_id=1, source_target_pairs={{0,2},{2,0},{1,3},{3,1},{4,6},{6,4},{5,7},{7,5},{8,10},{10,8},{9,1... | collective-permute-start | bytes 2469896 | tf_op jit(solution)/shard_map/ppermute | solution.py:127
  57.5 1.2 constant_dynamic-slice_fusion.5
  58.7 1.6 %collective-permute-start.5 = (bf16[512,768]{1,0:T(8,128)(2,1)S(1)}, bf16[512,768]{1,0:T(8,128)(2,1)}, u32[]{:S(2)}, u32[]{:S(2)}) collective-permute-start(bf16[512,768]{1,0:T(8,128)(2,1)S(1)} %constant_dynamic-slice_fusion.5), channel_id=1, source_target_pairs={{0,16},{16,0},{1,17},{17,1},{2,18},{18,2},{3,19},{19,3},{4,20},{20... | collective-permute-start | bytes 2359304 | tf_op jit(solution)/shard_map/ppermute | solution.py:127
  60.3 0.0 collective-permute-start.6
  60.3 0.5 collective-permute-start.4
  60.8 17.4 %collective-permute-done.5.refs_6_ = bf16[512,768]{1,0:T(8,128)(2,1)} collective-permute-done((bf16[512,768]{1,0:T(8,128)(2,1)S(1)}, bf16[512,768]{1,0:T(8,128)(2,1)}, u32[]{:S(2)}, u32[]{:S(2)}) %collective-permute-start.5) | collective-permute-done | bytes 786464 | tf_op jit(solution)/shard_map/ppermute | solution.py:127
  78.2 0.0 collective-permute-done.10.refs_10_
  78.2 0.0 collective-permute-start.11
  78.2 0.5 collective-permute-start.7
  78.7 1.8 %constant_dynamic-slice_fusion.3 = bf16[768,256]{1,0:T(8,128)(2,1)} fusion(bf16[768,1024]{1,0:T(8,128)(2,1)} %param.6, s32[]{:T(128)S(6)} %select_n.30), kind=kLoop, calls=%fused_computation.16 | loop fusion | bytes 786436 | tf_op jit(solution)/shard_map/dynamic_slice | solution.py:445
  80.4 2.1 %constant_dynamic-slice_fusion = (bf16[768,128]{1,0:T(8,128)(2,1)}, bf16[768,128]{1,0:T(8,128)(2,1)}, bf16[768,128]{1,0:T(8,128)(2,1)}, bf16[768,128]{1,0:T(8,128)(2,1)S(1)}) fusion(bf16[768,1024]{1,0:T(8,128)(2,1)} %param.6, s32[]{:T(128)S(6)} %select_n.32, s32[]{:T(128)S(6)} %select_n.30, s32[]{:T(128)S(6)} %select_n.29, s32[]{:T(128)S(6)} %select_n.31), kind=kLoop, calls=%fused_computation.13 | loop fusion | bytes 1572880 | tf_op jit(solution)/shard_map/dynamic_slice | solution.py:445
  82.5 1.3 collective-permute-start.12
  83.9 0.0 collective-permute-done.6.refs_7_
  83.9 2.4 %collective-permute-start.13 = (bf16[768,128]{1,0:T(8,128)(2,1)}, bf16[768,128]{1,0:T(8,128)(2,1)}, u32[]{:S(2)}, u32[]{:S(2)}) collective-permute-start(bf16[768,128]{1,0:T(8,128)(2,1)} %get-tuple-element.41.refs_13_), channel_id=1, source_target_pairs={{0,8},{4,12},{8,0},{12,4},{1,9},{5,13},{9,1},{13,5},{2,10},{6,14},... | collective-permute-start | bytes 589832 | tf_op jit(solution)/shard_map/ppermute | solution.py:127
  86.2 0.0 collective-permute-done.7.refs_8_
  86.2 0.7 collective-permute-start.14
  86.9 0.0 collective-permute-done.4.refs_4_
  86.9 0.0 all-to-all-done.refs_14_
  87.0 9.2 %key_value.2 = (bf16[4,512,128]{2,1,0:T(8,128)(2,1)S(1)}, bf16[4,512,128]{2,1,0:T(8,128)(2,1)S(1)}, f32[1,4,4,128,128]{4,3,2,1,0:T(8,128)S(1)}, f32[4,1,512]{2,1...) custom-call(s32[4]{0:T(128)S(1)} %pad_add_fusion.places, ...), custom_call_target="tpu_custom_call" | custom-call | flops 3221225472 | bytes 14155776 | tf_op jit(solution)/shard_map/key_value/pallas_call | solution.py:472
  96.1 3.3 %collective-permute-start.15 = (bf16[1,2,128,128]{3,2,1,0:T(8,128)(2,1)S(1)}, bf16[1,2,128,128]{3,2,1,0:T(8,128)(2,1)S(1)}, u32[]{:S(2)}, u32[]{:S(2)}) collective-permute-start(bf16[1,2,128,128]{3,2,1,0:T(8,128)(2,1)S(1)} %get-tuple-element.49), channel_id=1, source_target_pairs={{0,8},{4,12},{1,9},{5,13},{2,10},{6,14},{3,11},{7,15},{16,24},{20,... | collective-permute-start | bytes 196616 | tf_op jit(solution)/shard_map/ppermute | solution.py:497
  99.5 0.0 collective-permute-done.12.refs_14_
  99.5 0.6 collective-permute-start.16
  100.0 4.1 %collective-permute-start.17 = (bf16[768,128]{1,0:T(8,128)(2,1)S(1)}, bf16[768,128]{1,0:T(8,128)(2,1)S(1)}, u32[]{:S(2)}, u32[]{:S(2)}) collective-permute-start(bf16[768,128]{1,0:T(8,128)(2,1)S(1)} %copy-done.4), channel_id=1, source_target_pairs={{0,12},{4,8},{8,4},{12,0},{1,13},{5,9},{9,5},{13,1},{2,14},{6,10},... | collective-permute-start | bytes 589832 | tf_op jit(solution)/shard_map/ppermute | solution.py:127
  104.2 9.3 %key_value.3 = (bf16[4,512,128]{2,1,0:T(8,128)(2,1)S(1)}, bf16[4,512,128]{2,1,0:T(8,128)(2,1)S(1)}, f32[1,4,4,128,128]{4,3,2,1,0:T(8,128)S(1)}, f32[4,1,512]{2,1...) custom-call(s32[4]{0:T(128)S(1)} %pad_add_fusion.places, ...), custom_call_target="tpu_custom_call" | custom-call | flops 3221225472 | bytes 14155776 | tf_op jit(solution)/shard_map/key_value/pallas_call | solution.py:472
  113.5 0.0 collective-permute-done.13.refs_15_
  113.5 1.9 %collective-permute-start.18 = (bf16[1,2,128,128]{3,2,1,0:T(8,128)(2,1)S(1)}, bf16[1,2,128,128]{3,2,1,0:T(8,128)(2,1)S(1)}, u32[]{:S(2)}, u32[]{:S(2)}) collective-permute-start(bf16[1,2,128,128]{3,2,1,0:T(8,128)(2,1)S(1)} %get-tuple-element.59), channel_id=1, source_target_pairs={{0,8},{4,12},{1,9},{5,13},{2,10},{6,14},{3,11},{7,15},{16,24},{20,... | collective-permute-start | bytes 196616 | tf_op jit(solution)/shard_map/ppermute | solution.py:497
  115.3 0.0 collective-permute-done.14.refs_16_
  115.4 0.0 collective-permute-done.15.refs_23_
  115.4 9.0 %query.3 = (bf16[512,128]{1,0:T(8,128)(2,1)S(1)}, bf16[512,128]{1,0:T(8,128)(2,1)S(1)}, bf16[512,128]{1,0:T(8,128)(2,1)S(1)}, bf16[512,128]{1,0:T(8,128)(2,1)S(1)}) custom-call(s32[4]{0:T(128)S(1)} %pad_add_fusion.places, bf16[512,3072]{1,0:T(8,128)(2,1)S(1)} %copy-done, bf16[536,768]{1,0:T(8,128)(2,1)S(1)} %collective-permute-done.refs_1_, ...), custom_call_target="tpu_custom_call" | custom-call | flops 1879048192 | bytes 13369344 | tf_op jit(solution)/shard_map/query/pallas_call | solution.py:507
  124.4 1.7 %collective-permute-start.19 = (bf16[512,128]{1,0:T(8,128)(2,1)S(1)}, bf16[512,128]{1,0:T(8,128)(2,1)S(1)}, u32[]{:S(2)}, u32[]{:S(2)}) collective-permute-start(bf16[512,128]{1,0:T(8,128)(2,1)S(1)} %get-tuple-element.62), channel_id=1, source_target_pairs={{0,4},{4,0},{8,12},{12,8},{1,5},{5,1},{9,13},{13,9},{2,6},{6,2},{1... | collective-permute-start | bytes 393224 | tf_op jit(solution)/shard_map/ppermute | solution.py:127
  126.1 1.5 %collective-permute-start.21 = (bf16[512,128]{1,0:T(8,128)(2,1)S(1)}, bf16[512,128]{1,0:T(8,128)(2,1)S(1)}, u32[]{:S(2)}, u32[]{:S(2)}) collective-permute-start(bf16[512,128]{1,0:T(8,128)(2,1)S(1)} %get-tuple-element.63), channel_id=1, source_target_pairs={{0,16},{16,0},{1,17},{17,1},{2,18},{18,2},{3,19},{19,3},{4,20},{20... | collective-permute-start | bytes 393224 | tf_op jit(solution)/shard_map/ppermute | solution.py:127
  127.6 0.3 collective-permute-start.23
  128.0 0.0 collective-permute-done.16.refs_15_
  128.0 0.0 collective-permute-done.17.refs_16_
  128.0 7.7 %query.4 = (bf16[512,128]{1,0:T(8,128)(2,1)S(1)}, bf16[512,128]{1,0:T(8,128)(2,1)S(1)}, bf16[512,128]{1,0:T(8,128)(2,1)S(1)}) custom-call(s32[4]{0:T(128)S(1)} %pad_add_fusion.places, bf16[512,3072]{1,0:T(8,128)(2,1)S(1)} %copy-done, bf16[536,768]{1,0:T(8,128)(2,1)S(1)} %collective-permute-done.refs_1_, bf16[536,768]{1,0:T(8,128)(2,1)} %collective-permute-done.3.refs_2_, ...), custom_call_target="tpu_custom_call" | custom-call | flops 1409286144 | bytes 10223616 | tf_op jit(solution)/shard_map/query/pallas_call | solution.py:507
  135.6 1.6 %collective-permute-start.20 = (bf16[512,128]{1,0:T(8,128)(2,1)S(1)}, bf16[512,128]{1,0:T(8,128)(2,1)S(1)}, u32[]{:S(2)}, u32[]{:S(2)}) collective-permute-start(bf16[512,128]{1,0:T(8,128)(2,1)S(1)} %get-tuple-element.60), channel_id=1, source_target_pairs={{0,4},{4,0},{8,12},{12,8},{1,5},{5,1},{9,13},{13,9},{2,6},{6,2},{1... | collective-permute-start | bytes 393224 | tf_op jit(solution)/shard_map/ppermute | solution.py:127
  137.3 1.5 %collective-permute-start.22 = (bf16[512,128]{1,0:T(8,128)(2,1)S(1)}, bf16[512,128]{1,0:T(8,128)(2,1)S(1)}, u32[]{:S(2)}, u32[]{:S(2)}) collective-permute-start(bf16[512,128]{1,0:T(8,128)(2,1)S(1)} %get-tuple-element.64), channel_id=1, source_target_pairs={{0,16},{16,0},{1,17},{17,1},{2,18},{18,2},{3,19},{19,3},{4,20},{20... | collective-permute-start | bytes 393224 | tf_op jit(solution)/shard_map/ppermute | solution.py:127
  138.8 0.0 collective-permute-done.19.refs_2_
  138.8 0.4 collective-permute-start.24
  139.2 3.5 %query.5.refs_1_ = bf16[512,128]{1,0:T(8,128)(2,1)S(1)} custom-call(s32[4]{0:T(128)S(1)} %pad_add_fusion.places, bf16[512,3072]{1,0:T(8,128)(2,1)S(1)} %copy-done, bf16[536,768]{1,0:T(8,128)(2,1)S(1)} %collective-permute-done.refs_1_, bf16[536,768]{1,0:T(8,128)(2,1)} %collective-permute-done.3.refs_2_, bf16[536,768]{1,0:T(8,128)(2,1)S(1)} %collective-permute-done.1.refs_3_, ...), custom_call_target="tpu_custom_call" | custom-call | flops 469762048 | bytes 3932160 | tf_op jit(solution)/shard_map/query/pallas_call | solution.py:507
  142.8 0.0 collective-permute-done.23.refs_6_
  142.8 0.0 collective-permute-done.20.refs_3_
  142.8 1.9 %collective-permute-done.24.refs_7_ = bf16[512,128]{1,0:T(8,128)(2,1)S(1)} collective-permute-done((bf16[512,128]{1,0:T(8,128)(2,1)S(1)}, bf16[512,128]{1,0:T(8,128)(2,1)S(1)}, u32[]{:S(2)}, u32[]{:S(2)}) %collective-permute-start.24) | collective-permute-done | bytes 131104 | tf_op jit(solution)/shard_map/ppermute | solution.py:536
  144.7 1.8 %merge.1 = bf16[512,1024]{1,0:T(8,128)(2,1)} custom-call(s32[4]{0:T(128)S(1)} %pad_add_fusion.places, bf16[512,128]{1,0:T(8,128)(2,1)S(1)} %get-tuple-element.50.refs_0_, bf16[512,128]{1,0:T(8,128)(2,1)S(1)} %query.5.refs_1_, bf16[512,128]{1,0:T(8,128)(2,1)S(1)} %collective-permute-done.19.refs_2_, bf16[512,128]{1,0:T(8,128)(2,1)S(1)} %collective-permute-done.20.refs_3_, ...), custom_call_target="tpu_custom_call" | custom-call | tf_op jit(solution)/shard_map/merge/pallas_call | solution.py:539
  (13 shorter events, 0.0 us)
Async XLA Ops:
  0.7 4.6 %copy-start.2 = (bf16[768,1024]{1,0:T(8,128)(2,1)S(1)}, bf16[768,1024]{1,0:T(8,128)(2,1)}, u32[]{:S(2)}) copy-start(bf16[768,1024]{1,0:T(8,128)(2,1)} %refs_2_.1) | copy-start | bytes 4718596
  2.1 22.2 %collective-permute-start = (bf16[536,768]{1,0:T(8,128)(2,1)S(1)}, bf16[536,768]{1,0:T(8,128)(2,1)S(1)}, u32[]{:S(2)}, u32[]{:S(2)}) collective-permute-start(bf16[536,768]{1,0:T(8,128)(2,1)S(1)} %pad_maximum_fusion), channel_id=1, source_target_pairs={{0,4},{4,0},{8,12},{12,8},{1,5},{5,1},{9,13},{13,9},{2,6},{6,2},{1... | collective-permute-start | bytes 2469896 | tf_op jit(solution)/shard_map/ppermute | solution.py:127
  5.3 1.4 copy-start.3
  8.3 1.7 %copy-start.1 = (bf16[4,768,512]{2,1,0:T(8,128)(2,1)}, bf16[4,768,512]{2,1,0:T(8,128)(2,1)S(1)}, u32[]{:S(2)}) copy-start(bf16[4,768,512]{2,1,0:T(8,128)(2,1)S(1)} %pack.1) | copy-start | bytes 9437188
  10.0 76.9 %all-to-all-start = ((bf16[4,768,512]{2,1,0:T(8,128)(2,1)}), bf16[4,768,512]{2,1,0:T(8,128)(2,1)}, u32[]{:S(2)}, u32[]{:S(2)}) async-start(bf16[4,768,512]{2,1,0:T(8,128)(2,1)} %copy-done.1), calls=%async_computation | async-start | bytes 6291456 | tf_op jit(solution)/shard_map/all_to_all | solution.py:423
  14.7 19.9 %collective-permute-start.2 = (bf16[536,768]{1,0:T(8,128)(2,1)S(1)}, bf16[536,768]{1,0:T(8,128)(2,1)S(1)}, u32[]{:S(2)}, u32[]{:S(2)}) collective-permute-start(bf16[536,768]{1,0:T(8,128)(2,1)S(1)} %pad_maximum_fusion), channel_id=1, source_target_pairs={{0,16},{16,0},{1,17},{17,1},{2,18},{18,2},{3,19},{19,3},{4,20},{20... | collective-permute-start | bytes 2469896 | tf_op jit(solution)/shard_map/ppermute | solution.py:127
  24.4 10.2 %collective-permute-start.1 = (bf16[536,768]{1,0:T(8,128)(2,1)S(1)}, bf16[536,768]{1,0:T(8,128)(2,1)S(1)}, u32[]{:S(2)}, u32[]{:S(2)}) collective-permute-start(bf16[536,768]{1,0:T(8,128)(2,1)S(1)} %collective-permute-done.refs_1_), channel_id=1, source_target_pairs={{0,1},{1,0},{2,3},{3,2},{4,5},{5,4},{6,7},{7,6},{8,9},{9,8},{10,11... | collective-permute-start | bytes 2469896 | tf_op jit(solution)/shard_map/ppermute | solution.py:127
  34.5 19.0 %collective-permute-start.8 = (bf16[536,768]{1,0:T(8,128)(2,1)S(1)}, bf16[536,768]{1,0:T(8,128)(2,1)S(1)}, u32[]{:S(2)}, u32[]{:S(2)}) collective-permute-start(bf16[536,768]{1,0:T(8,128)(2,1)S(1)} %collective-permute-done.refs_1_), channel_id=1, source_target_pairs={{0,16},{16,0},{1,17},{17,1},{2,18},{18,2},{3,19},{19,3},{4,20},{20... | collective-permute-start | bytes 2469896 | tf_op jit(solution)/shard_map/ppermute | solution.py:127
  36.1 18.8 %collective-permute-start.3 = (bf16[536,768]{1,0:T(8,128)(2,1)S(1)}, bf16[536,768]{1,0:T(8,128)(2,1)}, u32[]{:S(2)}, u32[]{:S(2)}) collective-permute-start(bf16[536,768]{1,0:T(8,128)(2,1)S(1)} %collective-permute-done.refs_1_), channel_id=1, source_target_pairs={{0,2},{2,0},{1,3},{3,1},{4,6},{6,4},{5,7},{7,5},{8,10},{10,8},{9,1... | collective-permute-start | bytes 2469896 | tf_op jit(solution)/shard_map/ppermute | solution.py:127
  53.5 2.5 %collective-permute-start.9 = (bf16[536,768]{1,0:T(8,128)(2,1)S(1)}, bf16[536,768]{1,0:T(8,128)(2,1)}, u32[]{:S(2)}, u32[]{:S(2)}) collective-permute-start(bf16[536,768]{1,0:T(8,128)(2,1)S(1)} %collective-permute-done.8.refs_9_), channel_id=1, source_target_pairs={{0,1},{1,0},{2,3},{3,2},{4,5},{5,4},{6,7},{7,6},{8,9},{9,8},{10,11... | collective-permute-start | bytes 2469896 | tf_op jit(solution)/shard_map/ppermute | solution.py:127
  56.0 22.2 %collective-permute-start.10 = (bf16[536,768]{1,0:T(8,128)(2,1)S(1)}, bf16[536,768]{1,0:T(8,128)(2,1)}, u32[]{:S(2)}, u32[]{:S(2)}) collective-permute-start(bf16[536,768]{1,0:T(8,128)(2,1)S(1)} %collective-permute-done.8.refs_9_), channel_id=1, source_target_pairs={{0,2},{2,0},{1,3},{3,1},{4,6},{6,4},{5,7},{7,5},{8,10},{10,8},{9,1... | collective-permute-start | bytes 2469896 | tf_op jit(solution)/shard_map/ppermute | solution.py:127
  58.7 19.5 %collective-permute-start.5 = (bf16[512,768]{1,0:T(8,128)(2,1)S(1)}, bf16[512,768]{1,0:T(8,128)(2,1)}, u32[]{:S(2)}, u32[]{:S(2)}) collective-permute-start(bf16[512,768]{1,0:T(8,128)(2,1)S(1)} %constant_dynamic-slice_fusion.5), channel_id=1, source_target_pairs={{0,16},{16,0},{1,17},{17,1},{2,18},{18,2},{3,19},{19,3},{4,20},{20... | collective-permute-start | bytes 2359304 | tf_op jit(solution)/shard_map/ppermute | solution.py:127
  60.3 23.6 %collective-permute-start.6 = (bf16[536,768]{1,0:T(8,128)(2,1)S(1)}, bf16[536,768]{1,0:T(8,128)(2,1)}, u32[]{:S(2)}, u32[]{:S(2)}) collective-permute-start(bf16[536,768]{1,0:T(8,128)(2,1)S(1)} %collective-permute-done.2.refs_5_), channel_id=1, source_target_pairs={{0,1},{1,0},{2,3},{3,2},{4,5},{5,4},{6,7},{7,6},{8,9},{9,8},{10,11... | collective-permute-start | bytes 2469896 | tf_op jit(solution)/shard_map/ppermute | solution.py:127
  60.3 26.7 %collective-permute-start.4 = (bf16[536,768]{1,0:T(8,128)(2,1)}, bf16[536,768]{1,0:T(8,128)(2,1)}, u32[]{:S(2)}, u32[]{:S(2)}) collective-permute-start(bf16[536,768]{1,0:T(8,128)(2,1)} %collective-permute-done.3.refs_2_), channel_id=1, source_target_pairs={{0,1},{1,0},{2,3},{3,2},{4,5},{5,4},{6,7},{7,6},{8,9},{9,8},{10,11... | collective-permute-start | bytes 2469896 | tf_op jit(solution)/shard_map/ppermute | solution.py:127
  78.2 8.8 %collective-permute-start.11 = (bf16[536,768]{1,0:T(8,128)(2,1)}, bf16[536,768]{1,0:T(8,128)(2,1)}, u32[]{:S(2)}, u32[]{:S(2)}) collective-permute-start(bf16[536,768]{1,0:T(8,128)(2,1)} %collective-permute-done.10.refs_10_), channel_id=1, source_target_pairs={{0,1},{1,0},{2,3},{3,2},{4,5},{5,4},{6,7},{7,6},{8,9},{9,8},{10,11... | collective-permute-start | bytes 2469896 | tf_op jit(solution)/shard_map/ppermute | solution.py:127
  78.2 8.1 %collective-permute-start.7 = (bf16[512,768]{1,0:T(8,128)(2,1)}, bf16[512,768]{1,0:T(8,128)(2,1)}, u32[]{:S(2)}, u32[]{:S(2)}) collective-permute-start(bf16[512,768]{1,0:T(8,128)(2,1)} %collective-permute-done.5.refs_6_), channel_id=1, source_target_pairs={{0,1},{1,0},{2,3},{3,2},{4,5},{5,4},{6,7},{7,6},{8,9},{9,8},{10,11... | collective-permute-start | bytes 2359304 | tf_op jit(solution)/shard_map/ppermute | solution.py:127
  82.5 16.9 %collective-permute-start.12 = (bf16[768,256]{1,0:T(8,128)(2,1)}, bf16[768,256]{1,0:T(8,128)(2,1)}, u32[]{:S(2)}, u32[]{:S(2)}) collective-permute-start(bf16[768,256]{1,0:T(8,128)(2,1)} %constant_dynamic-slice_fusion.3), channel_id=1, source_target_pairs={{0,4},{4,0},{8,12},{12,8},{1,5},{5,1},{9,13},{13,9},{2,6},{6,2},{1... | collective-permute-start | bytes 1179656 | tf_op jit(solution)/shard_map/ppermute | solution.py:127
  83.9 29.6 %collective-permute-start.13 = (bf16[768,128]{1,0:T(8,128)(2,1)}, bf16[768,128]{1,0:T(8,128)(2,1)}, u32[]{:S(2)}, u32[]{:S(2)}) collective-permute-start(bf16[768,128]{1,0:T(8,128)(2,1)} %get-tuple-element.41.refs_13_), channel_id=1, source_target_pairs={{0,8},{4,12},{8,0},{12,4},{1,9},{5,13},{9,1},{13,5},{2,10},{6,14},... | collective-permute-start | bytes 589832 | tf_op jit(solution)/shard_map/ppermute | solution.py:127
  86.2 29.1 %collective-permute-start.14 = (bf16[768,128]{1,0:T(8,128)(2,1)}, bf16[768,128]{1,0:T(8,128)(2,1)}, u32[]{:S(2)}, u32[]{:S(2)}) collective-permute-start(bf16[768,128]{1,0:T(8,128)(2,1)} %get-tuple-element.42), channel_id=1, source_target_pairs={{0,12},{4,8},{8,4},{12,0},{1,13},{5,9},{9,5},{13,1},{2,14},{6,10},... | collective-permute-start | bytes 589832 | tf_op jit(solution)/shard_map/ppermute | solution.py:127
  86.9 13.1 %copy-start.4 = (bf16[768,128]{1,0:T(8,128)(2,1)S(1)}, bf16[768,128]{1,0:T(8,128)(2,1)}, u32[]{:S(2)}) copy-start(bf16[768,128]{1,0:T(8,128)(2,1)} %get-tuple-element.52) | copy-start | bytes 589828
  96.1 19.2 %collective-permute-start.15 = (bf16[1,2,128,128]{3,2,1,0:T(8,128)(2,1)S(1)}, bf16[1,2,128,128]{3,2,1,0:T(8,128)(2,1)S(1)}, u32[]{:S(2)}, u32[]{:S(2)}) collective-permute-start(bf16[1,2,128,128]{3,2,1,0:T(8,128)(2,1)S(1)} %get-tuple-element.49), channel_id=1, source_target_pairs={{0,8},{4,12},{1,9},{5,13},{2,10},{6,14},{3,11},{7,15},{16,24},{20,... | collective-permute-start | bytes 196616 | tf_op jit(solution)/shard_map/ppermute | solution.py:497
  99.5 28.5 %collective-permute-start.16 = (bf16[768,128]{1,0:T(8,128)(2,1)S(1)}, bf16[768,128]{1,0:T(8,128)(2,1)S(1)}, u32[]{:S(2)}, u32[]{:S(2)}) collective-permute-start(bf16[768,128]{1,0:T(8,128)(2,1)S(1)} %get-tuple-element.61.refs_13_), channel_id=1, source_target_pairs={{0,8},{4,12},{8,0},{12,4},{1,9},{5,13},{9,1},{13,5},{2,10},{6,14},... | collective-permute-start | bytes 589832 | tf_op jit(solution)/shard_map/ppermute | solution.py:127
  100.0 27.9 %collective-permute-start.17 = (bf16[768,128]{1,0:T(8,128)(2,1)S(1)}, bf16[768,128]{1,0:T(8,128)(2,1)S(1)}, u32[]{:S(2)}, u32[]{:S(2)}) collective-permute-start(bf16[768,128]{1,0:T(8,128)(2,1)S(1)} %copy-done.4), channel_id=1, source_target_pairs={{0,12},{4,8},{8,4},{12,0},{1,13},{5,9},{9,5},{13,1},{2,14},{6,10},... | collective-permute-start | bytes 589832 | tf_op jit(solution)/shard_map/ppermute | solution.py:127
  104.2 11.2 %copy-start = (bf16[512,3072]{1,0:T(8,128)(2,1)S(1)}, bf16[512,3072]{1,0:T(8,128)(2,1)}, u32[]{:S(2)}) copy-start(bf16[512,3072]{1,0:T(8,128)(2,1)} %refs_0_.11) | copy-start | bytes 9437188
  113.5 14.2 %collective-permute-start.18 = (bf16[1,2,128,128]{3,2,1,0:T(8,128)(2,1)S(1)}, bf16[1,2,128,128]{3,2,1,0:T(8,128)(2,1)S(1)}, u32[]{:S(2)}, u32[]{:S(2)}) collective-permute-start(bf16[1,2,128,128]{3,2,1,0:T(8,128)(2,1)S(1)} %get-tuple-element.59), channel_id=1, source_target_pairs={{0,8},{4,12},{1,9},{5,13},{2,10},{6,14},{3,11},{7,15},{16,24},{20,... | collective-permute-start | bytes 196616 | tf_op jit(solution)/shard_map/ppermute | solution.py:497
  124.4 14.4 %collective-permute-start.19 = (bf16[512,128]{1,0:T(8,128)(2,1)S(1)}, bf16[512,128]{1,0:T(8,128)(2,1)S(1)}, u32[]{:S(2)}, u32[]{:S(2)}) collective-permute-start(bf16[512,128]{1,0:T(8,128)(2,1)S(1)} %get-tuple-element.62), channel_id=1, source_target_pairs={{0,4},{4,0},{8,12},{12,8},{1,5},{5,1},{9,13},{13,9},{2,6},{6,2},{1... | collective-permute-start | bytes 393224 | tf_op jit(solution)/shard_map/ppermute | solution.py:127
  126.1 16.7 %collective-permute-start.21 = (bf16[512,128]{1,0:T(8,128)(2,1)S(1)}, bf16[512,128]{1,0:T(8,128)(2,1)S(1)}, u32[]{:S(2)}, u32[]{:S(2)}) collective-permute-start(bf16[512,128]{1,0:T(8,128)(2,1)S(1)} %get-tuple-element.63), channel_id=1, source_target_pairs={{0,16},{16,0},{1,17},{17,1},{2,18},{18,2},{3,19},{19,3},{4,20},{20... | collective-permute-start | bytes 393224 | tf_op jit(solution)/shard_map/ppermute | solution.py:127
  127.6 15.1 %collective-permute-start.23 = (bf16[512,128]{1,0:T(8,128)(2,1)S(1)}, bf16[512,128]{1,0:T(8,128)(2,1)S(1)}, u32[]{:S(2)}, u32[]{:S(2)}) collective-permute-start(bf16[512,128]{1,0:T(8,128)(2,1)S(1)} %get-tuple-element.65), channel_id=1, source_target_pairs={{0,20},{4,16},{8,28},{12,24},{16,4},{20,0},{24,12},{28,8},{1,21},{... | collective-permute-start | bytes 393224 | tf_op jit(solution)/shard_map/ppermute | solution.py:536
  135.6 7.1 %collective-permute-start.20 = (bf16[512,128]{1,0:T(8,128)(2,1)S(1)}, bf16[512,128]{1,0:T(8,128)(2,1)S(1)}, u32[]{:S(2)}, u32[]{:S(2)}) collective-permute-start(bf16[512,128]{1,0:T(8,128)(2,1)S(1)} %get-tuple-element.60), channel_id=1, source_target_pairs={{0,4},{4,0},{8,12},{12,8},{1,5},{5,1},{9,13},{13,9},{2,6},{6,2},{1... | collective-permute-start | bytes 393224 | tf_op jit(solution)/shard_map/ppermute | solution.py:127
  137.3 5.5 %collective-permute-start.22 = (bf16[512,128]{1,0:T(8,128)(2,1)S(1)}, bf16[512,128]{1,0:T(8,128)(2,1)S(1)}, u32[]{:S(2)}, u32[]{:S(2)}) collective-permute-start(bf16[512,128]{1,0:T(8,128)(2,1)S(1)} %get-tuple-element.64), channel_id=1, source_target_pairs={{0,16},{16,0},{1,17},{17,1},{2,18},{18,2},{3,19},{19,3},{4,20},{20... | collective-permute-start | bytes 393224 | tf_op jit(solution)/shard_map/ppermute | solution.py:127
  138.8 5.9 %collective-permute-start.24 = (bf16[512,128]{1,0:T(8,128)(2,1)S(1)}, bf16[512,128]{1,0:T(8,128)(2,1)S(1)}, u32[]{:S(2)}, u32[]{:S(2)}) collective-permute-start(bf16[512,128]{1,0:T(8,128)(2,1)S(1)} %get-tuple-element.66), channel_id=1, source_target_pairs={{0,20},{4,16},{8,28},{12,24},{16,4},{20,0},{24,12},{28,8},{1,21},{... | collective-permute-start | bytes 393224 | tf_op jit(solution)/shard_map/ppermute | solution.py:536

commit v7 on v6

--- a/solution.py
+++ b/solution.py
@@ -416,7 +416,6 @@
         ),
         out_shape=jax.ShapeDtypeStruct(packed_shape, jnp.bfloat16),
         cost_estimate=pl.CostEstimate(flops=0, bytes_accessed=32 * depth * heads * size, transcendentals=0),
-        compiler_params=pltpu.CompilerParams(vmem_limit_bytes=16 << 20),
         name="pack",
     )(places, key_weight, value_weight, key_weight, value_weight)
 

time: 147 us -> 147 us (level)
  local copies, waits for them, and re-layouts: 9.46 us -> 6.23 us
  Pallas kernels: 42.1 us -> 44.3 us
    unnamed x10 -> x6, local copies, waits for them, and re-layouts: 3.11 us -> 0.01 us
    pallas_call x1, Pallas kernels: 1.64 us -> 3.84 us  [spread_body(): pl.pallas_call(functools.partial(pack_kernel, heads, size), grid_spec=plt...]
  transfers between devices with their start and end apart: 26 -> 26, of which waited for: 7 -> 7; matrix products, arithmetic and copies ran while one was open for 3% -> 4% of each run, Pallas kernels for 28% -> 29%
where the time goes in v7:
time: 147 us; the launch traced here: 146 us
  waiting for transfers between devices  56 us (38%)
  Pallas kernels  44.3 us (30%)
  starting transfers between devices  37.8 us (26%)
  local copies, waits for them, and re-layouts  6.23 us (4%)
    ppermute x21, waiting for transfers between devices, xor_permute(): lax.ppermute(array, axis, [(at, at ^ flip) for at in range(mesh.shape[axi...  54.1 us
    ppermute x21, starting transfers between devices, xor_permute(): lax.ppermute(array, axis, [(at, at ^ flip) for at in range(mesh.shape[axi...  27.2 us
    pallas_call x3, Pallas kernels, query(): pl.pallas_call(functools.partial(query_kernel, chosen, 0, slice(head * si...  20.2 us
    pallas_call x2, Pallas kernels, spread_body(): pl.pallas_call(functools.partial(key_value_kernel, head, heads, size, fli...  18.4 us
    ppermute x2, starting transfers between devices, spread_body(): lax.ppermute(pair_state, 'ctx', [(at, at + 2) for at in range(flips - 2)])  5.2 us
    all_to_all x1, starting transfers between devices, spread_body(): key_value = lax.all_to_all(packed, 'ctx', 0, 0)  4.65 us
    dynamic_slice x2, local copies, waits for them, and re-layouts, query_block(): lax.dynamic_slice(query_weight, (0, (owner * heads + head) * size), (dept...  3.85 us
    pallas_call x1, Pallas kernels, spread_body(): pl.pallas_call(functools.partial(pack_kernel, heads, size), grid_spec=plt...  3.84 us
  transfers between devices with their start and end apart: 26, of which 7 were waited for; matrix products, arithmetic and copies ran while one was open for 4% of the time, Pallas kernels for 29%

profile of v7, /device:TPU:0, one launch (start us, length us, event | category | flops | bytes accessed | tf_op | source)
XLA Modules:
  0.0 146.0 jit_solution(5861792391099423811)
XLA Ops:
  0.0 0.7 reduce-precision_convert_fusion.1
  0.7 1.2 constant_dynamic-slice_fusion.6
  1.9 0.1 pad_maximum_fusion
  2.0 3.1 %collective-permute-start = (bf16[536,768]{1,0:T(8,128)(2,1)S(1)}, bf16[536,768]{1,0:T(8,128)(2,1)S(1)}, u32[]{:S(2)}, u32[]{:S(2)}) collective-permute-start(bf16[536,768]{1,0:T(8,128)(2,1)S(1)} %pad_maximum_fusion), channel_id=1, source_target_pairs={{0,4},{4,0},{8,12},{12,8},{1,5},{5,1},{9,13},{13,9},{2,6},{6,2},{1... | collective-permute-start | bytes 2469896 | tf_op jit(solution)/shard_map/ppermute | solution.py:127
  5.1 0.7 pad_add_fusion.places
  5.7 3.8 %pack.1 = bf16[4,768,512]{2,1,0:T(8,128)(2,1)} custom-call(s32[4]{0:T(128)} %pad_add_fusion.places, bf16[768,1024]{1,0:T(8,128)(2,1)} %refs_2_.1, bf16[768,1024]{1,0:T(8,128)(2,1)} %refs_3_.1, bf16[768,1024]{1,0:T(8,128)(2,1)} %refs_2_.1, bf16[768,1024]{1,0:T(8,128)(2,1)} %refs_3_.1), custom_call_target="tpu_custom_call" | custom-call | bytes 6291456 | tf_op jit(solution)/shard_map/pack/pallas_call | solution.py:409
  9.6 4.7 %all-to-all-start = ((bf16[4,768,512]{2,1,0:T(8,128)(2,1)}), bf16[4,768,512]{2,1,0:T(8,128)(2,1)}, u32[]{:S(2)}, u32[]{:S(2)}) async-start(bf16[4,768,512]{2,1,0:T(8,128)(2,1)} %pack.1), calls=%async_computation | async-start | bytes 6291456 | tf_op jit(solution)/shard_map/all_to_all | solution.py:422
  14.2 1.6 %collective-permute-start.2 = (bf16[536,768]{1,0:T(8,128)(2,1)S(1)}, bf16[536,768]{1,0:T(8,128)(2,1)S(1)}, u32[]{:S(2)}, u32[]{:S(2)}) collective-permute-start(bf16[536,768]{1,0:T(8,128)(2,1)S(1)} %pad_maximum_fusion), channel_id=1, source_target_pairs={{0,16},{16,0},{1,17},{17,1},{2,18},{18,2},{3,19},{19,3},{4,20},{20... | collective-permute-start | bytes 2469896 | tf_op jit(solution)/shard_map/ppermute | solution.py:127
  15.8 8.4 %collective-permute-done.refs_1_ = bf16[536,768]{1,0:T(8,128)(2,1)S(1)} collective-permute-done((bf16[536,768]{1,0:T(8,128)(2,1)S(1)}, bf16[536,768]{1,0:T(8,128)(2,1)S(1)}, u32[]{:S(2)}, u32[]{:S(2)}) %collective-permute-start) | collective-permute-done | bytes 823328 | tf_op jit(solution)/shard_map/ppermute | solution.py:127
  24.2 0.0 collective-permute-start.1
  24.2 9.9 %collective-permute-done.2.refs_5_ = bf16[536,768]{1,0:T(8,128)(2,1)S(1)} collective-permute-done((bf16[536,768]{1,0:T(8,128)(2,1)S(1)}, bf16[536,768]{1,0:T(8,128)(2,1)S(1)}, u32[]{:S(2)}, u32[]{:S(2)}) %collective-permute-start.2) | collective-permute-done | bytes 823328 | tf_op jit(solution)/shard_map/ppermute | solution.py:127
  34.1 0.0 collective-permute-done.1.refs_3_
  34.1 1.5 %collective-permute-start.8 = (bf16[536,768]{1,0:T(8,128)(2,1)S(1)}, bf16[536,768]{1,0:T(8,128)(2,1)S(1)}, u32[]{:S(2)}, u32[]{:S(2)}) collective-permute-start(bf16[536,768]{1,0:T(8,128)(2,1)S(1)} %collective-permute-done.refs_1_), channel_id=1, source_target_pairs={{0,16},{16,0},{1,17},{17,1},{2,18},{18,2},{3,19},{19,3},{4,20},{20... | collective-permute-start | bytes 2469896 | tf_op jit(solution)/shard_map/ppermute | solution.py:127
  35.6 1.5 %collective-permute-start.3 = (bf16[536,768]{1,0:T(8,128)(2,1)S(1)}, bf16[536,768]{1,0:T(8,128)(2,1)}, u32[]{:S(2)}, u32[]{:S(2)}) collective-permute-start(bf16[536,768]{1,0:T(8,128)(2,1)S(1)} %collective-permute-done.refs_1_), channel_id=1, source_target_pairs={{0,2},{2,0},{1,3},{3,1},{4,6},{6,4},{5,7},{7,5},{8,10},{10,8},{9,1... | collective-permute-start | bytes 2469896 | tf_op jit(solution)/shard_map/ppermute | solution.py:127
  37.1 16.0 %collective-permute-done.8.refs_9_ = bf16[536,768]{1,0:T(8,128)(2,1)S(1)} collective-permute-done((bf16[536,768]{1,0:T(8,128)(2,1)S(1)}, bf16[536,768]{1,0:T(8,128)(2,1)S(1)}, u32[]{:S(2)}, u32[]{:S(2)}) %collective-permute-start.8) | collective-permute-done | bytes 823328 | tf_op jit(solution)/shard_map/ppermute | solution.py:127
  53.1 0.0 collective-permute-start.9
  53.1 1.3 collective-permute-done.3.refs_2_
  54.4 1.1 collective-permute-done.9.refs_11_
  55.6 1.5 %collective-permute-start.10 = (bf16[536,768]{1,0:T(8,128)(2,1)S(1)}, bf16[536,768]{1,0:T(8,128)(2,1)}, u32[]{:S(2)}, u32[]{:S(2)}) collective-permute-start(bf16[536,768]{1,0:T(8,128)(2,1)S(1)} %collective-permute-done.8.refs_9_), channel_id=1, source_target_pairs={{0,2},{2,0},{1,3},{3,1},{4,6},{6,4},{5,7},{7,5},{8,10},{10,8},{9,1... | collective-permute-start | bytes 2469896 | tf_op jit(solution)/shard_map/ppermute | solution.py:127
  57.1 1.2 constant_dynamic-slice_fusion.5
  58.2 1.6 %collective-permute-start.5 = (bf16[512,768]{1,0:T(8,128)(2,1)S(1)}, bf16[512,768]{1,0:T(8,128)(2,1)}, u32[]{:S(2)}, u32[]{:S(2)}) collective-permute-start(bf16[512,768]{1,0:T(8,128)(2,1)S(1)} %constant_dynamic-slice_fusion.5), channel_id=1, source_target_pairs={{0,16},{16,0},{1,17},{17,1},{2,18},{18,2},{3,19},{19,3},{4,20},{20... | collective-permute-start | bytes 2359304 | tf_op jit(solution)/shard_map/ppermute | solution.py:127
  59.8 0.0 collective-permute-start.6
  59.8 0.5 collective-permute-start.4
  60.3 17.4 %collective-permute-done.5.refs_6_ = bf16[512,768]{1,0:T(8,128)(2,1)} collective-permute-done((bf16[512,768]{1,0:T(8,128)(2,1)S(1)}, bf16[512,768]{1,0:T(8,128)(2,1)}, u32[]{:S(2)}, u32[]{:S(2)}) %collective-permute-start.5) | collective-permute-done | bytes 786464 | tf_op jit(solution)/shard_map/ppermute | solution.py:127
  77.7 0.0 collective-permute-done.10.refs_10_
  77.7 0.0 collective-permute-start.11
  77.7 0.5 collective-permute-start.7
  78.2 1.8 %constant_dynamic-slice_fusion.3 = bf16[768,256]{1,0:T(8,128)(2,1)} fusion(bf16[768,1024]{1,0:T(8,128)(2,1)} %param.6, s32[]{:T(128)S(6)} %select_n.30), kind=kLoop, calls=%fused_computation.16 | loop fusion | bytes 786436 | tf_op jit(solution)/shard_map/dynamic_slice | solution.py:444
  80.0 2.1 %constant_dynamic-slice_fusion = (bf16[768,128]{1,0:T(8,128)(2,1)}, bf16[768,128]{1,0:T(8,128)(2,1)}, bf16[768,128]{1,0:T(8,128)(2,1)}, bf16[768,128]{1,0:T(8,128)(2,1)S(1)}) fusion(bf16[768,1024]{1,0:T(8,128)(2,1)} %param.6, s32[]{:T(128)S(6)} %select_n.32, s32[]{:T(128)S(6)} %select_n.30, s32[]{:T(128)S(6)} %select_n.29, s32[]{:T(128)S(6)} %select_n.31), kind=kLoop, calls=%fused_computation.13 | loop fusion | bytes 1572880 | tf_op jit(solution)/shard_map/dynamic_slice | solution.py:444
  82.1 1.3 collective-permute-start.12
  83.4 0.0 collective-permute-done.6.refs_7_
  83.4 2.4 %collective-permute-start.13 = (bf16[768,128]{1,0:T(8,128)(2,1)}, bf16[768,128]{1,0:T(8,128)(2,1)}, u32[]{:S(2)}, u32[]{:S(2)}) collective-permute-start(bf16[768,128]{1,0:T(8,128)(2,1)} %get-tuple-element.41.refs_13_), channel_id=1, source_target_pairs={{0,8},{4,12},{8,0},{12,4},{1,9},{5,13},{9,1},{13,5},{2,10},{6,14},... | collective-permute-start | bytes 589832 | tf_op jit(solution)/shard_map/ppermute | solution.py:127
  85.8 0.0 collective-permute-done.7.refs_8_
  85.8 0.7 collective-permute-start.14
  86.5 0.0 collective-permute-done.4.refs_4_
  86.5 0.0 all-to-all-done.refs_14_
  86.5 0.0 collective-permute-done.11.refs_12_
  86.5 9.2 %key_value.2 = (bf16[4,512,128]{2,1,0:T(8,128)(2,1)S(1)}, bf16[4,512,128]{2,1,0:T(8,128)(2,1)S(1)}, f32[1,4,4,128,128]{4,3,2,1,0:T(8,128)S(1)}, f32[4,1,512]{2,1...) custom-call(s32[4]{0:T(128)S(1)} %copy-done.1, ...), custom_call_target="tpu_custom_call" | custom-call | flops 3221225472 | bytes 14155776 | tf_op jit(solution)/shard_map/key_value/pallas_call | solution.py:471
  95.7 3.4 %collective-permute-start.15 = (bf16[1,2,128,128]{3,2,1,0:T(8,128)(2,1)S(1)}, bf16[1,2,128,128]{3,2,1,0:T(8,128)(2,1)S(1)}, u32[]{:S(2)}, u32[]{:S(2)}) collective-permute-start(bf16[1,2,128,128]{3,2,1,0:T(8,128)(2,1)S(1)} %get-tuple-element.49), channel_id=1, source_target_pairs={{0,8},{4,12},{1,9},{5,13},{2,10},{6,14},{3,11},{7,15},{16,24},{20,... | collective-permute-start | bytes 196616 | tf_op jit(solution)/shard_map/ppermute | solution.py:496
  99.0 0.0 collective-permute-done.12.refs_14_
  99.0 0.5 collective-permute-start.16
  99.6 4.2 %collective-permute-start.17 = (bf16[768,128]{1,0:T(8,128)(2,1)S(1)}, bf16[768,128]{1,0:T(8,128)(2,1)S(1)}, u32[]{:S(2)}, u32[]{:S(2)}) collective-permute-start(bf16[768,128]{1,0:T(8,128)(2,1)S(1)} %copy-done.2), channel_id=1, source_target_pairs={{0,12},{4,8},{8,4},{12,0},{1,13},{5,9},{9,5},{13,1},{2,14},{6,10},... | collective-permute-start | bytes 589832 | tf_op jit(solution)/shard_map/ppermute | solution.py:127
  103.7 9.3 %key_value.3 = (bf16[4,512,128]{2,1,0:T(8,128)(2,1)S(1)}, bf16[4,512,128]{2,1,0:T(8,128)(2,1)S(1)}, f32[1,4,4,128,128]{4,3,2,1,0:T(8,128)S(1)}, f32[4,1,512]{2,1...) custom-call(s32[4]{0:T(128)S(1)} %copy-done.1, ...), custom_call_target="tpu_custom_call" | custom-call | flops 3221225472 | bytes 14155776 | tf_op jit(solution)/shard_map/key_value/pallas_call | solution.py:471
  113.0 0.0 collective-permute-done.13.refs_15_
  113.0 1.8 %collective-permute-start.18 = (bf16[1,2,128,128]{3,2,1,0:T(8,128)(2,1)S(1)}, bf16[1,2,128,128]{3,2,1,0:T(8,128)(2,1)S(1)}, u32[]{:S(2)}, u32[]{:S(2)}) collective-permute-start(bf16[1,2,128,128]{3,2,1,0:T(8,128)(2,1)S(1)} %get-tuple-element.59), channel_id=1, source_target_pairs={{0,8},{4,12},{1,9},{5,13},{2,10},{6,14},{3,11},{7,15},{16,24},{20,... | collective-permute-start | bytes 196616 | tf_op jit(solution)/shard_map/ppermute | solution.py:496
  114.9 0.0 collective-permute-done.14.refs_16_
  114.9 0.0 collective-permute-done.15.refs_23_
  114.9 9.0 %query.3 = (bf16[512,128]{1,0:T(8,128)(2,1)S(1)}, bf16[512,128]{1,0:T(8,128)(2,1)S(1)}, bf16[512,128]{1,0:T(8,128)(2,1)S(1)}, bf16[512,128]{1,0:T(8,128)(2,1)S(1)}) custom-call(s32[4]{0:T(128)S(1)} %copy-done.1, bf16[512,3072]{1,0:T(8,128)(2,1)S(1)} %copy-done, bf16[536,768]{1,0:T(8,128)(2,1)S(1)} %collective-permute-done.refs_1_, ...), custom_call_target="tpu_custom_call" | custom-call | flops 1879048192 | bytes 13369344 | tf_op jit(solution)/shard_map/query/pallas_call | solution.py:506
  124.0 1.7 %collective-permute-start.19 = (bf16[512,128]{1,0:T(8,128)(2,1)S(1)}, bf16[512,128]{1,0:T(8,128)(2,1)S(1)}, u32[]{:S(2)}, u32[]{:S(2)}) collective-permute-start(bf16[512,128]{1,0:T(8,128)(2,1)S(1)} %get-tuple-element.62), channel_id=1, source_target_pairs={{0,4},{4,0},{8,12},{12,8},{1,5},{5,1},{9,13},{13,9},{2,6},{6,2},{1... | collective-permute-start | bytes 393224 | tf_op jit(solution)/shard_map/ppermute | solution.py:127
  125.7 1.5 %collective-permute-start.21 = (bf16[512,128]{1,0:T(8,128)(2,1)S(1)}, bf16[512,128]{1,0:T(8,128)(2,1)S(1)}, u32[]{:S(2)}, u32[]{:S(2)}) collective-permute-start(bf16[512,128]{1,0:T(8,128)(2,1)S(1)} %get-tuple-element.63), channel_id=1, source_target_pairs={{0,16},{16,0},{1,17},{17,1},{2,18},{18,2},{3,19},{19,3},{4,20},{20... | collective-permute-start | bytes 393224 | tf_op jit(solution)/shard_map/ppermute | solution.py:127
  127.2 0.0 collective-permute-done.18.refs_23_
  127.2 0.3 collective-permute-start.23
  127.5 0.0 collective-permute-done.16.refs_15_
  127.5 0.0 collective-permute-done.17.refs_16_
  127.5 7.7 %query.4 = (bf16[512,128]{1,0:T(8,128)(2,1)S(1)}, bf16[512,128]{1,0:T(8,128)(2,1)S(1)}, bf16[512,128]{1,0:T(8,128)(2,1)S(1)}) custom-call(s32[4]{0:T(128)S(1)} %copy-done.1, bf16[512,3072]{1,0:T(8,128)(2,1)S(1)} %copy-done, bf16[536,768]{1,0:T(8,128)(2,1)S(1)} %collective-permute-done.refs_1_, bf16[536,768]{1,0:T(8,128)(2,1)} %collective-permute-done.3.refs_2_, ...), custom_call_target="tpu_custom_call" | custom-call | flops 1409286144 | bytes 10223616 | tf_op jit(solution)/shard_map/query/pallas_call | solution.py:506
  135.2 1.6 %collective-permute-start.20 = (bf16[512,128]{1,0:T(8,128)(2,1)S(1)}, bf16[512,128]{1,0:T(8,128)(2,1)S(1)}, u32[]{:S(2)}, u32[]{:S(2)}) collective-permute-start(bf16[512,128]{1,0:T(8,128)(2,1)S(1)} %get-tuple-element.60), channel_id=1, source_target_pairs={{0,4},{4,0},{8,12},{12,8},{1,5},{5,1},{9,13},{13,9},{2,6},{6,2},{1... | collective-permute-start | bytes 393224 | tf_op jit(solution)/shard_map/ppermute | solution.py:127
  136.8 1.5 %collective-permute-start.22 = (bf16[512,128]{1,0:T(8,128)(2,1)S(1)}, bf16[512,128]{1,0:T(8,128)(2,1)S(1)}, u32[]{:S(2)}, u32[]{:S(2)}) collective-permute-start(bf16[512,128]{1,0:T(8,128)(2,1)S(1)} %get-tuple-element.64), channel_id=1, source_target_pairs={{0,16},{16,0},{1,17},{17,1},{2,18},{18,2},{3,19},{19,3},{4,20},{20... | collective-permute-start | bytes 393224 | tf_op jit(solution)/shard_map/ppermute | solution.py:127
  138.3 0.0 collective-permute-done.19.refs_2_
  138.4 0.4 collective-permute-start.24
  138.7 3.5 %query.5.refs_1_ = bf16[512,128]{1,0:T(8,128)(2,1)S(1)} custom-call(s32[4]{0:T(128)S(1)} %copy-done.1, bf16[512,3072]{1,0:T(8,128)(2,1)S(1)} %copy-done, bf16[536,768]{1,0:T(8,128)(2,1)S(1)} %collective-permute-done.refs_1_, bf16[536,768]{1,0:T(8,128)(2,1)} %collective-permute-done.3.refs_2_, bf16[536,768]{1,0:T(8,128)(2,1)S(1)} %collective-permute-done.1.refs_3_, ...), custom_call_target="tpu_custom_call" | custom-call | flops 469762048 | bytes 3932160 | tf_op jit(solution)/shard_map/query/pallas_call | solution.py:506
  142.3 0.0 collective-permute-done.23.refs_6_
  142.3 0.0 collective-permute-done.20.refs_3_
  142.3 1.9 %collective-permute-done.24.refs_7_ = bf16[512,128]{1,0:T(8,128)(2,1)S(1)} collective-permute-done((bf16[512,128]{1,0:T(8,128)(2,1)S(1)}, bf16[512,128]{1,0:T(8,128)(2,1)S(1)}, u32[]{:S(2)}, u32[]{:S(2)}) %collective-permute-start.24) | collective-permute-done | bytes 131104 | tf_op jit(solution)/shard_map/ppermute | solution.py:535
  144.2 1.8 %merge.1 = bf16[512,1024]{1,0:T(8,128)(2,1)} custom-call(s32[4]{0:T(128)S(1)} %copy-done.1, bf16[512,128]{1,0:T(8,128)(2,1)S(1)} %get-tuple-element.50.refs_0_, bf16[512,128]{1,0:T(8,128)(2,1)S(1)} %query.5.refs_1_, bf16[512,128]{1,0:T(8,128)(2,1)S(1)} %collective-permute-done.19.refs_2_, bf16[512,128]{1,0:T(8,128)(2,1)S(1)} %collective-permute-done.20.refs_3_, ...), custom_call_target="tpu_custom_call" | custom-call | tf_op jit(solution)/shard_map/merge/pallas_call | solution.py:538
  (9 shorter events, 0.0 us)
Async XLA Ops:
  2.0 22.2 %collective-permute-start = (bf16[536,768]{1,0:T(8,128)(2,1)S(1)}, bf16[536,768]{1,0:T(8,128)(2,1)S(1)}, u32[]{:S(2)}, u32[]{:S(2)}) collective-permute-start(bf16[536,768]{1,0:T(8,128)(2,1)S(1)} %pad_maximum_fusion), channel_id=1, source_target_pairs={{0,4},{4,0},{8,12},{12,8},{1,5},{5,1},{9,13},{13,9},{2,6},{6,2},{1... | collective-permute-start | bytes 2469896 | tf_op jit(solution)/shard_map/ppermute | solution.py:127
  9.6 76.9 %all-to-all-start = ((bf16[4,768,512]{2,1,0:T(8,128)(2,1)}), bf16[4,768,512]{2,1,0:T(8,128)(2,1)}, u32[]{:S(2)}, u32[]{:S(2)}) async-start(bf16[4,768,512]{2,1,0:T(8,128)(2,1)} %pack.1), calls=%async_computation | async-start | bytes 6291456 | tf_op jit(solution)/shard_map/all_to_all | solution.py:422
  14.2 19.9 %collective-permute-start.2 = (bf16[536,768]{1,0:T(8,128)(2,1)S(1)}, bf16[536,768]{1,0:T(8,128)(2,1)S(1)}, u32[]{:S(2)}, u32[]{:S(2)}) collective-permute-start(bf16[536,768]{1,0:T(8,128)(2,1)S(1)} %pad_maximum_fusion), channel_id=1, source_target_pairs={{0,16},{16,0},{1,17},{17,1},{2,18},{18,2},{3,19},{19,3},{4,20},{20... | collective-permute-start | bytes 2469896 | tf_op jit(solution)/shard_map/ppermute | solution.py:127
  24.2 9.9 %collective-permute-start.1 = (bf16[536,768]{1,0:T(8,128)(2,1)S(1)}, bf16[536,768]{1,0:T(8,128)(2,1)S(1)}, u32[]{:S(2)}, u32[]{:S(2)}) collective-permute-start(bf16[536,768]{1,0:T(8,128)(2,1)S(1)} %collective-permute-done.refs_1_), channel_id=1, source_target_pairs={{0,1},{1,0},{2,3},{3,2},{4,5},{5,4},{6,7},{7,6},{8,9},{9,8},{10,11... | collective-permute-start | bytes 2469896 | tf_op jit(solution)/shard_map/ppermute | solution.py:127
  34.1 19.0 %collective-permute-start.8 = (bf16[536,768]{1,0:T(8,128)(2,1)S(1)}, bf16[536,768]{1,0:T(8,128)(2,1)S(1)}, u32[]{:S(2)}, u32[]{:S(2)}) collective-permute-start(bf16[536,768]{1,0:T(8,128)(2,1)S(1)} %collective-permute-done.refs_1_), channel_id=1, source_target_pairs={{0,16},{16,0},{1,17},{17,1},{2,18},{18,2},{3,19},{19,3},{4,20},{20... | collective-permute-start | bytes 2469896 | tf_op jit(solution)/shard_map/ppermute | solution.py:127
  35.6 18.8 %collective-permute-start.3 = (bf16[536,768]{1,0:T(8,128)(2,1)S(1)}, bf16[536,768]{1,0:T(8,128)(2,1)}, u32[]{:S(2)}, u32[]{:S(2)}) collective-permute-start(bf16[536,768]{1,0:T(8,128)(2,1)S(1)} %collective-permute-done.refs_1_), channel_id=1, source_target_pairs={{0,2},{2,0},{1,3},{3,1},{4,6},{6,4},{5,7},{7,5},{8,10},{10,8},{9,1... | collective-permute-start | bytes 2469896 | tf_op jit(solution)/shard_map/ppermute | solution.py:127
  53.1 2.5 %collective-permute-start.9 = (bf16[536,768]{1,0:T(8,128)(2,1)S(1)}, bf16[536,768]{1,0:T(8,128)(2,1)}, u32[]{:S(2)}, u32[]{:S(2)}) collective-permute-start(bf16[536,768]{1,0:T(8,128)(2,1)S(1)} %collective-permute-done.8.refs_9_), channel_id=1, source_target_pairs={{0,1},{1,0},{2,3},{3,2},{4,5},{5,4},{6,7},{7,6},{8,9},{9,8},{10,11... | collective-permute-start | bytes 2469896 | tf_op jit(solution)/shard_map/ppermute | solution.py:127
  53.1 33.4 %copy-start.1 = (s32[4]{0:T(128)S(1)}, s32[4]{0:T(128)}, u32[]{:S(2)}) copy-start(s32[4]{0:T(128)} %pad_add_fusion.places) | copy-start | bytes 52
  55.6 22.2 %collective-permute-start.10 = (bf16[536,768]{1,0:T(8,128)(2,1)S(1)}, bf16[536,768]{1,0:T(8,128)(2,1)}, u32[]{:S(2)}, u32[]{:S(2)}) collective-permute-start(bf16[536,768]{1,0:T(8,128)(2,1)S(1)} %collective-permute-done.8.refs_9_), channel_id=1, source_target_pairs={{0,2},{2,0},{1,3},{3,1},{4,6},{6,4},{5,7},{7,5},{8,10},{10,8},{9,1... | collective-permute-start | bytes 2469896 | tf_op jit(solution)/shard_map/ppermute | solution.py:127
  58.2 19.5 %collective-permute-start.5 = (bf16[512,768]{1,0:T(8,128)(2,1)S(1)}, bf16[512,768]{1,0:T(8,128)(2,1)}, u32[]{:S(2)}, u32[]{:S(2)}) collective-permute-start(bf16[512,768]{1,0:T(8,128)(2,1)S(1)} %constant_dynamic-slice_fusion.5), channel_id=1, source_target_pairs={{0,16},{16,0},{1,17},{17,1},{2,18},{18,2},{3,19},{19,3},{4,20},{20... | collective-permute-start | bytes 2359304 | tf_op jit(solution)/shard_map/ppermute | solution.py:127
  59.8 23.6 %collective-permute-start.6 = (bf16[536,768]{1,0:T(8,128)(2,1)S(1)}, bf16[536,768]{1,0:T(8,128)(2,1)}, u32[]{:S(2)}, u32[]{:S(2)}) collective-permute-start(bf16[536,768]{1,0:T(8,128)(2,1)S(1)} %collective-permute-done.2.refs_5_), channel_id=1, source_target_pairs={{0,1},{1,0},{2,3},{3,2},{4,5},{5,4},{6,7},{7,6},{8,9},{9,8},{10,11... | collective-permute-start | bytes 2469896 | tf_op jit(solution)/shard_map/ppermute | solution.py:127
  59.8 26.7 %collective-permute-start.4 = (bf16[536,768]{1,0:T(8,128)(2,1)}, bf16[536,768]{1,0:T(8,128)(2,1)}, u32[]{:S(2)}, u32[]{:S(2)}) collective-permute-start(bf16[536,768]{1,0:T(8,128)(2,1)} %collective-permute-done.3.refs_2_), channel_id=1, source_target_pairs={{0,1},{1,0},{2,3},{3,2},{4,5},{5,4},{6,7},{7,6},{8,9},{9,8},{10,11... | collective-permute-start | bytes 2469896 | tf_op jit(solution)/shard_map/ppermute | solution.py:127
  77.7 8.8 %collective-permute-start.11 = (bf16[536,768]{1,0:T(8,128)(2,1)}, bf16[536,768]{1,0:T(8,128)(2,1)}, u32[]{:S(2)}, u32[]{:S(2)}) collective-permute-start(bf16[536,768]{1,0:T(8,128)(2,1)} %collective-permute-done.10.refs_10_), channel_id=1, source_target_pairs={{0,1},{1,0},{2,3},{3,2},{4,5},{5,4},{6,7},{7,6},{8,9},{9,8},{10,11... | collective-permute-start | bytes 2469896 | tf_op jit(solution)/shard_map/ppermute | solution.py:127
  77.7 8.1 %collective-permute-start.7 = (bf16[512,768]{1,0:T(8,128)(2,1)}, bf16[512,768]{1,0:T(8,128)(2,1)}, u32[]{:S(2)}, u32[]{:S(2)}) collective-permute-start(bf16[512,768]{1,0:T(8,128)(2,1)} %collective-permute-done.5.refs_6_), channel_id=1, source_target_pairs={{0,1},{1,0},{2,3},{3,2},{4,5},{5,4},{6,7},{7,6},{8,9},{9,8},{10,11... | collective-permute-start | bytes 2359304 | tf_op jit(solution)/shard_map/ppermute | solution.py:127
  82.1 16.9 %collective-permute-start.12 = (bf16[768,256]{1,0:T(8,128)(2,1)}, bf16[768,256]{1,0:T(8,128)(2,1)}, u32[]{:S(2)}, u32[]{:S(2)}) collective-permute-start(bf16[768,256]{1,0:T(8,128)(2,1)} %constant_dynamic-slice_fusion.3), channel_id=1, source_target_pairs={{0,4},{4,0},{8,12},{12,8},{1,5},{5,1},{9,13},{13,9},{2,6},{6,2},{1... | collective-permute-start | bytes 1179656 | tf_op jit(solution)/shard_map/ppermute | solution.py:127
  83.4 29.6 %collective-permute-start.13 = (bf16[768,128]{1,0:T(8,128)(2,1)}, bf16[768,128]{1,0:T(8,128)(2,1)}, u32[]{:S(2)}, u32[]{:S(2)}) collective-permute-start(bf16[768,128]{1,0:T(8,128)(2,1)} %get-tuple-element.41.refs_13_), channel_id=1, source_target_pairs={{0,8},{4,12},{8,0},{12,4},{1,9},{5,13},{9,1},{13,5},{2,10},{6,14},... | collective-permute-start | bytes 589832 | tf_op jit(solution)/shard_map/ppermute | solution.py:127
  85.8 29.1 %collective-permute-start.14 = (bf16[768,128]{1,0:T(8,128)(2,1)}, bf16[768,128]{1,0:T(8,128)(2,1)}, u32[]{:S(2)}, u32[]{:S(2)}) collective-permute-start(bf16[768,128]{1,0:T(8,128)(2,1)} %get-tuple-element.42), channel_id=1, source_target_pairs={{0,12},{4,8},{8,4},{12,0},{1,13},{5,9},{9,5},{13,1},{2,14},{6,10},... | collective-permute-start | bytes 589832 | tf_op jit(solution)/shard_map/ppermute | solution.py:127
  86.5 13.1 %copy-start.2 = (bf16[768,128]{1,0:T(8,128)(2,1)S(1)}, bf16[768,128]{1,0:T(8,128)(2,1)}, u32[]{:S(2)}) copy-start(bf16[768,128]{1,0:T(8,128)(2,1)} %get-tuple-element.52) | copy-start | bytes 589828
  95.7 19.2 %collective-permute-start.15 = (bf16[1,2,128,128]{3,2,1,0:T(8,128)(2,1)S(1)}, bf16[1,2,128,128]{3,2,1,0:T(8,128)(2,1)S(1)}, u32[]{:S(2)}, u32[]{:S(2)}) collective-permute-start(bf16[1,2,128,128]{3,2,1,0:T(8,128)(2,1)S(1)} %get-tuple-element.49), channel_id=1, source_target_pairs={{0,8},{4,12},{1,9},{5,13},{2,10},{6,14},{3,11},{7,15},{16,24},{20,... | collective-permute-start | bytes 196616 | tf_op jit(solution)/shard_map/ppermute | solution.py:496
  99.0 28.5 %collective-permute-start.16 = (bf16[768,128]{1,0:T(8,128)(2,1)S(1)}, bf16[768,128]{1,0:T(8,128)(2,1)S(1)}, u32[]{:S(2)}, u32[]{:S(2)}) collective-permute-start(bf16[768,128]{1,0:T(8,128)(2,1)S(1)} %get-tuple-element.61.refs_13_), channel_id=1, source_target_pairs={{0,8},{4,12},{8,0},{12,4},{1,9},{5,13},{9,1},{13,5},{2,10},{6,14},... | collective-permute-start | bytes 589832 | tf_op jit(solution)/shard_map/ppermute | solution.py:127
  99.6 27.9 %collective-permute-start.17 = (bf16[768,128]{1,0:T(8,128)(2,1)S(1)}, bf16[768,128]{1,0:T(8,128)(2,1)S(1)}, u32[]{:S(2)}, u32[]{:S(2)}) collective-permute-start(bf16[768,128]{1,0:T(8,128)(2,1)S(1)} %copy-done.2), channel_id=1, source_target_pairs={{0,12},{4,8},{8,4},{12,0},{1,13},{5,9},{9,5},{13,1},{2,14},{6,10},... | collective-permute-start | bytes 589832 | tf_op jit(solution)/shard_map/ppermute | solution.py:127
  103.7 11.2 %copy-start = (bf16[512,3072]{1,0:T(8,128)(2,1)S(1)}, bf16[512,3072]{1,0:T(8,128)(2,1)}, u32[]{:S(2)}) copy-start(bf16[512,3072]{1,0:T(8,128)(2,1)} %refs_0_.11) | copy-start | bytes 9437188
  113.0 14.2 %collective-permute-start.18 = (bf16[1,2,128,128]{3,2,1,0:T(8,128)(2,1)S(1)}, bf16[1,2,128,128]{3,2,1,0:T(8,128)(2,1)S(1)}, u32[]{:S(2)}, u32[]{:S(2)}) collective-permute-start(bf16[1,2,128,128]{3,2,1,0:T(8,128)(2,1)S(1)} %get-tuple-element.59), channel_id=1, source_target_pairs={{0,8},{4,12},{1,9},{5,13},{2,10},{6,14},{3,11},{7,15},{16,24},{20,... | collective-permute-start | bytes 196616 | tf_op jit(solution)/shard_map/ppermute | solution.py:496
  124.0 14.4 %collective-permute-start.19 = (bf16[512,128]{1,0:T(8,128)(2,1)S(1)}, bf16[512,128]{1,0:T(8,128)(2,1)S(1)}, u32[]{:S(2)}, u32[]{:S(2)}) collective-permute-start(bf16[512,128]{1,0:T(8,128)(2,1)S(1)} %get-tuple-element.62), channel_id=1, source_target_pairs={{0,4},{4,0},{8,12},{12,8},{1,5},{5,1},{9,13},{13,9},{2,6},{6,2},{1... | collective-permute-start | bytes 393224 | tf_op jit(solution)/shard_map/ppermute | solution.py:127
  125.7 16.6 %collective-permute-start.21 = (bf16[512,128]{1,0:T(8,128)(2,1)S(1)}, bf16[512,128]{1,0:T(8,128)(2,1)S(1)}, u32[]{:S(2)}, u32[]{:S(2)}) collective-permute-start(bf16[512,128]{1,0:T(8,128)(2,1)S(1)} %get-tuple-element.63), channel_id=1, source_target_pairs={{0,16},{16,0},{1,17},{17,1},{2,18},{18,2},{3,19},{19,3},{4,20},{20... | collective-permute-start | bytes 393224 | tf_op jit(solution)/shard_map/ppermute | solution.py:127
  127.2 15.1 %collective-permute-start.23 = (bf16[512,128]{1,0:T(8,128)(2,1)S(1)}, bf16[512,128]{1,0:T(8,128)(2,1)S(1)}, u32[]{:S(2)}, u32[]{:S(2)}) collective-permute-start(bf16[512,128]{1,0:T(8,128)(2,1)S(1)} %get-tuple-element.65), channel_id=1, source_target_pairs={{0,20},{4,16},{8,28},{12,24},{16,4},{20,0},{24,12},{28,8},{1,21},{... | collective-permute-start | bytes 393224 | tf_op jit(solution)/shard_map/ppermute | solution.py:535
  135.2 7.1 %collective-permute-start.20 = (bf16[512,128]{1,0:T(8,128)(2,1)S(1)}, bf16[512,128]{1,0:T(8,128)(2,1)S(1)}, u32[]{:S(2)}, u32[]{:S(2)}) collective-permute-start(bf16[512,128]{1,0:T(8,128)(2,1)S(1)} %get-tuple-element.60), channel_id=1, source_target_pairs={{0,4},{4,0},{8,12},{12,8},{1,5},{5,1},{9,13},{13,9},{2,6},{6,2},{1... | collective-permute-start | bytes 393224 | tf_op jit(solution)/shard_map/ppermute | solution.py:127
  136.8 5.5 %collective-permute-start.22 = (bf16[512,128]{1,0:T(8,128)(2,1)S(1)}, bf16[512,128]{1,0:T(8,128)(2,1)S(1)}, u32[]{:S(2)}, u32[]{:S(2)}) collective-permute-start(bf16[512,128]{1,0:T(8,128)(2,1)S(1)} %get-tuple-element.64), channel_id=1, source_target_pairs={{0,16},{16,0},{1,17},{17,1},{2,18},{18,2},{3,19},{19,3},{4,20},{20... | collective-permute-start | bytes 393224 | tf_op jit(solution)/shard_map/ppermute | solution.py:127
  138.4 5.9 %collective-permute-start.24 = (bf16[512,128]{1,0:T(8,128)(2,1)S(1)}, bf16[512,128]{1,0:T(8,128)(2,1)S(1)}, u32[]{:S(2)}, u32[]{:S(2)}) collective-permute-start(bf16[512,128]{1,0:T(8,128)(2,1)S(1)} %get-tuple-element.66), channel_id=1, source_target_pairs={{0,20},{4,16},{8,28},{12,24},{16,4},{20,0},{24,12},{28,8},{1,21},{... | collective-permute-start | bytes 393224 | tf_op jit(solution)/shard_map/ppermute | solution.py:535

commit v8 on v7

--- a/solution.py
+++ b/solution.py
@@ -433,7 +433,7 @@
     both_core = xor_permute(from_both, mesh, "head", 1)
     (from_both,) = after((from_both,), both_core, ctx_plane)
     both_plane = xor_permute(from_both, mesh, "fsdp", 1)
-    (both_plane,) = after((both_plane,), groups_plane)
+
     token_sets = [tokens]
     token_sets += [from_ctx, ctx_plane, ctx_core, xor_permute(ctx_plane, mesh, "head", 1)]
     for array in (from_groups, groups_plane):

time: 147 us -> 146 us (level)
  transfers between devices with their start and end apart: 26 -> 26, of which waited for: 7 -> 8; matrix products, arithmetic and copies ran while one was open for 4% -> 4% of each run, Pallas kernels for 29% -> 29%
where the time goes in v8:
time: 146 us; the launch traced here: 145 us
  waiting for transfers between devices  55.9 us (38%)
  Pallas kernels  44.3 us (30%)
  starting transfers between devices  37.2 us (25%)
  local copies, waits for them, and re-layouts  6.23 us (4%)
    ppermute x21, waiting for transfers between devices, xor_permute(): lax.ppermute(array, axis, [(at, at ^ flip) for at in range(mesh.shape[axi...  54.1 us
    ppermute x21, starting transfers between devices, xor_permute(): lax.ppermute(array, axis, [(at, at ^ flip) for at in range(mesh.shape[axi...  26.5 us
    pallas_call x3, Pallas kernels, query(): pl.pallas_call(functools.partial(query_kernel, chosen, 0, slice(head * si...  20.2 us
    pallas_call x2, Pallas kernels, spread_body(): pl.pallas_call(functools.partial(key_value_kernel, head, heads, size, fli...  18.4 us
    ppermute x2, starting transfers between devices, spread_body(): lax.ppermute(pair_state, 'ctx', [(at, at + 2) for at in range(flips - 2)])  5.13 us
    all_to_all x1, starting transfers between devices, spread_body(): key_value = lax.all_to_all(packed, 'ctx', 0, 0)  4.65 us
    dynamic_slice x2, local copies, waits for them, and re-layouts, query_block(): lax.dynamic_slice(query_weight, (0, (owner * heads + head) * size), (dept...  3.85 us
    pallas_call x1, Pallas kernels, spread_body(): pl.pallas_call(functools.partial(pack_kernel, heads, size), grid_spec=plt...  3.84 us
  transfers between devices with their start and end apart: 26, of which 8 were waited for; matrix products, arithmetic and copies ran while one was open for 4% of the time, Pallas kernels for 29%

profile of v8, /device:TPU:0, one launch (start us, length us, event | category | flops | bytes accessed | tf_op | source)
XLA Modules:
  0.0 145.3 jit_solution(4336426985633966468)
XLA Ops:
  0.0 0.7 reduce-precision_convert_fusion.1
  0.7 1.2 constant_dynamic-slice_fusion.6
  1.9 0.1 pad_maximum_fusion
  2.0 3.1 %collective-permute-start = (bf16[536,768]{1,0:T(8,128)(2,1)S(1)}, bf16[536,768]{1,0:T(8,128)(2,1)S(1)}, u32[]{:S(2)}, u32[]{:S(2)}) collective-permute-start(bf16[536,768]{1,0:T(8,128)(2,1)S(1)} %pad_maximum_fusion), channel_id=1, source_target_pairs={{0,4},{4,0},{8,12},{12,8},{1,5},{5,1},{9,13},{13,9},{2,6},{6,2},{1... | collective-permute-start | bytes 2469896 | tf_op jit(solution)/shard_map/ppermute | solution.py:127
  5.1 0.7 pad_add_fusion.places
  5.7 3.8 %pack.1 = bf16[4,768,512]{2,1,0:T(8,128)(2,1)} custom-call(s32[4]{0:T(128)} %pad_add_fusion.places, bf16[768,1024]{1,0:T(8,128)(2,1)} %refs_2_.1, bf16[768,1024]{1,0:T(8,128)(2,1)} %refs_3_.1, bf16[768,1024]{1,0:T(8,128)(2,1)} %refs_2_.1, bf16[768,1024]{1,0:T(8,128)(2,1)} %refs_3_.1), custom_call_target="tpu_custom_call" | custom-call | bytes 6291456 | tf_op jit(solution)/shard_map/pack/pallas_call | solution.py:409
  9.6 4.7 %all-to-all-start = ((bf16[4,768,512]{2,1,0:T(8,128)(2,1)}), bf16[4,768,512]{2,1,0:T(8,128)(2,1)}, u32[]{:S(2)}, u32[]{:S(2)}) async-start(bf16[4,768,512]{2,1,0:T(8,128)(2,1)} %pack.1), calls=%async_computation | async-start | bytes 6291456 | tf_op jit(solution)/shard_map/all_to_all | solution.py:422
  14.2 1.6 %collective-permute-start.2 = (bf16[536,768]{1,0:T(8,128)(2,1)S(1)}, bf16[536,768]{1,0:T(8,128)(2,1)S(1)}, u32[]{:S(2)}, u32[]{:S(2)}) collective-permute-start(bf16[536,768]{1,0:T(8,128)(2,1)S(1)} %pad_maximum_fusion), channel_id=1, source_target_pairs={{0,16},{16,0},{1,17},{17,1},{2,18},{18,2},{3,19},{19,3},{4,20},{20... | collective-permute-start | bytes 2469896 | tf_op jit(solution)/shard_map/ppermute | solution.py:127
  15.8 8.4 %collective-permute-done.refs_1_ = bf16[536,768]{1,0:T(8,128)(2,1)S(1)} collective-permute-done((bf16[536,768]{1,0:T(8,128)(2,1)S(1)}, bf16[536,768]{1,0:T(8,128)(2,1)S(1)}, u32[]{:S(2)}, u32[]{:S(2)}) %collective-permute-start) | collective-permute-done | bytes 823328 | tf_op jit(solution)/shard_map/ppermute | solution.py:127
  24.2 0.0 collective-permute-start.1
  24.2 9.9 %collective-permute-done.2.refs_5_ = bf16[536,768]{1,0:T(8,128)(2,1)S(1)} collective-permute-done((bf16[536,768]{1,0:T(8,128)(2,1)S(1)}, bf16[536,768]{1,0:T(8,128)(2,1)S(1)}, u32[]{:S(2)}, u32[]{:S(2)}) %collective-permute-start.2) | collective-permute-done | bytes 823328 | tf_op jit(solution)/shard_map/ppermute | solution.py:127
  34.1 0.0 collective-permute-done.1.refs_3_
  34.1 1.5 %collective-permute-start.8 = (bf16[536,768]{1,0:T(8,128)(2,1)S(1)}, bf16[536,768]{1,0:T(8,128)(2,1)S(1)}, u32[]{:S(2)}, u32[]{:S(2)}) collective-permute-start(bf16[536,768]{1,0:T(8,128)(2,1)S(1)} %collective-permute-done.refs_1_), channel_id=1, source_target_pairs={{0,16},{16,0},{1,17},{17,1},{2,18},{18,2},{3,19},{19,3},{4,20},{20... | collective-permute-start | bytes 2469896 | tf_op jit(solution)/shard_map/ppermute | solution.py:127
  35.6 1.5 %collective-permute-start.3 = (bf16[536,768]{1,0:T(8,128)(2,1)S(1)}, bf16[536,768]{1,0:T(8,128)(2,1)}, u32[]{:S(2)}, u32[]{:S(2)}) collective-permute-start(bf16[536,768]{1,0:T(8,128)(2,1)S(1)} %collective-permute-done.refs_1_), channel_id=1, source_target_pairs={{0,2},{2,0},{1,3},{3,1},{4,6},{6,4},{5,7},{7,5},{8,10},{10,8},{9,1... | collective-permute-start | bytes 2469896 | tf_op jit(solution)/shard_map/ppermute | solution.py:127
  37.1 16.0 %collective-permute-done.8.refs_9_ = bf16[536,768]{1,0:T(8,128)(2,1)S(1)} collective-permute-done((bf16[536,768]{1,0:T(8,128)(2,1)S(1)}, bf16[536,768]{1,0:T(8,128)(2,1)S(1)}, u32[]{:S(2)}, u32[]{:S(2)}) %collective-permute-start.8) | collective-permute-done | bytes 823328 | tf_op jit(solution)/shard_map/ppermute | solution.py:127
  53.1 0.0 collective-permute-start.9
  53.1 1.3 collective-permute-done.3.refs_2_
  54.4 1.1 collective-permute-done.9.refs_11_
  55.6 1.5 %collective-permute-start.10 = (bf16[536,768]{1,0:T(8,128)(2,1)S(1)}, bf16[536,768]{1,0:T(8,128)(2,1)}, u32[]{:S(2)}, u32[]{:S(2)}) collective-permute-start(bf16[536,768]{1,0:T(8,128)(2,1)S(1)} %collective-permute-done.8.refs_9_), channel_id=1, source_target_pairs={{0,2},{2,0},{1,3},{3,1},{4,6},{6,4},{5,7},{7,5},{8,10},{10,8},{9,1... | collective-permute-start | bytes 2469896 | tf_op jit(solution)/shard_map/ppermute | solution.py:127
  57.1 1.2 constant_dynamic-slice_fusion.5
  58.2 1.6 %collective-permute-start.5 = (bf16[512,768]{1,0:T(8,128)(2,1)S(1)}, bf16[512,768]{1,0:T(8,128)(2,1)}, u32[]{:S(2)}, u32[]{:S(2)}) collective-permute-start(bf16[512,768]{1,0:T(8,128)(2,1)S(1)} %constant_dynamic-slice_fusion.5), channel_id=1, source_target_pairs={{0,16},{16,0},{1,17},{17,1},{2,18},{18,2},{3,19},{19,3},{4,20},{20... | collective-permute-start | bytes 2359304 | tf_op jit(solution)/shard_map/ppermute | solution.py:127
  59.8 0.0 collective-permute-start.6
  59.8 0.5 collective-permute-start.4
  60.3 15.7 %collective-permute-done.10.refs_10_ = bf16[536,768]{1,0:T(8,128)(2,1)} collective-permute-done((bf16[536,768]{1,0:T(8,128)(2,1)S(1)}, bf16[536,768]{1,0:T(8,128)(2,1)}, u32[]{:S(2)}, u32[]{:S(2)}) %collective-permute-start.10) | collective-permute-done | bytes 823328 | tf_op jit(solution)/shard_map/ppermute | solution.py:127
  76.0 0.0 collective-permute-start.11
  76.0 1.7 %collective-permute-done.5.refs_6_ = bf16[512,768]{1,0:T(8,128)(2,1)} collective-permute-done((bf16[512,768]{1,0:T(8,128)(2,1)S(1)}, bf16[512,768]{1,0:T(8,128)(2,1)}, u32[]{:S(2)}, u32[]{:S(2)}) %collective-permute-start.5) | collective-permute-done | bytes 786464 | tf_op jit(solution)/shard_map/ppermute | solution.py:127
  77.7 0.0 collective-permute-start.7
  77.7 1.8 %constant_dynamic-slice_fusion.3 = bf16[768,256]{1,0:T(8,128)(2,1)} fusion(bf16[768,1024]{1,0:T(8,128)(2,1)} %param.6, s32[]{:T(128)S(6)} %select_n.30), kind=kLoop, calls=%fused_computation.16 | loop fusion | bytes 786436 | tf_op jit(solution)/shard_map/dynamic_slice | solution.py:444
  79.5 2.1 %constant_dynamic-slice_fusion = (bf16[768,128]{1,0:T(8,128)(2,1)}, bf16[768,128]{1,0:T(8,128)(2,1)}, bf16[768,128]{1,0:T(8,128)(2,1)}, bf16[768,128]{1,0:T(8,128)(2,1)S(1)}) fusion(bf16[768,1024]{1,0:T(8,128)(2,1)} %param.6, s32[]{:T(128)S(6)} %select_n.32, s32[]{:T(128)S(6)} %select_n.30, s32[]{:T(128)S(6)} %select_n.29, s32[]{:T(128)S(6)} %select_n.31), kind=kLoop, calls=%fused_computation.13 | loop fusion | bytes 1572880 | tf_op jit(solution)/shard_map/dynamic_slice | solution.py:444
  81.6 1.3 collective-permute-start.12
  82.9 0.0 collective-permute-done.6.refs_7_
  82.9 2.4 %collective-permute-start.13 = (bf16[768,128]{1,0:T(8,128)(2,1)}, bf16[768,128]{1,0:T(8,128)(2,1)}, u32[]{:S(2)}, u32[]{:S(2)}) collective-permute-start(bf16[768,128]{1,0:T(8,128)(2,1)} %get-tuple-element.39.refs_13_), channel_id=1, source_target_pairs={{0,8},{4,12},{8,0},{12,4},{1,9},{5,13},{9,1},{13,5},{2,10},{6,14},... | collective-permute-start | bytes 589832 | tf_op jit(solution)/shard_map/ppermute | solution.py:127
  85.3 0.0 collective-permute-done.7.refs_8_
  85.3 0.7 collective-permute-start.14
  86.0 0.0 collective-permute-done.4.refs_4_
  86.0 0.0 all-to-all-done.refs_14_
  86.0 0.0 collective-permute-done.11.refs_12_
  86.0 9.1 %key_value.2 = (bf16[4,512,128]{2,1,0:T(8,128)(2,1)S(1)}, bf16[4,512,128]{2,1,0:T(8,128)(2,1)S(1)}, f32[1,4,4,128,128]{4,3,2,1,0:T(8,128)S(1)}, f32[4,1,512]{2,1...) custom-call(s32[4]{0:T(128)S(1)} %copy-done.1, ...), custom_call_target="tpu_custom_call" | custom-call | flops 3221225472 | bytes 14155776 | tf_op jit(solution)/shard_map/key_value/pallas_call | solution.py:471
  95.2 3.4 %collective-permute-start.15 = (bf16[1,2,128,128]{3,2,1,0:T(8,128)(2,1)S(1)}, bf16[1,2,128,128]{3,2,1,0:T(8,128)(2,1)S(1)}, u32[]{:S(2)}, u32[]{:S(2)}) collective-permute-start(bf16[1,2,128,128]{3,2,1,0:T(8,128)(2,1)S(1)} %get-tuple-element.47), channel_id=1, source_target_pairs={{0,8},{4,12},{1,9},{5,13},{2,10},{6,14},{3,11},{7,15},{16,24},{20,... | collective-permute-start | bytes 196616 | tf_op jit(solution)/shard_map/ppermute | solution.py:496
  98.5 0.0 collective-permute-done.12.refs_14_
  98.5 0.5 collective-permute-start.16
  99.0 4.2 %collective-permute-start.17 = (bf16[768,128]{1,0:T(8,128)(2,1)S(1)}, bf16[768,128]{1,0:T(8,128)(2,1)S(1)}, u32[]{:S(2)}, u32[]{:S(2)}) collective-permute-start(bf16[768,128]{1,0:T(8,128)(2,1)S(1)} %copy-done.2), channel_id=1, source_target_pairs={{0,12},{4,8},{8,4},{12,0},{1,13},{5,9},{9,5},{13,1},{2,14},{6,10},... | collective-permute-start | bytes 589832 | tf_op jit(solution)/shard_map/ppermute | solution.py:127
  103.2 9.3 %key_value.3 = (bf16[4,512,128]{2,1,0:T(8,128)(2,1)S(1)}, bf16[4,512,128]{2,1,0:T(8,128)(2,1)S(1)}, f32[1,4,4,128,128]{4,3,2,1,0:T(8,128)S(1)}, f32[4,1,512]{2,1...) custom-call(s32[4]{0:T(128)S(1)} %copy-done.1, ...), custom_call_target="tpu_custom_call" | custom-call | flops 3221225472 | bytes 14155776 | tf_op jit(solution)/shard_map/key_value/pallas_call | solution.py:471
  112.5 0.0 collective-permute-done.13.refs_15_
  112.5 1.8 %collective-permute-start.18 = (bf16[1,2,128,128]{3,2,1,0:T(8,128)(2,1)S(1)}, bf16[1,2,128,128]{3,2,1,0:T(8,128)(2,1)S(1)}, u32[]{:S(2)}, u32[]{:S(2)}) collective-permute-start(bf16[1,2,128,128]{3,2,1,0:T(8,128)(2,1)S(1)} %get-tuple-element.57), channel_id=1, source_target_pairs={{0,8},{4,12},{1,9},{5,13},{2,10},{6,14},{3,11},{7,15},{16,24},{20,... | collective-permute-start | bytes 196616 | tf_op jit(solution)/shard_map/ppermute | solution.py:496
  114.3 0.0 collective-permute-done.14.refs_16_
  114.3 0.0 collective-permute-done.15.refs_23_
  114.3 9.0 %query.3 = (bf16[512,128]{1,0:T(8,128)(2,1)S(1)}, bf16[512,128]{1,0:T(8,128)(2,1)S(1)}, bf16[512,128]{1,0:T(8,128)(2,1)S(1)}, bf16[512,128]{1,0:T(8,128)(2,1)S(1)}) custom-call(s32[4]{0:T(128)S(1)} %copy-done.1, bf16[512,3072]{1,0:T(8,128)(2,1)S(1)} %copy-done, bf16[536,768]{1,0:T(8,128)(2,1)S(1)} %collective-permute-done.refs_1_, ...), custom_call_target="tpu_custom_call" | custom-call | flops 1879048192 | bytes 13369344 | tf_op jit(solution)/shard_map/query/pallas_call | solution.py:506
  123.4 1.6 %collective-permute-start.19 = (bf16[512,128]{1,0:T(8,128)(2,1)S(1)}, bf16[512,128]{1,0:T(8,128)(2,1)S(1)}, u32[]{:S(2)}, u32[]{:S(2)}) collective-permute-start(bf16[512,128]{1,0:T(8,128)(2,1)S(1)} %get-tuple-element.60), channel_id=1, source_target_pairs={{0,4},{4,0},{8,12},{12,8},{1,5},{5,1},{9,13},{13,9},{2,6},{6,2},{1... | collective-permute-start | bytes 393224 | tf_op jit(solution)/shard_map/ppermute | solution.py:127
  125.0 1.5 %collective-permute-start.21 = (bf16[512,128]{1,0:T(8,128)(2,1)S(1)}, bf16[512,128]{1,0:T(8,128)(2,1)S(1)}, u32[]{:S(2)}, u32[]{:S(2)}) collective-permute-start(bf16[512,128]{1,0:T(8,128)(2,1)S(1)} %get-tuple-element.61), channel_id=1, source_target_pairs={{0,16},{16,0},{1,17},{17,1},{2,18},{18,2},{3,19},{19,3},{4,20},{20... | collective-permute-start | bytes 393224 | tf_op jit(solution)/shard_map/ppermute | solution.py:127
  126.5 0.0 collective-permute-done.18.refs_23_
  126.5 0.4 collective-permute-start.23
  126.9 0.0 collective-permute-done.16.refs_15_
  126.9 7.7 %query.4 = (bf16[512,128]{1,0:T(8,128)(2,1)S(1)}, bf16[512,128]{1,0:T(8,128)(2,1)S(1)}, bf16[512,128]{1,0:T(8,128)(2,1)S(1)}) custom-call(s32[4]{0:T(128)S(1)} %copy-done.1, bf16[512,3072]{1,0:T(8,128)(2,1)S(1)} %copy-done, bf16[536,768]{1,0:T(8,128)(2,1)S(1)} %collective-permute-done.refs_1_, bf16[536,768]{1,0:T(8,128)(2,1)} %collective-permute-done.3.refs_2_, ...), custom_call_target="tpu_custom_call" | custom-call | flops 1409286144 | bytes 10223616 | tf_op jit(solution)/shard_map/query/pallas_call | solution.py:506
  134.6 1.5 %collective-permute-start.20 = (bf16[512,128]{1,0:T(8,128)(2,1)S(1)}, bf16[512,128]{1,0:T(8,128)(2,1)S(1)}, u32[]{:S(2)}, u32[]{:S(2)}) collective-permute-start(bf16[512,128]{1,0:T(8,128)(2,1)S(1)} %get-tuple-element.58), channel_id=1, source_target_pairs={{0,4},{4,0},{8,12},{12,8},{1,5},{5,1},{9,13},{13,9},{2,6},{6,2},{1... | collective-permute-start | bytes 393224 | tf_op jit(solution)/shard_map/ppermute | solution.py:127
  136.1 1.5 %collective-permute-start.22 = (bf16[512,128]{1,0:T(8,128)(2,1)S(1)}, bf16[512,128]{1,0:T(8,128)(2,1)S(1)}, u32[]{:S(2)}, u32[]{:S(2)}) collective-permute-start(bf16[512,128]{1,0:T(8,128)(2,1)S(1)} %get-tuple-element.62), channel_id=1, source_target_pairs={{0,16},{16,0},{1,17},{17,1},{2,18},{18,2},{3,19},{19,3},{4,20},{20... | collective-permute-start | bytes 393224 | tf_op jit(solution)/shard_map/ppermute | solution.py:127
  137.7 0.0 collective-permute-done.19.refs_2_
  137.7 0.5 collective-permute-start.24
  138.2 3.5 %query.5.refs_1_ = bf16[512,128]{1,0:T(8,128)(2,1)S(1)} custom-call(s32[4]{0:T(128)S(1)} %copy-done.1, bf16[512,3072]{1,0:T(8,128)(2,1)S(1)} %copy-done, bf16[536,768]{1,0:T(8,128)(2,1)S(1)} %collective-permute-done.refs_1_, bf16[536,768]{1,0:T(8,128)(2,1)} %collective-permute-done.3.refs_2_, bf16[536,768]{1,0:T(8,128)(2,1)S(1)} %collective-permute-done.1.refs_3_, ...), custom_call_target="tpu_custom_call" | custom-call | flops 469762048 | bytes 3932160 | tf_op jit(solution)/shard_map/query/pallas_call | solution.py:506
  141.7 0.0 collective-permute-done.21.refs_4_
  141.7 0.0 collective-permute-done.23.refs_6_
  141.7 0.0 collective-permute-done.22.refs_5_
  141.8 1.8 %collective-permute-done.24.refs_7_ = bf16[512,128]{1,0:T(8,128)(2,1)S(1)} collective-permute-done((bf16[512,128]{1,0:T(8,128)(2,1)S(1)}, bf16[512,128]{1,0:T(8,128)(2,1)S(1)}, u32[]{:S(2)}, u32[]{:S(2)}) %collective-permute-start.24) | collective-permute-done | bytes 131104 | tf_op jit(solution)/shard_map/ppermute | solution.py:535
  143.5 1.8 %merge.1 = bf16[512,1024]{1,0:T(8,128)(2,1)} custom-call(s32[4]{0:T(128)S(1)} %copy-done.1, bf16[512,128]{1,0:T(8,128)(2,1)S(1)} %get-tuple-element.48.refs_0_, bf16[512,128]{1,0:T(8,128)(2,1)S(1)} %query.5.refs_1_, bf16[512,128]{1,0:T(8,128)(2,1)S(1)} %collective-permute-done.19.refs_2_, bf16[512,128]{1,0:T(8,128)(2,1)S(1)} %collective-permute-done.20.refs_3_, ...), custom_call_target="tpu_custom_call" | custom-call | tf_op jit(solution)/shard_map/merge/pallas_call | solution.py:538
  (9 shorter events, 0.0 us)
Async XLA Ops:
  2.0 22.2 %collective-permute-start = (bf16[536,768]{1,0:T(8,128)(2,1)S(1)}, bf16[536,768]{1,0:T(8,128)(2,1)S(1)}, u32[]{:S(2)}, u32[]{:S(2)}) collective-permute-start(bf16[536,768]{1,0:T(8,128)(2,1)S(1)} %pad_maximum_fusion), channel_id=1, source_target_pairs={{0,4},{4,0},{8,12},{12,8},{1,5},{5,1},{9,13},{13,9},{2,6},{6,2},{1... | collective-permute-start | bytes 2469896 | tf_op jit(solution)/shard_map/ppermute | solution.py:127
  9.6 76.4 %all-to-all-start = ((bf16[4,768,512]{2,1,0:T(8,128)(2,1)}), bf16[4,768,512]{2,1,0:T(8,128)(2,1)}, u32[]{:S(2)}, u32[]{:S(2)}) async-start(bf16[4,768,512]{2,1,0:T(8,128)(2,1)} %pack.1), calls=%async_computation | async-start | bytes 6291456 | tf_op jit(solution)/shard_map/all_to_all | solution.py:422
  14.2 19.9 %collective-permute-start.2 = (bf16[536,768]{1,0:T(8,128)(2,1)S(1)}, bf16[536,768]{1,0:T(8,128)(2,1)S(1)}, u32[]{:S(2)}, u32[]{:S(2)}) collective-permute-start(bf16[536,768]{1,0:T(8,128)(2,1)S(1)} %pad_maximum_fusion), channel_id=1, source_target_pairs={{0,16},{16,0},{1,17},{17,1},{2,18},{18,2},{3,19},{19,3},{4,20},{20... | collective-permute-start | bytes 2469896 | tf_op jit(solution)/shard_map/ppermute | solution.py:127
  24.2 9.9 %collective-permute-start.1 = (bf16[536,768]{1,0:T(8,128)(2,1)S(1)}, bf16[536,768]{1,0:T(8,128)(2,1)S(1)}, u32[]{:S(2)}, u32[]{:S(2)}) collective-permute-start(bf16[536,768]{1,0:T(8,128)(2,1)S(1)} %collective-permute-done.refs_1_), channel_id=1, source_target_pairs={{0,1},{1,0},{2,3},{3,2},{4,5},{5,4},{6,7},{7,6},{8,9},{9,8},{10,11... | collective-permute-start | bytes 2469896 | tf_op jit(solution)/shard_map/ppermute | solution.py:127
  34.1 19.0 %collective-permute-start.8 = (bf16[536,768]{1,0:T(8,128)(2,1)S(1)}, bf16[536,768]{1,0:T(8,128)(2,1)S(1)}, u32[]{:S(2)}, u32[]{:S(2)}) collective-permute-start(bf16[536,768]{1,0:T(8,128)(2,1)S(1)} %collective-permute-done.refs_1_), channel_id=1, source_target_pairs={{0,16},{16,0},{1,17},{17,1},{2,18},{18,2},{3,19},{19,3},{4,20},{20... | collective-permute-start | bytes 2469896 | tf_op jit(solution)/shard_map/ppermute | solution.py:127
  35.6 18.8 %collective-permute-start.3 = (bf16[536,768]{1,0:T(8,128)(2,1)S(1)}, bf16[536,768]{1,0:T(8,128)(2,1)}, u32[]{:S(2)}, u32[]{:S(2)}) collective-permute-start(bf16[536,768]{1,0:T(8,128)(2,1)S(1)} %collective-permute-done.refs_1_), channel_id=1, source_target_pairs={{0,2},{2,0},{1,3},{3,1},{4,6},{6,4},{5,7},{7,5},{8,10},{10,8},{9,1... | collective-permute-start | bytes 2469896 | tf_op jit(solution)/shard_map/ppermute | solution.py:127
  53.1 2.5 %collective-permute-start.9 = (bf16[536,768]{1,0:T(8,128)(2,1)S(1)}, bf16[536,768]{1,0:T(8,128)(2,1)}, u32[]{:S(2)}, u32[]{:S(2)}) collective-permute-start(bf16[536,768]{1,0:T(8,128)(2,1)S(1)} %collective-permute-done.8.refs_9_), channel_id=1, source_target_pairs={{0,1},{1,0},{2,3},{3,2},{4,5},{5,4},{6,7},{7,6},{8,9},{9,8},{10,11... | collective-permute-start | bytes 2469896 | tf_op jit(solution)/shard_map/ppermute | solution.py:127
  53.1 32.9 %copy-start.1 = (s32[4]{0:T(128)S(1)}, s32[4]{0:T(128)}, u32[]{:S(2)}) copy-start(s32[4]{0:T(128)} %pad_add_fusion.places) | copy-start | bytes 52
  55.6 20.5 %collective-permute-start.10 = (bf16[536,768]{1,0:T(8,128)(2,1)S(1)}, bf16[536,768]{1,0:T(8,128)(2,1)}, u32[]{:S(2)}, u32[]{:S(2)}) collective-permute-start(bf16[536,768]{1,0:T(8,128)(2,1)S(1)} %collective-permute-done.8.refs_9_), channel_id=1, source_target_pairs={{0,2},{2,0},{1,3},{3,1},{4,6},{6,4},{5,7},{7,5},{8,10},{10,8},{9,1... | collective-permute-start | bytes 2469896 | tf_op jit(solution)/shard_map/ppermute | solution.py:127
  58.2 19.5 %collective-permute-start.5 = (bf16[512,768]{1,0:T(8,128)(2,1)S(1)}, bf16[512,768]{1,0:T(8,128)(2,1)}, u32[]{:S(2)}, u32[]{:S(2)}) collective-permute-start(bf16[512,768]{1,0:T(8,128)(2,1)S(1)} %constant_dynamic-slice_fusion.5), channel_id=1, source_target_pairs={{0,16},{16,0},{1,17},{17,1},{2,18},{18,2},{3,19},{19,3},{4,20},{20... | collective-permute-start | bytes 2359304 | tf_op jit(solution)/shard_map/ppermute | solution.py:127
  59.8 23.1 %collective-permute-start.6 = (bf16[536,768]{1,0:T(8,128)(2,1)S(1)}, bf16[536,768]{1,0:T(8,128)(2,1)}, u32[]{:S(2)}, u32[]{:S(2)}) collective-permute-start(bf16[536,768]{1,0:T(8,128)(2,1)S(1)} %collective-permute-done.2.refs_5_), channel_id=1, source_target_pairs={{0,1},{1,0},{2,3},{3,2},{4,5},{5,4},{6,7},{7,6},{8,9},{9,8},{10,11... | collective-permute-start | bytes 2469896 | tf_op jit(solution)/shard_map/ppermute | solution.py:127
  59.8 26.1 %collective-permute-start.4 = (bf16[536,768]{1,0:T(8,128)(2,1)}, bf16[536,768]{1,0:T(8,128)(2,1)}, u32[]{:S(2)}, u32[]{:S(2)}) collective-permute-start(bf16[536,768]{1,0:T(8,128)(2,1)} %collective-permute-done.3.refs_2_), channel_id=1, source_target_pairs={{0,1},{1,0},{2,3},{3,2},{4,5},{5,4},{6,7},{7,6},{8,9},{9,8},{10,11... | collective-permute-start | bytes 2469896 | tf_op jit(solution)/shard_map/ppermute | solution.py:127
  76.0 9.9 %collective-permute-start.11 = (bf16[536,768]{1,0:T(8,128)(2,1)}, bf16[536,768]{1,0:T(8,128)(2,1)}, u32[]{:S(2)}, u32[]{:S(2)}) collective-permute-start(bf16[536,768]{1,0:T(8,128)(2,1)} %collective-permute-done.10.refs_10_), channel_id=1, source_target_pairs={{0,1},{1,0},{2,3},{3,2},{4,5},{5,4},{6,7},{7,6},{8,9},{9,8},{10,11... | collective-permute-start | bytes 2469896 | tf_op jit(solution)/shard_map/ppermute | solution.py:127
  77.7 7.6 %collective-permute-start.7 = (bf16[512,768]{1,0:T(8,128)(2,1)}, bf16[512,768]{1,0:T(8,128)(2,1)}, u32[]{:S(2)}, u32[]{:S(2)}) collective-permute-start(bf16[512,768]{1,0:T(8,128)(2,1)} %collective-permute-done.5.refs_6_), channel_id=1, source_target_pairs={{0,1},{1,0},{2,3},{3,2},{4,5},{5,4},{6,7},{7,6},{8,9},{9,8},{10,11... | collective-permute-start | bytes 2359304 | tf_op jit(solution)/shard_map/ppermute | solution.py:127
  81.6 16.9 %collective-permute-start.12 = (bf16[768,256]{1,0:T(8,128)(2,1)}, bf16[768,256]{1,0:T(8,128)(2,1)}, u32[]{:S(2)}, u32[]{:S(2)}) collective-permute-start(bf16[768,256]{1,0:T(8,128)(2,1)} %constant_dynamic-slice_fusion.3), channel_id=1, source_target_pairs={{0,4},{4,0},{8,12},{12,8},{1,5},{5,1},{9,13},{13,9},{2,6},{6,2},{1... | collective-permute-start | bytes 1179656 | tf_op jit(solution)/shard_map/ppermute | solution.py:127
  82.9 29.6 %collective-permute-start.13 = (bf16[768,128]{1,0:T(8,128)(2,1)}, bf16[768,128]{1,0:T(8,128)(2,1)}, u32[]{:S(2)}, u32[]{:S(2)}) collective-permute-start(bf16[768,128]{1,0:T(8,128)(2,1)} %get-tuple-element.39.refs_13_), channel_id=1, source_target_pairs={{0,8},{4,12},{8,0},{12,4},{1,9},{5,13},{9,1},{13,5},{2,10},{6,14},... | collective-permute-start | bytes 589832 | tf_op jit(solution)/shard_map/ppermute | solution.py:127
  85.3 29.0 %collective-permute-start.14 = (bf16[768,128]{1,0:T(8,128)(2,1)}, bf16[768,128]{1,0:T(8,128)(2,1)}, u32[]{:S(2)}, u32[]{:S(2)}) collective-permute-start(bf16[768,128]{1,0:T(8,128)(2,1)} %get-tuple-element.40), channel_id=1, source_target_pairs={{0,12},{4,8},{8,4},{12,0},{1,13},{5,9},{9,5},{13,1},{2,14},{6,10},... | collective-permute-start | bytes 589832 | tf_op jit(solution)/shard_map/ppermute | solution.py:127
  86.0 13.0 %copy-start.2 = (bf16[768,128]{1,0:T(8,128)(2,1)S(1)}, bf16[768,128]{1,0:T(8,128)(2,1)}, u32[]{:S(2)}) copy-start(bf16[768,128]{1,0:T(8,128)(2,1)} %get-tuple-element.50) | copy-start | bytes 589828
  95.2 19.2 %collective-permute-start.15 = (bf16[1,2,128,128]{3,2,1,0:T(8,128)(2,1)S(1)}, bf16[1,2,128,128]{3,2,1,0:T(8,128)(2,1)S(1)}, u32[]{:S(2)}, u32[]{:S(2)}) collective-permute-start(bf16[1,2,128,128]{3,2,1,0:T(8,128)(2,1)S(1)} %get-tuple-element.47), channel_id=1, source_target_pairs={{0,8},{4,12},{1,9},{5,13},{2,10},{6,14},{3,11},{7,15},{16,24},{20,... | collective-permute-start | bytes 196616 | tf_op jit(solution)/shard_map/ppermute | solution.py:496
  98.5 28.4 %collective-permute-start.16 = (bf16[768,128]{1,0:T(8,128)(2,1)S(1)}, bf16[768,128]{1,0:T(8,128)(2,1)S(1)}, u32[]{:S(2)}, u32[]{:S(2)}) collective-permute-start(bf16[768,128]{1,0:T(8,128)(2,1)S(1)} %get-tuple-element.59.refs_13_), channel_id=1, source_target_pairs={{0,8},{4,12},{8,0},{12,4},{1,9},{5,13},{9,1},{13,5},{2,10},{6,14},... | collective-permute-start | bytes 589832 | tf_op jit(solution)/shard_map/ppermute | solution.py:127
  99.0 27.9 %collective-permute-start.17 = (bf16[768,128]{1,0:T(8,128)(2,1)S(1)}, bf16[768,128]{1,0:T(8,128)(2,1)S(1)}, u32[]{:S(2)}, u32[]{:S(2)}) collective-permute-start(bf16[768,128]{1,0:T(8,128)(2,1)S(1)} %copy-done.2), channel_id=1, source_target_pairs={{0,12},{4,8},{8,4},{12,0},{1,13},{5,9},{9,5},{13,1},{2,14},{6,10},... | collective-permute-start | bytes 589832 | tf_op jit(solution)/shard_map/ppermute | solution.py:127
  103.2 11.1 %copy-start = (bf16[512,3072]{1,0:T(8,128)(2,1)S(1)}, bf16[512,3072]{1,0:T(8,128)(2,1)}, u32[]{:S(2)}) copy-start(bf16[512,3072]{1,0:T(8,128)(2,1)} %refs_0_.11) | copy-start | bytes 9437188
  112.5 14.0 %collective-permute-start.18 = (bf16[1,2,128,128]{3,2,1,0:T(8,128)(2,1)S(1)}, bf16[1,2,128,128]{3,2,1,0:T(8,128)(2,1)S(1)}, u32[]{:S(2)}, u32[]{:S(2)}) collective-permute-start(bf16[1,2,128,128]{3,2,1,0:T(8,128)(2,1)S(1)} %get-tuple-element.57), channel_id=1, source_target_pairs={{0,8},{4,12},{1,9},{5,13},{2,10},{6,14},{3,11},{7,15},{16,24},{20,... | collective-permute-start | bytes 196616 | tf_op jit(solution)/shard_map/ppermute | solution.py:496
  123.4 14.3 %collective-permute-start.19 = (bf16[512,128]{1,0:T(8,128)(2,1)S(1)}, bf16[512,128]{1,0:T(8,128)(2,1)S(1)}, u32[]{:S(2)}, u32[]{:S(2)}) collective-permute-start(bf16[512,128]{1,0:T(8,128)(2,1)S(1)} %get-tuple-element.60), channel_id=1, source_target_pairs={{0,4},{4,0},{8,12},{12,8},{1,5},{5,1},{9,13},{13,9},{2,6},{6,2},{1... | collective-permute-start | bytes 393224 | tf_op jit(solution)/shard_map/ppermute | solution.py:127
  125.0 16.7 %collective-permute-start.21 = (bf16[512,128]{1,0:T(8,128)(2,1)S(1)}, bf16[512,128]{1,0:T(8,128)(2,1)S(1)}, u32[]{:S(2)}, u32[]{:S(2)}) collective-permute-start(bf16[512,128]{1,0:T(8,128)(2,1)S(1)} %get-tuple-element.61), channel_id=1, source_target_pairs={{0,16},{16,0},{1,17},{17,1},{2,18},{18,2},{3,19},{19,3},{4,20},{20... | collective-permute-start | bytes 393224 | tf_op jit(solution)/shard_map/ppermute | solution.py:127
  126.5 15.2 %collective-permute-start.23 = (bf16[512,128]{1,0:T(8,128)(2,1)S(1)}, bf16[512,128]{1,0:T(8,128)(2,1)S(1)}, u32[]{:S(2)}, u32[]{:S(2)}) collective-permute-start(bf16[512,128]{1,0:T(8,128)(2,1)S(1)} %get-tuple-element.63), channel_id=1, source_target_pairs={{0,20},{4,16},{8,28},{12,24},{16,4},{20,0},{24,12},{28,8},{1,21},{... | collective-permute-start | bytes 393224 | tf_op jit(solution)/shard_map/ppermute | solution.py:535
  134.6 7.1 %collective-permute-start.20 = (bf16[512,128]{1,0:T(8,128)(2,1)S(1)}, bf16[512,128]{1,0:T(8,128)(2,1)S(1)}, u32[]{:S(2)}, u32[]{:S(2)}) collective-permute-start(bf16[512,128]{1,0:T(8,128)(2,1)S(1)} %get-tuple-element.58), channel_id=1, source_target_pairs={{0,4},{4,0},{8,12},{12,8},{1,5},{5,1},{9,13},{13,9},{2,6},{6,2},{1... | collective-permute-start | bytes 393224 | tf_op jit(solution)/shard_map/ppermute | solution.py:127
  136.1 5.6 %collective-permute-start.22 = (bf16[512,128]{1,0:T(8,128)(2,1)S(1)}, bf16[512,128]{1,0:T(8,128)(2,1)S(1)}, u32[]{:S(2)}, u32[]{:S(2)}) collective-permute-start(bf16[512,128]{1,0:T(8,128)(2,1)S(1)} %get-tuple-element.62), channel_id=1, source_target_pairs={{0,16},{16,0},{1,17},{17,1},{2,18},{18,2},{3,19},{19,3},{4,20},{20... | collective-permute-start | bytes 393224 | tf_op jit(solution)/shard_map/ppermute | solution.py:127
  137.7 5.9 %collective-permute-start.24 = (bf16[512,128]{1,0:T(8,128)(2,1)S(1)}, bf16[512,128]{1,0:T(8,128)(2,1)S(1)}, u32[]{:S(2)}, u32[]{:S(2)}) collective-permute-start(bf16[512,128]{1,0:T(8,128)(2,1)S(1)} %get-tuple-element.64), channel_id=1, source_target_pairs={{0,20},{4,16},{8,28},{12,24},{16,4},{20,0},{24,12},{28,8},{1,21},{... | collective-permute-start | bytes 393224 | tf_op jit(solution)/shard_map/ppermute | solution.py:535
